TPU v7x, 32 devices: a whole 2x2x4 slice. The times are simulated.
32 devices in a mesh: fsdp: 8 (over y, x, core), tp: 4 (over z).
Axes of the slice: x: 2, y: 2, z: 4, core: 2. Of those that a mesh axis runs over, the one named last changes fastest.
Arguments:
- hidden: bfloat16 [8192, 2048], P(('fsdp', 'tp')), may hold values from -6 to 6
- embed: bfloat16 [8192, 2048], P(('fsdp', 'tp')), may hold values from -6 to 6
- lengths: int32 [8, 3], P('fsdp'), may hold values from 1 to 768, 1024 in all within a row
- attention_norm_gain: bfloat16 [4096], P('fsdp'), may hold values from 0.5 to 1.5
- query_key_value_weight: bfloat16 [4096, 3, 4096], P('fsdp', None, 'tp'), may hold values from -0.09375 to 0.09375
- attention_adapter_down: bfloat16 [4096, 3, 128], P('fsdp'), may hold values from -0.09375 to 0.09375
- attention_adapter_up: bfloat16 [128, 3, 4096], P('fsdp', None, 'tp'), may hold values from -0.25 to 0.25
- attention_output_weight: bfloat16 [4096, 2048], P('tp', 'fsdp'), may hold values from -0.25 to 0.25
- feedforward_norm_gain: bfloat16 [2048], P('fsdp'), may hold values from 0.5 to 1.5
- gate_up_weight: bfloat16 [2048, 2, 8192], P('fsdp', None, 'tp'), may hold values from -0.125 to 0.125
- feedforward_adapter_down: bfloat16 [2048, 128], P('fsdp'), may hold values from -0.125 to 0.125
- feedforward_adapter_up: bfloat16 [128, 2, 8192], P('fsdp', None, 'tp'), may hold values from -0.25 to 0.25
- down_weight: bfloat16 [8192, 2048], P('tp', 'fsdp'), may hold values from -0.0625 to 0.0625
- mixer_norm_gain: bfloat16 [2048], P('fsdp'), may hold values from 0.5 to 1.5
- gate_inner_weight: bfloat16 [2048, 2, 4096], P('fsdp', None, 'tp'), may hold values from -0.125 to 0.125
- state_input_weight: bfloat16 [2048, 2, 64], P('fsdp'), may hold values from -0.125 to 0.125
- step_projection: bfloat16 [2048, 64], P('fsdp', 'tp'), may hold values from -0.125 to 0.125
- inner_conv_taps: bfloat16 [4, 64, 64], P(None, 'tp', 'fsdp'), may hold values from -2 to 2
- state_conv_taps: bfloat16 [4, 2, 64], P(None, None, 'fsdp'), may hold values from -2 to 2
- head_step_bias: float32 [64], P('tp'), may hold values from -6 to -3.5
- decay_log_rate: float32 [64], P('tp'), may hold values from -0.5 to 1
- inner_skip_gains: bfloat16 [64, 64], P('tp', 'fsdp'), may hold values from 0.5 to 1.5
- gated_norm_gain: bfloat16 [64, 64], P('tp', 'fsdp'), may hold values from 0.5 to 1.5
- mixer_output_weight: bfloat16 [4096, 2048], P('tp', 'fsdp'), may hold values from -0.09375 to 0.09375
- output_cotangent: bfloat16 [8192, 2048], P(('fsdp', 'tp')), may hold values from -6 to 6
Outputs:
- out: float32 [8192, 2048], P(('fsdp', 'tp'))
- grad_hidden: float32 [8192, 2048], P(('fsdp', 'tp'))
- grad_embed: float32 [8192, 2048], P(('fsdp', 'tp'))
- attention_gain_gradient: float32 [4096], P(('fsdp', 'tp'))
- grad_w_qkv: float32 [4096, 3, 4096], P('fsdp', None, 'tp')
- attention_down_gradient: float32 [4096, 3, 128], P(('fsdp', 'tp'))
- attention_up_gradient: float32 [128, 3, 4096], P('fsdp', None, 'tp')
- grad_w_o: float32 [4096, 2048], P('tp', 'fsdp')
- grad_mlp_gain: float32 [2048], P('fsdp')
- grad_w_fc1: float32 [2048, 2, 8192], P('fsdp', None, 'tp')
- feedforward_down_gradient: float32 [2048, 128], P('fsdp')
- feedforward_up_gradient: float32 [128, 2, 8192], P('fsdp', None, 'tp')
- grad_w_fc2: float32 [8192, 2048], P('tp', 'fsdp')
- grad_mixer_gain: float32 [2048], P('fsdp')
- grad_w_in_zx: float32 [2048, 2, 4096], P('fsdp', None, 'tp')
- grad_w_in_bc: float32 [2048, 2, 64], P('fsdp')
- grad_w_dt: float32 [2048, 64], P('fsdp', 'tp')
- grad_conv_x: float32 [4, 64, 64], P(None, 'tp', 'fsdp')
- grad_conv_bc: float32 [4, 2, 64], P(None, None, 'fsdp')
- grad_dt_bias: float32 [64], P('tp')
- grad_a_log: float32 [64], P('tp')
- grad_d_skip: float32 [64, 64], P('tp', 'fsdp')
- grad_gate_gain: float32 [64, 64], P('tp', 'fsdp')
- grad_w_out: float32 [4096, 2048], P('tp', 'fsdp')
Inputs may be any that keep to these rules, and one draw needn't show every extreme that they name: Each row holds the lengths of the 3 sequences of one group; a row sums to 1024 and its longest is exactly 768.
All inputs are finite; a program needn't handle non-finite values.
Results may differ from a plain program's by a relative error of at most 0.025.
Values may be sent and summed in bfloat16 or wider, within the bound.
No kernel may reach another device: no remote copies, remote signals or barrier semaphores. Data moves between devices by JAX's collectives and lax.ppermute only.
A program may use at most 320 MiB of HBM per device.

v0:
```python
import math

import jax
import jax.numpy as jnp
from jax import lax
from jax.sharding import PartitionSpec as P

HDA = 128
HD = 64


PRECISE_MODE = lax.Precision.HIGHEST
norm_eps = 1e-05


def batched_product(left, right):
    return jnp.dot(left, right, preferred_element_type=jnp.float32)


def segments_of(lengths_row, count):
    ends = jnp.cumsum(lengths_row)
    starts = ends - lengths_row
    places = jnp.arange(count, dtype=jnp.int32)
    segment = jnp.sum((places[:, None] >= ends[None, :]).astype(jnp.int32), axis=1)
    owners = segment[:, None] == jnp.arange(ends.shape[0], dtype=jnp.int32)[None, :]
    offsets = jnp.sum(jnp.where(owners, starts[None, :], 0), axis=1)
    return (segment, places - offsets)


def rotate(values, position, direction):
    half = values.shape[-1] // 2
    freqs = jnp.exp(
        jnp.arange(half, dtype=jnp.float32) * (-2.0 * math.log(10000.0) / values.shape[-1])
    )
    angles = position.astype(jnp.float32)[:, None] * freqs[None, :]
    cosine = jnp.cos(angles)[:, None, :]
    sine_part = direction * jnp.sin(angles)[:, None, :]
    front = values[..., :half]
    behind = values[..., half:]
    return jnp.concatenate(
        [front * cosine - behind * sine_part, behind * cosine + front * sine_part], axis=-1
    )


def causal_conv(values, taps, segment):
    count = taps.shape[0]
    sequence_length = values.shape[0]
    total = jnp.zeros_like(values)
    for shift_by in range(count):
        moved = jnp.concatenate(
            [
                jnp.zeros((shift_by,) + values.shape[1:], values.dtype),
                values[: sequence_length - shift_by],
            ],
            0,
        )
        moved_seg = jnp.concatenate(
            [jnp.full((shift_by,), -1, jnp.int32), segment[: sequence_length - shift_by]], 0
        )
        keeper = (
            (moved_seg == segment)
            .astype(values.dtype)
            .reshape((sequence_length,) + (1,) * (values.ndim - 1))
        )
        total = total + taps[count - 1 - shift_by] * moved * keeper
    return total


def mixer_core(
    x_heads, state_in, step_raw, taps_x, taps_state, bias_step, log_rate, skip_gain, segment
):
    x_conv = jax.nn.silu(causal_conv(x_heads, taps_x, segment))
    state_conv = jax.nn.silu(causal_conv(state_in, taps_state, segment))
    step = jax.nn.softplus(step_raw + bias_step)
    cumul = jnp.cumsum(-step * jnp.exp(log_rate), axis=0)
    sequence_length = x_heads.shape[0]
    places = jnp.arange(sequence_length, dtype=jnp.int32)
    allowed = (segment[:, None] == segment[None, :]) & (places[None, :] <= places[:, None])
    inner = jnp.dot(state_conv[:, 1], state_conv[:, 0].T, precision=PRECISE_MODE)

    def one_head(pieces):
        cum_head, step_head, x_head = pieces
        spread = jnp.where(allowed, cum_head[:, None] - cum_head[None, :], -1e30)
        mixing = jnp.exp(spread) * inner
        return jnp.dot(mixing, step_head[:, None] * x_head, precision=PRECISE_MODE)

    heads_out = lax.map(
        jax.checkpoint(one_head), (cumul.T, step.T, jnp.transpose(x_conv, (1, 0, 2)))
    )
    return jnp.transpose(heads_out, (1, 0, 2)) + skip_gain * x_conv


def rms_backward(values, inv_root, gain, grad_out):
    unit_rows = values * inv_root
    grad_gain = jnp.sum(grad_out * unit_rows, axis=0)
    grad_unit = grad_out * gain.astype(jnp.float32)
    grad_values = inv_root * (
        grad_unit - unit_rows * jnp.mean(grad_unit * unit_rows, axis=-1, keepdims=True)
    )
    return (grad_values, grad_gain)


def local(
    hidden,
    embed,
    lengths,
    attention_norm_gain,
    query_key_value_weight,
    attention_adapter_down,
    attention_adapter_up,
    attention_output_weight,
    feedforward_norm_gain,
    gate_up_weight,
    feedforward_adapter_down,
    feedforward_adapter_up,
    down_weight,
    mixer_norm_gain,
    gate_inner_weight,
    state_input_weight,
    step_projection,
    inner_conv_taps,
    state_conv_taps,
    head_step_bias,
    decay_log_rate,
    inner_skip_gains,
    gated_norm_gain,
    mixer_output_weight,
    output_cotangent,
):
    tp_count = lax.axis_size("tp")
    fsdp_count = lax.axis_size("fsdp")
    share_rows = hidden.shape[0]
    grouped_rows = share_rows * tp_count
    share_start = lax.axis_index("tp") * share_rows
    width = hidden.shape[1]

    def fetch_weights():
        return (
            lax.all_gather(attention_norm_gain, "fsdp", axis=0, tiled=True),
            lax.all_gather(query_key_value_weight, "fsdp", axis=0, tiled=True),
            lax.all_gather(attention_adapter_down, "fsdp", axis=0, tiled=True),
            lax.all_gather(attention_adapter_up, "fsdp", axis=0, tiled=True),
            lax.all_gather(attention_output_weight, "fsdp", axis=1, tiled=True),
            lax.all_gather(feedforward_norm_gain, "fsdp", axis=0, tiled=True),
            lax.all_gather(gate_up_weight, "fsdp", axis=0, tiled=True),
            lax.all_gather(feedforward_adapter_down, "fsdp", axis=0, tiled=True),
            lax.all_gather(feedforward_adapter_up, "fsdp", axis=0, tiled=True),
            lax.all_gather(down_weight, "fsdp", axis=1, tiled=True),
            lax.all_gather(mixer_norm_gain, "fsdp", axis=0, tiled=True),
            lax.all_gather(gate_inner_weight, "fsdp", axis=0, tiled=True),
            lax.all_gather(state_input_weight, "fsdp", axis=0, tiled=True),
            lax.all_gather(step_projection, "fsdp", axis=0, tiled=True),
            lax.all_gather(inner_conv_taps, "fsdp", axis=2, tiled=True),
            lax.all_gather(state_conv_taps, "fsdp", axis=2, tiled=True),
            lax.all_gather(inner_skip_gains, "fsdp", axis=1, tiled=True),
            lax.all_gather(gated_norm_gain, "fsdp", axis=1, tiled=True),
            lax.all_gather(mixer_output_weight, "fsdp", axis=1, tiled=True),
        )

    (
        full_attn_gain,
        full_w_qkv,
        complete_adapter_down,
        complete_adapter_up,
        full_w_o,
        full_mlp_gain,
        full_w_fc1,
        full_fc1_a,
        full_fc1_b,
        full_w_fc2,
        full_mixer_gain,
        full_w_zx,
        full_w_bc,
        full_w_dt,
        full_taps_x,
        full_taps_state,
        full_skip,
        full_gate_gain,
        full_w_out,
    ) = fetch_weights()
    segment, position = segments_of(lengths[0], grouped_rows)
    places = jnp.arange(grouped_rows, dtype=jnp.int32)
    allowed = (segment[:, None] == segment[None, :]) & (places[None, :] <= places[:, None])
    attention_width = 2 * width
    adapter_rank_size = attention_adapter_down.shape[2]
    joined = jnp.concatenate([hidden.astype(jnp.float32), embed.astype(jnp.float32)], axis=1)
    attn_root = lax.rsqrt(jnp.mean(joined * joined, axis=1, keepdims=True) + norm_eps)
    normalized_portion = (joined * attn_root * full_attn_gain.astype(jnp.float32)).astype(
        jnp.bfloat16
    )
    adapter_portion = batched_product(
        normalized_portion, complete_adapter_down.reshape(attention_width, 3 * adapter_rank_size)
    ).astype(jnp.bfloat16)
    normalized_grouped, adapter_grouped = (
        lax.all_gather(normalized_portion, "tp", axis=0, tiled=True),
        lax.all_gather(adapter_portion, "tp", axis=0, tiled=True),
    )
    head_cols = full_w_qkv.shape[2]
    heads_here = head_cols // HDA
    adapter_heads = adapter_grouped.reshape(grouped_rows, 3, adapter_rank_size)
    projected_rows = batched_product(
        normalized_grouped, full_w_qkv.reshape(attention_width, 3 * head_cols)
    ).reshape(grouped_rows, 3, head_cols)
    projected_rows = projected_rows + jnp.einsum(
        "kdp,pdw->kdw", adapter_heads, complete_adapter_up, preferred_element_type=jnp.float32
    )
    queries = rotate(
        projected_rows[:, 0].reshape(grouped_rows, heads_here, HDA), position, 1.0
    ).astype(jnp.bfloat16)
    keys_low = rotate(
        projected_rows[:, 1].reshape(grouped_rows, heads_here, HDA), position, 1.0
    ).astype(jnp.bfloat16)
    values_low = projected_rows[:, 2].reshape(grouped_rows, heads_here, HDA).astype(jnp.bfloat16)
    scale = HDA ** (-0.5)
    scores = (
        jnp.einsum("qhd,khd->hqk", queries, keys_low, preferred_element_type=jnp.float32) * scale
    )
    scores = jnp.where(allowed[None], scores, -1e30)
    peak = jnp.max(scores, axis=-1, keepdims=True)
    raised = jnp.exp(scores - peak)
    totals = jnp.sum(raised, axis=-1, keepdims=True)
    log_total = peak + jnp.log(totals)
    probs = (raised / totals).astype(jnp.bfloat16)
    attended = (
        jnp.einsum("hqk,khd->qhd", probs, values_low, preferred_element_type=jnp.float32)
        .reshape(grouped_rows, head_cols)
        .astype(jnp.bfloat16)
    )
    partial_mixed = batched_product(attended, full_w_o)
    gain_mlp = full_mlp_gain.astype(jnp.float32)
    mixed = lax.psum(partial_mixed, "tp")
    mlp_root = lax.rsqrt(jnp.mean(mixed * mixed, axis=1, keepdims=True) + norm_eps)
    feedforward_input = (mixed * mlp_root * gain_mlp).astype(jnp.bfloat16)
    mixed_share = lax.dynamic_slice_in_dim(mixed, share_start, share_rows, 0)
    feedforward_middle = batched_product(feedforward_input, full_fc1_a).astype(jnp.bfloat16)
    feedforward_columns = full_w_fc1.shape[2]
    gate_up_product = batched_product(
        feedforward_input, full_w_fc1.reshape(width, 2 * feedforward_columns)
    ) + batched_product(
        feedforward_middle, full_fc1_b.reshape(adapter_rank_size, 2 * feedforward_columns)
    )
    gate_up_product = gate_up_product.reshape(grouped_rows, 2, feedforward_columns)
    gelu_gate, gelu_back = jax.vjp(jax.nn.gelu, gate_up_product[:, 0])
    units = (gelu_gate * gate_up_product[:, 1]).astype(jnp.bfloat16)
    branch_share = lax.psum_scatter(
        batched_product(units, full_w_fc2), "tp", scatter_dimension=0, tiled=True
    )
    residual_share = hidden.astype(jnp.float32) + mixed_share + branch_share
    residual_group, out_grad = (
        lax.all_gather(residual_share, "tp", axis=0, tiled=True),
        lax.all_gather(output_cotangent.astype(jnp.float32), "tp", axis=0, tiled=True),
    )
    mixer_root = lax.rsqrt(
        jnp.mean(residual_group * residual_group, axis=1, keepdims=True) + norm_eps
    )
    mixer_in = (residual_group * mixer_root * full_mixer_gain.astype(jnp.float32)).astype(
        jnp.bfloat16
    )
    inner_cols = full_w_zx.shape[2]
    states = full_w_bc.shape[2]
    mixer_heads = inner_cols // HD
    gate_inner = batched_product(mixer_in, full_w_zx.reshape(width, 2 * inner_cols)).reshape(
        grouped_rows, 2, inner_cols
    )
    state_in = batched_product(mixer_in, full_w_bc.reshape(width, 2 * states)).reshape(
        grouped_rows, 2, states
    )
    step_raw = batched_product(mixer_in, full_w_dt)

    def scan_part(
        x_heads, state_part, step_part, taps_x, taps_state, bias_step, log_rate, skip_gain
    ):
        return mixer_core(
            x_heads,
            state_part,
            step_part,
            taps_x,
            taps_state,
            bias_step,
            log_rate,
            skip_gain,
            segment,
        )

    scan_y, scan_back = jax.vjp(
        scan_part,
        gate_inner[:, 1].reshape(grouped_rows, mixer_heads, HD),
        state_in,
        step_raw,
        full_taps_x.astype(jnp.float32),
        full_taps_state.astype(jnp.float32),
        head_step_bias,
        decay_log_rate,
        full_skip.astype(jnp.float32),
    )
    scan_flat = scan_y.reshape(grouped_rows, inner_cols)
    gate_z = gate_inner[:, 0]
    silu_z = jax.nn.silu(gate_z)
    gated = scan_flat * silu_z
    square_sum = lax.psum(jnp.sum(gated * gated, axis=1), "tp")
    inner_total = inner_cols * tp_count
    gate_root = lax.rsqrt(square_sum / inner_total + norm_eps)[:, None]
    gain_flat = full_gate_gain.astype(jnp.float32).reshape(inner_cols)
    scaled = (gated * gate_root * gain_flat).astype(jnp.bfloat16)
    out_share = residual_share + lax.psum_scatter(
        batched_product(scaled, full_w_out), "tp", scatter_dimension=0, tiled=True
    )
    (
        full_attn_gain,
        full_w_qkv,
        complete_adapter_down,
        complete_adapter_up,
        full_w_o,
        full_mlp_gain,
        full_w_fc1,
        full_fc1_a,
        full_fc1_b,
        full_w_fc2,
        full_mixer_gain,
        full_w_zx,
        full_w_bc,
        full_w_dt,
        full_taps_x,
        full_taps_state,
        full_skip,
        full_gate_gain,
        full_w_out,
    ) = fetch_weights()
    out_grad_low = out_grad.astype(jnp.bfloat16)
    grad_w_out = batched_product(scaled.T, out_grad_low)
    grad_scaled = batched_product(out_grad_low, full_w_out.T)
    grad_gate_gain = jnp.sum(grad_scaled * gated * gate_root, axis=0).reshape(mixer_heads, HD)
    weighted = grad_scaled * gain_flat
    cross = lax.psum(jnp.sum(weighted * gated, axis=1), "tp")
    grad_gated = gate_root * weighted - gated * gate_root**3 * (cross[:, None] / inner_total)
    grad_scan = grad_gated * silu_z
    sigmoid_z = jax.nn.sigmoid(gate_z)
    grad_z = grad_gated * scan_flat * sigmoid_z * (1.0 + gate_z * (1.0 - sigmoid_z))
    (
        grad_x_in,
        grad_state,
        grad_step,
        grad_conv_x,
        grad_conv_bc_part,
        grad_dt_bias,
        grad_a_log,
        grad_d_skip,
    ) = scan_back(grad_scan.reshape(grouped_rows, mixer_heads, HD))
    grad_gate_inner = (
        jnp.stack([grad_z, grad_x_in.reshape(grouped_rows, inner_cols)], axis=1)
        .astype(jnp.bfloat16)
        .reshape(grouped_rows, 2 * inner_cols)
    )
    grad_state_flat = grad_state.reshape(grouped_rows, 2 * states)
    bc_weight = full_w_bc.astype(jnp.float32).reshape(width, 2 * states)
    step_weight = full_w_dt.astype(jnp.float32)
    mixer_in_wide = mixer_in.astype(jnp.float32)
    part_in = (
        batched_product(grad_gate_inner, full_w_zx.reshape(width, 2 * inner_cols).T)
        + jnp.dot(grad_step, step_weight.T, precision=PRECISE_MODE)
        + jnp.dot(grad_state_flat, bc_weight.T, precision=PRECISE_MODE)
    )
    part_bc = jnp.dot(mixer_in_wide.T, grad_state_flat, precision=PRECISE_MODE)
    grad_w_in_zx = batched_product(mixer_in.T, grad_gate_inner).reshape(width, 2, inner_cols)
    grad_w_dt = jnp.dot(mixer_in_wide.T, grad_step, precision=PRECISE_MODE)
    grad_mixer_in, grad_bc_flat, grad_conv_bc = lax.psum(
        (part_in, part_bc, grad_conv_bc_part), "tp"
    )
    grad_w_in_bc = grad_bc_flat.reshape(width, 2, states)
    grad_resid_norm, grad_mixer_gain = rms_backward(
        residual_group, mixer_root, full_mixer_gain, grad_mixer_in
    )
    grad_residual = out_grad + grad_resid_norm
    grad_branch = grad_residual.astype(jnp.bfloat16)
    grad_w_fc2 = batched_product(units.T, grad_branch)
    grad_units = batched_product(grad_branch, full_w_fc2.T)
    grad_gate = gelu_back(grad_units * gate_up_product[:, 1])[0]
    grad_up = grad_units * gelu_gate
    gate_up_gradient = (
        jnp.stack([grad_gate, grad_up], axis=1)
        .astype(jnp.bfloat16)
        .reshape(grouped_rows, 2 * feedforward_columns)
    )
    grad_w_fc1 = batched_product(feedforward_input.T, gate_up_gradient).reshape(
        width, 2, feedforward_columns
    )
    feedforward_up_gradient = batched_product(feedforward_middle.T, gate_up_gradient).reshape(
        adapter_rank_size, 2, feedforward_columns
    )
    grad_fc_mid = batched_product(
        gate_up_gradient, full_fc1_b.reshape(adapter_rank_size, 2 * feedforward_columns).T
    )
    partial_feedforward = batched_product(
        gate_up_gradient, full_w_fc1.reshape(width, 2 * feedforward_columns).T
    ) + jnp.dot(grad_fc_mid, full_fc1_a.astype(jnp.float32).T, precision=PRECISE_MODE)
    partial_feedforward_down = jnp.dot(
        feedforward_input.astype(jnp.float32).T, grad_fc_mid, precision=PRECISE_MODE
    )
    feedforward_input_gradient, feedforward_down_gradient = lax.psum(
        (partial_feedforward, partial_feedforward_down), "tp"
    )
    grad_mixed_norm, grad_mlp_gain = rms_backward(
        mixed, mlp_root, full_mlp_gain, feedforward_input_gradient
    )
    grad_mixed_low = (grad_residual + grad_mixed_norm).astype(jnp.bfloat16)
    grad_w_o = batched_product(attended.T, grad_mixed_low)
    grad_attended = (
        batched_product(grad_mixed_low, full_w_o.T)
        .astype(jnp.bfloat16)
        .reshape(grouped_rows, heads_here, HDA)
    )
    scores_again = (
        jnp.einsum("qhd,khd->hqk", queries, keys_low, preferred_element_type=jnp.float32) * scale
    )
    scores_again = jnp.where(allowed[None], scores_again, -1e30)
    probs_back = jnp.exp(scores_again - log_total)
    grad_values = jnp.einsum(
        "hqk,qhd->khd",
        probs_back.astype(jnp.bfloat16),
        grad_attended,
        preferred_element_type=jnp.float32,
    )
    grad_probs = jnp.einsum(
        "qhd,khd->hqk", grad_attended, values_low, preferred_element_type=jnp.float32
    )
    grad_scores = (
        probs_back * (grad_probs - jnp.sum(probs_back * grad_probs, axis=-1, keepdims=True))
    ).astype(jnp.bfloat16)
    grad_queries = (
        jnp.einsum("hqk,khd->qhd", grad_scores, keys_low, preferred_element_type=jnp.float32)
        * scale
    )
    grad_keys = (
        jnp.einsum("hqk,qhd->khd", grad_scores, queries, preferred_element_type=jnp.float32) * scale
    )
    projection_gradient = jnp.stack(
        [
            rotate(grad_queries, position, -1.0).reshape(grouped_rows, head_cols),
            rotate(grad_keys, position, -1.0).reshape(grouped_rows, head_cols),
            grad_values.reshape(grouped_rows, head_cols),
        ],
        axis=1,
    ).astype(jnp.bfloat16)
    flattened_gradient = projection_gradient.reshape(grouped_rows, 3 * head_cols)
    grad_w_qkv = batched_product(normalized_grouped.T, flattened_gradient).reshape(
        attention_width, 3, head_cols
    )
    attention_up_gradient = jnp.einsum(
        "nel,nex->lex", adapter_heads, projection_gradient, preferred_element_type=jnp.float32
    )
    adapter_middle_gradient = jnp.einsum(
        "dek,sek->des", projection_gradient, complete_adapter_up, preferred_element_type=jnp.float32
    ).reshape(grouped_rows, 3 * adapter_rank_size)
    partial_attention_down = jnp.dot(
        normalized_grouped.astype(jnp.float32).T, adapter_middle_gradient, precision=PRECISE_MODE
    ).reshape(attention_width, 3, adapter_rank_size)
    adapter_down_flattened = complete_adapter_down.astype(jnp.float32).reshape(
        attention_width, 3 * adapter_rank_size
    )
    query_key_value_flattened = full_w_qkv.reshape(attention_width, 3 * head_cols)
    grad_normed = lax.psum_scatter(
        batched_product(flattened_gradient, query_key_value_flattened.T)
        + jnp.dot(adapter_middle_gradient, adapter_down_flattened.T, precision=PRECISE_MODE),
        "tp",
        scatter_dimension=0,
        tiled=True,
    )
    grad_joined, part_attn_gain = rms_backward(joined, attn_root, full_attn_gain, grad_normed)
    grad_hidden = (
        lax.dynamic_slice_in_dim(grad_residual, share_start, share_rows, 0) + grad_joined[:, :width]
    )
    grad_embed = grad_joined[:, width:]
    attention_gain_gradient, attention_down_gradient = (
        lax.psum_scatter(part_attn_gain, ("fsdp", "tp"), scatter_dimension=0, tiled=True),
        lax.psum_scatter(partial_attention_down, ("fsdp", "tp"), scatter_dimension=0, tiled=True),
    )
    rate_grads = jnp.tile(jnp.stack([grad_dt_bias, grad_a_log], axis=0), (1, fsdp_count))
    (
        sum_w_qkv,
        summed_adapter_up,
        sum_w_o,
        sum_mlp_gain,
        sum_w_fc1,
        sum_fc1_a,
        sum_fc1_b,
        sum_w_fc2,
        sum_mixer_gain,
        sum_w_zx,
        sum_w_bc,
        sum_w_dt,
        sum_conv_x,
        sum_conv_bc,
        sum_skip,
        sum_gate_gain,
        sum_w_out,
        sum_rates,
    ) = (
        lax.psum_scatter(grad_w_qkv, "fsdp", scatter_dimension=0, tiled=True),
        lax.psum_scatter(attention_up_gradient, "fsdp", scatter_dimension=0, tiled=True),
        lax.psum_scatter(grad_w_o, "fsdp", scatter_dimension=1, tiled=True),
        lax.psum_scatter(grad_mlp_gain, "fsdp", scatter_dimension=0, tiled=True),
        lax.psum_scatter(grad_w_fc1, "fsdp", scatter_dimension=0, tiled=True),
        lax.psum_scatter(feedforward_down_gradient, "fsdp", scatter_dimension=0, tiled=True),
        lax.psum_scatter(feedforward_up_gradient, "fsdp", scatter_dimension=0, tiled=True),
        lax.psum_scatter(grad_w_fc2, "fsdp", scatter_dimension=1, tiled=True),
        lax.psum_scatter(grad_mixer_gain, "fsdp", scatter_dimension=0, tiled=True),
        lax.psum_scatter(grad_w_in_zx, "fsdp", scatter_dimension=0, tiled=True),
        lax.psum_scatter(grad_w_in_bc, "fsdp", scatter_dimension=0, tiled=True),
        lax.psum_scatter(grad_w_dt, "fsdp", scatter_dimension=0, tiled=True),
        lax.psum_scatter(grad_conv_x, "fsdp", scatter_dimension=2, tiled=True),
        lax.psum_scatter(grad_conv_bc, "fsdp", scatter_dimension=2, tiled=True),
        lax.psum_scatter(grad_d_skip, "fsdp", scatter_dimension=1, tiled=True),
        lax.psum_scatter(grad_gate_gain, "fsdp", scatter_dimension=1, tiled=True),
        lax.psum_scatter(grad_w_out, "fsdp", scatter_dimension=1, tiled=True),
        lax.psum_scatter(rate_grads, "fsdp", scatter_dimension=1, tiled=True),
    )
    return (
        out_share,
        grad_hidden,
        grad_embed,
        attention_gain_gradient,
        sum_w_qkv,
        attention_down_gradient,
        summed_adapter_up,
        sum_w_o,
        sum_mlp_gain,
        sum_w_fc1,
        sum_fc1_a,
        sum_fc1_b,
        sum_w_fc2,
        sum_mixer_gain,
        sum_w_zx,
        sum_w_bc,
        sum_w_dt,
        sum_conv_x,
        sum_conv_bc,
        sum_rates[0],
        sum_rates[1],
        sum_skip,
        sum_gate_gain,
        sum_w_out,
    )


def solution(mesh):
    placed = (
        P(("fsdp", "tp"), None),
        P(("fsdp", "tp"), None),
        P("fsdp", None),
        P("fsdp"),
        P("fsdp", None, "tp"),
        P("fsdp", None, None),
        P("fsdp", None, "tp"),
        P("tp", "fsdp"),
        P("fsdp"),
        P("fsdp", None, "tp"),
        P("fsdp", None),
        P("fsdp", None, "tp"),
        P("tp", "fsdp"),
        P("fsdp"),
        P("fsdp", None, "tp"),
        P("fsdp", None, None),
        P("fsdp", "tp"),
        P(None, "tp", "fsdp"),
        P(None, None, "fsdp"),
        P("tp"),
        P("tp"),
        P("tp", "fsdp"),
        P("tp", "fsdp"),
        P("tp", "fsdp"),
        P(("fsdp", "tp"), None),
    )
    return jax.shard_map(
        local,
        mesh=mesh,
        in_specs=placed,
        out_specs=(
            P(("fsdp", "tp"), None),
            P(("fsdp", "tp"), None),
            P(("fsdp", "tp"), None),
            P(("fsdp", "tp")),
            P("fsdp", None, "tp"),
            P(("fsdp", "tp"), None, None),
            P("fsdp", None, "tp"),
            P("tp", "fsdp"),
            P("fsdp"),
            P("fsdp", None, "tp"),
            P("fsdp", None),
            P("fsdp", None, "tp"),
            P("tp", "fsdp"),
            P("fsdp"),
            P("fsdp", None, "tp"),
            P("fsdp", None, None),
            P("fsdp", "tp"),
            P(None, "tp", "fsdp"),
            P(None, None, "fsdp"),
            P("tp"),
            P("tp"),
            P("tp", "fsdp"),
            P("tp", "fsdp"),
            P("tp", "fsdp"),
        ),
        check_vma=False,
    )
```

profile of v0, /device:TPU:0, one launch (start us, length us, event | category | flops | bytes accessed | tf_op | source)
XLA Modules:
  0.0 4345.7 jit_solution(15531588846438598722)
XLA Ops:
  53.8 19.8 all_gather.88
  73.9 99.4 %all-gather.17.cloned.1.call-done = bf16[4096,3,1024]{2,0,1:T(8,128)(2,1)} async-done(((bf16[512,3,1024]{2,0,1:T(8,128)(2,1)}), bf16[4096,3,1024]{2,0,1:T(8,128)(2,1)}) %all-gather.17.cloned.1.call-update) | async-done | bytes 25165840 | tf_op jit(solution)/shard_map/all_gather | solution.py:140
  173.4 33.6 copy.424
  207.0 118.2 %all-gather.15.cloned.1.call-done = bf16[1024,4096]{1,0:T(8,128)(2,1)} async-done(((bf16[256,4096]{1,0:T(8,128)(2,1)}), bf16[1024,4096]{1,0:T(8,128)(2,1)}) %all-gather.15.cloned.1.call-update) | async-done | bytes 8388624 | tf_op jit(solution)/shard_map/all_gather | solution.py:195
  325.2 33.6 fusion.39
  399.0 20.1 fusion.132
  419.1 13.5 fusion.37
  432.6 15.8 fusion.90
  483.0 22.6 copy.434
  505.6 270.6 %all-reduce.39.cloned.1.call-done = f32[1024,2048]{1,0:T(8,128)} async-done(((f32[1024,2048]{1,0:T(8,128)}), f32[1024,2048]{1,0:T(8,128)}) %all-reduce.39.cloned.1.call-update) | async-done | bytes 8388624 | tf_op jit(solution)/shard_map/psum | solution.py:231
  792.2 24.5 convolution_add_fusion
  816.7 22.2 reshape.480
  838.9 21.6 fusion.124
  876.3 14.4 fusion.137
  893.3 141.8 %reduce-scatter.20.cloned.1.call-done = f32[256,2048]{1,0:T(8,128)} async-done(((f32[1024,2048]{1,0:T(8,128)}), f32[256,2048]{1,0:T(8,128)}) %reduce-scatter.20.cloned.1.call-update) | async-done | bytes 2097168 | tf_op jit(solution)/shard_map/reduce_scatter | solution.py:245
  1050.6 13.0 all_gather.100
  1125.8 120.4 %all-gather.29.cloned.1.call-done = f32[1024,2048]{1,0:T(8,128)} async-done(((f32[256,2048]{1,0:T(8,128)}), f32[1024,2048]{1,0:T(8,128)}) %all-gather.29.cloned.1.call-update) | async-done | bytes 8388624 | tf_op jit(solution)/shard_map/all_gather | solution.py:250
  1306.6 157.7 %while.33 = (s32[]{:T(128)}, f32[16,1024,64]{1,2,0:T(8,128)}, f32[16,1024]{1,0:T(8,128)}, f32[1024,1024]{1,0:T(8,128)}, f32[16,1024]{1,0:T(8,128)}, /*index=5*/f32[16,1024,64]{1,2,0:T(8,128)}, s32[1024]{0:T(1024)S(1)}, s32[]{:T(128)}) while((s32[]{:T(128)}, f32[16,1024,64]{1,2,0:T(8,128)}, f32[16,1024]{1,0:T(8,128)}, ...), condition=%wide.region_13.14_spmd.clone, body=%wide.region_12.13_spmd.clone.sunk | while | flops 811663360 | bytes 6066781 | solution.py:87
  1480.7 16.1 multiply_reduce_fusion.8
  1524.6 353.1 %while.34 = (s32[]{:T(128)}, f32[1024,1024]{1,0:T(8,128)}, f32[16,1024]{1,0:T(8,128)}, f32[16,1024]{1,0:T(8,128)}, f32[16,1024,64]{1,2,0:T(8,128)}, /*index=5*/f...) while((s32[]{:T(128)}, f32[1024,1024]{1,0:T(8,128)}, ...), condition=%wide.region_23.24_spmd.clone, body=%wide.region_19.23_spmd.clone.sunk | while | flops 1627651072 | bytes 23408820 | solution.py:87
  1919.8 19.8 reduce-window.21
  1960.2 17.3 bitcast_add_fusion.3
  1982.7 284.1 %all-reduce.41.cloned.1.call-done = f32[1024,2048]{1,0:T(8,128)} async-done(((f32[1024,2048]{1,0:T(8,128)}), f32[1024,2048]{1,0:T(8,128)}) %all-reduce.41.cloned.1.call-update) | async-done | bytes 8388624 | tf_op jit(solution)/shard_map/psum | solution.py:366
  2285.7 26.1 fusion.51
  2330.8 21.4 fusion.141
  2398.8 270.4 %all-reduce.45.cloned.1.call-done = (f32[1024,2048]{1,0:T(8,128)}, f32[256,128]{1,0:T(8,128)}, f32[256,2,64]{0,2,1:T(8,128)}) async-done(((f32[1024,2048]{1,0:T(8,128)}, f32[256,128]{1,0:T(8,128)}, f32[256,2,64]{0,2,1:T(8,128)}), (f32[1024,2048]{1,0:T(8,128)}, f32[256,128]{1,0:T(8,128)}, f32[256,2,64]{0,2,1:T(8,128)})) %all-reduce.45.cloned.1.call-update) | async-done | bytes 8650768 | tf_op jit(solution)/shard_map/psum | solution.py:399
  2694.0 22.6 multiply_reduce_fusion.1
  2716.6 29.1 multiply_convert_fusion
  2757.7 14.1 multiply_bitcast_fusion.1
  2796.5 15.1 fusion.41
  2826.2 15.5 fusion.66
  2847.8 33.7 fusion.142
  2881.5 24.5 bitcast_add_fusion
  2906.1 25.8 fusion.56
  2937.4 12.7 fusion.85
  2961.2 19.9 fusion.58
  2981.1 17.4 fusion.81
  3007.3 35.1 fusion.60
  3053.0 31.3 all-reduce.32
  3104.9 262.7 %reduce-scatter.24.cloned.1.call-done = f32[256,4096]{1,0:T(8,128)} async-done(((f32[1024,4096]{1,0:T(8,128)}), f32[256,4096]{1,0:T(8,128)}) %reduce-scatter.24.cloned.1.call-update) | async-done | bytes 4194320 | tf_op jit(solution)/shard_map/reduce_scatter | solution.py:461
  3371.6 41.4 all-reduce.24
  3423.5 153.9 %reduce-scatter.32.cloned.1.call-done = f32[256,2,2048]{2,0,1:T(8,128)} async-done(((f32[2048,2,2048]{2,0,1:T(8,128)}), f32[256,2,2048]{2,0,1:T(8,128)}) %reduce-scatter.32.cloned.1.call-update) | async-done | bytes 4194320 | tf_op jit(solution)/shard_map/reduce_scatter | solution.py:502
  3584.9 30.1 reduce-scatter.40.cloned.1.call-done
  3614.9 75.6 %reduce-scatter.42.cloned.1.call-done = f32[1024,256]{1,0:T(8,128)} async-done(((f32[1024,2048]{1,0:T(8,128)}), f32[1024,256]{1,0:T(8,128)}) %reduce-scatter.42.cloned.1.call-update) | async-done | bytes 1048592 | tf_op jit(solution)/shard_map/reduce_scatter | solution.py:514
  3690.5 75.2 %reduce-scatter.30.cloned.1.call-done = f32[1024,256]{1,0:T(8,128)} async-done(((f32[1024,2048]{1,0:T(8,128)}), f32[1024,256]{1,0:T(8,128)}) %reduce-scatter.30.cloned.1.call-update) | async-done | bytes 1048592 | tf_op jit(solution)/shard_map/reduce_scatter | solution.py:500
  3765.7 161.8 %reduce-scatter.28.cloned.1.call-done = f32[128,3,128]{2,0,1:T(8,128)} async-done(((f32[4096,3,128]{2,0,1:T(8,128)}), f32[128,3,128]{2,0,1:T(8,128)}) %reduce-scatter.28.cloned.1.call-update) | async-done | bytes 196624 | tf_op jit(solution)/shard_map/reduce_scatter | solution.py:475
  3927.5 119.1 %reduce-scatter.36.cloned.1.call-done = f32[2048,256]{1,0:T(8,128)} async-done(((f32[2048,2048]{1,0:T(8,128)}), f32[2048,256]{1,0:T(8,128)}) %reduce-scatter.36.cloned.1.call-update) | async-done | bytes 2097168 | tf_op jit(solution)/shard_map/reduce_scatter | solution.py:505
  4046.7 290.4 %reduce-scatter.26.cloned.1.call-done = f32[512,3,1024]{2,0,1:T(8,128)} async-done(((f32[4096,3,1024]{2,0,1:T(8,128)}), f32[512,3,1024]{2,0,1:T(8,128)}) %reduce-scatter.26.cloned.1.call-update) | async-done | bytes 6291472 | tf_op jit(solution)/shard_map/reduce_scatter | solution.py:498
  (806 shorter events, 1158.8 us)
Async XLA Ops:
  7.2 38.8 all-gather.19.cloned.1.call-start
  8.0 165.4 %all-gather.17.cloned.1.call-start = ((), (), s32[]{:S(2)}) async-start(), calls=%async_computation.16 | async-start | bytes 28311552 | tf_op jit(solution)/shard_map/all_gather | solution.py:140
  8.7 316.5 %all-gather.15.cloned.1.call-start = ((), (), s32[]{:S(2)}) async-start(), calls=%async_computation.15 | async-start | bytes 10485760 | tf_op jit(solution)/shard_map/all_gather | solution.py:195
  22.6 425.9 %all-gather.21.cloned.1.call-start = ((), (), s32[]{:S(2)}) async-start(), calls=%async_computation.18 | async-start | bytes 4718592 | tf_op jit(solution)/shard_map/all_gather | solution.py:143
  23.2 458.0 %all-gather.25.cloned.1.call-start = ((), (), s32[]{:S(2)}) async-start(), calls=%async_computation.21 | async-start | bytes 1179648 | tf_op jit(solution)/shard_map/all_gather | solution.py:147
  23.9 459.0 %all-gather.23.cloned.1.call-start = ((), (), s32[]{:S(2)}) async-start(), calls=%async_computation.20 | async-start | bytes 18874368 | tf_op jit(solution)/shard_map/all_gather | solution.py:145
  26.2 750.0 %all-reduce.39.cloned.1.call-start = ((), (), s32[]{:S(2)}) async-start(), calls=%async_computation.19 | async-start | bytes 16777216 | tf_op jit(solution)/shard_map/psum | solution.py:231
  38.9 319.9 %copy-start.29 = (bf16[128,3,1024]{2,0,1:T(8,128)(2,1)}, bf16[128,3,1024]{2,0,1:T(8,128)(2,1)S(1)}, u32[]{:S(2)}) copy-start(bf16[128,3,1024]{2,0,1:T(8,128)(2,1)S(1)} %all_gather.89) | copy-start | bytes 2359300
  42.0 347.3 %copy-start.40 = (f32[1024,64]{1,0:T(8,128)}, f32[1024,64]{1,0:T(8,128)S(1)}, u32[]{:S(2)}) copy-start(f32[1024,64]{1,0:T(8,128)S(1)} %get-tuple-element.811) | copy-start | bytes 786436
  73.9 284.9 %copy-start.31 = (bf16[1024,384]{0,1:T(8,128)(2,1)}, bf16[1024,384]{0,1:T(8,128)(2,1)S(1)}, u32[]{:S(2)}) copy-start(bf16[1024,384]{0,1:T(8,128)(2,1)S(1)} %copy.426) | copy-start | bytes 2359300
  459.2 417.1 %all-gather.27.cloned.1.call-start = ((), (), s32[]{:S(2)}) async-start(), calls=%async_computation.22 | async-start | bytes 9437184 | tf_op jit(solution)/shard_map/all_gather | solution.py:148
  460.0 575.1 %reduce-scatter.20.cloned.1.call-start = ((), (), s32[]{:S(2)}) async-start(), calls=%async_computation.23 | async-start | bytes 10485760 | tf_op jit(solution)/shard_map/reduce_scatter | solution.py:245
  469.2 311.2 %copy-start.71 = (f32[8,1,256]{2,1,0:T(1,128)}, f32[8,1,256]{2,1,0:T(1,128)S(1)}, u32[]{:S(2)}) copy-start(f32[8,1,256]{2,1,0:T(1,128)S(1)} %convert_element_type.185) | copy-start | bytes 24580
  481.2 301.6 %copy-start.46 = (bf16[2048,128]{1,0:T(8,128)(2,1)}, bf16[2048,128]{1,0:T(8,128)(2,1)S(1)}, u32[]{:S(2)}) copy-start(bf16[2048,128]{1,0:T(8,128)(2,1)S(1)} %all_gather.93) | copy-start | bytes 1572868
  890.8 222.8 %all-gather.31.cloned.1.call-start = ((), (), s32[]{:S(2)}) async-start(), calls=%async_computation.25 | async-start | bytes 9437184 | tf_op jit(solution)/shard_map/all_gather | solution.py:150
  893.2 353.0 %all-gather.29.cloned.1.call-start = ((), (), s32[]{:S(2)}) async-start(), calls=%async_computation.24 | async-start | bytes 10485760 | tf_op jit(solution)/shard_map/all_gather | solution.py:250
  1039.3 441.3 %all-gather.33.cloned.1.call-start = ((), (), s32[]{:S(2)}) async-start(), calls=%async_computation.26 | async-start | bytes 4718592 | tf_op jit(solution)/shard_map/all_gather | solution.py:157
  1039.9 440.8 %all-gather.35.cloned.1.call-start = ((), (), s32[]{:S(2)}) async-start(), calls=%async_computation.28 | async-start | bytes 10485760 | tf_op jit(solution)/shard_map/all_gather | solution.py:251
  1041.6 1225.2 %all-reduce.41.cloned.1.call-start = ((), (), s32[]{:S(2)}) async-start(), calls=%async_computation.29 | async-start | bytes 16777216 | tf_op jit(solution)/shard_map/psum | solution.py:366
  1050.5 199.8 %copy-start.80 = (f32[8,1,256]{2,1,0:T(1,128)}, f32[8,1,256]{2,1,0:T(1,128)S(1)}, u32[]{:S(2)}) copy-start(f32[8,1,256]{2,1,0:T(1,128)S(1)} %convert_element_type.186) | copy-start | bytes 24580
  1073.0 205.5 %copy-start.115 = (f32[1,2,64]{2,1,0:T(2,128)}, f32[1,2,64]{2,1,0:T(2,128)S(1)}, u32[]{:S(2)}) copy-start(f32[1,2,64]{2,1,0:T(2,128)S(1)} %copy.442) | copy-start | bytes 1540
  1113.5 401.5 %copy-start.61 = (f32[1024]{0:T(1024)}, f32[1024]{0:T(1024)S(1)}, u32[]{:S(2)}) copy-start(f32[1024]{0:T(1024)S(1)} %reshape.504) | copy-start | bytes 12292
  1113.6 178.8 %copy-start.84 = (f32[1024]{0:T(1024)}, f32[1024]{0:T(1024)S(1)}, u32[]{:S(2)}) copy-start(f32[1024]{0:T(1024)S(1)} %get-tuple-element.816) | copy-start | bytes 12292
  1977.6 380.3 %reduce-scatter.46.cloned.1.call-start = ((), (), s32[]{:S(2)}) async-start(), calls=%async_computation.41 | async-start | bytes 1179648 | tf_op jit(solution)/shard_map/reduce_scatter | solution.py:508
  1977.6 289.2 %copy-start.81 = (f32[8,1,256]{2,1,0:T(1,128)S(1)}, f32[8,1,256]{2,1,0:T(1,128)}, u32[]{:S(2)}) copy-start(f32[8,1,256]{2,1,0:T(1,128)} %copy-done.80) | copy-start | bytes 24580
  1977.6 289.2 %copy-start.105 = (f32[1024]{0:T(1024)S(1)}, f32[1024]{0:T(1024)}, u32[]{:S(2)}) copy-start(f32[1024]{0:T(1024)} %copy-done.104) | copy-start | bytes 12292
  1982.6 383.3 %reduce-scatter.44.cloned.1.call-start = ((), (), s32[]{:S(2)}) async-start(), calls=%async_computation.40 | async-start | bytes 1179648 | tf_op jit(solution)/shard_map/reduce_scatter | solution.py:503
  2330.7 338.5 %all-reduce.45.cloned.1.call-start = ((), (), s32[]{:S(2)}) async-start(), calls=%async_computation.44 | async-start | bytes 17301504 | tf_op jit(solution)/shard_map/psum | solution.py:399
  2365.9 680.0 %reduce-scatter.48.cloned.1.call-start = ((), (), s32[]{:S(2)}) async-start(), calls=%async_computation.42 | async-start | bytes 73728
  2367.3 680.6 %reduce-scatter.34.cloned.1.call-start = ((), (), s32[]{:S(2)}) async-start(), calls=%async_computation.35 | async-start | bytes 2359296 | tf_op jit(solution)/shard_map/reduce_scatter | solution.py:504
  2387.2 662.6 %reduce-scatter.22.cloned.1.call-start = ((), (), s32[]{:S(2)}) async-start(), calls=%async_computation.27 | async-start | bytes 10485760 | tf_op jit(solution)/shard_map/reduce_scatter | solution.py:305
  2398.7 270.5 %copy-start.72 = (f32[8,1,256]{2,1,0:T(1,128)S(1)}, f32[8,1,256]{2,1,0:T(1,128)}, u32[]{:S(2)}) copy-start(f32[8,1,256]{2,1,0:T(1,128)} %copy-done.71) | copy-start | bytes 24580
  2398.7 270.5 %copy-start.101 = (f32[1024]{0:T(1024)S(1)}, f32[1024]{0:T(1024)}, u32[]{:S(2)}) copy-start(f32[1024]{0:T(1024)} %copy-done.100) | copy-start | bytes 12292
  2398.7 699.8 %all-reduce.43.cloned.1.call-start = ((), (), s32[]{:S(2)}) async-start(), calls=%async_computation.43 | async-start | bytes 4194304
  2826.1 274.2 %reduce-scatter.38.cloned.1.call-start = ((), (), s32[]{:S(2)}) async-start(), calls=%async_computation.37 | async-start | bytes 18874368 | tf_op jit(solution)/shard_map/reduce_scatter | solution.py:507
  2841.7 525.9 %reduce-scatter.24.cloned.1.call-start = ((), (), s32[]{:S(2)}) async-start(), calls=%async_computation.30 | async-start | bytes 20971520 | tf_op jit(solution)/shard_map/reduce_scatter | solution.py:461
  2906.0 671.4 %reduce-scatter.32.cloned.1.call-start = ((), (), s32[]{:S(2)}) async-start(), calls=%async_computation.34 | async-start | bytes 37748736 | tf_op jit(solution)/shard_map/reduce_scatter | solution.py:502
  2931.9 683.0 %reduce-scatter.40.cloned.1.call-start = ((), (), s32[]{:S(2)}) async-start(), calls=%async_computation.38 | async-start | bytes 147456 | tf_op jit(solution)/shard_map/reduce_scatter | solution.py:509
  2937.3 753.2 %reduce-scatter.42.cloned.1.call-start = ((), (), s32[]{:S(2)}) async-start(), calls=%async_computation.39 | async-start | bytes 9437184 | tf_op jit(solution)/shard_map/reduce_scatter | solution.py:514
  2950.1 815.6 %reduce-scatter.30.cloned.1.call-start = ((), (), s32[]{:S(2)}) async-start(), calls=%async_computation.33 | async-start | bytes 9437184 | tf_op jit(solution)/shard_map/reduce_scatter | solution.py:500
  2961.1 966.4 %reduce-scatter.28.cloned.1.call-start = ((), (), s32[]{:S(2)}) async-start(), calls=%async_computation.32 | async-start | bytes 6488064 | tf_op jit(solution)/shard_map/reduce_scatter | solution.py:475
  2981.1 1065.6 %reduce-scatter.36.cloned.1.call-start = ((), (), s32[]{:S(2)}) async-start(), calls=%async_computation.36 | async-start | bytes 18874368 | tf_op jit(solution)/shard_map/reduce_scatter | solution.py:505
  2998.6 1338.5 %reduce-scatter.26.cloned.1.call-start = ((), (), s32[]{:S(2)}) async-start(), calls=%async_computation.31 | async-start | bytes 56623104 | tf_op jit(solution)/shard_map/reduce_scatter | solution.py:498
  3053.0 314.6 %copy-start.7 = (f32[256,2048]{1,0:T(8,128)S(1)}, f32[256,2048]{1,0:T(8,128)}, u32[]{:S(2)}) copy-start(f32[256,2048]{1,0:T(8,128)} %copy-done.6) | copy-start | bytes 6291460
  3053.0 314.6 %copy-start.68 = (f32[8,1,512]{2,1,0:T(1,128)S(1)}, f32[8,1,512]{2,1,0:T(1,128)}, u32[]{:S(2)}) copy-start(f32[8,1,512]{2,1,0:T(1,128)} %copy-done.67) | copy-start | bytes 49156
  3053.0 314.6 %copy-start.114 = (f32[256]{0:T(256)S(1)}, f32[256]{0:T(256)}, u32[]{:S(2)}) copy-start(f32[256]{0:T(256)} %copy-done.113) | copy-start | bytes 3076
  3423.5 913.6 %copy-start.75 = (f32[256,128]{1,0:T(8,128)S(1)}, f32[256,128]{1,0:T(8,128)}, u32[]{:S(2)}) copy-start(f32[256,128]{1,0:T(8,128)} %get-tuple-element.1040) | copy-start | bytes 393220
  3423.5 914.2 %copy-start.74 = (f32[256,2,64]{0,2,1:T(8,128)S(1)}, f32[256,2,64]{0,2,1:T(8,128)}, u32[]{:S(2)}) copy-start(f32[256,2,64]{0,2,1:T(8,128)} %get-tuple-element.1045) | copy-start | bytes 393220
  (128 other events, 1998.1 us)
Sparse Core Ops, SparseCore 0:
  10.0 36.0 all-gather.18
  48.0 125.3 all-gather.16
  175.5 149.6 all-gather.14
  326.9 35.6 all-gather.20
  364.9 23.4 all-gather.24
  390.8 91.8 all-gather.22
  485.2 290.9 all-reduce.38
  778.1 54.9 all-gather.26
  890.9 144.1 reduce-scatter.19
  1037.4 56.9 all-gather.30
  1096.6 149.6 all-gather.28
  1248.0 35.6 all-gather.32
  1285.2 149.6 all-gather.34
  1977.7 289.0 all-reduce.40
  2270.4 35.0 reduce-scatter.45
  2330.9 34.9 reduce-scatter.43
  2368.5 300.6 all-reduce.44
  2672.7 32.1 reduce-scatter.47
  2708.5 41.2 reduce-scatter.33
  2752.0 144.4 reduce-scatter.21
  2900.3 62.1 all-reduce.42
  2966.0 118.7 reduce-scatter.37
  3087.2 280.3 reduce-scatter.23
  3371.4 205.9 reduce-scatter.31
  3581.6 33.3 reduce-scatter.39
  3619.2 71.2 reduce-scatter.41
  3694.4 71.2 reduce-scatter.29
  3768.7 158.7 reduce-scatter.27
  3932.1 114.5 reduce-scatter.35
  4051.1 285.8 reduce-scatter.25
where the time goes:
time: 4360 us; the launch traced here: 4350 us
  waiting for transfers between devices  2490 us (57%)
  matrix products  943 us (22%)
  local copies, waits for them, and re-layouts  388 us (9%)
  other arithmetic  273 us (6%)
  blocking collectives  231 us (5%)
    dot_general x25, matrix products, batched_product(): return jnp.dot(left, right, preferred_element_type=jnp.float32)  373 us
    dot_general x48, matrix products, one_head(): return jnp.dot(mixing, step_head[:, None] * x_head, precision=PRECISE_MODE)  366 us
    reduce_scatter x1, waiting for transfers between devices, local(): lax.psum_scatter(grad_w_qkv, 'fsdp', scatter_dimension=0, tiled=True)  290 us
    psum x1, waiting for transfers between devices, local(): lax.psum((part_in, part_bc, grad_conv_bc_part), 'tp')  284 us
    psum x1, waiting for transfers between devices, local(): mixed = lax.psum(partial_mixed, 'tp')  271 us
    psum x1, waiting for transfers between devices, local(): lax.psum((partial_feedforward, partial_feedforward_down), 'tp')  270 us
    reduce_scatter x1, waiting for transfers between devices, local(): lax.psum_scatter(batched_product(flattened_gradient, query_key_value_flat...  263 us
    reduce_scatter x1, waiting for transfers between devices, local(): lax.psum_scatter(partial_attention_down, ('fsdp', 'tp'), scatter_dimensio...  162 us
  transfers between devices with their start and end apart: 30, of which 17 were waited for; matrix products, arithmetic and copies ran while one was open for 25% of the time, Pallas kernels for 0%

commit v1 on v0

v1 whole, which is shorter than its diff:
```python
import functools
import math

import jax
import jax.numpy as jnp
from jax import lax
from jax.experimental import pallas as pl
from jax.experimental.pallas import tpu as pltpu
from jax.sharding import PartitionSpec as P

HDA = 128
HD = 64
LANES = 128
CHUNK = 128

norm_eps = 1e-05
f32 = jnp.float32
bf16 = jnp.bfloat16
HIGHEST = lax.Precision.HIGHEST
VMEM_LIMIT = 56 * 1024 * 1024


def mm(left, right):
    return jnp.dot(left, right, preferred_element_type=f32)


def mm_nt(left, right):
    return lax.dot_general(left, right, (((1,), (1,)), ((), ())), preferred_element_type=f32)


def mm_tn(left, right):
    return lax.dot_general(left, right, (((0,), (0,)), ((), ())), preferred_element_type=f32)


def starts_of(index, ends):
    start = jnp.zeros_like(index)
    for end in ends:
        start = jnp.where(index >= end, end, start)
    return start


def ends_of(lengths_ref):
    ends = []
    end = jnp.int32(0)
    for i in range(lengths_ref.shape[0] - 1):
        end = end + lengths_ref[i]
        ends.append(end)
    return ends


def iota(shape, axis):
    return lax.broadcasted_iota(jnp.int32, shape, axis)


def attention_forward_kernel(tp, place_ref, lengths_ref, cosine_ref, sine_ref, *refs):
    q_in, k_in, v_in = refs[:tp], refs[tp : 2 * tp], refs[2 * tp : 3 * tp]
    attended_ref, q_ref, k_ref, v_ref, held = refs[3 * tp :]
    rows = q_ref.shape[0]
    share = rows // tp
    here = place_ref[0]
    ends = ends_of(lengths_ref)
    for p in range(tp):
        owner = lax.rem(here - p + tp, tp)
        part = pl.ds(pl.multiple_of(owner * share, share), share)
        cosine, sine = cosine_ref[part, :], sine_ref[part, :]
        for source, target in ((q_in[p], q_ref), (k_in[p], k_ref)):
            value = source[...]
            turned = value * cosine + pltpu.roll(value, HDA // 2, 1) * sine
            target[part, :] = turned.astype(bf16)
        v_ref[part, :] = v_in[p][...].astype(bf16)
    block = min(256, rows)
    scale = HDA ** (-0.5)
    for at in range(0, rows, block):
        upto = at + block
        scores = mm_nt(q_ref[at:upto, :], k_ref[:upto, :]) * scale
        query = at + iota((block, 1), 0)
        key = iota((1, upto), 1)
        seen = (key <= query) & (key >= starts_of(query, ends))
        scores = jnp.where(seen, scores, -1e30)
        raised = jnp.exp(scores - jnp.max(scores, axis=1, keepdims=True))
        probs = (raised * (1.0 / jnp.sum(raised, axis=1, keepdims=True))).astype(bf16)
        held[at:upto, :] = mm(probs, v_ref[:upto, :]).astype(bf16)
    for p in range(tp):
        owner = lax.rem(here - p + tp, tp)
        part = pl.ds(pl.multiple_of(owner * share, share), share)
        attended_ref[p * share : (p + 1) * share, :] = held[part, :]


def attention_forward(place, lengths, pieces, cosine, sine):
    tp = len(pieces)
    share, columns = pieces[0][0].shape
    rows = share * tp
    heads = columns // HDA
    piece_spec = pl.BlockSpec((share, HDA), lambda h, *_: (0, h))
    table_spec = pl.BlockSpec((rows, HDA), lambda h, *_: (0, 0))
    head_spec = pl.BlockSpec((rows, HDA), lambda h, *_: (0, h))
    flat = [pieces[p][j] for j in range(3) for p in range(tp)]
    work = heads * rows * rows * HDA
    return pl.pallas_call(
        functools.partial(attention_forward_kernel, tp),
        out_shape=[jax.ShapeDtypeStruct((rows, columns), bf16)] * 4,
        grid_spec=pltpu.PrefetchScalarGridSpec(
            num_scalar_prefetch=2,
            grid=(heads,),
            in_specs=[table_spec, table_spec] + [piece_spec] * (3 * tp),
            out_specs=[head_spec] * 4,
            scratch_shapes=[pltpu.VMEM((rows, HDA), bf16)],
        ),
        compiler_params=pltpu.CompilerParams(vmem_limit_bytes=VMEM_LIMIT),
        cost_estimate=pl.CostEstimate(
            flops=4 * work, bytes_accessed=20 * rows * columns, transcendentals=heads * rows * rows
        ),
        name="attention_forward",
    )(place, lengths, cosine, sine, *flat)


def attention_backward_kernel(tp, place_ref, lengths_ref, cosine_ref, sine_ref, *refs):
    q_ref, k_ref, v_ref = refs[:3]
    grad_in = refs[3 : 3 + tp]
    out_refs = refs[3 + tp : 6 + tp]
    held, dq, dk, dv = refs[6 + tp :]
    rows = q_ref.shape[0]
    share = rows // tp
    here = place_ref[0]
    ends = ends_of(lengths_ref)
    for p in range(tp):
        owner = lax.rem(here - p + tp, tp)
        part = pl.ds(pl.multiple_of(owner * share, share), share)
        held[part, :] = grad_in[p][...]
    dk[...] = jnp.zeros_like(dk)
    dv[...] = jnp.zeros_like(dv)
    block = min(256, rows)
    scale = HDA ** (-0.5)
    for at in range(0, rows, block):
        upto = at + block
        query_rows = q_ref[at:upto, :]
        grad_rows = held[at:upto, :]
        scores = mm_nt(k_ref[:upto, :], query_rows) * scale
        query = at + iota((1, block), 1)
        key = iota((upto, 1), 0)
        seen = (key <= query) & (key >= starts_of(query, ends))
        scores = jnp.where(seen, scores, -1e30)
        raised = jnp.exp(scores - jnp.max(scores, axis=0, keepdims=True))
        probs = raised * (1.0 / jnp.sum(raised, axis=0, keepdims=True))
        grad_probs = mm_nt(v_ref[:upto, :], grad_rows)
        cross = jnp.sum(probs * grad_probs, axis=0, keepdims=True)
        grad_scores = (probs * (grad_probs - cross)).astype(bf16)
        dv[:upto, :] += mm(probs.astype(bf16), grad_rows)
        dk[:upto, :] += mm(grad_scores, query_rows)
        dq[at:upto, :] = mm_tn(grad_scores, k_ref[:upto, :])
    for p in range(tp):
        owner = lax.rem(here - p + tp, tp)
        part = pl.ds(pl.multiple_of(owner * share, share), share)
        cosine, sine = cosine_ref[part, :], sine_ref[part, :]
        mine = slice(p * share, (p + 1) * share)
        for source, target in ((dq, out_refs[0]), (dk, out_refs[1])):
            value = source[part, :] * scale
            turned = value * cosine - pltpu.roll(value, HDA // 2, 1) * sine
            target[mine, :] = turned.astype(bf16)
        out_refs[2][mine, :] = dv[part, :].astype(bf16)


def attention_backward(place, lengths, queries, keys, values, pieces, cosine, sine):
    tp = len(pieces)
    share, columns = pieces[0].shape
    rows = share * tp
    heads = columns // HDA
    piece_spec = pl.BlockSpec((share, HDA), lambda h, *_: (0, h))
    table_spec = pl.BlockSpec((rows, HDA), lambda h, *_: (0, 0))
    head_spec = pl.BlockSpec((rows, HDA), lambda h, *_: (0, h))
    work = heads * rows * rows * HDA
    return pl.pallas_call(
        functools.partial(attention_backward_kernel, tp),
        out_shape=[jax.ShapeDtypeStruct((rows, columns), bf16)] * 3,
        grid_spec=pltpu.PrefetchScalarGridSpec(
            num_scalar_prefetch=2,
            grid=(heads,),
            in_specs=[table_spec, table_spec] + [head_spec] * 3 + [piece_spec] * tp,
            out_specs=[head_spec] * 3,
            scratch_shapes=[pltpu.VMEM((rows, HDA), bf16)] + [pltpu.VMEM((rows, HDA), f32)] * 3,
        ),
        compiler_params=pltpu.CompilerParams(vmem_limit_bytes=VMEM_LIMIT),
        cost_estimate=pl.CostEstimate(
            flops=10 * work, bytes_accessed=14 * rows * columns, transcendentals=heads * rows * rows
        ),
        name="attention_backward",
    )(place, lengths, cosine, sine, queries, keys, values, *pieces)


def conv_rows(extended, taps, position):
    count = 4
    rows = extended.shape[0] - 8
    total = None
    for k in range(count):
        moved = extended[8 - k : 8 - k + rows, :]
        if k:
            moved = jnp.where(position >= k, moved, 0.0)
        term = taps[count - 1 - k : count - k, :] * moved
        total = term if total is None else total + term
    return total


def conv_back(extended, taps, position):
    count = 4
    rows = extended.shape[0] - 8
    total = None
    for k in range(count):
        kept = jnp.where(position >= k, extended, 0.0) if k else extended
        term = taps[count - 1 - k : count - k, :] * kept[k : k + rows, :]
        total = term if total is None else total + term
    return total


def taps_back(extended, grad, position, target):
    count = 4
    rows = extended.shape[0] - 8
    for k in range(count):
        moved = extended[8 - k : 8 - k + rows, :]
        if k:
            moved = jnp.where(position >= k, moved, 0.0)
        at = count - 1 - k
        target[at : at + 1, :] += jnp.sum(grad * moved, axis=0, keepdims=True)


def silu_grad(value, gate):
    return gate * (1.0 + value * (1.0 - gate))


class Chunk:
    def __init__(self, c0, ends, zx, before, sd, sd_before, wide, narrow, rates):
        rows = zx.shape[0]
        width = zx.shape[1] // 2
        self.rows, self.width = rows, width
        index = c0 + iota((rows, 1), 0)
        start = starts_of(index, ends)
        self.index, self.start = index, start
        self.position = index - start
        last_start = starts_of(c0 + rows - 1, ends)
        self.z = zx[:, :width].astype(f32)
        self.x_ext = jnp.concatenate(
            [before[...].astype(f32)[8:16, :], zx[:, width:].astype(f32)], axis=0
        )
        self.s_ext = jnp.concatenate([sd_before[:, : 2 * LANES], sd[:, : 2 * LANES]], axis=0)
        self.pre = conv_rows(self.x_ext, wide, self.position)
        self.gate_x = jax.nn.sigmoid(self.pre)
        self.xc = self.pre * self.gate_x
        self.pre_s = conv_rows(self.s_ext, narrow, self.position)
        self.gate_s = jax.nn.sigmoid(self.pre_s)
        sc = self.pre_s * self.gate_s
        self.b_low = sc[:, :HD].astype(bf16)
        self.c_low = sc[:, LANES : LANES + HD].astype(bf16)
        self.raw = sd[:, 2 * LANES : 3 * LANES] + rates[0:1, :]
        self.step = jnp.maximum(self.raw, 0.0) + jnp.log1p(jnp.exp(-jnp.abs(self.raw)))
        self.rate = jnp.exp(rates[1:2, :])
        row, col = iota((rows, rows), 0), iota((rows, rows), 1)
        below = (col <= row).astype(f32)
        self.cum = jnp.dot(below, -self.step * self.rate, precision=HIGHEST, preferred_element_type=f32)
        self.cum_t = self.cum.T
        self.allowed = (col <= row) & ((c0 + col) >= start)
        self.inner = jnp.where(self.allowed, mm_nt(self.c_low, self.b_low), 0.0)
        last = self.cum[rows - 1 : rows, :]
        self.into = jnp.exp(self.cum) * (start < c0).astype(f32)
        self.onto = jnp.exp(last - self.cum) * (index >= last_start).astype(f32)
        self.decay = jnp.exp(last) * (last_start < c0).astype(f32)
        self.low_half = iota((1, LANES), 1) < HD

    def pair(self, table, i):
        return jnp.where(self.low_half, table[:, 2 * i : 2 * i + 1], table[:, 2 * i + 1 : 2 * i + 2])

    def spread(self, h):
        return jnp.exp(jnp.minimum(self.cum[:, h : h + 1] - self.cum_t[h : h + 1, :], 0.0))


def mixer_forward_kernel(
    place_ref, lengths_ref, zx, before, sd, sd_before, wide, narrow, rates, gated, states, state
):
    rows = zx.shape[0]
    c0 = pl.program_id(0) * rows
    ends = ends_of(lengths_ref)

    @pl.when(pl.program_id(0) == 0)
    def _():
        state[...] = jnp.zeros_like(state)

    v = Chunk(c0, ends, zx, before, sd, sd_before, wide, narrow, rates)
    state_low = state[...].astype(bf16)
    states[...] = state_low
    for i in range(v.width // LANES):
        cols = slice(i * LANES, (i + 1) * LANES)
        xc = v.xc[:, cols]
        xs = v.pair(v.step, i) * xc
        xs_low = xs.astype(bf16)
        first = (v.spread(2 * i) * v.inner).astype(bf16)
        second = (v.spread(2 * i + 1) * v.inner).astype(bf16)
        y = jnp.where(v.low_half, mm(first, xs_low), mm(second, xs_low))
        y = y + v.pair(v.into, i) * mm(v.c_low, state_low[:, cols])
        y = y + wide[4:5, cols] * xc
        z = v.z[:, cols]
        gated[:, cols] = (y * z * jax.nn.sigmoid(z)).astype(bf16)
        state[:, cols] = v.pair(v.decay, i) * state[:, cols] + mm_tn(
            v.b_low, (v.pair(v.onto, i) * xs).astype(bf16)
        )


def split_sum(values, ones):
    high = values.astype(bf16)
    low = (values - high.astype(f32)).astype(bf16)
    return mm(high, ones) + mm(low, ones)


def mixer_backward_kernel(
    chunks,
    place_ref,
    lengths_ref,
    zx,
    before,
    sd,
    sd_before,
    grad_scaled,
    stats,
    states,
    wide,
    narrow,
    rates,
    grad_zx,
    grad_sd,
    grad_wide,
    grad_narrow,
    grad_rates,
    grad_state,
    next_pre,
    next_pre_s,
    carry,
    products,
    directs,
    grad_pre,
):
    rows = zx.shape[0]
    turn = pl.program_id(0)
    c0 = (chunks - 1 - turn) * rows
    ends = ends_of(lengths_ref)

    @pl.when(turn == 0)
    def _():
        for ref in (grad_state, next_pre, next_pre_s, carry, grad_wide, grad_narrow, grad_rates):
            ref[...] = jnp.zeros_like(ref)

    v = Chunk(c0, ends, zx, before, sd, sd_before, wide, narrow, rates)
    width = v.width
    root, pull = stats[:, 0:1], stats[:, 1:2]
    grad_inner = jnp.zeros((rows, rows), f32)
    grad_b = jnp.zeros((rows, HD), f32)
    grad_c = jnp.zeros((rows, HD), f32)
    for i in range(width // LANES):
        cols = slice(i * LANES, (i + 1) * LANES)
        xc = v.xc[:, cols]
        step = v.pair(v.step, i)
        xs = step * xc
        xs_low = xs.astype(bf16)
        spread_a, spread_b = v.spread(2 * i), v.spread(2 * i + 1)
        first = (spread_a * v.inner).astype(bf16)
        second = (spread_b * v.inner).astype(bf16)
        state_low = states[:, cols]
        into, onto = v.pair(v.into, i), v.pair(v.onto, i)
        y = jnp.where(v.low_half, mm(first, xs_low), mm(second, xs_low))
        y = y + into * mm(v.c_low, state_low)
        skip, gain = wide[4:5, cols], wide[5:6, cols]
        whole = y + skip * xc
        z = v.z[:, cols]
        gate = jax.nn.sigmoid(z)
        gated = whole * z * gate
        incoming = grad_scaled[:, cols].astype(f32)
        rooted = incoming * root
        grad_wide[5:6, cols] += jnp.sum(rooted * gated, axis=0, keepdims=True)
        grad_gated = rooted * gain - gated * pull
        grad_y = grad_gated * z * gate
        grad_zx[:, cols] = (grad_gated * whole * silu_grad(z, gate)).astype(bf16)
        grad_wide[4:5, cols] += jnp.sum(grad_y * xc, axis=0, keepdims=True)
        low = grad_y.astype(bf16)
        low_a = jnp.where(v.low_half, grad_y, 0.0).astype(bf16)
        low_b = jnp.where(v.low_half, 0.0, grad_y).astype(bf16)
        grad_inner = grad_inner + spread_a * mm_nt(low_a, xs_low) + spread_b * mm_nt(low_b, xs_low)
        grad_end = grad_state[:, cols]
        grad_end_low = grad_end.astype(bf16)
        grad_xs = jnp.where(v.low_half, mm_tn(first, low), mm_tn(second, low))
        grad_xs = grad_xs + onto * mm(v.b_low, grad_end_low)
        into_y = (into * grad_y).astype(bf16)
        onto_x = (onto * xs).astype(bf16)
        grad_b = grad_b + mm_nt(onto_x, grad_end_low)
        grad_c = grad_c + mm_nt(into_y, state_low)
        grad_state[:, cols] = v.pair(v.decay, i) * grad_end + mm_tn(v.c_low, into_y)
        products[:, cols] = low.astype(f32) * y - xs_low.astype(f32) * grad_xs
        directs[:, cols] = xc * grad_xs
        grad_xc = step * grad_xs + skip * grad_y
        grad_pre[:, cols] = grad_xc * silu_grad(v.pre[:, cols], v.gate_x[:, cols])
    grad_inner = jnp.where(v.allowed, grad_inner, 0.0).astype(bf16)
    grad_b = grad_b + mm_tn(grad_inner, v.c_low)
    grad_c = grad_c + mm(grad_inner, v.b_low)

    lane, head = iota((width, LANES), 0), iota((width, LANES), 1)
    ones = ((lane >= head * HD) & (lane < head * HD + HD)).astype(bf16)
    grad_cum = split_sum(products[...], ones)
    direct = split_sum(directs[...], ones)
    row, col = iota((rows, rows), 0), iota((rows, rows), 1)
    col_start = starts_of(c0 + iota((1, rows), 1), ends)
    above = ((col >= row) & (col_start <= c0 + row)).astype(f32)
    next_start = starts_of(c0 + rows, ends)
    reaches = (v.index >= next_start).astype(f32)
    after = jnp.dot(above, grad_cum, precision=HIGHEST, preferred_element_type=f32) + reaches * carry[0:1, :]
    flux = jnp.sum(grad_state[...] * states[...].astype(f32), axis=0, keepdims=True)
    carry[...] = split_sum(jnp.broadcast_to(flux, (8, width)), ones)
    grad_log = -v.step * v.rate * after
    grad_raw = (direct - v.rate * after) * jax.nn.sigmoid(v.raw)
    grad_rates[0:1, :] += jnp.sum(grad_raw, axis=0, keepdims=True)
    grad_rates[1:2, :] += jnp.sum(grad_log, axis=0, keepdims=True)

    index_ext = c0 + iota((rows + 8, 1), 0)
    position_ext = index_ext - starts_of(index_ext, ends)
    taps_back(v.x_ext, grad_pre[...], v.position, grad_wide)
    extended = jnp.concatenate([grad_pre[...], next_pre[...]], axis=0)
    grad_zx[:, width:] = conv_back(extended, wide, position_ext).astype(bf16)
    next_pre[...] = grad_pre[0:8, :]

    blank = jnp.zeros((rows, LANES - HD), f32)
    grad_sc = jnp.concatenate([grad_b, blank, grad_c, blank], axis=1)
    grad_pre_s = grad_sc * silu_grad(v.pre_s, v.gate_s)
    taps_back(v.s_ext, grad_pre_s, v.position, grad_narrow)
    extended_s = jnp.concatenate([grad_pre_s, next_pre_s[...]], axis=0)
    grad_sd[:, : 2 * LANES] = conv_back(extended_s, narrow, position_ext).astype(bf16)
    next_pre_s[...] = grad_pre_s[0:8, :]
    grad_sd[:, 2 * LANES :] = grad_raw.astype(bf16)


def mixer_specs(tp, rows, width, order):
    share = rows // tp
    per_share = share // CHUNK

    def here(place, c):
        owner = lax.div(c, per_share)
        piece = lax.rem(place[0] - owner + tp, tp)
        return piece * per_share + lax.rem(c, per_share)

    def chunk_map(i, place, lengths):
        return (here(place, order(i)), 0)

    def before_map(unit, column):
        def index(i, place, lengths):
            c = order(i)
            previous = jnp.maximum(c - 1, 0)
            return (here(place, previous) * (CHUNK // unit) + CHUNK // unit - 1, column)

        return index

    def fixed(i, place, lengths):
        return (0, 0)

    return chunk_map, before_map, fixed


def mixer_forward(place, lengths, tp, zx, sd, wide, narrow, rates):
    rows, width = zx.shape[0], zx.shape[1] // 2
    chunks = rows // CHUNK
    chunk_map, before_map, fixed = mixer_specs(tp, rows, width, lambda i: i)
    work = rows * width * CHUNK
    return pl.pallas_call(
        mixer_forward_kernel,
        out_shape=[
            jax.ShapeDtypeStruct((rows, width), bf16),
            jax.ShapeDtypeStruct((chunks, HD, width), bf16),
        ],
        grid_spec=pltpu.PrefetchScalarGridSpec(
            num_scalar_prefetch=2,
            grid=(chunks,),
            in_specs=[
                pl.BlockSpec((CHUNK, 2 * width), chunk_map),
                pl.BlockSpec((16, width), before_map(16, 1)),
                pl.BlockSpec((CHUNK, 3 * LANES), chunk_map),
                pl.BlockSpec((8, 3 * LANES), before_map(8, 0)),
                pl.BlockSpec((8, width), fixed),
                pl.BlockSpec((8, 2 * LANES), fixed),
                pl.BlockSpec((8, LANES), fixed),
            ],
            out_specs=[
                pl.BlockSpec((CHUNK, width), chunk_map),
                pl.BlockSpec((None, HD, width), lambda i, *_: (i, 0, 0)),
            ],
            scratch_shapes=[pltpu.VMEM((HD, width), f32)],
        ),
        compiler_params=pltpu.CompilerParams(vmem_limit_bytes=VMEM_LIMIT),
        cost_estimate=pl.CostEstimate(
            flops=8 * work, bytes_accessed=8 * rows * width, transcendentals=4 * rows * width
        ),
        name="mixer_forward",
    )(place, lengths, zx, zx, sd, sd, wide, narrow, rates)


def mixer_backward(place, lengths, tp, zx, sd, grad_scaled, stats, states, wide, narrow, rates):
    rows, width = zx.shape[0], zx.shape[1] // 2
    chunks = rows // CHUNK
    chunk_map, before_map, fixed = mixer_specs(tp, rows, width, lambda i: chunks - 1 - i)
    work = rows * width * CHUNK
    return pl.pallas_call(
        functools.partial(mixer_backward_kernel, chunks),
        out_shape=[
            jax.ShapeDtypeStruct((rows, 2 * width), bf16),
            jax.ShapeDtypeStruct((rows, 3 * LANES), bf16),
            jax.ShapeDtypeStruct((8, width), f32),
            jax.ShapeDtypeStruct((8, 2 * LANES), f32),
            jax.ShapeDtypeStruct((8, LANES), f32),
        ],
        grid_spec=pltpu.PrefetchScalarGridSpec(
            num_scalar_prefetch=2,
            grid=(chunks,),
            in_specs=[
                pl.BlockSpec((CHUNK, 2 * width), chunk_map),
                pl.BlockSpec((16, width), before_map(16, 1)),
                pl.BlockSpec((CHUNK, 3 * LANES), chunk_map),
                pl.BlockSpec((8, 3 * LANES), before_map(8, 0)),
                pl.BlockSpec((CHUNK, width), chunk_map),
                pl.BlockSpec((CHUNK, 2), chunk_map),
                pl.BlockSpec((None, HD, width), lambda i, *_: (chunks - 1 - i, 0, 0)),
                pl.BlockSpec((8, width), fixed),
                pl.BlockSpec((8, 2 * LANES), fixed),
                pl.BlockSpec((8, LANES), fixed),
            ],
            out_specs=[
                pl.BlockSpec((CHUNK, 2 * width), chunk_map),
                pl.BlockSpec((CHUNK, 3 * LANES), chunk_map),
                pl.BlockSpec((8, width), fixed),
                pl.BlockSpec((8, 2 * LANES), fixed),
                pl.BlockSpec((8, LANES), fixed),
            ],
            scratch_shapes=[
                pltpu.VMEM((HD, width), f32),
                pltpu.VMEM((8, width), f32),
                pltpu.VMEM((8, 2 * LANES), f32),
                pltpu.VMEM((8, LANES), f32),
                pltpu.VMEM((CHUNK, width), f32),
                pltpu.VMEM((CHUNK, width), f32),
                pltpu.VMEM((CHUNK, width), f32),
            ],
        ),
        compiler_params=pltpu.CompilerParams(vmem_limit_bytes=VMEM_LIMIT),
        cost_estimate=pl.CostEstimate(
            flops=24 * work, bytes_accessed=12 * rows * width, transcendentals=5 * rows * width
        ),
        name="mixer_backward",
    )(place, lengths, zx, zx, sd, sd, grad_scaled, stats, states, wide, narrow, rates)


def ring_gather(own):
    tp = lax.axis_size("tp")
    pairs = [(i, (i + 1) % tp) for i in range(tp)]
    pieces = [own]
    for _ in range(tp - 1):
        pieces.append(lax.ppermute(pieces[-1], "tp", pairs))
    return pieces


def ring_scatter(part):
    tp = lax.axis_size("tp")
    pairs = [(i, (i + 1) % tp) for i in range(tp)]
    total = part(1 % tp)
    for p in range(2, tp + 1):
        moved = lax.ppermute(total.astype(bf16), "tp", pairs)
        total = moved.astype(f32) + part(p % tp)
    return total


def inverse_root(values):
    return lax.rsqrt(jnp.mean(values * values, axis=1, keepdims=True) + norm_eps)


def rms_backward(values, inv_root, gain, grad_out):
    unit_rows = values * inv_root
    grad_gain = jnp.sum(grad_out * unit_rows, axis=0)
    grad_unit = grad_out * gain
    grad_values = inv_root * (
        grad_unit - unit_rows * jnp.mean(grad_unit * unit_rows, axis=-1, keepdims=True)
    )
    return (grad_values, grad_gain)


def gather(values, axis=0):
    return lax.all_gather(values, "fsdp", axis=axis, tiled=True)


def scatter(values, axis=0):
    return lax.psum_scatter(values, "fsdp", scatter_dimension=axis, tiled=True)


def local(
    hidden,
    embed,
    lengths,
    attention_norm_gain,
    query_key_value_weight,
    attention_adapter_down,
    attention_adapter_up,
    attention_output_weight,
    feedforward_norm_gain,
    gate_up_weight,
    feedforward_adapter_down,
    feedforward_adapter_up,
    down_weight,
    mixer_norm_gain,
    gate_inner_weight,
    state_input_weight,
    step_projection,
    inner_conv_taps,
    state_conv_taps,
    head_step_bias,
    decay_log_rate,
    inner_skip_gains,
    gated_norm_gain,
    mixer_output_weight,
    output_cotangent,
):
    tp = lax.axis_size("tp")
    fsdp = lax.axis_size("fsdp")
    share, width = hidden.shape
    rows = share * tp
    here = lax.axis_index("tp").astype(jnp.int32)
    place = here.reshape(1)
    lengths = lengths.reshape(-1)
    rank = attention_adapter_down.shape[2]
    head_cols = query_key_value_weight.shape[2]
    units_here = gate_up_weight.shape[2]
    inner_cols = gate_inner_weight.shape[2]
    mixer_heads = inner_cols // HD
    states = state_input_weight.shape[2]
    count = inner_conv_taps.shape[0]
    inner_total = inner_cols * tp

    small = [
        attention_norm_gain,
        feedforward_norm_gain,
        mixer_norm_gain,
        inner_conv_taps.reshape(-1),
        state_conv_taps.reshape(-1),
        inner_skip_gains.reshape(-1),
        gated_norm_gain.reshape(-1),
    ]
    sizes = [v.shape[0] for v in small]
    padding = -sum(sizes) % LANES
    packed = jnp.concatenate(small + [jnp.zeros((padding,), bf16)]).reshape(1, -1)
    spread = gather(packed).astype(f32)
    cuts = [sum(sizes[:i]) for i in range(len(sizes) + 1)]
    parts = [spread[:, cuts[i] : cuts[i + 1]] for i in range(len(sizes))]
    gain_attn, gain_mlp, gain_mixer = (parts[i].reshape(1, -1) for i in range(3))
    taps_x = parts[3].reshape(fsdp, count, mixer_heads, -1)
    taps_x = jnp.transpose(taps_x, (1, 2, 0, 3)).reshape(count, inner_cols)
    taps_s = parts[4].reshape(fsdp, count, 2, -1)
    taps_s = jnp.transpose(taps_s, (1, 2, 0, 3)).reshape(count, 2, states)
    skip = jnp.transpose(parts[5].reshape(fsdp, mixer_heads, -1), (1, 0, 2)).reshape(1, inner_cols)
    gain_gate = jnp.transpose(parts[6].reshape(fsdp, mixer_heads, -1), (1, 0, 2)).reshape(1, inner_cols)
    wide = jnp.concatenate([taps_x, skip, gain_gate, jnp.zeros((2, inner_cols), f32)], axis=0)
    narrow = jnp.pad(taps_s, ((0, 8 - count), (0, 0), (0, LANES - states))).reshape(8, 2 * LANES)
    rates = jnp.pad(
        jnp.stack([head_step_bias, decay_log_rate]), ((0, 6), (0, LANES - mixer_heads))
    )

    weights_qkv = [gather(query_key_value_weight[:, j, :]) for j in range(3)]
    adapter_down = gather(attention_adapter_down.reshape(-1, 3 * rank))
    ups = jnp.concatenate(
        [attention_adapter_up.reshape(-1, 3 * head_cols), feedforward_adapter_up.reshape(-1, 2 * units_here)],
        axis=1,
    )
    ups = gather(ups)
    adapter_up = [ups[:, j * head_cols : (j + 1) * head_cols] for j in range(3)]
    fc_up = ups[:, 3 * head_cols :]
    weight_o = gather(attention_output_weight, 1)
    lanes_s = jnp.pad(state_input_weight, ((0, 0), (0, 0), (0, LANES - states))).reshape(-1, 2 * LANES)
    lanes_t = jnp.pad(step_projection, ((0, 0), (0, LANES - mixer_heads)))
    downs = gather(jnp.concatenate([lanes_s, lanes_t, feedforward_adapter_down], axis=1))
    weight_sd, fc_down = downs[:, : 3 * LANES], downs[:, 3 * LANES :]
    weight_fc1 = gather(gate_up_weight.reshape(-1, 2 * units_here))
    weight_fc2 = gather(down_weight, 1)
    weight_zx = gather(gate_inner_weight.reshape(-1, 2 * inner_cols))
    weight_out = gather(mixer_output_weight, 1)

    places = jnp.arange(rows, dtype=jnp.int32)
    ends = [jnp.sum(lengths[: i + 1]) for i in range(lengths.shape[0] - 1)]
    position = places - starts_of(places, ends)
    freqs = jnp.exp(jnp.arange(HDA // 2, dtype=f32) * (-2.0 * math.log(10000.0) / HDA))
    angles = position.astype(f32)[:, None] * freqs[None, :]
    cosine = jnp.cos(angles)
    sine = jnp.sin(angles)
    cosine = jnp.concatenate([cosine, cosine], axis=1)
    sine = jnp.concatenate([-sine, sine], axis=1)

    joined = jnp.concatenate([hidden.astype(f32), embed.astype(f32)], axis=1)
    attn_root = inverse_root(joined)
    normed = ring_gather((joined * attn_root * gain_attn).astype(bf16))
    lora_mid = [mm(piece, adapter_down).astype(bf16) for piece in normed]

    def project(p, j):
        middle = lora_mid[p][:, j * rank : (j + 1) * rank]
        return mm(normed[p], weights_qkv[j]) + mm(middle, adapter_up[j])

    projected = [[project(p, j) for j in range(3)] for p in range(tp)]
    attended, queries, keys, values = attention_forward(place, lengths, projected, cosine, sine)

    def piece(values, p):
        return values[p * share : (p + 1) * share]

    mixed = ring_scatter(lambda p: mm(piece(attended, p), weight_o))

    mlp_root = inverse_root(mixed)
    mlp_in = ring_gather((mixed * mlp_root * gain_mlp).astype(bf16))
    fc_mid = [mm(v, fc_down).astype(bf16) for v in mlp_in]
    gate_up = [(mm(mlp_in[p], weight_fc1) + mm(fc_mid[p], fc_up)).astype(bf16) for p in range(tp)]

    def unit_rows(p):
        gate = gate_up[p][:, :units_here].astype(f32)
        up = gate_up[p][:, units_here:].astype(f32)
        return (jax.nn.gelu(gate) * up).astype(bf16)

    units = [unit_rows(p) for p in range(tp)]
    branch = ring_scatter(lambda p: mm(units[p], weight_fc2))
    residual = hidden.astype(f32) + mixed + branch

    mixer_root = inverse_root(residual)
    mixer_in = ring_gather((residual * mixer_root * gain_mixer).astype(bf16))
    out_grad = ring_gather(output_cotangent)
    mixer_rows = jnp.concatenate(mixer_in, axis=0)
    zx = jnp.concatenate([mm(v, weight_zx).astype(bf16) for v in mixer_in], axis=0)
    sd = mm(mixer_rows, weight_sd)
    gated, chunk_states = mixer_forward(place, lengths, tp, zx, sd, wide, narrow, rates)
    out_grad_rows = jnp.concatenate(out_grad, axis=0)
    grad_scaled = mm_nt(out_grad_rows, weight_out).astype(bf16)
    gated_wide = gated.astype(f32)
    sums = jnp.stack(
        [
            jnp.sum(gated_wide * gated_wide, axis=1),
            jnp.sum(grad_scaled.astype(f32) * gain_gate * gated_wide, axis=1),
        ],
        axis=0,
    )
    sums = jnp.roll(jnp.flip(sums.reshape(2, tp, share), axis=1), here + 1, axis=1)
    sums = lax.psum(sums, "tp")
    sums = jnp.flip(jnp.roll(sums, -(here + 1), axis=1), axis=1).reshape(2, rows)
    gate_root = lax.rsqrt(sums[0] / inner_total + norm_eps)
    stats = jnp.stack([gate_root, gate_root**3 * sums[1] / inner_total], axis=1)
    scaled = (gated_wide * gate_root[:, None] * gain_gate).astype(bf16)
    out = residual + ring_scatter(lambda p: mm(piece(scaled, p), weight_out))
    grad_w_out = scatter(mm_tn(scaled, out_grad_rows).astype(bf16), 1).astype(f32)

    grad_zx, grad_sd, grad_wide, grad_narrow, grad_rates = mixer_backward(
        place, lengths, tp, zx, sd, grad_scaled, stats, chunk_states, wide, narrow, rates
    )
    grad_mixer_in = ring_scatter(
        lambda p: mm_nt(piece(grad_zx, p), weight_zx) + mm_nt(piece(grad_sd, p), weight_sd)
    )
    grad_w_zx = scatter(mm_tn(mixer_rows, grad_zx).astype(bf16)).astype(f32)
    grad_w_sd = mm_tn(mixer_rows, grad_sd)
    grad_resid_norm, grad_gain_mixer = rms_backward(residual, mixer_root, gain_mixer, grad_mixer_in)
    grad_residual = output_cotangent.astype(f32) + grad_resid_norm

    grad_branch = ring_gather(grad_residual.astype(bf16))

    def gate_up_back(p):
        grad_units = mm_nt(grad_branch[p], weight_fc2)
        gate = gate_up[p][:, :units_here].astype(f32)
        up = gate_up[p][:, units_here:].astype(f32)
        raised, back = jax.vjp(jax.nn.gelu, gate)
        return jnp.concatenate(
            [back(grad_units * up)[0].astype(bf16), (grad_units * raised).astype(bf16)], axis=1
        )

    grad_gate_up = [gate_up_back(p) for p in range(tp)]
    grad_fc_mid = [mm_nt(v, fc_up).astype(bf16) for v in grad_gate_up]
    grad_mlp_in = ring_scatter(
        lambda p: mm_nt(grad_gate_up[p], weight_fc1) + mm_nt(grad_fc_mid[p], fc_down)
    )
    mlp_rows = jnp.concatenate(mlp_in, axis=0)
    grad_gate_up_rows = jnp.concatenate(grad_gate_up, axis=0)
    grad_w_fc2 = scatter(
        mm_tn(jnp.concatenate(units, axis=0), jnp.concatenate(grad_branch, axis=0)).astype(bf16), 1
    ).astype(f32)
    grad_w_fc1 = scatter(mm_tn(mlp_rows, grad_gate_up_rows).astype(bf16)).astype(f32)
    grad_fc_up = mm_tn(jnp.concatenate(fc_mid, axis=0), grad_gate_up_rows)
    grad_fc_down = mm_tn(mlp_rows, jnp.concatenate(grad_fc_mid, axis=0))
    grad_mixed_norm, grad_gain_mlp = rms_backward(mixed, mlp_root, gain_mlp, grad_mlp_in)

    grad_mixed = ring_gather((grad_residual + grad_mixed_norm).astype(bf16))
    grad_attended = [mm_nt(v, weight_o).astype(bf16) for v in grad_mixed]
    grad_w_o = scatter(mm_tn(attended, jnp.concatenate(grad_mixed, axis=0)).astype(bf16), 1).astype(f32)
    grad_projected = attention_backward(
        place, lengths, queries, keys, values, grad_attended, cosine, sine
    )
    normed_rows = jnp.concatenate(normed, axis=0)
    lora_rows = jnp.concatenate(lora_mid, axis=0)
    grad_lora = jnp.concatenate(
        [mm_nt(grad_projected[j], adapter_up[j]).astype(bf16) for j in range(3)], axis=1
    )

    def normed_back(p):
        total = mm_nt(piece(grad_lora, p), adapter_down)
        for j in range(3):
            total = total + mm_nt(piece(grad_projected[j], p), weights_qkv[j])
        return total

    grad_normed = ring_scatter(normed_back)
    grad_w_qkv = [
        scatter(mm_tn(normed_rows, grad_projected[j]).astype(bf16)).astype(f32) for j in range(3)
    ]
    grad_up = [
        mm_tn(lora_rows[:, j * rank : (j + 1) * rank], grad_projected[j]) for j in range(3)
    ]
    grad_down = scatter(mm_tn(normed_rows, grad_lora).astype(bf16))
    grad_down = lax.psum_scatter(grad_down, "tp", scatter_dimension=0, tiled=True).astype(f32)
    grad_joined, grad_gain_attn = rms_backward(joined, attn_root, gain_attn, grad_normed)
    grad_hidden = grad_residual + grad_joined[:, :width]
    grad_embed = grad_joined[:, width:]

    grad_ups = scatter(jnp.concatenate(grad_up + [grad_fc_up], axis=1).astype(bf16)).astype(f32)
    grad_downs = scatter(jnp.concatenate([grad_w_sd, grad_fc_down], axis=1).astype(bf16)).astype(f32)
    grad_w_dt = grad_downs[:, 2 * LANES : 2 * LANES + mixer_heads]
    shared = jnp.concatenate([grad_downs[:, : 2 * LANES], grad_downs[:, 3 * LANES :]], axis=1)

    def by_fsdp(values):
        lead = values.shape[:-1]
        cut = values.reshape(lead + (fsdp, values.shape[-1] // fsdp))
        return jnp.moveaxis(cut, -2, 0).reshape(fsdp, -1)

    grad_taps_x = grad_wide[:count].reshape(count, mixer_heads, HD)
    grad_taps_s = grad_narrow[:count].reshape(count, 2, LANES)[:, :, :states]
    local_small = [
        by_fsdp(grad_taps_x),
        by_fsdp(grad_wide[4].reshape(mixer_heads, HD)),
        by_fsdp(grad_wide[5].reshape(mixer_heads, HD)),
        jnp.broadcast_to(grad_rates[:2, :mixer_heads].reshape(1, -1), (fsdp, 2 * mixer_heads)),
    ]
    shared_small = [by_fsdp(grad_taps_s), by_fsdp(grad_gain_mixer), by_fsdp(grad_gain_mlp)]
    small_sizes = [v.shape[1] for v in local_small + shared_small]
    small_cuts = [sum(small_sizes[:i]) for i in range(len(small_sizes) + 1)]
    small_sum = lax.psum_scatter(
        jnp.concatenate(local_small + shared_small, axis=1), "fsdp", scatter_dimension=0, tiled=True
    ).reshape(-1)
    small_parts = [small_sum[small_cuts[i] : small_cuts[i + 1]] for i in range(len(small_sizes))]
    shared, tail = lax.psum((shared, small_sum[small_cuts[4] :]), "tp")
    tail_cuts = [v - small_cuts[4] for v in small_cuts[4:]]
    grad_conv_bc, sum_gain_mixer, sum_gain_mlp = (
        tail[tail_cuts[i] : tail_cuts[i + 1]] for i in range(3)
    )
    grad_gain_attn = lax.psum_scatter(grad_gain_attn, ("fsdp", "tp"), scatter_dimension=0, tiled=True)
    sum_rates = small_parts[3].reshape(2, mixer_heads)
    return (
        out,
        grad_hidden,
        grad_embed,
        grad_gain_attn,
        jnp.stack(grad_w_qkv, axis=1),
        grad_down.reshape(-1, 3, rank),
        grad_ups[:, : 3 * head_cols].reshape(-1, 3, head_cols),
        grad_w_o,
        sum_gain_mlp,
        grad_w_fc1.reshape(-1, 2, units_here),
        shared[:, 2 * LANES :],
        grad_ups[:, 3 * head_cols :].reshape(-1, 2, units_here),
        grad_w_fc2,
        sum_gain_mixer,
        grad_w_zx.reshape(-1, 2, inner_cols),
        shared[:, : 2 * LANES].reshape(-1, 2, LANES)[:, :, :states],
        grad_w_dt,
        small_parts[0].reshape(count, mixer_heads, -1),
        grad_conv_bc.reshape(count, 2, -1),
        sum_rates[0],
        sum_rates[1],
        small_parts[1].reshape(mixer_heads, -1),
        small_parts[2].reshape(mixer_heads, -1),
        grad_w_out,
    )


def solution(mesh):
    placed = (
        P(("fsdp", "tp"), None),
        P(("fsdp", "tp"), None),
        P("fsdp", None),
        P("fsdp"),
        P("fsdp", None, "tp"),
        P("fsdp", None, None),
        P("fsdp", None, "tp"),
        P("tp", "fsdp"),
        P("fsdp"),
        P("fsdp", None, "tp"),
        P("fsdp", None),
        P("fsdp", None, "tp"),
        P("tp", "fsdp"),
        P("fsdp"),
        P("fsdp", None, "tp"),
        P("fsdp", None, None),
        P("fsdp", "tp"),
        P(None, "tp", "fsdp"),
        P(None, None, "fsdp"),
        P("tp"),
        P("tp"),
        P("tp", "fsdp"),
        P("tp", "fsdp"),
        P("tp", "fsdp"),
        P(("fsdp", "tp"), None),
    )
    return jax.shard_map(
        local,
        mesh=mesh,
        in_specs=placed,
        out_specs=(
            P(("fsdp", "tp"), None),
            P(("fsdp", "tp"), None),
            P(("fsdp", "tp"), None),
            P(("fsdp", "tp")),
            P("fsdp", None, "tp"),
            P(("fsdp", "tp"), None, None),
            P("fsdp", None, "tp"),
            P("tp", "fsdp"),
            P("fsdp"),
            P("fsdp", None, "tp"),
            P("fsdp", None),
            P("fsdp", None, "tp"),
            P("tp", "fsdp"),
            P("fsdp"),
            P("fsdp", None, "tp"),
            P("fsdp", None, None),
            P("fsdp", "tp"),
            P(None, "tp", "fsdp"),
            P(None, None, "fsdp"),
            P("tp"),
            P("tp"),
            P("tp", "fsdp"),
            P("tp", "fsdp"),
            P("tp", "fsdp"),
        ),
        check_vma=False,
    )
```

time: 4360 us -> 2000 us (0.46)
  waiting for transfers between devices: 2490 us -> 1050 us
  matrix products: 943 us -> 577 us
  local copies, waits for them, and re-layouts: 388 us -> 74.3 us
  other arithmetic: 273 us -> 56.6 us
  blocking collectives: 231 us -> 93.9 us
  Pallas kernels: 0 us -> 115 us
    reduce_scatter x14 -> x12, waiting for transfers between devices: 1320 us -> 337 us  [the longest x11 337 us: scatter(): return lax.psum_scatter(values, 'fsdp', scatter_dimension=axis, tiled=True)]
    psum x3 -> x1, waiting for transfers between devices: 825 us -> 0.01 us  [local(): shared, tail = lax.psum((shared, small_sum[small_cuts[4]:]), 'tp')]
    ppermute x0 -> x36, waiting for transfers between devices: none -> 671 us  [the longest x18 376 us: ring_gather(): pieces.append(lax.ppermute(pieces[-1], 'tp', pairs))]
    dot_general x93 -> x120, matrix products: 943 us -> 577 us  [the longest x48 229 us: mm_nt(): lax.dot_general(left, right, (((1,), (1,)), ((), ())), preferred_element_...]
    all_gather x11, waiting for transfers between devices: 341 us -> 37.1 us  [gather(): return lax.all_gather(values, 'fsdp', axis=axis, tiled=True)]
    all_gather x12 -> x1, blocking collectives: 129 us -> 10.7 us  [gather(): return lax.all_gather(values, 'fsdp', axis=axis, tiled=True)]
    pallas_call x0 -> x4, Pallas kernels: none -> 115 us  [the longest x1 37 us: mixer_backward(): pl.pallas_call(functools.partial(mixer_backward_kernel, chunks), out_shap...]
    all_gather x8 -> x0, local copies, waits for them, and re-layouts: 75.2 us -> none  [the longest x1 33.6 us: fetch_weights(): lax.all_gather(query_key_value_weight, 'fsdp', axis=0, tiled=True)]
  transfers between devices with their start and end apart: 30 -> 60, of which waited for: 17 -> 37; matrix products, arithmetic and copies ran while one was open for 25% -> 32% of each run, Pallas kernels for 0% -> 6%
where the time goes in v1:
time: 2000 us
  waiting for transfers between devices  1050 us (52%)
  matrix products  577 us (29%)
  Pallas kernels  115 us (6%)
  blocking collectives  93.9 us (5%)
  local copies, waits for them, and re-layouts  74.3 us (4%)
  other arithmetic  56.6 us (3%)
    ppermute x18, waiting for transfers between devices, ring_gather(): pieces.append(lax.ppermute(pieces[-1], 'tp', pairs))  376 us
    reduce_scatter x11, waiting for transfers between devices, scatter(): return lax.psum_scatter(values, 'fsdp', scatter_dimension=axis, tiled=True)  337 us
    ppermute x18, waiting for transfers between devices, ring_scatter(): moved = lax.ppermute(total.astype(bf16), 'tp', pairs)  296 us
    dot_general x48, matrix products, mm_nt(): lax.dot_general(left, right, (((1,), (1,)), ((), ())), preferred_element_...  229 us
    dot_general x57, matrix products, mm(): return jnp.dot(left, right, preferred_element_type=f32)  204 us
    dot_general x15, matrix products, mm_tn(): lax.dot_general(left, right, (((0,), (0,)), ((), ())), preferred_element_...  144 us
    unnamed x2, blocking collectives  66.1 us
  transfers between devices with their start and end apart: 60, of which 37 were waited for; matrix products, arithmetic and copies ran while one was open for 32% of the time, Pallas kernels for 6%

profile of v1, /device:TPU:0, one launch (start us, length us, event | category | flops | bytes accessed | tf_op | source)
XLA Modules:
  0.0 1996.8 jit_solution(14365448457950056543)
XLA Ops:
  39.3 48.1 %collective-permute-done = bf16[256,4096]{1,0:T(8,128)(2,1)S(1)} collective-permute-done((bf16[256,4096]{1,0:T(8,128)(2,1)S(1)}, bf16[256,4096]{1,0:T(8,128)(2,1)S(1)}, u32[]{:S(2)}, u32[]{:S(2)}) %collective-permute-start) | collective-permute-done | bytes 2097184 | tf_op jit(solution)/shard_map/ppermute | solution.py:556
  93.6 42.8 %collective-permute-done.1 = bf16[256,4096]{1,0:T(8,128)(2,1)} collective-permute-done((bf16[256,4096]{1,0:T(8,128)(2,1)S(1)}, bf16[256,4096]{1,0:T(8,128)(2,1)}, u32[]{:S(2)}, u32[]{:S(2)}) %collective-permute-start.1) | collective-permute-done | bytes 2097184 | tf_op jit(solution)/shard_map/ppermute | solution.py:556
  154.9 30.1 %collective-permute-done.2 = bf16[256,4096]{1,0:T(8,128)(2,1)} collective-permute-done((bf16[256,4096]{1,0:T(8,128)(2,1)}, bf16[256,4096]{1,0:T(8,128)(2,1)}, u32[]{:S(2)}, u32[]{:S(2)}) %collective-permute-start.2) | collective-permute-done | bytes 2097184 | tf_op jit(solution)/shard_map/ppermute | solution.py:556
  208.6 37.0 %all-gather.33.cloned.1.call-done = bf16[4096,1,1024]{2,0,1:T(8,128)(2,1)} async-done(((bf16[512,1,1024]{2,0,1:T(8,128)(2,1)}), bf16[4096,1,1024]{2,0,1:T(8,128)(2,1)}) %all-gather.33.cloned.1.call-update) | async-done | bytes 8388624 | tf_op jit(solution)/shard_map/all_gather | solution.py:585
  299.0 24.9 %attention_forward.1 = (bf16[1024,1024]{1,0:T(8,128)(2,1)}, bf16[1024,1024]{1,0:T(8,128)(2,1)}, bf16[1024,1024]{1,0:T(8,128)(2,1)}, bf16[1024,1024]{1,0:T(8,128)(2,1)}) custom-call(s32[1]{0:T(128)} %bitcast.place_ref, s32[3]{0:T(128)} %bitcast.297, f32[1024,128]{1,0:T(8,128)} %get-tuple-element.202.cosine_ref, f32[1024,128]{1,0:T(8,128)} %get-tuple-element.203.sine_ref, ...), custom_call_target="tpu_custom_call" | custom-call | flops 4294967296 | bytes 20971520 | tf_op jit(solution)/shard_map/attention_forward/pallas_call | solution.py:99
  330.2 25.8 %collective-permute-done.3 = bf16[256,2048]{1,0:T(8,128)(2,1)S(1)} collective-permute-done((bf16[256,2048]{1,0:T(8,128)(2,1)S(1)}, bf16[256,2048]{1,0:T(8,128)(2,1)S(1)}, u32[]{:S(2)}, u32[]{:S(2)}) %collective-permute-start.3) | collective-permute-done | bytes 1048608 | tf_op jit(solution)/shard_map/ppermute | solution.py:565
  358.6 25.2 %collective-permute-done.4 = bf16[256,2048]{1,0:T(8,128)(2,1)S(1)} collective-permute-done((bf16[256,2048]{1,0:T(8,128)(2,1)S(1)}, bf16[256,2048]{1,0:T(8,128)(2,1)S(1)}, u32[]{:S(2)}, u32[]{:S(2)}) %collective-permute-start.4) | collective-permute-done | bytes 1048608 | tf_op jit(solution)/shard_map/ppermute | solution.py:565
  385.5 24.3 %collective-permute-done.5 = bf16[256,2048]{1,0:T(8,128)(2,1)S(1)} collective-permute-done((bf16[256,2048]{1,0:T(8,128)(2,1)S(1)}, bf16[256,2048]{1,0:T(8,128)(2,1)S(1)}, u32[]{:S(2)}, u32[]{:S(2)}) %collective-permute-start.5) | collective-permute-done | bytes 1048608 | tf_op jit(solution)/shard_map/ppermute | solution.py:565
  412.1 27.2 %collective-permute-done.6 = bf16[256,2048]{1,0:T(8,128)(2,1)} collective-permute-done((bf16[256,2048]{1,0:T(8,128)(2,1)S(1)}, bf16[256,2048]{1,0:T(8,128)(2,1)}, u32[]{:S(2)}, u32[]{:S(2)}) %collective-permute-start.6) | collective-permute-done | bytes 1048608 | tf_op jit(solution)/shard_map/ppermute | solution.py:556
  439.5 22.4 %collective-permute-done.15 = bf16[256,2048]{1,0:T(8,128)(2,1)} collective-permute-done((bf16[256,2048]{1,0:T(8,128)(2,1)S(1)}, bf16[256,2048]{1,0:T(8,128)(2,1)}, u32[]{:S(2)}, u32[]{:S(2)}) %collective-permute-start.15) | collective-permute-done | bytes 1048608 | tf_op jit(solution)/shard_map/ppermute | solution.py:556
  463.8 20.5 %collective-permute-done.8 = bf16[256,2048]{1,0:T(8,128)(2,1)} collective-permute-done((bf16[256,2048]{1,0:T(8,128)(2,1)}, bf16[256,2048]{1,0:T(8,128)(2,1)}, u32[]{:S(2)}, u32[]{:S(2)}) %collective-permute-start.8) | collective-permute-done | bytes 1048608 | tf_op jit(solution)/shard_map/ppermute | solution.py:556
  493.5 32.4 %collective-permute-done.10 = bf16[256,2048]{1,0:T(8,128)(2,1)S(1)} collective-permute-done((bf16[256,2048]{1,0:T(8,128)(2,1)}, bf16[256,2048]{1,0:T(8,128)(2,1)S(1)}, u32[]{:S(2)}, u32[]{:S(2)}) %collective-permute-start.10) | collective-permute-done | bytes 1048608 | tf_op jit(solution)/shard_map/ppermute | solution.py:556
  529.6 12.4 fusion.59
  587.5 15.9 collective-permute-done.7
  609.5 19.8 collective-permute-done.9
  633.1 19.1 collective-permute-done.11
  661.2 21.3 %collective-permute-done.12 = bf16[256,2048]{1,0:T(8,128)(2,1)} collective-permute-done((bf16[256,2048]{1,0:T(8,128)(2,1)S(1)}, bf16[256,2048]{1,0:T(8,128)(2,1)}, u32[]{:S(2)}, u32[]{:S(2)}) %collective-permute-start.12) | collective-permute-done | bytes 1048608 | tf_op jit(solution)/shard_map/ppermute | solution.py:556
  684.8 20.1 %collective-permute-done.17 = bf16[256,2048]{1,0:T(8,128)(2,1)S(1)} collective-permute-done((bf16[256,2048]{1,0:T(8,128)(2,1)}, bf16[256,2048]{1,0:T(8,128)(2,1)S(1)}, u32[]{:S(2)}, u32[]{:S(2)}) %collective-permute-start.17) | collective-permute-done | bytes 1048608 | tf_op jit(solution)/shard_map/ppermute | solution.py:556
  729.9 13.6 collective-permute-done.14
  753.8 17.6 mixer_forward.1
  801.6 37.0 %mixer_backward.1 = (bf16[1024,2048]{1,0:T(8,128)(2,1)}, bf16[1024,384]{1,0:T(8,128)(2,1)}, f32[8,1024]{1,0:T(8,128)}, f32[8,256]{1,0:T(8,128)}, f32[8,128]{1,0:T(8,128)}) custom-call(s32[1]{0:T(128)} %bitcast.place_ref, s32[3]{0:T(128)} %bitcast.299, bf16[1024,2048]{1,0:T(8,128)(2,1)} %pad_maximum_fusion.2.zx.before, ...), custom_call_target="tpu_custom_call" | custom-call | flops 3221225472 | bytes 12582912 | tf_op jit(solution)/shard_map/mixer_backward/pallas_call | solution.py:502
  851.8 16.2 collective-permute-done.21
  877.1 19.8 collective-permute-done.22
  898.5 20.8 %collective-permute-done.19 = bf16[256,2048]{1,0:T(8,128)(2,1)S(1)} collective-permute-done((bf16[256,2048]{1,0:T(8,128)(2,1)S(1)}, bf16[256,2048]{1,0:T(8,128)(2,1)S(1)}, u32[]{:S(2)}, u32[]{:S(2)}) %collective-permute-start.19) | collective-permute-done | bytes 1048608 | tf_op jit(solution)/shard_map/ppermute | solution.py:565
  921.0 20.7 %collective-permute-done.23 = bf16[256,2048]{1,0:T(8,128)(2,1)S(1)} collective-permute-done((bf16[256,2048]{1,0:T(8,128)(2,1)S(1)}, bf16[256,2048]{1,0:T(8,128)(2,1)S(1)}, u32[]{:S(2)}, u32[]{:S(2)}) %collective-permute-start.23) | collective-permute-done | bytes 1048608 | tf_op jit(solution)/shard_map/ppermute | solution.py:565
  943.4 12.8 collective-permute-done.20
  1037.2 18.9 collective-permute-done.28
  1083.1 12.3 fusion.134
  1095.5 14.7 collective-permute-done.29
  1114.3 23.1 %collective-permute-done.30 = bf16[256,2048]{1,0:T(8,128)(2,1)S(1)} collective-permute-done((bf16[256,2048]{1,0:T(8,128)(2,1)S(1)}, bf16[256,2048]{1,0:T(8,128)(2,1)S(1)}, u32[]{:S(2)}, u32[]{:S(2)}) %collective-permute-start.30) | collective-permute-done | bytes 1048608 | tf_op jit(solution)/shard_map/ppermute | solution.py:556
  1145.3 13.4 collective-permute-done.31
  1177.6 35.0 %attention_backward.1 = (bf16[1024,1024]{1,0:T(8,128)(2,1)}, bf16[1024,1024]{1,0:T(8,128)(2,1)}, bf16[1024,1024]{1,0:T(8,128)(2,1)}) custom-call(s32[1]{0:T(128)} %bitcast.place_ref, s32[3]{0:T(128)} %bitcast.300, f32[1024,128]{1,0:T(8,128)} %get-tuple-element.202.cosine_ref, f32[1024,128]{1,0:T(8,128)} %get-tuple-element.203.sine_ref, ...), custom_call_target="tpu_custom_call" | custom-call | flops 10737418240 | bytes 14680064 | tf_op jit(solution)/shard_map/attention_backward/pallas_call | solution.py:172
  1240.2 13.8 convolution_convert_fusion.1
  1255.4 14.8 convolution_convert_fusion.7
  1285.5 14.0 convolution_convert_fusion.2
  1300.0 13.3 convolution_convert_fusion.3
  1313.4 14.3 convolution_convert_fusion.5
  1327.9 14.0 convolution_convert_fusion.4
  1343.2 25.4 %convolution_convert_fusion = bf16[2048,4096]{1,0:T(8,128)(2,1)} fusion(bf16[256,2048]{1,0:T(8,128)(2,1)} %copy-done.134, bf16[256,2048]{1,0:T(8,128)(2,1)} %collective-permute-done.8, bf16[256,2048]{1,0:T(8,128)(2,1)} %collective-permute-done.6, bf16[256,2048]{1,0:T(8,128)(2,1)S(1)} %copy-done.57, bf16[256,2048]{1,0:T(8,128)(2,1)} %get-tuple-element.174, ...), kind=kOutput, calls=%fused_computation | convolution fusion | flops 17272143872 | bytes 29360128 | tf_op jit(solution)/shard_map/dot_general | solution.py:32
  1373.9 22.8 %all-reduce.5 = f32[8,1376]{1,0:T(8,128)S(1)} all-reduce(f32[8,1376]{1,0:T(8,128)S(1)} %concatenate.111), channel_id=14, replica_groups=mesh['fsdp'=8,'tp'=4] {'fsdp'}, use_global_device_ids=true, to_apply=%region_21.23.clone | all-reduce | flops 11008 | bytes 88064
  1453.2 20.0 %collective-permute-done.33 = bf16[256,4096]{1,0:T(8,128)(2,1)S(1)} collective-permute-done((bf16[256,4096]{1,0:T(8,128)(2,1)S(1)}, bf16[256,4096]{1,0:T(8,128)(2,1)S(1)}, u32[]{:S(2)}, u32[]{:S(2)}) %collective-permute-start.33) | collective-permute-done | bytes 2097184 | tf_op jit(solution)/shard_map/ppermute | solution.py:565
  1489.4 37.2 %collective-permute-done.34 = bf16[256,4096]{1,0:T(8,128)(2,1)S(1)} collective-permute-done((bf16[256,4096]{1,0:T(8,128)(2,1)S(1)}, bf16[256,4096]{1,0:T(8,128)(2,1)S(1)}, u32[]{:S(2)}, u32[]{:S(2)}) %collective-permute-start.34) | collective-permute-done | bytes 2097184 | tf_op jit(solution)/shard_map/ppermute | solution.py:565
  1572.8 12.7 multiply_reduce_fusion
  1585.5 43.2 %all-reduce.4 = f32[4096]{0:T(1024)S(1)} all-reduce(f32[4096]{0:T(1024)S(1)} %get-tuple-element.149), channel_id=6, replica_groups=mesh['fsdp'=8,'tp'=4] {'fsdp','tp'}, use_global_device_ids=true, to_apply=%region_11.13.clone | all-reduce | flops 4096 | bytes 32768
  1641.5 71.9 %reduce-scatter.17.cloned.1.call-done = bf16[512,1024]{1,0:T(8,128)(2,1)} async-done(((bf16[4096,1024]{1,0:T(8,128)(2,1)}), bf16[512,1024]{1,0:T(8,128)(2,1)}) %reduce-scatter.17.cloned.1.call-update) | async-done | bytes 1048592 | tf_op jit(solution)/shard_map/reduce_scatter | solution.py:589
  1713.4 75.1 %reduce-scatter.13.cloned.1.call-done = bf16[512,1024]{1,0:T(8,128)(2,1)} async-done(((bf16[4096,1024]{1,0:T(8,128)(2,1)}), bf16[512,1024]{1,0:T(8,128)(2,1)}) %reduce-scatter.13.cloned.1.call-update) | async-done | bytes 1048592 | tf_op jit(solution)/shard_map/reduce_scatter | solution.py:589
  1788.5 74.8 %reduce-scatter.15.cloned.1.call-done = bf16[512,1024]{1,0:T(8,128)(2,1)} async-done(((bf16[4096,1024]{1,0:T(8,128)(2,1)}), bf16[512,1024]{1,0:T(8,128)(2,1)}) %reduce-scatter.15.cloned.1.call-update) | async-done | bytes 1048592 | tf_op jit(solution)/shard_map/reduce_scatter | solution.py:589
  1868.4 114.8 %reduce-scatter.27.cloned.1.call-done = bf16[256,4096]{1,0:T(8,128)(2,1)} async-done(((bf16[2048,4096]{1,0:T(8,128)(2,1)}), bf16[256,4096]{1,0:T(8,128)(2,1)}) %reduce-scatter.27.cloned.1.call-update) | async-done | bytes 2097168 | tf_op jit(solution)/shard_map/reduce_scatter | solution.py:589
  (715 shorter events, 652.1 us)
Async XLA Ops:
  7.2 129.5 %all-gather.17.cloned.1.call-start = ((), (), s32[]{:S(2)}) async-start(), calls=%async_computation.12 | async-start | bytes 3538944 | tf_op jit(solution)/shard_map/all_gather | solution.py:585
  9.2 130.7 %all-gather.19.cloned.1.call-start = ((), (), s32[]{:S(2)}) async-start(), calls=%async_computation.13 | async-start | bytes 2064384 | tf_op jit(solution)/shard_map/all_gather | solution.py:585
  11.8 179.9 %all-gather.37.cloned.1.call-start = ((), (), s32[]{:S(2)}) async-start(), calls=%async_computation.35 | async-start | bytes 9437184 | tf_op jit(solution)/shard_map/all_gather | solution.py:585
  15.5 186.5 %all-gather.35.cloned.1.call-start = ((), (), s32[]{:S(2)}) async-start(), calls=%async_computation.34 | async-start | bytes 9437184 | tf_op jit(solution)/shard_map/all_gather | solution.py:585
  16.1 229.6 %all-gather.33.cloned.1.call-start = ((), (), s32[]{:S(2)}) async-start(), calls=%async_computation.33 | async-start | bytes 9437184 | tf_op jit(solution)/shard_map/all_gather | solution.py:585
  16.7 307.3 %all-gather.21.cloned.1.call-start = ((), (), s32[]{:S(2)}) async-start(), calls=%async_computation.14 | async-start | bytes 4718592 | tf_op jit(solution)/shard_map/all_gather | solution.py:585
  17.2 444.6 %all-gather.25.cloned.1.call-start = ((), (), s32[]{:S(2)}) async-start(), calls=%async_computation.16 | async-start | bytes 2359296 | tf_op jit(solution)/shard_map/all_gather | solution.py:585
  18.2 511.4 %all-gather.23.cloned.1.call-start = ((), (), s32[]{:S(2)}) async-start(), calls=%async_computation.15 | async-start | bytes 18874368 | tf_op jit(solution)/shard_map/all_gather | solution.py:585
  20.6 552.3 %all-gather.27.cloned.1.call-start = ((), (), s32[]{:S(2)}) async-start(), calls=%async_computation.17 | async-start | bytes 9437184 | tf_op jit(solution)/shard_map/all_gather | solution.py:585
  21.3 684.6 %all-gather.29.cloned.1.call-start = ((), (), s32[]{:S(2)}) async-start(), calls=%async_computation.18 | async-start | bytes 9437184 | tf_op jit(solution)/shard_map/all_gather | solution.py:585
  37.7 49.7 %collective-permute-start = (bf16[256,4096]{1,0:T(8,128)(2,1)S(1)}, bf16[256,4096]{1,0:T(8,128)(2,1)S(1)}, u32[]{:S(2)}, u32[]{:S(2)}) collective-permute-start(bf16[256,4096]{1,0:T(8,128)(2,1)S(1)} %multiply_convert_fusion), channel_id=1, source_target_pairs={{0,1},{1,2},{2,3},{3,0},{4,5},{5,6},{6,7},{7,4},{8,9},{9,10},{10,1... | collective-permute-start | bytes 6291464 | tf_op jit(solution)/shard_map/ppermute | solution.py:556
  87.4 49.0 %collective-permute-start.1 = (bf16[256,4096]{1,0:T(8,128)(2,1)S(1)}, bf16[256,4096]{1,0:T(8,128)(2,1)}, u32[]{:S(2)}, u32[]{:S(2)}) collective-permute-start(bf16[256,4096]{1,0:T(8,128)(2,1)S(1)} %collective-permute-done), channel_id=1, source_target_pairs={{0,1},{1,2},{2,3},{3,0},{4,5},{5,6},{6,7},{7,4},{8,9},{9,10},{10,1... | collective-permute-start | bytes 6291464 | tf_op jit(solution)/shard_map/ppermute | solution.py:556
  88.9 682.5 %all-gather.31.cloned.1.call-start = ((), (), s32[]{:S(2)}) async-start(), calls=%async_computation.19 | async-start | bytes 4718592 | tf_op jit(solution)/shard_map/all_gather | solution.py:585
  136.4 48.5 %collective-permute-start.2 = (bf16[256,4096]{1,0:T(8,128)(2,1)}, bf16[256,4096]{1,0:T(8,128)(2,1)}, u32[]{:S(2)}, u32[]{:S(2)}) collective-permute-start(bf16[256,4096]{1,0:T(8,128)(2,1)} %collective-permute-done.1), channel_id=1, source_target_pairs={{0,1},{1,2},{2,3},{3,0},{4,5},{5,6},{6,7},{7,4},{8,9},{9,10},{10,1... | collective-permute-start | bytes 6291464 | tf_op jit(solution)/shard_map/ppermute | solution.py:556
  328.6 27.3 %collective-permute-start.3 = (bf16[256,2048]{1,0:T(8,128)(2,1)S(1)}, bf16[256,2048]{1,0:T(8,128)(2,1)S(1)}, u32[]{:S(2)}, u32[]{:S(2)}) collective-permute-start(bf16[256,2048]{1,0:T(8,128)(2,1)S(1)} %convolution_convert_fusion.11), channel_id=1, source_target_pairs={{0,1},{1,2},{2,3},{3,0},{4,5},{5,6},{6,7},{7,4},{8,9},{9,10},{10,1... | collective-permute-start | bytes 3145736 | tf_op jit(solution)/shard_map/ppermute | solution.py:565
  411.4 28.0 %collective-permute-start.6 = (bf16[256,2048]{1,0:T(8,128)(2,1)S(1)}, bf16[256,2048]{1,0:T(8,128)(2,1)}, u32[]{:S(2)}, u32[]{:S(2)}) collective-permute-start(bf16[256,2048]{1,0:T(8,128)(2,1)S(1)} %multiply_convert_fusion.6), channel_id=1, source_target_pairs={{0,1},{1,2},{2,3},{3,0},{4,5},{5,6},{6,7},{7,4},{8,9},{9,10},{10,1... | collective-permute-start | bytes 3145736 | tf_op jit(solution)/shard_map/ppermute | solution.py:556
  412.1 49.7 %collective-permute-start.15 = (bf16[256,2048]{1,0:T(8,128)(2,1)S(1)}, bf16[256,2048]{1,0:T(8,128)(2,1)}, u32[]{:S(2)}, u32[]{:S(2)}) collective-permute-start(bf16[256,2048]{1,0:T(8,128)(2,1)S(1)} %copy-done.21), channel_id=1, source_target_pairs={{0,1},{1,2},{2,3},{3,0},{4,5},{5,6},{6,7},{7,4},{8,9},{9,10},{10,1... | collective-permute-start | bytes 3145736 | tf_op jit(solution)/shard_map/ppermute | solution.py:556
  439.4 44.9 %collective-permute-start.8 = (bf16[256,2048]{1,0:T(8,128)(2,1)}, bf16[256,2048]{1,0:T(8,128)(2,1)}, u32[]{:S(2)}, u32[]{:S(2)}) collective-permute-start(bf16[256,2048]{1,0:T(8,128)(2,1)} %collective-permute-done.6), channel_id=1, source_target_pairs={{0,1},{1,2},{2,3},{3,0},{4,5},{5,6},{6,7},{7,4},{8,9},{9,10},{10,1... | collective-permute-start | bytes 3145736 | tf_op jit(solution)/shard_map/ppermute | solution.py:556
  439.4 798.0 %reduce-scatter.29.cloned.1.call-start = ((), (), s32[]{:S(2)}) async-start(), calls=%async_computation.28 | async-start | bytes 2359296 | tf_op jit(solution)/shard_map/reduce_scatter | solution.py:589
  461.9 194.7 %collective-permute-start.16 = (bf16[256,2048]{1,0:T(8,128)(2,1)}, bf16[256,2048]{1,0:T(8,128)(2,1)}, u32[]{:S(2)}, u32[]{:S(2)}) collective-permute-start(bf16[256,2048]{1,0:T(8,128)(2,1)} %collective-permute-done.15), channel_id=1, source_target_pairs={{0,1},{1,2},{2,3},{3,0},{4,5},{5,6},{6,7},{7,4},{8,9},{9,10},{10,1... | collective-permute-start | bytes 3145736 | tf_op jit(solution)/shard_map/ppermute | solution.py:556
  484.3 41.6 %collective-permute-start.10 = (bf16[256,2048]{1,0:T(8,128)(2,1)}, bf16[256,2048]{1,0:T(8,128)(2,1)S(1)}, u32[]{:S(2)}, u32[]{:S(2)}) collective-permute-start(bf16[256,2048]{1,0:T(8,128)(2,1)} %collective-permute-done.8), channel_id=1, source_target_pairs={{0,1},{1,2},{2,3},{3,0},{4,5},{5,6},{6,7},{7,4},{8,9},{9,10},{10,1... | collective-permute-start | bytes 3145736 | tf_op jit(solution)/shard_map/ppermute | solution.py:556
  654.5 28.1 %collective-permute-start.12 = (bf16[256,2048]{1,0:T(8,128)(2,1)S(1)}, bf16[256,2048]{1,0:T(8,128)(2,1)}, u32[]{:S(2)}, u32[]{:S(2)}) collective-permute-start(bf16[256,2048]{1,0:T(8,128)(2,1)S(1)} %multiply_convert_fusion.5), channel_id=1, source_target_pairs={{0,1},{1,2},{2,3},{3,0},{4,5},{5,6},{6,7},{7,4},{8,9},{9,10},{10,1... | collective-permute-start | bytes 3145736 | tf_op jit(solution)/shard_map/ppermute | solution.py:556
  656.6 48.3 %collective-permute-start.17 = (bf16[256,2048]{1,0:T(8,128)(2,1)}, bf16[256,2048]{1,0:T(8,128)(2,1)S(1)}, u32[]{:S(2)}, u32[]{:S(2)}) collective-permute-start(bf16[256,2048]{1,0:T(8,128)(2,1)} %collective-permute-done.16), channel_id=1, source_target_pairs={{0,1},{1,2},{2,3},{3,0},{4,5},{5,6},{6,7},{7,4},{8,9},{9,10},{10,1... | collective-permute-start | bytes 3145736 | tf_op jit(solution)/shard_map/ppermute | solution.py:556
  682.5 40.1 %collective-permute-start.13 = (bf16[256,2048]{1,0:T(8,128)(2,1)}, bf16[256,2048]{1,0:T(8,128)(2,1)}, u32[]{:S(2)}, u32[]{:S(2)}) collective-permute-start(bf16[256,2048]{1,0:T(8,128)(2,1)} %collective-permute-done.12), channel_id=1, source_target_pairs={{0,1},{1,2},{2,3},{3,0},{4,5},{5,6},{6,7},{7,4},{8,9},{9,10},{10,1... | collective-permute-start | bytes 3145736 | tf_op jit(solution)/shard_map/ppermute | solution.py:556
  799.7 73.1 %collective-permute-start.18 = (bf16[256,2048]{1,0:T(8,128)(2,1)}, bf16[256,2048]{1,0:T(8,128)(2,1)}, u32[]{:S(2)}, u32[]{:S(2)}) collective-permute-start(bf16[256,2048]{1,0:T(8,128)(2,1)} %convolution_convert_fusion.10), channel_id=1, source_target_pairs={{0,1},{1,2},{2,3},{3,0},{4,5},{5,6},{6,7},{7,4},{8,9},{9,10},{10,1... | collective-permute-start | bytes 3145736 | tf_op jit(solution)/shard_map/ppermute | solution.py:565
  868.7 28.1 %collective-permute-start.22 = (bf16[256,2048]{1,0:T(8,128)(2,1)S(1)}, bf16[256,2048]{1,0:T(8,128)(2,1)S(1)}, u32[]{:S(2)}, u32[]{:S(2)}) collective-permute-start(bf16[256,2048]{1,0:T(8,128)(2,1)S(1)} %add_convert_fusion.6), channel_id=1, source_target_pairs={{0,1},{1,2},{2,3},{3,0},{4,5},{5,6},{6,7},{7,4},{8,9},{9,10},{10,1... | collective-permute-start | bytes 3145736 | tf_op jit(solution)/shard_map/ppermute | solution.py:565
  875.2 44.1 %collective-permute-start.19 = (bf16[256,2048]{1,0:T(8,128)(2,1)S(1)}, bf16[256,2048]{1,0:T(8,128)(2,1)S(1)}, u32[]{:S(2)}, u32[]{:S(2)}) collective-permute-start(bf16[256,2048]{1,0:T(8,128)(2,1)S(1)} %add_convert_fusion.8), channel_id=1, source_target_pairs={{0,1},{1,2},{2,3},{3,0},{4,5},{5,6},{6,7},{7,4},{8,9},{9,10},{10,1... | collective-permute-start | bytes 3145736 | tf_op jit(solution)/shard_map/ppermute | solution.py:565
  897.2 44.5 %collective-permute-start.23 = (bf16[256,2048]{1,0:T(8,128)(2,1)S(1)}, bf16[256,2048]{1,0:T(8,128)(2,1)S(1)}, u32[]{:S(2)}, u32[]{:S(2)}) collective-permute-start(bf16[256,2048]{1,0:T(8,128)(2,1)S(1)} %add_convert_fusion.5), channel_id=1, source_target_pairs={{0,1},{1,2},{2,3},{3,0},{4,5},{5,6},{6,7},{7,4},{8,9},{9,10},{10,1... | collective-permute-start | bytes 3145736 | tf_op jit(solution)/shard_map/ppermute | solution.py:565
  919.6 36.5 %collective-permute-start.20 = (bf16[256,2048]{1,0:T(8,128)(2,1)S(1)}, bf16[256,2048]{1,0:T(8,128)(2,1)S(1)}, u32[]{:S(2)}, u32[]{:S(2)}) collective-permute-start(bf16[256,2048]{1,0:T(8,128)(2,1)S(1)} %add_convert_fusion.7), channel_id=1, source_target_pairs={{0,1},{1,2},{2,3},{3,0},{4,5},{5,6},{6,7},{7,4},{8,9},{9,10},{10,1... | collective-permute-start | bytes 3145736 | tf_op jit(solution)/shard_map/ppermute | solution.py:565
  999.1 36.0 %collective-permute-start.25 = (bf16[256,2048]{1,0:T(8,128)(2,1)S(1)}, bf16[256,2048]{1,0:T(8,128)(2,1)}, u32[]{:S(2)}, u32[]{:S(2)}) collective-permute-start(bf16[256,2048]{1,0:T(8,128)(2,1)S(1)} %fusion.95), channel_id=1, source_target_pairs={{0,1},{1,2},{2,3},{3,0},{4,5},{5,6},{6,7},{7,4},{8,9},{9,10},{10,1... | collective-permute-start | bytes 3145736 | tf_op jit(solution)/shard_map/ppermute | solution.py:565
  1020.1 36.0 %collective-permute-start.28 = (bf16[256,2048]{1,0:T(8,128)(2,1)}, bf16[256,2048]{1,0:T(8,128)(2,1)}, u32[]{:S(2)}, u32[]{:S(2)}) collective-permute-start(bf16[256,2048]{1,0:T(8,128)(2,1)} %collective-permute-done.26), channel_id=1, source_target_pairs={{0,1},{1,2},{2,3},{3,0},{4,5},{5,6},{6,7},{7,4},{8,9},{9,10},{10,1... | collective-permute-start | bytes 3145736 | tf_op jit(solution)/shard_map/ppermute | solution.py:556
  1037.0 43.4 %collective-permute-start.27 = (bf16[256,2048]{1,0:T(8,128)(2,1)S(1)}, bf16[256,2048]{1,0:T(8,128)(2,1)}, u32[]{:S(2)}, u32[]{:S(2)}) collective-permute-start(bf16[256,2048]{1,0:T(8,128)(2,1)S(1)} %add_convert_fusion.4), channel_id=1, source_target_pairs={{0,1},{1,2},{2,3},{3,0},{4,5},{5,6},{6,7},{7,4},{8,9},{9,10},{10,1... | collective-permute-start | bytes 3145736 | tf_op jit(solution)/shard_map/ppermute | solution.py:565
  1082.9 27.3 %collective-permute-start.29 = (bf16[256,2048]{1,0:T(8,128)(2,1)}, bf16[256,2048]{1,0:T(8,128)(2,1)S(1)}, u32[]{:S(2)}, u32[]{:S(2)}) collective-permute-start(bf16[256,2048]{1,0:T(8,128)(2,1)} %add_convert_fusion.3), channel_id=1, source_target_pairs={{0,1},{1,2},{2,3},{3,0},{4,5},{5,6},{6,7},{7,4},{8,9},{9,10},{10,1... | collective-permute-start | bytes 3145736 | tf_op jit(solution)/shard_map/ppermute | solution.py:565
  1145.3 128.9 %reduce-scatter.19.cloned.1.call-start = ((), (), s32[]{:S(2)}) async-start(), calls=%async_computation.23 | async-start | bytes 3538944 | tf_op jit(solution)/shard_map/reduce_scatter | solution.py:589
  1227.4 144.3 %reduce-scatter.35.cloned.1.call-start = ((), (), s32[]{:S(2)}) async-start(), calls=%async_computation.32 | async-start | bytes 4718592 | tf_op jit(solution)/shard_map/reduce_scatter | solution.py:589
  1237.4 298.2 %all-reduce.8.cloned.1.call-start = ((), (), s32[]{:S(2)}) async-start(), calls=%async_computation.29 | async-start | bytes 786432 | tf_op jit(solution)/shard_map/psum | solution.py:842
  1240.1 319.5 %reduce-scatter.33.cloned.1.call-start = ((), (), s32[]{:S(2)}) async-start(), calls=%async_computation.31 | async-start | bytes 9437184 | tf_op jit(solution)/shard_map/reduce_scatter | solution.py:589
  1254.1 309.8 %reduce-scatter.23.cloned.1.call-start = ((), (), s32[]{:S(2)}) async-start(), calls=%async_computation.25 | async-start | bytes 2064384 | tf_op jit(solution)/shard_map/reduce_scatter | solution.py:589
  1274.1 293.2 %reduce-scatter.21.cloned.1.call-start = ((), (), s32[]{:S(2)}) async-start(), calls=%async_computation.24 | async-start | bytes 491520 | tf_op jit(solution)/shard_map/reduce_scatter | solution.py:812
  1274.7 354.6 %reduce-scatter.25.cloned.1.call-start = ((), (), s32[]{:S(2)}) async-start(), calls=%async_computation.26 | async-start | bytes 4718592 | tf_op jit(solution)/shard_map/reduce_scatter | solution.py:589
  1284.1 354.7 %reduce-scatter.31.cloned.1.call-start = ((), (), s32[]{:S(2)}) async-start(), calls=%async_computation.30 | async-start | bytes 9437184 | tf_op jit(solution)/shard_map/reduce_scatter | solution.py:589
  1299.5 413.9 %reduce-scatter.17.cloned.1.call-start = ((), (), s32[]{:S(2)}) async-start(), calls=%async_computation.22 | async-start | bytes 9437184 | tf_op jit(solution)/shard_map/reduce_scatter | solution.py:589
  1313.4 475.2 %reduce-scatter.13.cloned.1.call-start = ((), (), s32[]{:S(2)}) async-start(), calls=%async_computation.20 | async-start | bytes 9437184 | tf_op jit(solution)/shard_map/reduce_scatter | solution.py:589
  1327.7 535.6 %reduce-scatter.15.cloned.1.call-start = ((), (), s32[]{:S(2)}) async-start(), calls=%async_computation.21 | async-start | bytes 9437184 | tf_op jit(solution)/shard_map/reduce_scatter | solution.py:589
  1342.0 641.2 %reduce-scatter.27.cloned.1.call-start = ((), (), s32[]{:S(2)}) async-start(), calls=%async_computation.27 | async-start | bytes 18874368 | tf_op jit(solution)/shard_map/reduce_scatter | solution.py:589
  1427.3 45.9 %collective-permute-start.33 = (bf16[256,4096]{1,0:T(8,128)(2,1)S(1)}, bf16[256,4096]{1,0:T(8,128)(2,1)S(1)}, u32[]{:S(2)}, u32[]{:S(2)}) collective-permute-start(bf16[256,4096]{1,0:T(8,128)(2,1)S(1)} %fusion.56), channel_id=1, source_target_pairs={{0,1},{1,2},{2,3},{3,0},{4,5},{5,6},{6,7},{7,4},{8,9},{9,10},{10,1... | collective-permute-start | bytes 6291464 | tf_op jit(solution)/shard_map/ppermute | solution.py:565
  1475.0 51.6 %collective-permute-start.34 = (bf16[256,4096]{1,0:T(8,128)(2,1)S(1)}, bf16[256,4096]{1,0:T(8,128)(2,1)S(1)}, u32[]{:S(2)}, u32[]{:S(2)}) collective-permute-start(bf16[256,4096]{1,0:T(8,128)(2,1)S(1)} %add_convert_fusion.1), channel_id=1, source_target_pairs={{0,1},{1,2},{2,3},{3,0},{4,5},{5,6},{6,7},{7,4},{8,9},{9,10},{10,1... | collective-permute-start | bytes 6291464 | tf_op jit(solution)/shard_map/ppermute | solution.py:565
  1528.5 44.2 %collective-permute-start.35 = (bf16[256,4096]{1,0:T(8,128)(2,1)}, bf16[256,4096]{1,0:T(8,128)(2,1)}, u32[]{:S(2)}, u32[]{:S(2)}) collective-permute-start(bf16[256,4096]{1,0:T(8,128)(2,1)} %add_convert_fusion), channel_id=1, source_target_pairs={{0,1},{1,2},{2,3},{3,0},{4,5},{5,6},{6,7},{7,4},{8,9},{9,10},{10,1... | collective-permute-start | bytes 6291464 | tf_op jit(solution)/shard_map/ppermute | solution.py:565
  (172 other events, 2390.8 us)
Sparse Core Ops, SparseCore 0:
  10.5 35.5 all-gather.16
  48.5 26.7 all-gather.18
  77.8 54.3 all-gather.36
  134.5 54.3 all-gather.34
  191.3 54.3 all-gather.32
  247.4 37.4 all-gather.20
  287.3 28.2 all-gather.24
  318.1 89.8 all-gather.22
  409.8 55.9 all-gather.26
  467.6 54.3 all-gather.28
  523.9 37.4 all-gather.30
  1145.4 40.4 reduce-scatter.28
  1227.5 42.1 reduce-scatter.18
  1273.5 51.2 reduce-scatter.34
  1327.7 37.0 all-reduce.7
  1368.1 70.8 reduce-scatter.32
  1443.2 39.6 reduce-scatter.22
  1485.1 24.2 reduce-scatter.20
  1512.8 49.9 reduce-scatter.24
  1566.5 72.2 reduce-scatter.30
  1642.3 71.0 reduce-scatter.16
  1717.2 71.2 reduce-scatter.12
  1792.0 71.2 reduce-scatter.14
  1867.2 115.9 reduce-scatter.26

commit v2 on v1

--- a/solution.py
+++ b/solution.py
@@ -52,22 +52,35 @@
     return lax.broadcasted_iota(jnp.int32, shape, axis)
 
 
-def attention_forward_kernel(tp, place_ref, lengths_ref, cosine_ref, sine_ref, *refs):
-    q_in, k_in, v_in = refs[:tp], refs[tp : 2 * tp], refs[2 * tp : 3 * tp]
-    attended_ref, q_ref, k_ref, v_ref, held = refs[3 * tp :]
+def attention_forward_kernel(
+    tp,
+    place_ref,
+    lengths_ref,
+    cosine_ref,
+    sine_ref,
+    q_up,
+    k_up,
+    v_up,
+    *refs,
+):
+    pieces = refs[: 4 * tp]
+    attended_ref, q_ref, k_ref, v_ref, held = refs[4 * tp :]
     rows = q_ref.shape[0]
     share = rows // tp
+    rank = q_up.shape[0]
     here = place_ref[0]
     ends = ends_of(lengths_ref)
     for p in range(tp):
         owner = lax.rem(here - p + tp, tp)
         part = pl.ds(pl.multiple_of(owner * share, share), share)
         cosine, sine = cosine_ref[part, :], sine_ref[part, :]
-        for source, target in ((q_in[p], q_ref), (k_in[p], k_ref)):
-            value = source[...]
-            turned = value * cosine + pltpu.roll(value, HDA // 2, 1) * sine
-            target[part, :] = turned.astype(bf16)
-        v_ref[part, :] = v_in[p][...].astype(bf16)
+        middle = pieces[4 * p + 3]
+        for j, (up, target) in enumerate(((q_up, q_ref), (k_up, k_ref), (v_up, v_ref))):
+            low = middle[:, j * rank : (j + 1) * rank].astype(bf16)
+            value = pieces[4 * p + j][...] + mm(low, up[...])
+            if j < 2:
+                value = value * cosine + pltpu.roll(value, HDA // 2, 1) * sine
+            target[part, :] = value.astype(bf16)
     block = min(256, rows)
     scale = HDA ** (-0.5)
     for at in range(0, rows, block):
@@ -86,15 +99,17 @@
         attended_ref[p * share : (p + 1) * share, :] = held[part, :]
 
 
-def attention_forward(place, lengths, pieces, cosine, sine):
-    tp = len(pieces)
-    share, columns = pieces[0][0].shape
+def attention_forward(place, lengths, projected, ups, columns, cosine, sine):
+    tp = len(projected)
+    share = projected[0].shape[0]
     rows = share * tp
     heads = columns // HDA
-    piece_spec = pl.BlockSpec((share, HDA), lambda h, *_: (0, h))
+    rank = ups.shape[0]
     table_spec = pl.BlockSpec((rows, HDA), lambda h, *_: (0, 0))
-    head_spec = pl.BlockSpec((rows, HDA), lambda h, *_: (0, h))
-    flat = [pieces[p][j] for j in range(3) for p in range(tp)]
+
+    def head_spec(j, height=rows):
+        return pl.BlockSpec((height, HDA), lambda h, *_: (0, j * heads + h))
+
     work = heads * rows * rows * HDA
     return pl.pallas_call(
         functools.partial(attention_forward_kernel, tp),
@@ -102,8 +117,14 @@
         grid_spec=pltpu.PrefetchScalarGridSpec(
             num_scalar_prefetch=2,
             grid=(heads,),
-            in_specs=[table_spec, table_spec] + [piece_spec] * (3 * tp),
-            out_specs=[head_spec] * 4,
+            in_specs=[table_spec, table_spec]
+            + [head_spec(j, rank) for j in range(3)]
+            + (
+                [head_spec(j, share) for j in range(3)]
+                + [pl.BlockSpec((share, 3 * rank), lambda h, *_: (0, columns // rank))]
+            )
+            * tp,
+            out_specs=[head_spec(0)] * 4,
             scratch_shapes=[pltpu.VMEM((rows, HDA), bf16)],
         ),
         compiler_params=pltpu.CompilerParams(vmem_limit_bytes=VMEM_LIMIT),
@@ -111,17 +132,31 @@
             flops=4 * work, bytes_accessed=20 * rows * columns, transcendentals=heads * rows * rows
         ),
         name="attention_forward",
-    )(place, lengths, cosine, sine, *flat)
-
-
-def attention_backward_kernel(tp, place_ref, lengths_ref, cosine_ref, sine_ref, *refs):
-    q_ref, k_ref, v_ref = refs[:3]
-    grad_in = refs[3 : 3 + tp]
-    out_refs = refs[3 + tp : 6 + tp]
-    held, dq, dk, dv = refs[6 + tp :]
+    )(place, lengths, cosine, sine, ups, ups, ups, *[v for v in projected for _ in range(4)])
+
+
+def attention_backward_kernel(
+    tp,
+    heads,
+    place_ref,
+    lengths_ref,
+    cosine_ref,
+    sine_ref,
+    q_ref,
+    k_ref,
+    v_ref,
+    q_up,
+    k_up,
+    v_up,
+    *refs,
+):
+    grad_in = refs[:tp]
+    out_ref, held, dq, dk, dv, lora = refs[tp:]
     rows = q_ref.shape[0]
     share = rows // tp
+    rank = q_up.shape[0]
     here = place_ref[0]
+    head = pl.program_id(0)
     ends = ends_of(lengths_ref)
     for p in range(tp):
         owner = lax.rem(here - p + tp, tp)
@@ -129,6 +164,11 @@
         held[part, :] = grad_in[p][...]
     dk[...] = jnp.zeros_like(dk)
     dv[...] = jnp.zeros_like(dv)
+
+    @pl.when(head == 0)
+    def _():
+        lora[...] = jnp.zeros_like(lora)
+
     block = min(256, rows)
     scale = HDA ** (-0.5)
     for at in range(0, rows, block):
@@ -153,38 +193,57 @@
         part = pl.ds(pl.multiple_of(owner * share, share), share)
         cosine, sine = cosine_ref[part, :], sine_ref[part, :]
         mine = slice(p * share, (p + 1) * share)
-        for source, target in ((dq, out_refs[0]), (dk, out_refs[1])):
-            value = source[part, :] * scale
-            turned = value * cosine - pltpu.roll(value, HDA // 2, 1) * sine
-            target[mine, :] = turned.astype(bf16)
-        out_refs[2][mine, :] = dv[part, :].astype(bf16)
-
-
-def attention_backward(place, lengths, queries, keys, values, pieces, cosine, sine):
+        for j, (source, up) in enumerate(((dq, q_up), (dk, k_up), (dv, v_up))):
+            value = source[part, :]
+            if j < 2:
+                value = value * scale
+                value = value * cosine - pltpu.roll(value, HDA // 2, 1) * sine
+            low = value.astype(bf16)
+            at = pl.multiple_of((j * heads + head) * HDA, HDA)
+            out_ref[mine, pl.ds(at, HDA)] = low
+            lora[mine, j * rank : (j + 1) * rank] += mm_nt(low, up[...])
+
+    @pl.when(head == heads - 1)
+    def _():
+        out_ref[:, 3 * heads * HDA :] = lora[...].astype(bf16)
+
+
+def attention_backward(place, lengths, queries, keys, values, ups, pieces, cosine, sine):
     tp = len(pieces)
     share, columns = pieces[0].shape
     rows = share * tp
     heads = columns // HDA
+    rank = ups.shape[0]
     piece_spec = pl.BlockSpec((share, HDA), lambda h, *_: (0, h))
     table_spec = pl.BlockSpec((rows, HDA), lambda h, *_: (0, 0))
     head_spec = pl.BlockSpec((rows, HDA), lambda h, *_: (0, h))
+
+    def up_spec(j):
+        return pl.BlockSpec((rank, HDA), lambda h, *_: (0, j * heads + h))
+
+    total = 3 * columns + 3 * rank
     work = heads * rows * rows * HDA
     return pl.pallas_call(
-        functools.partial(attention_backward_kernel, tp),
-        out_shape=[jax.ShapeDtypeStruct((rows, columns), bf16)] * 3,
+        functools.partial(attention_backward_kernel, tp, heads),
+        out_shape=jax.ShapeDtypeStruct((rows, total), bf16),
         grid_spec=pltpu.PrefetchScalarGridSpec(
             num_scalar_prefetch=2,
             grid=(heads,),
-            in_specs=[table_spec, table_spec] + [head_spec] * 3 + [piece_spec] * tp,
-            out_specs=[head_spec] * 3,
-            scratch_shapes=[pltpu.VMEM((rows, HDA), bf16)] + [pltpu.VMEM((rows, HDA), f32)] * 3,
+            in_specs=[table_spec, table_spec]
+            + [head_spec] * 3
+            + [up_spec(j) for j in range(3)]
+            + [piece_spec] * tp,
+            out_specs=pl.BlockSpec((rows, total), lambda h, *_: (0, 0)),
+            scratch_shapes=[pltpu.VMEM((rows, HDA), bf16)]
+            + [pltpu.VMEM((rows, HDA), f32)] * 3
+            + [pltpu.VMEM((rows, 3 * rank), f32)],
         ),
         compiler_params=pltpu.CompilerParams(vmem_limit_bytes=VMEM_LIMIT),
         cost_estimate=pl.CostEstimate(
             flops=10 * work, bytes_accessed=14 * rows * columns, transcendentals=heads * rows * rows
         ),
         name="attention_backward",
-    )(place, lengths, cosine, sine, queries, keys, values, *pieces)
+    )(place, lengths, cosine, sine, queries, keys, values, ups, ups, ups, *pieces)
 
 
 def conv_rows(extended, taps, position):
@@ -322,8 +381,7 @@
     wide,
     narrow,
     rates,
-    grad_zx,
-    grad_sd,
+    grad_all,
     grad_wide,
     grad_narrow,
     grad_rates,
@@ -374,7 +432,7 @@
         grad_wide[5:6, cols] += jnp.sum(rooted * gated, axis=0, keepdims=True)
         grad_gated = rooted * gain - gated * pull
         grad_y = grad_gated * z * gate
-        grad_zx[:, cols] = (grad_gated * whole * silu_grad(z, gate)).astype(bf16)
+        grad_all[:, cols] = (grad_gated * whole * silu_grad(z, gate)).astype(bf16)
         grad_wide[4:5, cols] += jnp.sum(grad_y * xc, axis=0, keepdims=True)
         low = grad_y.astype(bf16)
         low_a = jnp.where(v.low_half, grad_y, 0.0).astype(bf16)
@@ -418,7 +476,7 @@
     position_ext = index_ext - starts_of(index_ext, ends)
     taps_back(v.x_ext, grad_pre[...], v.position, grad_wide)
     extended = jnp.concatenate([grad_pre[...], next_pre[...]], axis=0)
-    grad_zx[:, width:] = conv_back(extended, wide, position_ext).astype(bf16)
+    grad_all[:, width : 2 * width] = conv_back(extended, wide, position_ext).astype(bf16)
     next_pre[...] = grad_pre[0:8, :]
 
     blank = jnp.zeros((rows, LANES - HD), f32)
@@ -426,9 +484,9 @@
     grad_pre_s = grad_sc * silu_grad(v.pre_s, v.gate_s)
     taps_back(v.s_ext, grad_pre_s, v.position, grad_narrow)
     extended_s = jnp.concatenate([grad_pre_s, next_pre_s[...]], axis=0)
-    grad_sd[:, : 2 * LANES] = conv_back(extended_s, narrow, position_ext).astype(bf16)
+    grad_all[:, 2 * width : 2 * width + 2 * LANES] = conv_back(extended_s, narrow, position_ext).astype(bf16)
     next_pre_s[...] = grad_pre_s[0:8, :]
-    grad_sd[:, 2 * LANES :] = grad_raw.astype(bf16)
+    grad_all[:, 2 * width + 2 * LANES :] = grad_raw.astype(bf16)
 
 
 def mixer_specs(tp, rows, width, order):
@@ -502,8 +560,7 @@
     return pl.pallas_call(
         functools.partial(mixer_backward_kernel, chunks),
         out_shape=[
-            jax.ShapeDtypeStruct((rows, 2 * width), bf16),
-            jax.ShapeDtypeStruct((rows, 3 * LANES), bf16),
+            jax.ShapeDtypeStruct((rows, 2 * width + 3 * LANES), bf16),
             jax.ShapeDtypeStruct((8, width), f32),
             jax.ShapeDtypeStruct((8, 2 * LANES), f32),
             jax.ShapeDtypeStruct((8, LANES), f32),
@@ -524,8 +581,7 @@
                 pl.BlockSpec((8, LANES), fixed),
             ],
             out_specs=[
-                pl.BlockSpec((CHUNK, 2 * width), chunk_map),
-                pl.BlockSpec((CHUNK, 3 * LANES), chunk_map),
+                pl.BlockSpec((CHUNK, 2 * width + 3 * LANES), chunk_map),
                 pl.BlockSpec((8, width), fixed),
                 pl.BlockSpec((8, 2 * LANES), fixed),
                 pl.BlockSpec((8, LANES), fixed),
@@ -548,23 +604,114 @@
     )(place, lengths, zx, zx, sd, sd, grad_scaled, stats, states, wide, narrow, rates)
 
 
-def ring_gather(own):
+def tie(value, others):
+    return lax.optimization_barrier((value, others))[0]
+
+
+def ring_pairs():
     tp = lax.axis_size("tp")
-    pairs = [(i, (i + 1) % tp) for i in range(tp)]
-    pieces = [own]
-    for _ in range(tp - 1):
-        pieces.append(lax.ppermute(pieces[-1], "tp", pairs))
-    return pieces
-
-
-def ring_scatter(part):
+    return [(i, (i + 1) % tp) for i in range(tp)]
+
+
+def hop(values):
+    return lax.ppermute(values, "tp", ring_pairs())
+
+
+def ring_gather(own, use=None):
     tp = lax.axis_size("tp")
-    pairs = [(i, (i + 1) % tp) for i in range(tp)]
+    pieces, results = [own], []
+    for p in range(tp):
+        moved = hop(pieces[p]) if p < tp - 1 else None
+        if use is not None:
+            results.append(use(p, pieces[p]))
+            if moved is not None:
+                moved = tie(moved, results[-1])
+        if moved is not None:
+            pieces.append(moved)
+    return pieces, results
+
+
+def ring_scatter(part, fill=()):
+    tp = lax.axis_size("tp")
+    fill = list(fill)
+    filled = []
     total = part(1 % tp)
     for p in range(2, tp + 1):
-        moved = lax.ppermute(total.astype(bf16), "tp", pairs)
-        total = moved.astype(f32) + part(p % tp)
-    return total
+        low = total.astype(bf16)
+        moved = hop(low)
+        term = part(p % tp)
+        if fill:
+            filled.append(fill.pop(0)(low))
+            moved = tie(moved, filled[-1])
+        total = moved.astype(f32) + term
+    for thunk in fill:
+        filled.append(thunk(low))
+    return total, filled
+
+
+def ring_both(own, work, last=None, fill=()):
+    tp = lax.axis_size("tp")
+    fill = list(fill)
+    filled = []
+    pieces = [own]
+    moved = hop(own)
+    first = work(0, own)
+    moved = tie(moved, first)
+    total, ahead = None, None
+    for p in range(1, tp):
+        pieces.append(moved)
+        if p < tp - 1:
+            moved = hop(pieces[p])
+        elif last is not None:
+            filled.append(last(pieces))
+            pieces[p] = tie(pieces[p], filled[-1])
+        term = work(p, pieces[p])
+        total = term if total is None else ahead.astype(f32) + term
+        ahead = hop(total.astype(bf16))
+        if p < tp - 1:
+            moved = tie(moved, total)
+    if fill:
+        filled.extend(thunk() for thunk in fill)
+        ahead = tie(ahead, filled[-1])
+    return pieces, ahead.astype(f32) + first, filled
+
+
+def halving(values, name, sent_as=f32):
+    count = lax.axis_size(name)
+    here = lax.axis_index(name)
+    half = count // 2
+    while half:
+        upper = (here & half) != 0
+        low, high = values[:half], values[half:]
+        sent = jnp.where(upper, low, high)
+        kept = jnp.where(upper, high, low)
+        moved = lax.ppermute(sent.astype(sent_as), name, [(i, i ^ half) for i in range(count)])
+        values = kept + moved.astype(f32)
+        half //= 2
+    return values[0]
+
+
+def doubling_gather(values, name):
+    count = lax.axis_size(name)
+    here = lax.axis_index(name)
+    step = 1
+    while step < count:
+        moved = lax.ppermute(values, name, [(i, i ^ step) for i in range(count)])
+        upper = (here & step) != 0
+        values = jnp.concatenate(
+            [jnp.where(upper, moved, values), jnp.where(upper, values, moved)], axis=0
+        )
+        step *= 2
+    return values
+
+
+def doubling(values, name):
+    count = lax.axis_size(name)
+    step = 1
+    while step < count:
+        values = values + lax.ppermute(values, name, [(i, i ^ step) for i in range(count)])
+        step *= 2
+    return values
 
 
 def inverse_root(values):
@@ -632,6 +779,44 @@
     count = inner_conv_taps.shape[0]
     inner_total = inner_cols * tp
 
+    def piece(values, p):
+        return values[p * share : (p + 1) * share]
+
+    joined_low = jnp.concatenate([hidden, embed], axis=1)
+    query_key_value_weight = tie(query_key_value_weight, joined_low)
+    weight_qkv = gather(
+        jnp.concatenate(
+            [query_key_value_weight[:, j, :] for j in range(3)]
+            + [attention_adapter_down[:, j, :] for j in range(3)],
+            axis=1,
+        )
+    )
+    ups = doubling_gather(
+        jnp.concatenate(
+            [attention_adapter_up[:, j, :] for j in range(3)]
+            + [feedforward_adapter_up[:, j, :] for j in range(2)],
+            axis=1,
+        ),
+        "fsdp",
+    )
+    fc_up = ups[:, 3 * head_cols :]
+    weight_o = gather(attention_output_weight, 1)
+    weight_fc1 = gather(
+        jnp.concatenate(
+            [gate_up_weight[:, j, :] for j in range(2)] + [feedforward_adapter_down], axis=1
+        )
+    )
+    weight_down = gather(jnp.concatenate([down_weight, mixer_output_weight], axis=0), 1)
+    weight_fc2, weight_out = weight_down[:units_here], weight_down[units_here:]
+    weight_zx = gather(
+        jnp.concatenate(
+            [gate_inner_weight[:, j, :] for j in range(2)]
+            + [jnp.pad(state_input_weight[:, j, :], ((0, 0), (0, LANES - states))) for j in range(2)]
+            + [jnp.pad(step_projection, ((0, 0), (0, LANES - mixer_heads)))],
+            axis=1,
+        )
+    )
+
     small = [
         attention_norm_gain,
         feedforward_norm_gain,
@@ -660,25 +845,6 @@
         jnp.stack([head_step_bias, decay_log_rate]), ((0, 6), (0, LANES - mixer_heads))
     )
 
-    weights_qkv = [gather(query_key_value_weight[:, j, :]) for j in range(3)]
-    adapter_down = gather(attention_adapter_down.reshape(-1, 3 * rank))
-    ups = jnp.concatenate(
-        [attention_adapter_up.reshape(-1, 3 * head_cols), feedforward_adapter_up.reshape(-1, 2 * units_here)],
-        axis=1,
-    )
-    ups = gather(ups)
-    adapter_up = [ups[:, j * head_cols : (j + 1) * head_cols] for j in range(3)]
-    fc_up = ups[:, 3 * head_cols :]
-    weight_o = gather(attention_output_weight, 1)
-    lanes_s = jnp.pad(state_input_weight, ((0, 0), (0, 0), (0, LANES - states))).reshape(-1, 2 * LANES)
-    lanes_t = jnp.pad(step_projection, ((0, 0), (0, LANES - mixer_heads)))
-    downs = gather(jnp.concatenate([lanes_s, lanes_t, feedforward_adapter_down], axis=1))
-    weight_sd, fc_down = downs[:, : 3 * LANES], downs[:, 3 * LANES :]
-    weight_fc1 = gather(gate_up_weight.reshape(-1, 2 * units_here))
-    weight_fc2 = gather(down_weight, 1)
-    weight_zx = gather(gate_inner_weight.reshape(-1, 2 * inner_cols))
-    weight_out = gather(mixer_output_weight, 1)
-
     places = jnp.arange(rows, dtype=jnp.int32)
     ends = [jnp.sum(lengths[: i + 1]) for i in range(lengths.shape[0] - 1)]
     position = places - starts_of(places, ends)
@@ -689,46 +855,73 @@
     cosine = jnp.concatenate([cosine, cosine], axis=1)
     sine = jnp.concatenate([-sine, sine], axis=1)
 
-    joined = jnp.concatenate([hidden.astype(f32), embed.astype(f32)], axis=1)
+    joined = joined_low.astype(f32)
     attn_root = inverse_root(joined)
-    normed = ring_gather((joined * attn_root * gain_attn).astype(bf16))
-    lora_mid = [mm(piece, adapter_down).astype(bf16) for piece in normed]
-
-    def project(p, j):
-        middle = lora_mid[p][:, j * rank : (j + 1) * rank]
-        return mm(normed[p], weights_qkv[j]) + mm(middle, adapter_up[j])
-
-    projected = [[project(p, j) for j in range(3)] for p in range(tp)]
-    attended, queries, keys, values = attention_forward(place, lengths, projected, cosine, sine)
-
-    def piece(values, p):
-        return values[p * share : (p + 1) * share]
-
-    mixed = ring_scatter(lambda p: mm(piece(attended, p), weight_o))
+
+    def norm_rows(values):
+        values = values.astype(f32)
+        return (values * inverse_root(values) * gain_attn).astype(bf16)
+
+    raw, normed = [joined_low], []
+    for p in range(1, tp):
+        moved = hop(raw[-1])
+        if p > 1:
+            normed.append(norm_rows(raw[p - 2]))
+            moved = tie(moved, normed[-1])
+        raw.append(moved)
+    normed += [norm_rows(v) for v in raw[len(normed) :]]
+
+    out_grad = [tie(output_cotangent, raw[-1])]
+    projected = []
+    for i in range(tp - 1):
+        moved = hop(out_grad[-1])
+        if i < tp - 2:
+            low, high = (tp * i) // (tp - 2), (tp * (i + 1)) // (tp - 2)
+            projected += [mm(normed[p], weight_qkv) for p in range(low, high)]
+            moved = tie(moved, projected)
+        else:
+            attended, queries, keys, values = attention_forward(
+                place, lengths, projected, ups, head_cols, cosine, sine
+            )
+            moved = tie(moved, attended)
+        out_grad.append(moved)
+    attended = tie(attended, moved)
+    out_grad_rows = jnp.concatenate(out_grad, axis=0)
+    mixed, _ = ring_scatter(lambda p: mm(piece(attended, p), weight_o))
 
     mlp_root = inverse_root(mixed)
-    mlp_in = ring_gather((mixed * mlp_root * gain_mlp).astype(bf16))
-    fc_mid = [mm(v, fc_down).astype(bf16) for v in mlp_in]
-    gate_up = [(mm(mlp_in[p], weight_fc1) + mm(fc_mid[p], fc_up)).astype(bf16) for p in range(tp)]
-
-    def unit_rows(p):
-        gate = gate_up[p][:, :units_here].astype(f32)
-        up = gate_up[p][:, units_here:].astype(f32)
-        return (jax.nn.gelu(gate) * up).astype(bf16)
-
-    units = [unit_rows(p) for p in range(tp)]
-    branch = ring_scatter(lambda p: mm(units[p], weight_fc2))
+    gate_up, fc_mid, units = [], [], []
+
+    def feed(p, rows_in):
+        wide_rows = mm(rows_in, weight_fc1)
+        middle = wide_rows[:, 2 * units_here :].astype(bf16)
+        both = (wide_rows[:, : 2 * units_here] + mm(middle, fc_up)).astype(bf16)
+        gate, up = both[:, :units_here].astype(f32), both[:, units_here:].astype(f32)
+        unit = (jax.nn.gelu(gate) * up).astype(bf16)
+        fc_mid.append(middle)
+        gate_up.append(both)
+        units.append(unit)
+        return mm(unit, weight_fc2)
+
+    mlp_in, branch, _ = ring_both((mixed * mlp_root * gain_mlp).astype(bf16), feed)
     residual = hidden.astype(f32) + mixed + branch
 
     mixer_root = inverse_root(residual)
-    mixer_in = ring_gather((residual * mixer_root * gain_mixer).astype(bf16))
-    out_grad = ring_gather(output_cotangent)
+    scaled_grads = []
+
+    def mix(p, rows_in):
+        result = mm(rows_in, weight_zx)
+        if p == 0:
+            scaled_grads.append(mm_nt(tie(out_grad_rows, result), weight_out).astype(bf16))
+            result = tie(result, scaled_grads[0])
+        return result
+
+    mixer_in, zxs = ring_gather((residual * mixer_root * gain_mixer).astype(bf16), mix)
+    grad_scaled = scaled_grads[0]
     mixer_rows = jnp.concatenate(mixer_in, axis=0)
-    zx = jnp.concatenate([mm(v, weight_zx).astype(bf16) for v in mixer_in], axis=0)
-    sd = mm(mixer_rows, weight_sd)
+    zx = jnp.concatenate([v[:, : 2 * inner_cols].astype(bf16) for v in zxs], axis=0)
+    sd = jnp.concatenate([v[:, 2 * inner_cols :] for v in zxs], axis=0)
     gated, chunk_states = mixer_forward(place, lengths, tp, zx, sd, wide, narrow, rates)
-    out_grad_rows = jnp.concatenate(out_grad, axis=0)
-    grad_scaled = mm_nt(out_grad_rows, weight_out).astype(bf16)
     gated_wide = gated.astype(f32)
     sums = jnp.stack(
         [
@@ -743,81 +936,106 @@
     gate_root = lax.rsqrt(sums[0] / inner_total + norm_eps)
     stats = jnp.stack([gate_root, gate_root**3 * sums[1] / inner_total], axis=1)
     scaled = (gated_wide * gate_root[:, None] * gain_gate).astype(bf16)
-    out = residual + ring_scatter(lambda p: mm(piece(scaled, p), weight_out))
-    grad_w_out = scatter(mm_tn(scaled, out_grad_rows).astype(bf16), 1).astype(f32)
-
-    grad_zx, grad_sd, grad_wide, grad_narrow, grad_rates = mixer_backward(
+    out_terms = [mm(piece(scaled, p), weight_out) for p in range(tp)]
+    out = hop(out_terms[1 % tp].astype(bf16))
+
+    grad_all, grad_wide, grad_narrow, grad_rates = mixer_backward(
         place, lengths, tp, zx, sd, grad_scaled, stats, chunk_states, wide, narrow, rates
     )
-    grad_mixer_in = ring_scatter(
-        lambda p: mm_nt(piece(grad_zx, p), weight_zx) + mm_nt(piece(grad_sd, p), weight_sd)
-    )
-    grad_w_zx = scatter(mm_tn(mixer_rows, grad_zx).astype(bf16)).astype(f32)
-    grad_w_sd = mm_tn(mixer_rows, grad_sd)
+    out = tie(out, grad_all).astype(f32) + out_terms[2 % tp]
+    grad_mixer_in, (sum_w_out, sum_w_zx) = ring_scatter(
+        lambda p: mm_nt(piece(grad_all, p), weight_zx),
+        [
+            lambda t: mm_tn(tie(scaled, t), out_grad_rows).astype(bf16),
+            lambda t: mm_tn(tie(mixer_rows, t), grad_all).astype(bf16),
+        ],
+    )
+    sum_w_out = scatter(sum_w_out, 1)
+    sum_w_zx = scatter(sum_w_zx)
     grad_resid_norm, grad_gain_mixer = rms_backward(residual, mixer_root, gain_mixer, grad_mixer_in)
     grad_residual = output_cotangent.astype(f32) + grad_resid_norm
 
-    grad_branch = ring_gather(grad_residual.astype(bf16))
-
-    def gate_up_back(p):
-        grad_units = mm_nt(grad_branch[p], weight_fc2)
+    grad_gate_up = []
+
+    def feed_back(p, grad_rows):
+        grad_units = mm_nt(grad_rows, weight_fc2)
         gate = gate_up[p][:, :units_here].astype(f32)
         up = gate_up[p][:, units_here:].astype(f32)
         raised, back = jax.vjp(jax.nn.gelu, gate)
-        return jnp.concatenate(
+        both = jnp.concatenate(
             [back(grad_units * up)[0].astype(bf16), (grad_units * raised).astype(bf16)], axis=1
         )
-
-    grad_gate_up = [gate_up_back(p) for p in range(tp)]
-    grad_fc_mid = [mm_nt(v, fc_up).astype(bf16) for v in grad_gate_up]
-    grad_mlp_in = ring_scatter(
-        lambda p: mm_nt(grad_gate_up[p], weight_fc1) + mm_nt(grad_fc_mid[p], fc_down)
-    )
+        both = jnp.concatenate([both, mm_nt(both, fc_up).astype(bf16)], axis=1)
+        grad_gate_up.append(both)
+        return mm_nt(both, weight_fc1)
+
+    units_rows = jnp.concatenate(units, axis=0)
     mlp_rows = jnp.concatenate(mlp_in, axis=0)
+    grad_branch, grad_mlp_in, (sum_w_fc2, sum_w_fc1) = ring_both(
+        grad_residual.astype(bf16),
+        feed_back,
+        lambda pieces: mm_tn(tie(units_rows, sum_w_out), jnp.concatenate(pieces, axis=0)).astype(bf16),
+        [lambda: mm_tn(mlp_rows, jnp.concatenate(grad_gate_up, axis=0)).astype(bf16)],
+    )
+    sum_w_fc2 = scatter(sum_w_fc2, 1)
+    sum_w_fc1 = scatter(sum_w_fc1)
     grad_gate_up_rows = jnp.concatenate(grad_gate_up, axis=0)
-    grad_w_fc2 = scatter(
-        mm_tn(jnp.concatenate(units, axis=0), jnp.concatenate(grad_branch, axis=0)).astype(bf16), 1
-    ).astype(f32)
-    grad_w_fc1 = scatter(mm_tn(mlp_rows, grad_gate_up_rows).astype(bf16)).astype(f32)
-    grad_fc_up = mm_tn(jnp.concatenate(fc_mid, axis=0), grad_gate_up_rows)
-    grad_fc_down = mm_tn(mlp_rows, jnp.concatenate(grad_fc_mid, axis=0))
     grad_mixed_norm, grad_gain_mlp = rms_backward(mixed, mlp_root, gain_mlp, grad_mlp_in)
 
-    grad_mixed = ring_gather((grad_residual + grad_mixed_norm).astype(bf16))
-    grad_attended = [mm_nt(v, weight_o).astype(bf16) for v in grad_mixed]
-    grad_w_o = scatter(mm_tn(attended, jnp.concatenate(grad_mixed, axis=0)).astype(bf16), 1).astype(f32)
+    grad_mixed, grad_attended = ring_gather(
+        tie((grad_residual + grad_mixed_norm).astype(bf16), sum_w_zx),
+        lambda p, v: mm_nt(v, weight_o).astype(bf16),
+    )
+    sum_w_o = mm_tn(tie(attended, sum_w_fc2), jnp.concatenate(grad_mixed, axis=0)).astype(bf16)
+    grad_attended[-1] = tie(grad_attended[-1], sum_w_o)
+    sum_w_o = scatter(sum_w_o, 1)
+    out = hop(out.astype(bf16))
     grad_projected = attention_backward(
-        place, lengths, queries, keys, values, grad_attended, cosine, sine
-    )
+        place, lengths, queries, keys, values, ups, grad_attended, cosine, sine
+    )
+    out = tie(out, grad_projected).astype(f32) + out_terms[3 % tp]
     normed_rows = jnp.concatenate(normed, axis=0)
-    lora_rows = jnp.concatenate(lora_mid, axis=0)
-    grad_lora = jnp.concatenate(
-        [mm_nt(grad_projected[j], adapter_up[j]).astype(bf16) for j in range(3)], axis=1
-    )
-
-    def normed_back(p):
-        total = mm_nt(piece(grad_lora, p), adapter_down)
-        for j in range(3):
-            total = total + mm_nt(piece(grad_projected[j], p), weights_qkv[j])
-        return total
-
-    grad_normed = ring_scatter(normed_back)
-    grad_w_qkv = [
-        scatter(mm_tn(normed_rows, grad_projected[j]).astype(bf16)).astype(f32) for j in range(3)
-    ]
-    grad_up = [
-        mm_tn(lora_rows[:, j * rank : (j + 1) * rank], grad_projected[j]) for j in range(3)
-    ]
-    grad_down = scatter(mm_tn(normed_rows, grad_lora).astype(bf16))
-    grad_down = lax.psum_scatter(grad_down, "tp", scatter_dimension=0, tiled=True).astype(f32)
+    lora_rows = jnp.concatenate([v[:, 3 * head_cols :].astype(bf16) for v in projected], axis=0)
+
+    def finish(total):
+        for p in range(4, tp + 1):
+            total = hop(total.astype(bf16)).astype(f32) + out_terms[p % tp]
+        return residual + total
+
+    grad_normed, (sum_w_qkv, (grad_up, grad_fc_up), (out, late)) = ring_scatter(
+        lambda p: mm_nt(piece(grad_projected, p), weight_qkv),
+        [
+            lambda t: mm_tn(tie(normed_rows, t), grad_projected).astype(bf16),
+            lambda t: (
+                [
+                    mm_tn(
+                        tie(lora_rows, t)[:, j * rank : (j + 1) * rank],
+                        grad_projected[:, j * head_cols : (j + 1) * head_cols],
+                    )
+                    for j in range(3)
+                ],
+                mm_tn(tie(jnp.concatenate(fc_mid, axis=0), t), grad_gate_up_rows[:, : 2 * units_here]),
+            ),
+            lambda t: lax.optimization_barrier(
+                (finish(tie(out, t)), tie((grad_wide, grad_narrow, grad_rates), t))
+            ),
+        ],
+    )
+    sum_w_qkv = scatter(sum_w_qkv)
+    grad_wide, grad_narrow, grad_rates = late
     grad_joined, grad_gain_attn = rms_backward(joined, attn_root, gain_attn, grad_normed)
     grad_hidden = grad_residual + grad_joined[:, :width]
     grad_embed = grad_joined[:, width:]
-
-    grad_ups = scatter(jnp.concatenate(grad_up + [grad_fc_up], axis=1).astype(bf16)).astype(f32)
-    grad_downs = scatter(jnp.concatenate([grad_w_sd, grad_fc_down], axis=1).astype(bf16)).astype(f32)
-    grad_w_dt = grad_downs[:, 2 * LANES : 2 * LANES + mixer_heads]
-    shared = jnp.concatenate([grad_downs[:, : 2 * LANES], grad_downs[:, 3 * LANES :]], axis=1)
+    grad_down = halving(sum_w_qkv[:, 3 * head_cols :].astype(f32).reshape(tp, -1, 3 * rank), "tp")
+
+    grad_ups = jnp.concatenate(grad_up + [grad_fc_up], axis=1)
+    grad_ups = halving(grad_ups.reshape(fsdp, -1, grad_ups.shape[1]), "fsdp", bf16)
+    sum_w_zx = sum_w_zx.astype(f32)
+    sum_w_fc1 = sum_w_fc1.astype(f32)
+    at_t = 2 * inner_cols + 2 * LANES
+    grad_w_dt = sum_w_zx[:, at_t : at_t + mixer_heads]
+    shared = jnp.concatenate([sum_w_zx[:, 2 * inner_cols : at_t], sum_w_fc1[:, 2 * units_here :]], axis=1)
+    shared = doubling(shared, "tp")
 
     def by_fsdp(values):
         lead = values.shape[:-1]
@@ -835,33 +1053,33 @@
     shared_small = [by_fsdp(grad_taps_s), by_fsdp(grad_gain_mixer), by_fsdp(grad_gain_mlp)]
     small_sizes = [v.shape[1] for v in local_small + shared_small]
     small_cuts = [sum(small_sizes[:i]) for i in range(len(small_sizes) + 1)]
-    small_sum = lax.psum_scatter(
-        jnp.concatenate(local_small + shared_small, axis=1), "fsdp", scatter_dimension=0, tiled=True
-    ).reshape(-1)
+    small_sum = halving(jnp.concatenate(local_small + shared_small, axis=1), "fsdp")
     small_parts = [small_sum[small_cuts[i] : small_cuts[i + 1]] for i in range(len(small_sizes))]
-    shared, tail = lax.psum((shared, small_sum[small_cuts[4] :]), "tp")
+    tail = doubling(small_sum[small_cuts[4] :], "tp")
     tail_cuts = [v - small_cuts[4] for v in small_cuts[4:]]
     grad_conv_bc, sum_gain_mixer, sum_gain_mlp = (
         tail[tail_cuts[i] : tail_cuts[i + 1]] for i in range(3)
     )
-    grad_gain_attn = lax.psum_scatter(grad_gain_attn, ("fsdp", "tp"), scatter_dimension=0, tiled=True)
+    grad_gain_attn = halving(halving(grad_gain_attn.reshape(fsdp, -1), "fsdp").reshape(tp, -1), "tp")
     sum_rates = small_parts[3].reshape(2, mixer_heads)
     return (
         out,
         grad_hidden,
         grad_embed,
         grad_gain_attn,
-        jnp.stack(grad_w_qkv, axis=1),
+        jnp.stack(
+            [sum_w_qkv[:, j * head_cols : (j + 1) * head_cols].astype(f32) for j in range(3)], axis=1
+        ),
         grad_down.reshape(-1, 3, rank),
         grad_ups[:, : 3 * head_cols].reshape(-1, 3, head_cols),
-        grad_w_o,
+        sum_w_o.astype(f32),
         sum_gain_mlp,
-        grad_w_fc1.reshape(-1, 2, units_here),
+        sum_w_fc1[:, : 2 * units_here].reshape(-1, 2, units_here),
         shared[:, 2 * LANES :],
         grad_ups[:, 3 * head_cols :].reshape(-1, 2, units_here),
-        grad_w_fc2,
+        sum_w_fc2.astype(f32),
         sum_gain_mixer,
-        grad_w_zx.reshape(-1, 2, inner_cols),
+        sum_w_zx[:, : 2 * inner_cols].reshape(-1, 2, inner_cols),
         shared[:, : 2 * LANES].reshape(-1, 2, LANES)[:, :, :states],
         grad_w_dt,
         small_parts[0].reshape(count, mixer_heads, -1),
@@ -870,7 +1088,7 @@
         sum_rates[1],
         small_parts[1].reshape(mixer_heads, -1),
         small_parts[2].reshape(mixer_heads, -1),
-        grad_w_out,
+        sum_w_out.astype(f32),
     )
 
 

time: 2000 us -> 1490 us (0.74)
  waiting for transfers between devices: 1050 us -> 597 us
  matrix products: 577 us -> 485 us
  blocking collectives: 93.9 us -> 17.9 us
  other arithmetic: 56.6 us -> 99.9 us
  starting transfers between devices: 15.3 us -> 45.7 us
  local copies, waits for them, and re-layouts: 74.3 us -> 95.1 us
    reduce_scatter x11 -> x6, waiting for transfers between devices: 337 us -> 0.03 us  [scatter(): return lax.psum_scatter(values, 'fsdp', scatter_dimension=axis, tiled=True)]
    ppermute x36 -> x56, waiting for transfers between devices: 671 us -> 583 us  [the longest x36 462 us: hop(): return lax.ppermute(values, 'tp', ring_pairs())]
    unnamed x2 -> x0, blocking collectives: 66.1 us -> none
    dot_general x57 -> x28, matrix products: 204 us -> 172 us  [mm(): return jnp.dot(left, right, preferred_element_type=f32)]
    dot_general x15 -> x10, matrix products: 144 us -> 112 us  [mm_tn(): lax.dot_general(left, right, (((0,), (0,)), ((), ())), preferred_element_...]
    ppermute x36 -> x56, starting transfers between devices: 13.1 us -> 44.5 us  [the longest x36 24.8 us: hop(): return lax.ppermute(values, 'tp', ring_pairs())]
    dot_general x48 -> x25, matrix products: 229 us -> 201 us  [mm_nt(): lax.dot_general(left, right, (((1,), (1,)), ((), ())), preferred_element_...]
    all_gather x11 -> x5, waiting for transfers between devices: 37.1 us -> 13.7 us  [gather(): return lax.all_gather(values, 'fsdp', axis=axis, tiled=True)]
  transfers between devices with their start and end apart: 60 -> 67, of which waited for: 37 -> 38; matrix products, arithmetic and copies ran while one was open for 32% -> 42% of each run, Pallas kernels for 6% -> 5%
where the time goes in v2:
time: 1490 us; the launch traced here: 1480 us
  waiting for transfers between devices  597 us (40%)
  matrix products  485 us (33%)
  Pallas kernels  121 us (8%)
  other arithmetic  99.9 us (7%)
  local copies, waits for them, and re-layouts  95.1 us (6%)
  starting transfers between devices  45.7 us (3%)
  blocking collectives  17.9 us (1%)
  between operations  16.8 us (1%)
    ppermute x36, waiting for transfers between devices, hop(): return lax.ppermute(values, 'tp', ring_pairs())  462 us
    dot_general x25, matrix products, mm_nt(): lax.dot_general(left, right, (((1,), (1,)), ((), ())), preferred_element_...  201 us
    dot_general x28, matrix products, mm(): return jnp.dot(left, right, preferred_element_type=f32)  172 us
    dot_general x10, matrix products, mm_tn(): lax.dot_general(left, right, (((0,), (0,)), ((), ())), preferred_element_...  112 us
    ppermute x4, waiting for transfers between devices, doubling(): lax.ppermute(values, name, [(i, i ^ step) for i in range(count)])  55.9 us
    ppermute x13, waiting for transfers between devices, halving(): lax.ppermute(sent.astype(sent_as), name, [(i, i ^ half) for i in range(co...  43.6 us
    unnamed x327, local copies, waits for them, and re-layouts  43.5 us
    pallas_call x1, Pallas kernels, attention_backward(): pl.pallas_call(functools.partial(attention_backward_kernel, tp, heads), o...  40 us
  transfers between devices with their start and end apart: 67, of which 38 were waited for; matrix products, arithmetic and copies ran while one was open for 42% of the time, Pallas kernels for 5%

profile of v2, /device:TPU:0, one launch (start us, length us, event | category | flops | bytes accessed | tf_op | source)
XLA Modules:
  0.0 1478.3 jit_solution(11186967839437512417)
XLA Ops:
  53.5 21.0 %collective-permute-done.1 = bf16[32,7168]{1,0:T(8,128)(2,1)S(1)} collective-permute-done((bf16[32,7168]{1,0:T(8,128)(2,1)S(1)}, bf16[32,7168]{1,0:T(8,128)(2,1)S(1)}, u32[]{:S(2)}, u32[]{:S(2)}) %collective-permute-start.1) | collective-permute-done | bytes 458784 | tf_op jit(solution)/shard_map/ppermute | solution.py:699
  85.2 39.0 %collective-permute-done.4 = bf16[256,4096]{1,0:T(8,128)(2,1)S(1)} collective-permute-done((bf16[256,4096]{1,0:T(8,128)(2,1)}, bf16[256,4096]{1,0:T(8,128)(2,1)S(1)}, u32[]{:S(2)}, u32[]{:S(2)}) %collective-permute-start.4) | collective-permute-done | bytes 2097184 | tf_op jit(solution)/shard_map/ppermute | solution.py:617
  126.0 45.9 %collective-permute-done.5 = bf16[256,4096]{1,0:T(8,128)(2,1)S(1)} collective-permute-done((bf16[256,4096]{1,0:T(8,128)(2,1)S(1)}, bf16[256,4096]{1,0:T(8,128)(2,1)S(1)}, u32[]{:S(2)}, u32[]{:S(2)}) %collective-permute-start.5) | collective-permute-done | bytes 2097184 | tf_op jit(solution)/shard_map/ppermute | solution.py:617
  177.2 15.1 %fusion.313.refs_4_.refs_5_.refs_6_.refs_7_ = f32[256,3456]{1,0:T(8,128)} fusion(bf16[256,4096]{1,0:T(8,128)(2,1)S(1)} %copy-done.21, bf16[4096,3456]{1,0:T(8,128)(2,1)} %all-gather.8.cloned.1.call-done), kind=kOutput, calls=%fused_computation.510 | convolution fusion | flops 7247757312 | bytes 33947648 | tf_op jit(solution)/shard_map/dot_general | solution.py:24
  192.3 15.4 %fusion.312.refs_0_.refs_1_.refs_2_.refs_3_ = f32[256,3456]{1,0:T(8,128)} fusion(bf16[256,4096]{1,0:T(8,128)(2,1)S(1)} %copy-done.23, bf16[4096,3456]{1,0:T(8,128)(2,1)} %all-gather.8.cloned.1.call-done), kind=kOutput, calls=%fused_computation.509 | convolution fusion | flops 7247757312 | bytes 33947648 | tf_op jit(solution)/shard_map/dot_general | solution.py:24
  209.3 15.2 %fusion.315.refs_12_.refs_13_.refs_14_.refs_15_ = f32[256,3456]{1,0:T(8,128)} fusion(bf16[256,4096]{1,0:T(8,128)(2,1)S(1)} %copy-done.25, bf16[4096,3456]{1,0:T(8,128)(2,1)} %all-gather.8.cloned.1.call-done), kind=kOutput, calls=%fused_computation.512 | convolution fusion | flops 7247757312 | bytes 33947648 | tf_op jit(solution)/shard_map/dot_general | solution.py:24
  224.5 17.1 %fusion.314.refs_8_.refs_9_.refs_10_.refs_11_ = f32[256,3456]{1,0:T(8,128)} fusion(bf16[256,4096]{1,0:T(8,128)(2,1)S(1)} %copy-done.27, bf16[4096,3456]{1,0:T(8,128)(2,1)} %all-gather.8.cloned.1.call-done), kind=kOutput, calls=%fused_computation.511 | convolution fusion | flops 7247757312 | bytes 33947648 | tf_op jit(solution)/shard_map/dot_general | solution.py:24
  243.2 26.8 %attention_forward.1 = (bf16[1024,1024]{1,0:T(8,128)(2,1)}, bf16[1024,1024]{1,0:T(8,128)(2,1)}, bf16[1024,1024]{1,0:T(8,128)(2,1)}, bf16[1024,1024]{1,0:T(8,128)(2,1)}) custom-call(s32[1]{0:T(128)} %bitcast.place_ref, s32[3]{0:T(128)} %bitcast.236, f32[1024,128]{1,0:T(8,128)} %get-tuple-element.311.cosine_ref, f32[1024,128]{1,0:T(8,128)} %get-tuple-element.312.sine_ref, ...), custom_call_target="tpu_custom_call" | custom-call | flops 4294967296 | bytes 20971520 | tf_op jit(solution)/shard_map/attention_forward/pallas_call | solution.py:114
  280.1 21.7 %collective-permute-done.9 = bf16[256,2048]{1,0:T(8,128)(2,1)S(1)} collective-permute-done((bf16[256,2048]{1,0:T(8,128)(2,1)S(1)}, bf16[256,2048]{1,0:T(8,128)(2,1)S(1)}, u32[]{:S(2)}, u32[]{:S(2)}) %collective-permute-start.9) | collective-permute-done | bytes 1048608 | tf_op jit(solution)/shard_map/ppermute | solution.py:617
  312.8 18.8 %collective-permute-done.10 = bf16[256,2048]{1,0:T(8,128)(2,1)} collective-permute-done((bf16[256,2048]{1,0:T(8,128)(2,1)}, bf16[256,2048]{1,0:T(8,128)(2,1)}, u32[]{:S(2)}, u32[]{:S(2)}) %collective-permute-start.10) | collective-permute-done | bytes 1048608 | tf_op jit(solution)/shard_map/ppermute | solution.py:617
  335.7 22.8 %collective-permute-done.11 = bf16[256,2048]{1,0:T(8,128)(2,1)S(1)} collective-permute-done((bf16[256,2048]{1,0:T(8,128)(2,1)S(1)}, bf16[256,2048]{1,0:T(8,128)(2,1)S(1)}, u32[]{:S(2)}, u32[]{:S(2)}) %collective-permute-start.11) | collective-permute-done | bytes 1048608 | tf_op jit(solution)/shard_map/ppermute | solution.py:617
  374.6 12.9 all-gather.14.cloned.1.call-done
  396.7 10.5 fusion.317
  423.2 9.3 fusion.318
  436.0 9.6 collective-permute-done.13
  448.4 19.7 %collective-permute-done.16 = bf16[256,2048]{1,0:T(8,128)(2,1)S(1)} collective-permute-done((bf16[256,2048]{1,0:T(8,128)(2,1)S(1)}, bf16[256,2048]{1,0:T(8,128)(2,1)S(1)}, u32[]{:S(2)}, u32[]{:S(2)}) %collective-permute-start.16) | collective-permute-done | bytes 1048608 | tf_op jit(solution)/shard_map/ppermute | solution.py:617
  468.1 9.3 fusion.319
  497.0 20.8 %collective-permute-done.17 = bf16[256,2048]{1,0:T(8,128)(2,1)} collective-permute-done((bf16[256,2048]{1,0:T(8,128)(2,1)}, bf16[256,2048]{1,0:T(8,128)(2,1)}, u32[]{:S(2)}, u32[]{:S(2)}) %collective-permute-start.17) | collective-permute-done | bytes 1048608 | tf_op jit(solution)/shard_map/ppermute | solution.py:617
  555.4 16.4 %collective-permute-done.19 = bf16[256,2048]{1,0:T(8,128)(2,1)} collective-permute-done((bf16[256,2048]{1,0:T(8,128)(2,1)S(1)}, bf16[256,2048]{1,0:T(8,128)(2,1)}, u32[]{:S(2)}, u32[]{:S(2)}) %collective-permute-start.19) | collective-permute-done | bytes 1048608 | tf_op jit(solution)/shard_map/ppermute | solution.py:617
  577.1 18.4 %collective-permute-done.20 = bf16[256,2048]{1,0:T(8,128)(2,1)S(1)} collective-permute-done((bf16[256,2048]{1,0:T(8,128)(2,1)}, bf16[256,2048]{1,0:T(8,128)(2,1)S(1)}, u32[]{:S(2)}, u32[]{:S(2)}) %collective-permute-start.20) | collective-permute-done | bytes 1048608 | tf_op jit(solution)/shard_map/ppermute | solution.py:617
  602.2 17.7 %mixer_forward.1 = (bf16[1024,1024]{1,0:T(8,128)(2,1)}, bf16[8,64,1024]{2,1,0:T(8,128)(2,1)}) custom-call(s32[1]{0:T(128)} %bitcast.place_ref, s32[3]{0:T(128)} %bitcast.237, bf16[1024,2048]{1,0:T(8,128)(2,1)} %pad_maximum_fusion.1.zx.before, bf16[1024,2048]{1,0:T(8,128)(2,1)} %pad_maximum_fusion.1.zx.before, f32[1024,384]{1,0:T(8,128)} %pad_maximum_fusion.8.sd.sd_before, ...), custom_call_target="tpu_custom_call" | custom-call | flops 1073741824 | bytes 8388608 | tf_op jit(solution)/shard_map/mixer_forward/pallas_call | solution.py:523
  634.8 36.4 %mixer_backward.1 = (bf16[1024,2432]{1,0:T(8,128)(2,1)}, f32[8,1024]{1,0:T(8,128)}, f32[8,256]{1,0:T(8,128)}, f32[8,128]{1,0:T(8,128)}) custom-call(s32[1]{0:T(128)} %bitcast.place_ref, s32[3]{0:T(128)} %bitcast.238, bf16[1024,2048]{1,0:T(8,128)(2,1)} %pad_maximum_fusion.1.zx.before, bf16[1024,2048]{1,0:T(8,128)(2,1)} %pad_maximum_fusion.1.zx.before, ...), custom_call_target="tpu_custom_call" | custom-call | flops 3221225472 | bytes 12582912 | tf_op jit(solution)/shard_map/mixer_backward/pallas_call | solution.py:560
  710.8 13.6 convolution_convert_fusion.2
  736.3 15.7 %collective-permute-done.25 = bf16[256,2048]{1,0:T(8,128)(2,1)S(1)} collective-permute-done((bf16[256,2048]{1,0:T(8,128)(2,1)S(1)}, bf16[256,2048]{1,0:T(8,128)(2,1)S(1)}, u32[]{:S(2)}, u32[]{:S(2)}) %collective-permute-start.25) | collective-permute-done | bytes 1048608 | tf_op jit(solution)/shard_map/ppermute | solution.py:617
  775.5 13.4 fusion.112
  799.1 13.3 fusion.118
  826.2 14.4 collective-permute-done.27
  840.6 12.6 convert_add_fusion.7
  853.2 14.5 convolution_convert_fusion.3
  880.2 29.3 %convolution_convert_fusion.1 = bf16[2048,4224]{1,0:T(8,128)(2,1)} fusion(bf16[256,128]{1,0:T(8,128)(2,1)S(1)} %fusion.235, bf16[256,2048]{1,0:T(8,128)(2,1)} %copy-done.122, bf16[256,2048]{1,0:T(8,128)(2,1)} %copy-done.120, bf16[256,128]{1,0:T(8,128)(2,1)S(1)} %fusion.238, bf16[256,2048]{1,0:T(8,128)(2,1)} %copy-done.118, ...), kind=kOutput, calls=%fused_computation.1 | convolution fusion | flops 17845977088 | bytes 30146560 | tf_op jit(solution)/shard_map/dot_general | solution.py:32
  909.7 9.2 fusion.130
  919.0 17.2 %collective-permute-done.29 = bf16[256,2048]{1,0:T(8,128)(2,1)S(1)} collective-permute-done((bf16[256,2048]{1,0:T(8,128)(2,1)}, bf16[256,2048]{1,0:T(8,128)(2,1)S(1)}, u32[]{:S(2)}, u32[]{:S(2)}) %collective-permute-start.29) | collective-permute-done | bytes 1048608 | tf_op jit(solution)/shard_map/ppermute | solution.py:617
  936.5 25.9 %collective-permute-done.31 = bf16[256,2048]{1,0:T(8,128)(2,1)S(1)} collective-permute-done((bf16[256,2048]{1,0:T(8,128)(2,1)S(1)}, bf16[256,2048]{1,0:T(8,128)(2,1)S(1)}, u32[]{:S(2)}, u32[]{:S(2)}) %collective-permute-start.31) | collective-permute-done | bytes 1048608 | tf_op jit(solution)/shard_map/ppermute | solution.py:617
  969.8 21.3 %collective-permute-done.32 = bf16[256,2048]{1,0:T(8,128)(2,1)S(1)} collective-permute-done((bf16[256,2048]{1,0:T(8,128)(2,1)S(1)}, bf16[256,2048]{1,0:T(8,128)(2,1)S(1)}, u32[]{:S(2)}, u32[]{:S(2)}) %collective-permute-start.32) | collective-permute-done | bytes 1048608 | tf_op jit(solution)/shard_map/ppermute | solution.py:617
  993.1 24.2 %collective-permute-done.33 = bf16[256,2048]{1,0:T(8,128)(2,1)} collective-permute-done((bf16[256,2048]{1,0:T(8,128)(2,1)S(1)}, bf16[256,2048]{1,0:T(8,128)(2,1)}, u32[]{:S(2)}, u32[]{:S(2)}) %collective-permute-start.33) | collective-permute-done | bytes 1048608 | tf_op jit(solution)/shard_map/ppermute | solution.py:617
  1024.7 9.6 collective-permute-done.34
  1047.6 40.0 %attention_backward.1 = bf16[1024,3456]{1,0:T(8,128)(2,1)} custom-call(s32[1]{0:T(128)} %bitcast.place_ref, s32[3]{0:T(128)} %bitcast.239, f32[1024,128]{1,0:T(8,128)} %get-tuple-element.311.cosine_ref, f32[1024,128]{1,0:T(8,128)} %get-tuple-element.312.sine_ref, bf16[1024,1024]{1,0:T(8,128)(2,1)} %get-tuple-element.104.q_ref, ...), custom_call_target="tpu_custom_call" | custom-call | flops 10737418240 | bytes 14680064 | tf_op jit(solution)/shard_map/attention_backward/pallas_call | solution.py:226
  1087.5 15.2 %convolution_convert_fusion.4 = bf16[256,4096]{1,0:T(8,128)(2,1)} fusion(bf16[4096,3456]{1,0:T(8,128)(2,1)} %all-gather.8.cloned.1.call-done, bf16[1024,3456]{1,0:T(8,128)(2,1)} %attention_backward.1), kind=kOutput, calls=%fused_computation.69 | convolution fusion | flops 7248805888 | bytes 32178176 | tf_op jit(solution)/shard_map/dot_general | solution.py:28
  1102.7 37.3 %convolution_convert_fusion = bf16[4096,3456]{1,0:T(8,128)(2,1)} fusion(bf16[1024,4096]{1,0:T(8,128)(2,1)S(1)} %bitcast.191, bf16[1024,3456]{1,0:T(8,128)(2,1)} %attention_backward.1), kind=kOutput, calls=%fused_computation | convolution fusion | flops 29005185024 | bytes 43778048 | tf_op jit(solution)/shard_map/dot_general | solution.py:32
  1150.4 23.4 %collective-permute-done.21 = bf16[256,2048]{1,0:T(8,128)(2,1)S(1)} collective-permute-done((bf16[256,2048]{1,0:T(8,128)(2,1)S(1)}, bf16[256,2048]{1,0:T(8,128)(2,1)S(1)}, u32[]{:S(2)}, u32[]{:S(2)}) %collective-permute-start.21) | collective-permute-done | bytes 1048608 | tf_op jit(solution)/shard_map/ppermute | solution.py:617
  1198.9 28.2 %collective-permute-done.22 = bf16[256,2048]{1,0:T(8,128)(2,1)} collective-permute-done((bf16[256,2048]{1,0:T(8,128)(2,1)}, bf16[256,2048]{1,0:T(8,128)(2,1)}, u32[]{:S(2)}, u32[]{:S(2)}) %collective-permute-start.22) | collective-permute-done | bytes 1048608 | tf_op jit(solution)/shard_map/ppermute | solution.py:617
  1229.0 16.2 %add_convert_fusion.1 = bf16[256,4096]{1,0:T(8,128)(2,1)} fusion(bf16[256,4096]{1,0:T(8,128)(2,1)} %collective-permute-done.35, bf16[4096,3456]{1,0:T(8,128)(2,1)} %all-gather.8.cloned.1.call-done, bf16[1024,3456]{1,0:T(8,128)(2,1)} %attention_backward.1), kind=kOutput, calls=%fused_computation.122 | convolution fusion | flops 7250903040 | bytes 34275328 | tf_op jit(solution)/shard_map/dot_general | solution.py:28
  1250.8 30.7 %collective-permute-done.46 = bf16[4,16,7168]{2,1,0:T(8,128)(2,1)S(1)} collective-permute-done((bf16[4,16,7168]{2,1,0:T(8,128)(2,1)S(1)}, bf16[4,16,7168]{2,1,0:T(8,128)(2,1)S(1)}, u32[]{:S(2)}, u32[]{:S(2)}) %collective-permute-start.46) | collective-permute-done | bytes 917536 | tf_op jit(solution)/shard_map/ppermute | solution.py:688
  1281.8 16.9 %add_convert_fusion = bf16[256,4096]{1,0:T(8,128)(2,1)} fusion(bf16[256,4096]{1,0:T(8,128)(2,1)} %collective-permute-done.36, bf16[4096,3456]{1,0:T(8,128)(2,1)} %all-gather.8.cloned.1.call-done, bf16[1024,3456]{1,0:T(8,128)(2,1)} %attention_backward.1), kind=kOutput, calls=%fused_computation.121 | convolution fusion | flops 7250903040 | bytes 34275328 | tf_op jit(solution)/shard_map/dot_general | solution.py:28
  1301.8 13.6 collective-permute-done.37
  1333.2 41.2 %collective-permute-done.52 = f32[576]{0:T(1024)S(1)} collective-permute-done((f32[576]{0:T(1024)S(1)}, f32[576]{0:T(1024)S(1)}, u32[]{:S(2)}, u32[]{:S(2)}) %collective-permute-start.52) | collective-permute-done | bytes 2336 | tf_op jit(solution)/shard_map/ppermute | solution.py:712
  1381.2 16.1 %fusion.56 = (f32[4096]{0:T(1024)S(1)}, f32[256]{0:T(256)S(1)}, f32[256,4096]{1,0:T(8,128)}) fusion(bf16[256,4096]{1,0:T(8,128)(2,1)S(1)} %copy-done.6, f32[256]{0:T(256)S(1)} %copy-done.80, f32[4096]{0:T(1024)S(1)} %bitcast.207, bf16[4096,3456]{1,0:T(8,128)(2,1)} %all-gather.8.cloned.1.call-done, bf16[1024,3456]{1,0:T(8,128)(2,1)} %attention_backward.1, ...), kind=kOutput, calls=%fused_computation.74 | convolution fusion | flops 7257190400 | bytes 38504448 | tf_op jit(solution)/shard_map/dot_general | solution.py:28
  1440.8 13.3 collective-permute-done.55
  (714 shorter events, 495.2 us)
Async XLA Ops:
  7.2 170.0 %all-gather.8.cloned.1.call-start = ((), (), s32[]{:S(2)}) async-start(), calls=%async_computation.6 | async-start | bytes 31850496 | tf_op jit(solution)/shard_map/all_gather | solution.py:732
  15.2 255.9 %all-gather.10.cloned.1.call-start = ((), (), s32[]{:S(2)}) async-start(), calls=%async_computation.7 | async-start | bytes 4718592 | tf_op jit(solution)/shard_map/all_gather | solution.py:732
  15.9 344.3 %all-gather.12.cloned.1.call-start = ((), (), s32[]{:S(2)}) async-start(), calls=%async_computation.8 | async-start | bytes 19464192 | tf_op jit(solution)/shard_map/all_gather | solution.py:732
  24.5 362.9 %all-gather.14.cloned.1.call-start = ((), (), s32[]{:S(2)}) async-start(), calls=%async_computation.9 | async-start | bytes 14155776 | tf_op jit(solution)/shard_map/all_gather | solution.py:732
  24.6 50.8 %collective-permute-start.3 = (bf16[256,4096]{1,0:T(8,128)(2,1)S(1)}, bf16[256,4096]{1,0:T(8,128)(2,1)}, u32[]{:S(2)}, u32[]{:S(2)}) collective-permute-start(bf16[256,4096]{1,0:T(8,128)(2,1)S(1)} %constant_dynamic-update-slice_fusion.3), channel_id=1, source_target_pairs={{0,1},{1,2},{2,3},{3,0},{4,5},{5,6},{6,7},{7,4},{8,9},{9,10},{10,1... | collective-permute-start | bytes 6291464 | tf_op jit(solution)/shard_map/ppermute | solution.py:617
  32.8 488.6 %all-gather.16.cloned.1.call-start = ((), (), s32[]{:S(2)}) async-start(), calls=%async_computation.10 | async-start | bytes 11206656 | tf_op jit(solution)/shard_map/all_gather | solution.py:732
  75.4 48.8 %collective-permute-start.4 = (bf16[256,4096]{1,0:T(8,128)(2,1)}, bf16[256,4096]{1,0:T(8,128)(2,1)S(1)}, u32[]{:S(2)}, u32[]{:S(2)}) collective-permute-start(bf16[256,4096]{1,0:T(8,128)(2,1)} %collective-permute-done.3), channel_id=1, source_target_pairs={{0,1},{1,2},{2,3},{3,0},{4,5},{5,6},{6,7},{7,4},{8,9},{9,10},{10,1... | collective-permute-start | bytes 6291464 | tf_op jit(solution)/shard_map/ppermute | solution.py:617
  76.3 47.9 %collective-permute-start.2 = (bf16[64,7168]{1,0:T(8,128)(2,1)S(1)}, bf16[64,7168]{1,0:T(8,128)(2,1)S(1)}, u32[]{:S(2)}, u32[]{:S(2)}) collective-permute-start(bf16[64,7168]{1,0:T(8,128)(2,1)S(1)} %pad_maximum_fusion.9), channel_id=1, source_target_pairs={{0,16},{4,20},{8,24},{12,28},{16,0},{20,4},{24,8},{28,12},{1,17},{... | collective-permute-start | bytes 2752520 | tf_op jit(solution)/shard_map/ppermute | solution.py:699
  124.2 47.7 %collective-permute-start.5 = (bf16[256,4096]{1,0:T(8,128)(2,1)S(1)}, bf16[256,4096]{1,0:T(8,128)(2,1)S(1)}, u32[]{:S(2)}, u32[]{:S(2)}) collective-permute-start(bf16[256,4096]{1,0:T(8,128)(2,1)S(1)} %collective-permute-done.4), channel_id=1, source_target_pairs={{0,1},{1,2},{2,3},{3,0},{4,5},{5,6},{6,7},{7,4},{8,9},{9,10},{10,1... | collective-permute-start | bytes 6291464 | tf_op jit(solution)/shard_map/ppermute | solution.py:617
  171.9 35.8 %collective-permute-start.6 = (bf16[256,2048]{1,0:T(8,128)(2,1)}, bf16[256,2048]{1,0:T(8,128)(2,1)}, u32[]{:S(2)}, u32[]{:S(2)}) collective-permute-start(bf16[256,2048]{1,0:T(8,128)(2,1)} %param.51), channel_id=1, source_target_pairs={{0,1},{1,2},{2,3},{3,0},{4,5},{5,6},{6,7},{7,4},{8,9},{9,10},{10,1... | collective-permute-start | bytes 3145736 | tf_op jit(solution)/shard_map/ppermute | solution.py:617
  207.7 33.9 %collective-permute-start.7 = (bf16[256,2048]{1,0:T(8,128)(2,1)}, bf16[256,2048]{1,0:T(8,128)(2,1)S(1)}, u32[]{:S(2)}, u32[]{:S(2)}) collective-permute-start(bf16[256,2048]{1,0:T(8,128)(2,1)} %collective-permute-done.6), channel_id=1, source_target_pairs={{0,1},{1,2},{2,3},{3,0},{4,5},{5,6},{6,7},{7,4},{8,9},{9,10},{10,1... | collective-permute-start | bytes 3145736 | tf_op jit(solution)/shard_map/ppermute | solution.py:617
  241.6 28.4 %collective-permute-start.8 = (bf16[256,2048]{1,0:T(8,128)(2,1)S(1)}, bf16[256,2048]{1,0:T(8,128)(2,1)S(1)}, u32[]{:S(2)}, u32[]{:S(2)}) collective-permute-start(bf16[256,2048]{1,0:T(8,128)(2,1)S(1)} %collective-permute-done.7), channel_id=1, source_target_pairs={{0,1},{1,2},{2,3},{3,0},{4,5},{5,6},{6,7},{7,4},{8,9},{9,10},{10,1... | collective-permute-start | bytes 3145736 | tf_op jit(solution)/shard_map/ppermute | solution.py:617
  274.8 27.0 %collective-permute-start.9 = (bf16[256,2048]{1,0:T(8,128)(2,1)S(1)}, bf16[256,2048]{1,0:T(8,128)(2,1)S(1)}, u32[]{:S(2)}, u32[]{:S(2)}) collective-permute-start(bf16[256,2048]{1,0:T(8,128)(2,1)S(1)} %convolution_convert_fusion.8), channel_id=1, source_target_pairs={{0,1},{1,2},{2,3},{3,0},{4,5},{5,6},{6,7},{7,4},{8,9},{9,10},{10,1... | collective-permute-start | bytes 3145736 | tf_op jit(solution)/shard_map/ppermute | solution.py:617
  305.1 26.5 %collective-permute-start.10 = (bf16[256,2048]{1,0:T(8,128)(2,1)}, bf16[256,2048]{1,0:T(8,128)(2,1)}, u32[]{:S(2)}, u32[]{:S(2)}) collective-permute-start(bf16[256,2048]{1,0:T(8,128)(2,1)} %add_convert_fusion.9), channel_id=1, source_target_pairs={{0,1},{1,2},{2,3},{3,0},{4,5},{5,6},{6,7},{7,4},{8,9},{9,10},{10,1... | collective-permute-start | bytes 3145736 | tf_op jit(solution)/shard_map/ppermute | solution.py:617
  308.5 544.7 %reduce-scatter.7.cloned.1.call-start = ((), (), s32[]{:S(2)}) async-start(), calls=%async_computation.11 | async-start | bytes 4718592 | tf_op jit(solution)/shard_map/reduce_scatter | solution.py:736
  333.2 25.3 %collective-permute-start.11 = (bf16[256,2048]{1,0:T(8,128)(2,1)S(1)}, bf16[256,2048]{1,0:T(8,128)(2,1)S(1)}, u32[]{:S(2)}, u32[]{:S(2)}) collective-permute-start(bf16[256,2048]{1,0:T(8,128)(2,1)S(1)} %add_convert_fusion.8), channel_id=1, source_target_pairs={{0,1},{1,2},{2,3},{3,0},{4,5},{5,6},{6,7},{7,4},{8,9},{9,10},{10,1... | collective-permute-start | bytes 3145736 | tf_op jit(solution)/shard_map/ppermute | solution.py:617
  360.3 34.7 %collective-permute-start.12 = (bf16[256,2048]{1,0:T(8,128)(2,1)}, bf16[256,2048]{1,0:T(8,128)(2,1)}, u32[]{:S(2)}, u32[]{:S(2)}) collective-permute-start(bf16[256,2048]{1,0:T(8,128)(2,1)} %multiply_convert_fusion.5), channel_id=1, source_target_pairs={{0,1},{1,2},{2,3},{3,0},{4,5},{5,6},{6,7},{7,4},{8,9},{9,10},{10,1... | collective-permute-start | bytes 3145736 | tf_op jit(solution)/shard_map/ppermute | solution.py:617
  394.9 28.2 %collective-permute-start.14 = (bf16[256,2048]{1,0:T(8,128)(2,1)}, bf16[256,2048]{1,0:T(8,128)(2,1)S(1)}, u32[]{:S(2)}, u32[]{:S(2)}) collective-permute-start(bf16[256,2048]{1,0:T(8,128)(2,1)} %collective-permute-done.12), channel_id=1, source_target_pairs={{0,1},{1,2},{2,3},{3,0},{4,5},{5,6},{6,7},{7,4},{8,9},{9,10},{10,1... | collective-permute-start | bytes 3145736 | tf_op jit(solution)/shard_map/ppermute | solution.py:617
  413.0 32.6 %collective-permute-start.13 = (bf16[256,2048]{1,0:T(8,128)(2,1)S(1)}, bf16[256,2048]{1,0:T(8,128)(2,1)S(1)}, u32[]{:S(2)}, u32[]{:S(2)}) collective-permute-start(bf16[256,2048]{1,0:T(8,128)(2,1)S(1)} %fusion.222), channel_id=1, source_target_pairs={{0,1},{1,2},{2,3},{3,0},{4,5},{5,6},{6,7},{7,4},{8,9},{9,10},{10,1... | collective-permute-start | bytes 3145736 | tf_op jit(solution)/shard_map/ppermute | solution.py:617
  423.2 44.9 %collective-permute-start.16 = (bf16[256,2048]{1,0:T(8,128)(2,1)S(1)}, bf16[256,2048]{1,0:T(8,128)(2,1)S(1)}, u32[]{:S(2)}, u32[]{:S(2)}) collective-permute-start(bf16[256,2048]{1,0:T(8,128)(2,1)S(1)} %collective-permute-done.14), channel_id=1, source_target_pairs={{0,1},{1,2},{2,3},{3,0},{4,5},{5,6},{6,7},{7,4},{8,9},{9,10},{10,1... | collective-permute-start | bytes 3145736 | tf_op jit(solution)/shard_map/ppermute | solution.py:617
  448.1 41.8 %collective-permute-start.15 = (bf16[256,2048]{1,0:T(8,128)(2,1)S(1)}, bf16[256,2048]{1,0:T(8,128)(2,1)S(1)}, u32[]{:S(2)}, u32[]{:S(2)}) collective-permute-start(bf16[256,2048]{1,0:T(8,128)(2,1)S(1)} %convert_add_fusion.9), channel_id=1, source_target_pairs={{0,1},{1,2},{2,3},{3,0},{4,5},{5,6},{6,7},{7,4},{8,9},{9,10},{10,1... | collective-permute-start | bytes 3145736 | tf_op jit(solution)/shard_map/ppermute | solution.py:617
  491.2 26.6 %collective-permute-start.17 = (bf16[256,2048]{1,0:T(8,128)(2,1)}, bf16[256,2048]{1,0:T(8,128)(2,1)}, u32[]{:S(2)}, u32[]{:S(2)}) collective-permute-start(bf16[256,2048]{1,0:T(8,128)(2,1)} %add_convert_fusion.7), channel_id=1, source_target_pairs={{0,1},{1,2},{2,3},{3,0},{4,5},{5,6},{6,7},{7,4},{8,9},{9,10},{10,1... | collective-permute-start | bytes 3145736 | tf_op jit(solution)/shard_map/ppermute | solution.py:617
  521.3 25.4 %collective-permute-start.18 = (bf16[256,2048]{1,0:T(8,128)(2,1)S(1)}, bf16[256,2048]{1,0:T(8,128)(2,1)S(1)}, u32[]{:S(2)}, u32[]{:S(2)}) collective-permute-start(bf16[256,2048]{1,0:T(8,128)(2,1)S(1)} %multiply_convert_fusion.4), channel_id=1, source_target_pairs={{0,1},{1,2},{2,3},{3,0},{4,5},{5,6},{6,7},{7,4},{8,9},{9,10},{10,1... | collective-permute-start | bytes 3145736 | tf_op jit(solution)/shard_map/ppermute | solution.py:617
  546.8 25.0 %collective-permute-start.19 = (bf16[256,2048]{1,0:T(8,128)(2,1)S(1)}, bf16[256,2048]{1,0:T(8,128)(2,1)}, u32[]{:S(2)}, u32[]{:S(2)}) collective-permute-start(bf16[256,2048]{1,0:T(8,128)(2,1)S(1)} %collective-permute-done.18), channel_id=1, source_target_pairs={{0,1},{1,2},{2,3},{3,0},{4,5},{5,6},{6,7},{7,4},{8,9},{9,10},{10,1... | collective-permute-start | bytes 3145736 | tf_op jit(solution)/shard_map/ppermute | solution.py:617
  571.7 23.8 %collective-permute-start.20 = (bf16[256,2048]{1,0:T(8,128)(2,1)}, bf16[256,2048]{1,0:T(8,128)(2,1)S(1)}, u32[]{:S(2)}, u32[]{:S(2)}) collective-permute-start(bf16[256,2048]{1,0:T(8,128)(2,1)} %collective-permute-done.19), channel_id=1, source_target_pairs={{0,1},{1,2},{2,3},{3,0},{4,5},{5,6},{6,7},{7,4},{8,9},{9,10},{10,1... | collective-permute-start | bytes 3145736 | tf_op jit(solution)/shard_map/ppermute | solution.py:617
  685.7 278.2 %reduce-scatter.9.cloned.1.call-start = ((), (), s32[]{:S(2)}) async-start(), calls=%async_computation.12 | async-start | bytes 11206656 | tf_op jit(solution)/shard_map/reduce_scatter | solution.py:736
  685.8 23.4 %collective-permute-start.23 = (bf16[256,2048]{1,0:T(8,128)(2,1)}, bf16[256,2048]{1,0:T(8,128)(2,1)S(1)}, u32[]{:S(2)}, u32[]{:S(2)}) collective-permute-start(bf16[256,2048]{1,0:T(8,128)(2,1)} %convolution_convert_fusion.6), channel_id=1, source_target_pairs={{0,1},{1,2},{2,3},{3,0},{4,5},{5,6},{6,7},{7,4},{8,9},{9,10},{10,1... | collective-permute-start | bytes 3145736 | tf_op jit(solution)/shard_map/ppermute | solution.py:617
  724.4 300.2 %reduce-scatter.11.cloned.1.call-start = ((), (), s32[]{:S(2)}) async-start(), calls=%async_computation.13 | async-start | bytes 9437184 | tf_op jit(solution)/shard_map/reduce_scatter | solution.py:736
  764.3 24.7 %collective-permute-start.26 = (bf16[256,2048]{1,0:T(8,128)(2,1)}, bf16[256,2048]{1,0:T(8,128)(2,1)}, u32[]{:S(2)}, u32[]{:S(2)}) collective-permute-start(bf16[256,2048]{1,0:T(8,128)(2,1)} %get-tuple-element.249), channel_id=1, source_target_pairs={{0,1},{1,2},{2,3},{3,0},{4,5},{5,6},{6,7},{7,4},{8,9},{9,10},{10,1... | collective-permute-start | bytes 3145736 | tf_op jit(solution)/shard_map/ppermute | solution.py:617
  788.9 24.5 %collective-permute-start.28 = (bf16[256,2048]{1,0:T(8,128)(2,1)}, bf16[256,2048]{1,0:T(8,128)(2,1)}, u32[]{:S(2)}, u32[]{:S(2)}) collective-permute-start(bf16[256,2048]{1,0:T(8,128)(2,1)} %collective-permute-done.26), channel_id=1, source_target_pairs={{0,1},{1,2},{2,3},{3,0},{4,5},{5,6},{6,7},{7,4},{8,9},{9,10},{10,1... | collective-permute-start | bytes 3145736 | tf_op jit(solution)/shard_map/ppermute | solution.py:617
  812.4 28.2 %collective-permute-start.27 = (bf16[256,2048]{1,0:T(8,128)(2,1)}, bf16[256,2048]{1,0:T(8,128)(2,1)}, u32[]{:S(2)}, u32[]{:S(2)}) collective-permute-start(bf16[256,2048]{1,0:T(8,128)(2,1)} %fusion.118), channel_id=1, source_target_pairs={{0,1},{1,2},{2,3},{3,0},{4,5},{5,6},{6,7},{7,4},{8,9},{9,10},{10,1... | collective-permute-start | bytes 3145736 | tf_op jit(solution)/shard_map/ppermute | solution.py:617
  813.5 39.7 %collective-permute-start.30 = (bf16[256,2048]{1,0:T(8,128)(2,1)}, bf16[256,2048]{1,0:T(8,128)(2,1)}, u32[]{:S(2)}, u32[]{:S(2)}) collective-permute-start(bf16[256,2048]{1,0:T(8,128)(2,1)} %collective-permute-done.28), channel_id=1, source_target_pairs={{0,1},{1,2},{2,3},{3,0},{4,5},{5,6},{6,7},{7,4},{8,9},{9,10},{10,1... | collective-permute-start | bytes 3145736 | tf_op jit(solution)/shard_map/ppermute | solution.py:617
  867.7 544.8 %reduce-scatter.17.cloned.1.call-start = ((), (), s32[]{:S(2)}) async-start(), calls=%async_computation.16 | async-start | bytes 19464192 | tf_op jit(solution)/shard_map/reduce_scatter | solution.py:736
  909.6 509.4 %reduce-scatter.15.cloned.1.call-start = ((), (), s32[]{:S(2)}) async-start(), calls=%async_computation.15 | async-start | bytes 4718592 | tf_op jit(solution)/shard_map/reduce_scatter | solution.py:736
  909.6 26.5 %collective-permute-start.29 = (bf16[256,2048]{1,0:T(8,128)(2,1)}, bf16[256,2048]{1,0:T(8,128)(2,1)S(1)}, u32[]{:S(2)}, u32[]{:S(2)}) collective-permute-start(bf16[256,2048]{1,0:T(8,128)(2,1)} %convert_add_fusion.7), channel_id=1, source_target_pairs={{0,1},{1,2},{2,3},{3,0},{4,5},{5,6},{6,7},{7,4},{8,9},{9,10},{10,1... | collective-permute-start | bytes 3145736 | tf_op jit(solution)/shard_map/ppermute | solution.py:617
  936.5 25.9 %collective-permute-start.31 = (bf16[256,2048]{1,0:T(8,128)(2,1)S(1)}, bf16[256,2048]{1,0:T(8,128)(2,1)S(1)}, u32[]{:S(2)}, u32[]{:S(2)}) collective-permute-start(bf16[256,2048]{1,0:T(8,128)(2,1)S(1)} %add_convert_fusion.3), channel_id=1, source_target_pairs={{0,1},{1,2},{2,3},{3,0},{4,5},{5,6},{6,7},{7,4},{8,9},{9,10},{10,1... | collective-permute-start | bytes 3145736 | tf_op jit(solution)/shard_map/ppermute | solution.py:617
  963.9 27.1 %collective-permute-start.32 = (bf16[256,2048]{1,0:T(8,128)(2,1)S(1)}, bf16[256,2048]{1,0:T(8,128)(2,1)S(1)}, u32[]{:S(2)}, u32[]{:S(2)}) collective-permute-start(bf16[256,2048]{1,0:T(8,128)(2,1)S(1)} %add_convert_fusion.2), channel_id=1, source_target_pairs={{0,1},{1,2},{2,3},{3,0},{4,5},{5,6},{6,7},{7,4},{8,9},{9,10},{10,1... | collective-permute-start | bytes 3145736 | tf_op jit(solution)/shard_map/ppermute | solution.py:617
  991.0 26.3 %collective-permute-start.33 = (bf16[256,2048]{1,0:T(8,128)(2,1)S(1)}, bf16[256,2048]{1,0:T(8,128)(2,1)}, u32[]{:S(2)}, u32[]{:S(2)}) collective-permute-start(bf16[256,2048]{1,0:T(8,128)(2,1)S(1)} %collective-permute-done.32), channel_id=1, source_target_pairs={{0,1},{1,2},{2,3},{3,0},{4,5},{5,6},{6,7},{7,4},{8,9},{9,10},{10,1... | collective-permute-start | bytes 3145736 | tf_op jit(solution)/shard_map/ppermute | solution.py:617
  1047.1 379.1 %reduce-scatter.13.cloned.1.call-start = ((), (), s32[]{:S(2)}) async-start(), calls=%async_computation.14 | async-start | bytes 31850496 | tf_op jit(solution)/shard_map/reduce_scatter | solution.py:736
  1145.9 27.9 %collective-permute-start.21 = (bf16[256,2048]{1,0:T(8,128)(2,1)S(1)}, bf16[256,2048]{1,0:T(8,128)(2,1)S(1)}, u32[]{:S(2)}, u32[]{:S(2)}) collective-permute-start(bf16[256,2048]{1,0:T(8,128)(2,1)S(1)} %convolution_convert_fusion.7), channel_id=1, source_target_pairs={{0,1},{1,2},{2,3},{3,0},{4,5},{5,6},{6,7},{7,4},{8,9},{9,10},{10,1... | collective-permute-start | bytes 3145736 | tf_op jit(solution)/shard_map/ppermute | solution.py:617
  1173.8 55.1 %collective-permute-start.35 = (bf16[256,4096]{1,0:T(8,128)(2,1)}, bf16[256,4096]{1,0:T(8,128)(2,1)}, u32[]{:S(2)}, u32[]{:S(2)}) collective-permute-start(bf16[256,4096]{1,0:T(8,128)(2,1)} %convolution_convert_fusion.4), channel_id=1, source_target_pairs={{0,1},{1,2},{2,3},{3,0},{4,5},{5,6},{6,7},{7,4},{8,9},{9,10},{10,1... | collective-permute-start | bytes 6291464 | tf_op jit(solution)/shard_map/ppermute | solution.py:617
  1175.2 51.9 %collective-permute-start.22 = (bf16[256,2048]{1,0:T(8,128)(2,1)}, bf16[256,2048]{1,0:T(8,128)(2,1)}, u32[]{:S(2)}, u32[]{:S(2)}) collective-permute-start(bf16[256,2048]{1,0:T(8,128)(2,1)} %add_convert_fusion.6), channel_id=1, source_target_pairs={{0,1},{1,2},{2,3},{3,0},{4,5},{5,6},{6,7},{7,4},{8,9},{9,10},{10,1... | collective-permute-start | bytes 3145736 | tf_op jit(solution)/shard_map/ppermute | solution.py:617
  1245.2 36.6 %collective-permute-start.36 = (bf16[256,4096]{1,0:T(8,128)(2,1)}, bf16[256,4096]{1,0:T(8,128)(2,1)}, u32[]{:S(2)}, u32[]{:S(2)}) collective-permute-start(bf16[256,4096]{1,0:T(8,128)(2,1)} %add_convert_fusion.1), channel_id=1, source_target_pairs={{0,1},{1,2},{2,3},{3,0},{4,5},{5,6},{6,7},{7,4},{8,9},{9,10},{10,1... | collective-permute-start | bytes 6291464 | tf_op jit(solution)/shard_map/ppermute | solution.py:617
  1250.6 31.0 %collective-permute-start.46 = (bf16[4,16,7168]{2,1,0:T(8,128)(2,1)S(1)}, bf16[4,16,7168]{2,1,0:T(8,128)(2,1)S(1)}, u32[]{:S(2)}, u32[]{:S(2)}) collective-permute-start(bf16[4,16,7168]{2,1,0:T(8,128)(2,1)S(1)} %bitcast.201), channel_id=1, source_target_pairs={{0,16},{4,20},{8,24},{12,28},{16,0},{20,4},{24,8},{28,12},{1,17},{... | collective-permute-start | bytes 2752520 | tf_op jit(solution)/shard_map/ppermute | solution.py:688
  1328.2 53.0 %collective-permute-start.38 = (bf16[256,4096]{1,0:T(8,128)(2,1)}, bf16[256,4096]{1,0:T(8,128)(2,1)}, u32[]{:S(2)}, u32[]{:S(2)}) collective-permute-start(bf16[256,4096]{1,0:T(8,128)(2,1)} %add_convert_fusion), channel_id=1, source_target_pairs={{0,1},{1,2},{2,3},{3,0},{4,5},{5,6},{6,7},{7,4},{8,9},{9,10},{10,1... | collective-permute-start | bytes 6291464 | tf_op jit(solution)/shard_map/ppermute | solution.py:617
  1332.5 41.9 %collective-permute-start.52 = (f32[576]{0:T(1024)S(1)}, f32[576]{0:T(1024)S(1)}, u32[]{:S(2)}, u32[]{:S(2)}) collective-permute-start(f32[576]{0:T(1024)S(1)} %slice_reduce_fusion.2), channel_id=1, source_target_pairs={{0,1},{1,0},{2,3},{3,2},{4,5},{5,4},{6,7},{7,6},{8,9},{9,8},{10,11... | collective-permute-start | bytes 6920 | tf_op jit(solution)/shard_map/ppermute | solution.py:712
  1425.5 28.6 %collective-permute-start.55 = (f32[256,384]{1,0:T(8,128)}, f32[256,384]{1,0:T(8,128)}, u32[]{:S(2)}, u32[]{:S(2)}) collective-permute-start(f32[256,384]{1,0:T(8,128)} %fusion.297), channel_id=1, source_target_pairs={{0,2},{1,3},{2,0},{3,1},{4,6},{5,7},{6,4},{7,5},{8,10},{9,11},{10,... | collective-permute-start | bytes 1179656 | tf_op jit(solution)/shard_map/ppermute | solution.py:712
  1429.0 33.4 %collective-permute-start.44 = (f32[2,128,384]{1,2,0:T(8,128)}, f32[2,128,384]{1,2,0:T(8,128)}, u32[]{:S(2)}, u32[]{:S(2)}) collective-permute-start(f32[2,128,384]{1,2,0:T(8,128)} %copy.173), channel_id=1, source_target_pairs={{0,2},{1,3},{2,0},{3,1},{4,6},{5,7},{6,4},{7,5},{8,10},{9,11},{10,... | collective-permute-start | bytes 1179656 | tf_op jit(solution)/shard_map/ppermute | solution.py:688
  (166 other events, 2850.4 us)
Sparse Core Ops, SparseCore 0:
  15.3 161.8 all-gather.7
  179.0 37.4 all-gather.9
  219.0 92.0 all-gather.11
  312.9 74.5 all-gather.13
  389.2 61.0 all-gather.15
  685.8 50.0 reduce-scatter.6
  739.9 78.8 reduce-scatter.8
  867.9 69.9 reduce-scatter.10
  941.5 118.5 reduce-scatter.16
  1064.3 51.2 reduce-scatter.14
  1140.2 195.7 reduce-scatter.12

commit v3 on v2

--- a/solution.py
+++ b/solution.py
@@ -5,6 +5,7 @@
 import jax.numpy as jnp
 from jax import lax
 from jax.experimental import pallas as pl
+from jax.experimental.layout import Layout, with_layout_constraint
 from jax.experimental.pallas import tpu as pltpu
 from jax.sharding import PartitionSpec as P
 
@@ -54,6 +55,7 @@
 
 def attention_forward_kernel(
     tp,
+    parts,
     place_ref,
     lengths_ref,
     cosine_ref,
@@ -63,8 +65,8 @@
     v_up,
     *refs,
 ):
-    pieces = refs[: 4 * tp]
-    attended_ref, q_ref, k_ref, v_ref, held = refs[4 * tp :]
+    pieces = refs[: 4 * parts]
+    attended_ref, q_ref, k_ref, v_ref, held = refs[4 * parts :]
     rows = q_ref.shape[0]
     share = rows // tp
     rank = q_up.shape[0]
@@ -74,10 +76,15 @@
         owner = lax.rem(here - p + tp, tp)
         part = pl.ds(pl.multiple_of(owner * share, share), share)
         cosine, sine = cosine_ref[part, :], sine_ref[part, :]
-        middle = pieces[4 * p + 3]
+        at = p * share
+        source = 0
+        while at >= pieces[4 * source].shape[0]:
+            at -= pieces[4 * source].shape[0]
+            source += 1
+        mine = slice(at, at + share)
         for j, (up, target) in enumerate(((q_up, q_ref), (k_up, k_ref), (v_up, v_ref))):
-            low = middle[:, j * rank : (j + 1) * rank].astype(bf16)
-            value = pieces[4 * p + j][...] + mm(low, up[...])
+            low = pieces[4 * source + 3][mine, j * rank : (j + 1) * rank].astype(bf16)
+            value = pieces[4 * source + j][mine, :] + mm(low, up[...])
             if j < 2:
                 value = value * cosine + pltpu.roll(value, HDA // 2, 1) * sine
             target[part, :] = value.astype(bf16)
@@ -99,10 +106,8 @@
         attended_ref[p * share : (p + 1) * share, :] = held[part, :]
 
 
-def attention_forward(place, lengths, projected, ups, columns, cosine, sine):
-    tp = len(projected)
-    share = projected[0].shape[0]
-    rows = share * tp
+def attention_forward(place, lengths, tp, projected, ups, columns, cosine, sine):
+    rows = sum(v.shape[0] for v in projected)
     heads = columns // HDA
     rank = ups.shape[0]
     table_spec = pl.BlockSpec((rows, HDA), lambda h, *_: (0, 0))
@@ -112,18 +117,20 @@
 
     work = heads * rows * rows * HDA
     return pl.pallas_call(
-        functools.partial(attention_forward_kernel, tp),
+        functools.partial(attention_forward_kernel, tp, len(projected)),
         out_shape=[jax.ShapeDtypeStruct((rows, columns), bf16)] * 4,
         grid_spec=pltpu.PrefetchScalarGridSpec(
             num_scalar_prefetch=2,
             grid=(heads,),
             in_specs=[table_spec, table_spec]
             + [head_spec(j, rank) for j in range(3)]
-            + (
-                [head_spec(j, share) for j in range(3)]
-                + [pl.BlockSpec((share, 3 * rank), lambda h, *_: (0, columns // rank))]
-            )
-            * tp,
+            + [
+                pl.BlockSpec((v.shape[0], 3 * rank), lambda h, *_: (0, columns // rank))
+                if j == 3
+                else head_spec(j, v.shape[0])
+                for v in projected
+                for j in range(4)
+            ],
             out_specs=[head_spec(0)] * 4,
             scratch_shapes=[pltpu.VMEM((rows, HDA), bf16)],
         ),
@@ -604,6 +611,64 @@
     )(place, lengths, zx, zx, sd, sd, grad_scaled, stats, states, wide, narrow, rates)
 
 
+def norm_back_kernel(parts, with_base, with_low, *refs):
+    values, refs = refs[:parts], refs[parts:]
+    grad, gain, refs = refs[0], refs[1], refs[2:]
+    base, refs = (refs[0], refs[1:]) if with_base else (None, refs)
+    outs, refs = refs[:parts], refs[parts:]
+    low, refs = (refs[0], refs[1:]) if with_low else (None, refs)
+    grad_gain = refs[0]
+
+    @pl.when(pl.program_id(0) == 0)
+    def _():
+        grad_gain[...] = jnp.zeros_like(grad_gain)
+
+    width = grad.shape[1]
+    each = width // parts
+    wide = [v[...].astype(f32) for v in values]
+    squares = sum(jnp.sum(v * v, axis=1, keepdims=True) for v in wide)
+    inv_root = lax.rsqrt(squares / width + norm_eps)
+    units = [v * inv_root for v in wide]
+    grads = [grad[:, i * each : (i + 1) * each] for i in range(parts)]
+    grad_units = [g * gain[:, i * each : (i + 1) * each] for i, g in enumerate(grads)]
+    cross = sum(jnp.sum(g * u, axis=1, keepdims=True) for g, u in zip(grad_units, units)) / width
+    for i in range(parts):
+        cols = slice(i * each, (i + 1) * each)
+        grad_gain[0:1, cols] += jnp.sum(grads[i] * units[i], axis=0, keepdims=True)
+        result = inv_root * (grad_units[i] - units[i] * cross)
+        if with_base and i == 0:
+            result = result + base[...].astype(f32)
+        outs[i][...] = result
+        if with_low and i == 0:
+            low[...] = result.astype(bf16)
+
+
+def norm_back(values, grad, gain, base=None, with_low=False):
+    rows, width = grad.shape
+    parts = len(values)
+    block = math.gcd(rows, 64)
+    row_spec = pl.BlockSpec((block, width // parts), lambda i: (i, 0))
+    full_spec = pl.BlockSpec((block, width), lambda i: (i, 0))
+    operands = list(values) + [grad, gain] + ([base] if base is not None else [])
+    shapes = [jax.ShapeDtypeStruct((rows, width // parts), f32)] * parts
+    shapes += [jax.ShapeDtypeStruct((rows, width // parts), bf16)] if with_low else []
+    results = pl.pallas_call(
+        functools.partial(norm_back_kernel, parts, base is not None, with_low),
+        out_shape=shapes + [jax.ShapeDtypeStruct((8, width), f32)],
+        grid=(rows // block,),
+        in_specs=[row_spec] * parts
+        + [full_spec, pl.BlockSpec((1, width), lambda i: (0, 0))]
+        + ([row_spec] if base is not None else []),
+        out_specs=[row_spec] * (parts + int(with_low)) + [pl.BlockSpec((8, width), lambda i: (0, 0))],
+        compiler_params=pltpu.CompilerParams(vmem_limit_bytes=VMEM_LIMIT),
+        cost_estimate=pl.CostEstimate(
+            flops=20 * rows * width, bytes_accessed=14 * rows * width, transcendentals=rows
+        ),
+        name="norm_back",
+    )(*operands)
+    return list(results[:-1]) + [results[-1][0]]
+
+
 def tie(value, others):
     return lax.optimization_barrier((value, others))[0]
 
@@ -617,21 +682,89 @@
     return lax.ppermute(values, "tp", ring_pairs())
 
 
-def ring_gather(own, use=None):
+class Halving:
+    def __init__(self, values, name, sent_as=f32):
+        self.values, self.name, self.sent_as = values, name, sent_as
+        self.half = lax.axis_size(name) // 2
+
+    def live(self):
+        return self.half > 0
+
+    def start(self):
+        count, half = lax.axis_size(self.name), self.half
+        upper = (lax.axis_index(self.name) & half) != 0
+        low, high = self.values[:half], self.values[half:]
+        self.kept = jnp.where(upper, high, low)
+        sent = jnp.where(upper, low, high).astype(self.sent_as)
+        self.moved = lax.ppermute(sent, self.name, [(i, i ^ half) for i in range(count)])
+
+    def finish(self):
+        self.values = self.kept + self.moved.astype(f32)
+        self.half //= 2
+
+    def result(self):
+        while self.live():
+            self.start()
+            self.finish()
+        return self.values[0]
+
+
+class Doubling:
+    def __init__(self, values, name, sent_as=f32):
+        self.values, self.name, self.sent_as = values, name, sent_as
+        self.step = 1
+
+    def live(self):
+        return self.step < lax.axis_size(self.name)
+
+    def start(self):
+        count, step = lax.axis_size(self.name), self.step
+        self.moved = lax.ppermute(
+            self.values.astype(self.sent_as), self.name, [(i, i ^ step) for i in range(count)]
+        )
+
+    def finish(self):
+        self.values = self.values + self.moved.astype(f32)
+        self.step *= 2
+
+    def result(self):
+        while self.live():
+            self.start()
+            self.finish()
+        return self.values
+
+
+def begin(tasks):
+    live = [t for t in tasks if t.live()]
+    for t in live:
+        t.start()
+    return live
+
+
+def settle(moved, extras, live):
+    moved, extras, arrived = lax.optimization_barrier((moved, extras, [t.moved for t in live]))
+    for t, value in zip(live, arrived):
+        t.moved = value
+        t.finish()
+    return moved, extras
+
+
+def ring_gather(own, use, tasks=()):
     tp = lax.axis_size("tp")
     pieces, results = [own], []
     for p in range(tp):
-        moved = hop(pieces[p]) if p < tp - 1 else None
-        if use is not None:
-            results.append(use(p, pieces[p]))
-            if moved is not None:
-                moved = tie(moved, results[-1])
-        if moved is not None:
+        if p < tp - 1:
+            moved = hop(pieces[p])
+            live = begin(tasks)
+        result = use(p, pieces[p])
+        if p < tp - 1:
+            moved, result = settle(moved, result, live)
             pieces.append(moved)
+        results.append(result)
     return pieces, results
 
 
-def ring_scatter(part, fill=()):
+def ring_scatter(part, fill=(), tasks=()):
     tp = lax.axis_size("tp")
     fill = list(fill)
     filled = []
@@ -639,56 +772,48 @@
     for p in range(2, tp + 1):
         low = total.astype(bf16)
         moved = hop(low)
+        live = begin(tasks)
         term = part(p % tp)
-        if fill:
-            filled.append(fill.pop(0)(low))
-            moved = tie(moved, filled[-1])
+        extra = [fill.pop(0)(low, tasks)] if fill else []
+        moved, (term, extra) = settle(moved, (term, extra), live)
+        filled += extra
         total = moved.astype(f32) + term
     for thunk in fill:
-        filled.append(thunk(low))
+        filled.append(thunk(low, tasks))
     return total, filled
 
 
-def ring_both(own, work, last=None, fill=()):
+def ring_both(own, work, last=None, fill=None, tasks=()):
     tp = lax.axis_size("tp")
-    fill = list(fill)
-    filled = []
-    pieces = [own]
+    pieces, filled = [own], []
     moved = hop(own)
+    live = begin(tasks)
     first = work(0, own)
-    moved = tie(moved, first)
+    moved, first = settle(moved, first, live)
     total, ahead = None, None
     for p in range(1, tp):
         pieces.append(moved)
         if p < tp - 1:
             moved = hop(pieces[p])
         elif last is not None:
-            filled.append(last(pieces))
-            pieces[p] = tie(pieces[p], filled[-1])
+            pieces[p], result = lax.optimization_barrier((pieces[p], last(pieces)))
+            filled.append(result)
+        live = begin(tasks)
         term = work(p, pieces[p])
-        total = term if total is None else ahead.astype(f32) + term
-        ahead = hop(total.astype(bf16))
+        if total is not None:
+            ahead, term = lax.optimization_barrier((ahead, term))
+            term = ahead.astype(f32) + term
+        total = term
+        low = total.astype(bf16)
+        ahead = hop(low)
         if p < tp - 1:
-            moved = tie(moved, total)
-    if fill:
-        filled.extend(thunk() for thunk in fill)
-        ahead = tie(ahead, filled[-1])
+            moved, low = settle(moved, low, live)
+        elif fill is not None:
+            ahead, result = settle(ahead, fill(low), live)
+            filled.append(result)
+        else:
+            ahead, _ = settle(ahead, (), live)
     return pieces, ahead.astype(f32) + first, filled
-
-
-def halving(values, name, sent_as=f32):
-    count = lax.axis_size(name)
-    here = lax.axis_index(name)
-    half = count // 2
-    while half:
-        upper = (here & half) != 0
-        low, high = values[:half], values[half:]
-        sent = jnp.where(upper, low, high)
-        kept = jnp.where(upper, high, low)
-        moved = lax.ppermute(sent.astype(sent_as), name, [(i, i ^ half) for i in range(count)])
-        values = kept + moved.astype(f32)
-        half //= 2
-    return values[0]
 
 
 def doubling_gather(values, name):
@@ -705,27 +830,8 @@
     return values
 
 
-def doubling(values, name):
-    count = lax.axis_size(name)
-    step = 1
-    while step < count:
-        values = values + lax.ppermute(values, name, [(i, i ^ step) for i in range(count)])
-        step *= 2
-    return values
-
-
 def inverse_root(values):
     return lax.rsqrt(jnp.mean(values * values, axis=1, keepdims=True) + norm_eps)
-
-
-def rms_backward(values, inv_root, gain, grad_out):
-    unit_rows = values * inv_root
-    grad_gain = jnp.sum(grad_out * unit_rows, axis=0)
-    grad_unit = grad_out * gain
-    grad_values = inv_root * (
-        grad_unit - unit_rows * jnp.mean(grad_unit * unit_rows, axis=-1, keepdims=True)
-    )
-    return (grad_values, grad_gain)
 
 
 def gather(values, axis=0):
@@ -782,8 +888,6 @@
     def piece(values, p):
         return values[p * share : (p + 1) * share]
 
-    joined_low = jnp.concatenate([hidden, embed], axis=1)
-    query_key_value_weight = tie(query_key_value_weight, joined_low)
     weight_qkv = gather(
         jnp.concatenate(
             [query_key_value_weight[:, j, :] for j in range(3)]
@@ -806,8 +910,7 @@
             [gate_up_weight[:, j, :] for j in range(2)] + [feedforward_adapter_down], axis=1
         )
     )
-    weight_down = gather(jnp.concatenate([down_weight, mixer_output_weight], axis=0), 1)
-    weight_fc2, weight_out = weight_down[:units_here], weight_down[units_here:]
+    weight_fc2 = gather(down_weight, 1)
     weight_zx = gather(
         jnp.concatenate(
             [gate_inner_weight[:, j, :] for j in range(2)]
@@ -816,6 +919,8 @@
             axis=1,
         )
     )
+
+    weight_out = gather(mixer_output_weight, 1)
 
     small = [
         attention_norm_gain,
@@ -855,38 +960,43 @@
     cosine = jnp.concatenate([cosine, cosine], axis=1)
     sine = jnp.concatenate([-sine, sine], axis=1)
 
-    joined = joined_low.astype(f32)
-    attn_root = inverse_root(joined)
-
-    def norm_rows(values):
-        values = values.astype(f32)
-        return (values * inverse_root(values) * gain_attn).astype(bf16)
-
-    raw, normed = [joined_low], []
+    def norm_rows(pair):
+        pair = [v.astype(f32) for v in pair]
+        squares = sum(jnp.sum(v * v, axis=1, keepdims=True) for v in pair)
+        inv_root = lax.rsqrt(squares / (2 * width) + norm_eps)
+        return [
+            (v * inv_root * gain_attn[:, i * width : (i + 1) * width]).astype(bf16)
+            for i, v in enumerate(pair)
+        ]
+
+    raw, normed = [(hidden, embed)], []
     for p in range(1, tp):
-        moved = hop(raw[-1])
+        moved = tuple(hop(v) for v in raw[-1])
         if p > 1:
             normed.append(norm_rows(raw[p - 2]))
             moved = tie(moved, normed[-1])
         raw.append(moved)
     normed += [norm_rows(v) for v in raw[len(normed) :]]
 
-    out_grad = [tie(output_cotangent, raw[-1])]
-    projected = []
+    out_grad = [tie(output_cotangent, raw[-1][0])]
+    normed_parts, projected = [], []
     for i in range(tp - 1):
         moved = hop(out_grad[-1])
         if i < tp - 2:
             low, high = (tp * i) // (tp - 2), (tp * (i + 1)) // (tp - 2)
-            projected += [mm(normed[p], weight_qkv) for p in range(low, high)]
+            normed_parts.append(jnp.concatenate([jnp.concatenate(v, axis=1) for v in normed[low:high]], axis=0))
+            projected.append(mm(normed_parts[-1], weight_qkv))
             moved = tie(moved, projected)
         else:
             attended, queries, keys, values = attention_forward(
-                place, lengths, projected, ups, head_cols, cosine, sine
+                place, lengths, tp, projected, ups, head_cols, cosine, sine
             )
             moved = tie(moved, attended)
         out_grad.append(moved)
-    attended = tie(attended, moved)
+    lora_rows = jnp.concatenate([v[:, 3 * head_cols :].astype(bf16) for v in projected], axis=0)
+    attended, lora_rows, out_grad[-1] = lax.optimization_barrier((attended, lora_rows, moved))
     out_grad_rows = jnp.concatenate(out_grad, axis=0)
+    normed_rows = jnp.concatenate(normed_parts, axis=0)
     mixed, _ = ring_scatter(lambda p: mm(piece(attended, p), weight_o))
 
     mlp_root = inverse_root(mixed)
@@ -907,17 +1017,20 @@
     residual = hidden.astype(f32) + mixed + branch
 
     mixer_root = inverse_root(residual)
-    scaled_grads = []
+    kept = []
 
     def mix(p, rows_in):
         result = mm(rows_in, weight_zx)
         if p == 0:
-            scaled_grads.append(mm_nt(tie(out_grad_rows, result), weight_out).astype(bf16))
-            result = tie(result, scaled_grads[0])
-        return result
+            kept.append(mm_nt(tie(out_grad_rows, result), weight_out).astype(bf16))
+        elif p == 1:
+            kept.append(jnp.concatenate(tie(units, result), axis=0))
+            kept.append(jnp.concatenate(tie(mlp_in, result), axis=0))
+        return (result, kept[-1])
 
     mixer_in, zxs = ring_gather((residual * mixer_root * gain_mixer).astype(bf16), mix)
-    grad_scaled = scaled_grads[0]
+    zxs = [v[0] for v in zxs]
+    grad_scaled, units_rows, mlp_rows = kept
     mixer_rows = jnp.concatenate(mixer_in, axis=0)
     zx = jnp.concatenate([v[:, : 2 * inner_cols].astype(bf16) for v in zxs], axis=0)
     sd = jnp.concatenate([v[:, 2 * inner_cols :] for v in zxs], axis=0)
@@ -936,24 +1049,47 @@
     gate_root = lax.rsqrt(sums[0] / inner_total + norm_eps)
     stats = jnp.stack([gate_root, gate_root**3 * sums[1] / inner_total], axis=1)
     scaled = (gated_wide * gate_root[:, None] * gain_gate).astype(bf16)
-    out_terms = [mm(piece(scaled, p), weight_out) for p in range(tp)]
-    out = hop(out_terms[1 % tp].astype(bf16))
+    out_rows, stats = lax.optimization_barrier((mm(scaled, weight_out).astype(bf16), stats))
+    out_terms = [piece(out_rows, p) for p in range(tp)]
+    out = hop(out_terms[1 % tp])
 
     grad_all, grad_wide, grad_narrow, grad_rates = mixer_backward(
         place, lengths, tp, zx, sd, grad_scaled, stats, chunk_states, wide, narrow, rates
     )
-    out = tie(out, grad_all).astype(f32) + out_terms[2 % tp]
-    grad_mixer_in, (sum_w_out, sum_w_zx) = ring_scatter(
+    out, grad_all = lax.optimization_barrier((out, grad_all))
+    out = out.astype(f32) + out_terms[2 % tp].astype(f32)
+
+    def by_fsdp(values):
+        lead = values.shape[:-1]
+        cut = values.reshape(lead + (fsdp, values.shape[-1] // fsdp))
+        return jnp.moveaxis(cut, -2, 0).reshape(fsdp, -1)
+
+    def small_gradients(token):
+        taps, bars, sums_r = tie((grad_wide, grad_narrow, grad_rates), token)
+        return [
+            by_fsdp(taps[:count].reshape(count, mixer_heads, HD)),
+            by_fsdp(taps[4].reshape(mixer_heads, HD)),
+            by_fsdp(taps[5].reshape(mixer_heads, HD)),
+            jnp.broadcast_to(sums_r[:2, :mixer_heads].reshape(1, -1), (fsdp, 2 * mixer_heads)),
+            by_fsdp(bars[:count].reshape(count, 2, LANES)[:, :, :states]),
+        ]
+
+    grad_mixer_in, (sum_w_out, sum_w_zx, small) = ring_scatter(
         lambda p: mm_nt(piece(grad_all, p), weight_zx),
         [
-            lambda t: mm_tn(tie(scaled, t), out_grad_rows).astype(bf16),
-            lambda t: mm_tn(tie(mixer_rows, t), grad_all).astype(bf16),
+            lambda t, _: mm_tn(tie(scaled, t), out_grad_rows).astype(bf16),
+            lambda t, _: mm_tn(tie(mixer_rows, t), grad_all).astype(bf16),
+            lambda t, _: small_gradients(t),
         ],
     )
     sum_w_out = scatter(sum_w_out, 1)
     sum_w_zx = scatter(sum_w_zx)
-    grad_resid_norm, grad_gain_mixer = rms_backward(residual, mixer_root, gain_mixer, grad_mixer_in)
-    grad_residual = output_cotangent.astype(f32) + grad_resid_norm
+    small_sizes = [v.shape[1] for v in small]
+    small_cuts = [sum(small_sizes[:i]) for i in range(len(small_sizes) + 1)]
+    small_task = Halving(jnp.concatenate(small, axis=1), "fsdp")
+    grad_residual, grad_residual_low, grad_gain_mixer = norm_back(
+        [residual], grad_mixer_in, gain_mixer, output_cotangent, True
+    )
 
     grad_gate_up = []
 
@@ -969,23 +1105,33 @@
         grad_gate_up.append(both)
         return mm_nt(both, weight_fc1)
 
-    units_rows = jnp.concatenate(units, axis=0)
-    mlp_rows = jnp.concatenate(mlp_in, axis=0)
     grad_branch, grad_mlp_in, (sum_w_fc2, sum_w_fc1) = ring_both(
-        grad_residual.astype(bf16),
+        grad_residual_low,
         feed_back,
         lambda pieces: mm_tn(tie(units_rows, sum_w_out), jnp.concatenate(pieces, axis=0)).astype(bf16),
-        [lambda: mm_tn(mlp_rows, jnp.concatenate(grad_gate_up, axis=0)).astype(bf16)],
+        lambda t: mm_tn(tie(mlp_rows, t), jnp.concatenate(grad_gate_up, axis=0)).astype(bf16),
+        [small_task],
     )
     sum_w_fc2 = scatter(sum_w_fc2, 1)
     sum_w_fc1 = scatter(sum_w_fc1)
     grad_gate_up_rows = jnp.concatenate(grad_gate_up, axis=0)
-    grad_mixed_norm, grad_gain_mlp = rms_backward(mixed, mlp_root, gain_mlp, grad_mlp_in)
-
-    grad_mixed, grad_attended = ring_gather(
-        tie((grad_residual + grad_mixed_norm).astype(bf16), sum_w_zx),
-        lambda p, v: mm_nt(v, weight_o).astype(bf16),
-    )
+    _, grad_mixed_low, grad_gain_mlp = norm_back([mixed], grad_mlp_in, gain_mlp, grad_residual, True)
+    gain_task = Halving(
+        jnp.concatenate([grad_gain_mixer.reshape(fsdp, -1), grad_gain_mlp.reshape(fsdp, -1)], axis=1), "fsdp"
+    )
+
+    fc_ups = []
+
+    def attended_back(p, rows_in):
+        result = mm_nt(rows_in, weight_o).astype(bf16)
+        if p == 0:
+            fc_ups.append(
+                mm_tn(tie(jnp.concatenate(fc_mid, axis=0), rows_in), grad_gate_up_rows[:, : 2 * units_here])
+            )
+            result = tie(result, fc_ups[0])
+        return result
+
+    grad_mixed, grad_attended = ring_gather(tie(grad_mixed_low, sum_w_zx), attended_back, [gain_task])
     sum_w_o = mm_tn(tie(attended, sum_w_fc2), jnp.concatenate(grad_mixed, axis=0)).astype(bf16)
     grad_attended[-1] = tie(grad_attended[-1], sum_w_o)
     sum_w_o = scatter(sum_w_o, 1)
@@ -993,93 +1139,106 @@
     grad_projected = attention_backward(
         place, lengths, queries, keys, values, ups, grad_attended, cosine, sine
     )
-    out = tie(out, grad_projected).astype(f32) + out_terms[3 % tp]
-    normed_rows = jnp.concatenate(normed, axis=0)
-    lora_rows = jnp.concatenate([v[:, 3 * head_cols :].astype(bf16) for v in projected], axis=0)
-
-    def finish(total):
+    out, grad_projected, sum_w_fc1 = lax.optimization_barrier((out, grad_projected, sum_w_fc1))
+    out = out.astype(f32) + out_terms[3 % tp].astype(f32)
+    sum_w_qkv = mm_tn(normed_rows, grad_projected).astype(bf16)
+    grad_projected = tie(grad_projected, sum_w_qkv)
+    sum_w_qkv = scatter(sum_w_qkv)
+
+    at_t = 2 * inner_cols + 2 * LANES
+
+    def finish_out(token):
+        total = tie(out, token)
         for p in range(4, tp + 1):
-            total = hop(total.astype(bf16)).astype(f32) + out_terms[p % tp]
+            total = hop(total.astype(bf16)).astype(f32) + out_terms[p % tp].astype(f32)
         return residual + total
 
-    grad_normed, (sum_w_qkv, (grad_up, grad_fc_up), (out, late)) = ring_scatter(
-        lambda p: mm_nt(piece(grad_projected, p), weight_qkv),
-        [
-            lambda t: mm_tn(tie(normed_rows, t), grad_projected).astype(bf16),
-            lambda t: (
-                [
-                    mm_tn(
-                        tie(lora_rows, t)[:, j * rank : (j + 1) * rank],
-                        grad_projected[:, j * head_cols : (j + 1) * head_cols],
-                    )
-                    for j in range(3)
-                ],
-                mm_tn(tie(jnp.concatenate(fc_mid, axis=0), t), grad_gate_up_rows[:, : 2 * units_here]),
-            ),
-            lambda t: lax.optimization_barrier(
-                (finish(tie(out, t)), tie((grad_wide, grad_narrow, grad_rates), t))
-            ),
-        ],
-    )
-    sum_w_qkv = scatter(sum_w_qkv)
-    grad_wide, grad_narrow, grad_rates = late
-    grad_joined, grad_gain_attn = rms_backward(joined, attn_root, gain_attn, grad_normed)
-    grad_hidden = grad_residual + grad_joined[:, :width]
-    grad_embed = grad_joined[:, width:]
-    grad_down = halving(sum_w_qkv[:, 3 * head_cols :].astype(f32).reshape(tp, -1, 3 * rank), "tp")
-
-    grad_ups = jnp.concatenate(grad_up + [grad_fc_up], axis=1)
-    grad_ups = halving(grad_ups.reshape(fsdp, -1, grad_ups.shape[1]), "fsdp", bf16)
-    sum_w_zx = sum_w_zx.astype(f32)
-    sum_w_fc1 = sum_w_fc1.astype(f32)
-    at_t = 2 * inner_cols + 2 * LANES
-    grad_w_dt = sum_w_zx[:, at_t : at_t + mixer_heads]
-    shared = jnp.concatenate([sum_w_zx[:, 2 * inner_cols : at_t], sum_w_fc1[:, 2 * units_here :]], axis=1)
-    shared = doubling(shared, "tp")
-
-    def by_fsdp(values):
-        lead = values.shape[:-1]
-        cut = values.reshape(lead + (fsdp, values.shape[-1] // fsdp))
-        return jnp.moveaxis(cut, -2, 0).reshape(fsdp, -1)
-
-    grad_taps_x = grad_wide[:count].reshape(count, mixer_heads, HD)
-    grad_taps_s = grad_narrow[:count].reshape(count, 2, LANES)[:, :, :states]
-    local_small = [
-        by_fsdp(grad_taps_x),
-        by_fsdp(grad_wide[4].reshape(mixer_heads, HD)),
-        by_fsdp(grad_wide[5].reshape(mixer_heads, HD)),
-        jnp.broadcast_to(grad_rates[:2, :mixer_heads].reshape(1, -1), (fsdp, 2 * mixer_heads)),
-    ]
-    shared_small = [by_fsdp(grad_taps_s), by_fsdp(grad_gain_mixer), by_fsdp(grad_gain_mlp)]
-    small_sizes = [v.shape[1] for v in local_small + shared_small]
-    small_cuts = [sum(small_sizes[:i]) for i in range(len(small_sizes) + 1)]
-    small_sum = halving(jnp.concatenate(local_small + shared_small, axis=1), "fsdp")
+    def finish_adapters(token, tasks):
+        rows_in = tie(lora_rows, token)
+        grad_up = [
+            mm_tn(
+                rows_in[:, j * rank : (j + 1) * rank],
+                grad_projected[:, j * head_cols : (j + 1) * head_cols],
+            )
+            for j in range(3)
+        ]
+        ups_grad = jnp.concatenate(grad_up + fc_ups, axis=1)
+        tasks.append(Halving(ups_grad.reshape(fsdp, -1, ups_grad.shape[1]), "fsdp", bf16))
+        shared = jnp.concatenate([small_task.result()[small_cuts[4] :], gain_task.result()])
+        tasks.append(Doubling(shared, "tp"))
+        return ups_grad, shared
+
+    def finish_mixer(token, tasks):
+        zx_sum, w_out, w_fc2 = tie((sum_w_zx, sum_w_out, sum_w_fc2), token)
+        zx_sum = zx_sum.astype(f32)
+        bc_sums.append(zx_sum[:, 2 * inner_cols : at_t])
+        return (
+            stacked(zx_sum, inner_cols, 2),
+            zx_sum[:, at_t : at_t + mixer_heads],
+            w_out.astype(f32),
+            w_fc2.astype(f32),
+        )
+
+    def finish_feed(token, tasks):
+        fc1_sum, w_o = tie((sum_w_fc1, sum_w_o), token)
+        fc1_sum = fc1_sum.astype(f32)
+        tasks.append(
+            Doubling(jnp.concatenate([bc_sums[0], fc1_sum[:, 2 * units_here :]], axis=1), "tp", bf16)
+        )
+        return (
+            stacked(fc1_sum, units_here, 2),
+            w_o.astype(f32),
+            finish_out(token),
+        )
+
+    def stacked(values, each, parts):
+        values = jnp.stack([values[:, j * each : (j + 1) * each] for j in range(parts)], axis=1)
+        return with_layout_constraint(values, Layout(major_to_minor=(0, 1, 2)))
+
+    tasks, bc_sums = [], []
+    pair = mm_nt(grad_projected[share : 3 * share], weight_qkv)
+    grad_normed, (_, mixer_sums, feed_sums) = ring_scatter(
+        lambda p: piece(pair, p - 1) if p in (1, 2) else mm_nt(piece(grad_projected, p), weight_qkv),
+        [finish_adapters, finish_mixer, finish_feed],
+        tasks,
+    )
+    grad_w_zx, grad_w_dt, grad_w_out, grad_w_fc2 = mixer_sums
+    grad_w_fc1, grad_w_o, out = feed_sums
+    grad_hidden, grad_embed, grad_gain_attn = norm_back([hidden, embed], grad_normed, gain_attn, grad_residual)
+    gain_first = Halving(grad_gain_attn.reshape(fsdp, -1), "fsdp")
+    grad_gain_attn = Halving(gain_first.result().reshape(tp, -1), "tp").result()
+    grad_down = Halving(
+        sum_w_qkv[:, 3 * head_cols :].astype(f32).reshape(tp, -1, 3 * rank), "tp", bf16
+    ).result()
+    grad_w_qkv = jnp.stack(
+        [sum_w_qkv[:, j * head_cols : (j + 1) * head_cols].astype(f32) for j in range(3)], axis=1
+    )
+    small_sum = small_task.result()
     small_parts = [small_sum[small_cuts[i] : small_cuts[i + 1]] for i in range(len(small_sizes))]
-    tail = doubling(small_sum[small_cuts[4] :], "tp")
-    tail_cuts = [v - small_cuts[4] for v in small_cuts[4:]]
+    grad_ups, tail = tasks[0].result(), tasks[1].result()
+    shared = tasks[2].result()
+    tail_sizes = [small_sizes[4], width // fsdp, width // fsdp]
+    tail_cuts = [sum(tail_sizes[:i]) for i in range(4)]
     grad_conv_bc, sum_gain_mixer, sum_gain_mlp = (
         tail[tail_cuts[i] : tail_cuts[i + 1]] for i in range(3)
     )
-    grad_gain_attn = halving(halving(grad_gain_attn.reshape(fsdp, -1), "fsdp").reshape(tp, -1), "tp")
     sum_rates = small_parts[3].reshape(2, mixer_heads)
     return (
         out,
         grad_hidden,
         grad_embed,
         grad_gain_attn,
-        jnp.stack(
-            [sum_w_qkv[:, j * head_cols : (j + 1) * head_cols].astype(f32) for j in range(3)], axis=1
-        ),
+        grad_w_qkv,
         grad_down.reshape(-1, 3, rank),
         grad_ups[:, : 3 * head_cols].reshape(-1, 3, head_cols),
-        sum_w_o.astype(f32),
+        grad_w_o,
         sum_gain_mlp,
-        sum_w_fc1[:, : 2 * units_here].reshape(-1, 2, units_here),
+        grad_w_fc1,
         shared[:, 2 * LANES :],
         grad_ups[:, 3 * head_cols :].reshape(-1, 2, units_here),
-        sum_w_fc2.astype(f32),
+        grad_w_fc2,
         sum_gain_mixer,
-        sum_w_zx[:, : 2 * inner_cols].reshape(-1, 2, inner_cols),
+        grad_w_zx,
         shared[:, : 2 * LANES].reshape(-1, 2, LANES)[:, :, :states],
         grad_w_dt,
         small_parts[0].reshape(count, mixer_heads, -1),
@@ -1088,7 +1247,7 @@
         sum_rates[1],
         small_parts[1].reshape(mixer_heads, -1),
         small_parts[2].reshape(mixer_heads, -1),
-        sum_w_out.astype(f32),
+        grad_w_out,
     )
 
 

time: 1490 us -> 1370 us (0.919)
  waiting for transfers between devices: 597 us -> 467 us
  matrix products: 485 us -> 464 us
  Pallas kernels: 121 us -> 139 us
    ppermute x17 -> x20, waiting for transfers between devices: 99.5 us -> 23.6 us  [the longest x16 19.7 us: start(): lax.ppermute(sent, self.name, [(i, i ^ half) for i in range(count)])]
    ppermute x36 -> x39, waiting for transfers between devices: 462 us -> 387 us  [hop(): return lax.ppermute(values, 'tp', ring_pairs())]
    dot_general x28 -> x23, matrix products: 172 us -> 139 us  [mm(): return jnp.dot(left, right, preferred_element_type=f32)]
    dot_general x10, matrix products: 112 us -> 139 us  [mm_tn(): lax.dot_general(left, right, (((0,), (0,)), ((), ())), preferred_element_...]
    pallas_call x1 -> x4, Pallas kernels: 26.8 us -> 46 us  [the longest x1 26.9 us: attention_forward(): pl.pallas_call(functools.partial(attention_forward_kernel, tp, len(projec...]
    ppermute x3, waiting for transfers between devices: 21 us -> 39.4 us  [doubling_gather(): moved = lax.ppermute(values, name, [(i, i ^ step) for i in range(count)])]
    dot_general x25 -> x24, matrix products: 201 us -> 187 us  [mm_nt(): lax.dot_general(left, right, (((1,), (1,)), ((), ())), preferred_element_...]
    unnamed x327 -> x290, local copies, waits for them, and re-layouts: 43.5 us -> 52.8 us
  transfers between devices with their start and end apart: 67 -> 74, of which waited for: 38 -> 39; matrix products, arithmetic and copies ran while one was open for 42% -> 44% of each run, Pallas kernels for 5% -> 9%
where the time goes in v3:
time: 1370 us; the launch traced here: 1360 us
  waiting for transfers between devices  467 us (34%)
  matrix products  464 us (34%)
  Pallas kernels  139 us (10%)
  other arithmetic  111 us (8%)
  local copies, waits for them, and re-layouts  98.7 us (7%)
  starting transfers between devices  48.9 us (4%)
  blocking collectives  17.8 us (1%)
  between operations  17 us (1%)
    ppermute x39, waiting for transfers between devices, hop(): return lax.ppermute(values, 'tp', ring_pairs())  387 us
    dot_general x24, matrix products, mm_nt(): lax.dot_general(left, right, (((1,), (1,)), ((), ())), preferred_element_...  187 us
    dot_general x10, matrix products, mm_tn(): lax.dot_general(left, right, (((0,), (0,)), ((), ())), preferred_element_...  139 us
    dot_general x23, matrix products, mm(): return jnp.dot(left, right, preferred_element_type=f32)  139 us
    unnamed x290, local copies, waits for them, and re-layouts  52.8 us
    ppermute x3, waiting for transfers between devices, doubling_gather(): moved = lax.ppermute(values, name, [(i, i ^ step) for i in range(count)])  39.4 us
    pallas_call x1, Pallas kernels, attention_backward(): pl.pallas_call(functools.partial(attention_backward_kernel, tp, heads), o...  39.2 us
    pallas_call x1, Pallas kernels, mixer_backward(): pl.pallas_call(functools.partial(mixer_backward_kernel, chunks), out_shap...  36.4 us
  transfers between devices with their start and end apart: 74, of which 39 were waited for; matrix products, arithmetic and copies ran while one was open for 44% of the time, Pallas kernels for 9%

profile of v3, /device:TPU:0, one launch (start us, length us, event | category | flops | bytes accessed | tf_op | source)
XLA Modules:
  0.0 1363.8 jit_solution(11595076922376254446)
XLA Ops:
  38.9 9.3 all-gather.1
  55.4 18.2 %collective-permute-done.1 = bf16[32,7168]{1,0:T(8,128)(2,1)S(1)} collective-permute-done((bf16[32,7168]{1,0:T(8,128)(2,1)S(1)}, bf16[32,7168]{1,0:T(8,128)(2,1)S(1)}, u32[]{:S(2)}, u32[]{:S(2)}) %collective-permute-start.1) | collective-permute-done | bytes 458784 | tf_op jit(solution)/shard_map/ppermute | solution.py:824
  83.4 21.2 %collective-permute-done.2 = bf16[64,7168]{1,0:T(8,128)(2,1)S(1)} collective-permute-done((bf16[64,7168]{1,0:T(8,128)(2,1)S(1)}, bf16[64,7168]{1,0:T(8,128)(2,1)S(1)}, u32[]{:S(2)}, u32[]{:S(2)}) %collective-permute-start.2) | collective-permute-done | bytes 917536 | tf_op jit(solution)/shard_map/ppermute | solution.py:824
  106.7 20.7 %collective-permute-done.5 = bf16[256,2048]{1,0:T(8,128)(2,1)S(1)} collective-permute-done((bf16[256,2048]{1,0:T(8,128)(2,1)}, bf16[256,2048]{1,0:T(8,128)(2,1)S(1)}, u32[]{:S(2)}, u32[]{:S(2)}) %collective-permute-start.5) | collective-permute-done | bytes 1048608 | tf_op jit(solution)/shard_map/ppermute | solution.py:682
  133.0 22.3 %collective-permute-done.7 = bf16[256,2048]{1,0:T(8,128)(2,1)S(1)} collective-permute-done((bf16[256,2048]{1,0:T(8,128)(2,1)S(1)}, bf16[256,2048]{1,0:T(8,128)(2,1)S(1)}, u32[]{:S(2)}, u32[]{:S(2)}) %collective-permute-start.7) | collective-permute-done | bytes 1048608 | tf_op jit(solution)/shard_map/ppermute | solution.py:682
  155.3 19.8 %collective-permute-done.8 = bf16[256,2048]{1,0:T(8,128)(2,1)S(1)} collective-permute-done((bf16[256,2048]{1,0:T(8,128)(2,1)S(1)}, bf16[256,2048]{1,0:T(8,128)(2,1)S(1)}, u32[]{:S(2)}, u32[]{:S(2)}) %collective-permute-start.8) | collective-permute-done | bytes 1048608 | tf_op jit(solution)/shard_map/ppermute | solution.py:682
  177.7 21.7 %fusion.70.refs_0_.refs_1_.refs_2_.refs_3_ = f32[512,3456]{1,0:T(8,128)S(1)} fusion(bf16[4096,3456]{1,0:T(8,128)(2,1)} %all-gather.9.cloned.1.call-done, bf16[256,2048]{1,0:T(8,128)(2,1)} %get-tuple-element.427, bf16[256,2048]{1,0:T(8,128)(2,1)} %get-tuple-element.437, bf16[256,2048]{1,0:T(8,128)(2,1)} %get-tuple-element.444, ...), kind=kOutput, calls=%fused_computation.82 | convolution fusion | flops 14512291840 | bytes 39583744 | tf_op jit(solution)/shard_map/dot_general | solution.py:25
  199.6 24.1 %fusion.78.refs_4_.refs_5_.refs_6_.refs_7_ = f32[512,3456]{1,0:T(8,128)S(1)} fusion(bf16[4096,3456]{1,0:T(8,128)(2,1)} %all-gather.9.cloned.1.call-done, bf16[256,2048]{1,0:T(8,128)(2,1)} %get-tuple-element.442, bf16[256,2048]{1,0:T(8,128)(2,1)} %get-tuple-element.441, bf16[256,2048]{1,0:T(8,128)(2,1)} %get-tuple-element.426, ...), kind=kOutput, calls=%fused_computation.90 | convolution fusion | flops 14512291840 | bytes 39583744 | tf_op jit(solution)/shard_map/dot_general | solution.py:25
  228.8 26.9 %attention_forward.1 = (bf16[1024,1024]{1,0:T(8,128)(2,1)}, bf16[1024,1024]{1,0:T(8,128)(2,1)}, bf16[1024,1024]{1,0:T(8,128)(2,1)}, bf16[1024,1024]{1,0:T(8,128)(2,1)}) custom-call(s32[1]{0:T(128)} %bitcast.place_ref, s32[3]{0:T(128)} %bitcast.255, f32[1024,128]{1,0:T(8,128)} %get-tuple-element.445.cosine_ref, f32[1024,128]{1,0:T(8,128)} %get-tuple-element.446.sine_ref, ...), custom_call_target="tpu_custom_call" | custom-call | flops 4294967296 | bytes 20971520 | tf_op jit(solution)/shard_map/attention_forward/pallas_call | solution.py:119
  264.2 20.3 %collective-permute-done.12 = bf16[256,2048]{1,0:T(8,128)(2,1)S(1)} collective-permute-done((bf16[256,2048]{1,0:T(8,128)(2,1)S(1)}, bf16[256,2048]{1,0:T(8,128)(2,1)S(1)}, u32[]{:S(2)}, u32[]{:S(2)}) %collective-permute-start.12) | collective-permute-done | bytes 1048608 | tf_op jit(solution)/shard_map/ppermute | solution.py:682
  289.2 18.4 %collective-permute-done.13 = bf16[256,2048]{1,0:T(8,128)(2,1)} collective-permute-done((bf16[256,2048]{1,0:T(8,128)(2,1)S(1)}, bf16[256,2048]{1,0:T(8,128)(2,1)}, u32[]{:S(2)}, u32[]{:S(2)}) %collective-permute-start.13) | collective-permute-done | bytes 1048608 | tf_op jit(solution)/shard_map/ppermute | solution.py:682
  314.7 17.4 %collective-permute-done.14 = bf16[256,2048]{1,0:T(8,128)(2,1)} collective-permute-done((bf16[256,2048]{1,0:T(8,128)(2,1)}, bf16[256,2048]{1,0:T(8,128)(2,1)}, u32[]{:S(2)}, u32[]{:S(2)}) %collective-permute-start.14) | collective-permute-done | bytes 1048608 | tf_op jit(solution)/shard_map/ppermute | solution.py:682
  335.5 10.0 fusion.300
  349.8 15.7 %all-gather.15.cloned.1.call-done = bf16[2048,2048]{1,0:T(8,128)(2,1)} async-done(((bf16[2048,256]{1,0:T(8,128)(2,1)}), bf16[2048,2048]{1,0:T(8,128)(2,1)}) %all-gather.15.cloned.1.call-update) | async-done | bytes 8388624 | tf_op jit(solution)/shard_map/all_gather | solution.py:838
  392.0 8.8 collective-permute-done.17
  424.0 21.8 %collective-permute-done.19 = bf16[256,2048]{1,0:T(8,128)(2,1)S(1)} collective-permute-done((bf16[256,2048]{1,0:T(8,128)(2,1)S(1)}, bf16[256,2048]{1,0:T(8,128)(2,1)S(1)}, u32[]{:S(2)}, u32[]{:S(2)}) %collective-permute-start.19) | collective-permute-done | bytes 1048608 | tf_op jit(solution)/shard_map/ppermute | solution.py:682
  445.8 9.3 fusion.305
  477.2 18.3 %collective-permute-done.20 = bf16[256,2048]{1,0:T(8,128)(2,1)} collective-permute-done((bf16[256,2048]{1,0:T(8,128)(2,1)}, bf16[256,2048]{1,0:T(8,128)(2,1)}, u32[]{:S(2)}, u32[]{:S(2)}) %collective-permute-start.20) | collective-permute-done | bytes 1048608 | tf_op jit(solution)/shard_map/ppermute | solution.py:682
  499.3 8.5 fusion.307
  515.9 9.0 collective-permute-done.21
  532.0 17.6 %collective-permute-done.22 = bf16[256,2048]{1,0:T(8,128)(2,1)S(1)} collective-permute-done((bf16[256,2048]{1,0:T(8,128)(2,1)}, bf16[256,2048]{1,0:T(8,128)(2,1)S(1)}, u32[]{:S(2)}, u32[]{:S(2)}) %collective-permute-start.22) | collective-permute-done | bytes 1048608 | tf_op jit(solution)/shard_map/ppermute | solution.py:682
  553.8 19.5 %collective-permute-done.23 = bf16[256,2048]{1,0:T(8,128)(2,1)S(1)} collective-permute-done((bf16[256,2048]{1,0:T(8,128)(2,1)S(1)}, bf16[256,2048]{1,0:T(8,128)(2,1)S(1)}, u32[]{:S(2)}, u32[]{:S(2)}) %collective-permute-start.23) | collective-permute-done | bytes 1048608 | tf_op jit(solution)/shard_map/ppermute | solution.py:682
  580.2 17.6 %mixer_forward.1 = (bf16[1024,1024]{1,0:T(8,128)(2,1)}, bf16[8,64,1024]{2,1,0:T(8,128)(2,1)}) custom-call(s32[1]{0:T(128)} %bitcast.place_ref, s32[3]{0:T(128)} %bitcast.256, bf16[1024,2048]{1,0:T(8,128)(2,1)} %pad_maximum_fusion.zx.before, bf16[1024,2048]{1,0:T(8,128)(2,1)} %pad_maximum_fusion.zx.before, f32[1024,384]{1,0:T(8,128)} %pad_maximum_fusion.8.sd.sd_before, ...), custom_call_target="tpu_custom_call" | custom-call | flops 1073741824 | bytes 8388608 | tf_op jit(solution)/shard_map/mixer_forward/pallas_call | solution.py:530
  600.7 8.5 psum.7
  621.7 36.4 %mixer_backward.1 = (bf16[1024,2432]{1,0:T(8,128)(2,1)}, f32[8,1024]{1,0:T(8,128)}, f32[8,256]{1,0:T(8,128)}, f32[8,128]{1,0:T(8,128)}) custom-call(s32[1]{0:T(128)} %bitcast.place_ref, s32[3]{0:T(128)} %bitcast.257, bf16[1024,2048]{1,0:T(8,128)(2,1)} %pad_maximum_fusion.zx.before, bf16[1024,2048]{1,0:T(8,128)(2,1)} %pad_maximum_fusion.zx.before, ...), custom_call_target="tpu_custom_call" | custom-call | flops 3221225472 | bytes 12582912 | tf_op jit(solution)/shard_map/mixer_backward/pallas_call | solution.py:567
  658.1 8.5 convolution_convert_fusion.7
  690.4 9.7 fusion.222
  702.7 13.7 %convolution_convert_fusion.2 = bf16[2048,2432]{1,0:T(8,128)(2,1)} fusion(bf16[1024,2048]{1,0:T(8,128)(2,1)S(1)} %pad_maximum_fusion.1, bf16[1024,2432]{1,0:T(8,128)(2,1)S(1)} %bitcast.267), kind=kOutput, calls=%fused_computation.2 | convolution fusion | flops 10205528064 | bytes 19136512 | tf_op jit(solution)/shard_map/dot_general | solution.py:33
  754.7 8.4 fusion.169
  765.1 13.6 fusion.110
  790.1 12.6 convolution_convert_fusion.6
  817.9 9.2 fusion.121
  833.2 9.0 collective-permute-done.35
  842.3 14.0 %convolution_convert_fusion.3 = bf16[2048,2048]{1,0:T(8,128)(2,1)} fusion(bf16[1024,2048]{1,0:T(8,128)(2,1)} %pad_maximum_fusion.2, bf16[256,2048]{1,0:T(8,128)(2,1)} %collective-permute-done.35, bf16[256,2048]{1,0:T(8,128)(2,1)} %collective-permute-done.32, bf16[256,2048]{1,0:T(8,128)(2,1)} %collective-permute-done.29, ...), kind=kOutput, calls=%fused_computation.65 | convolution fusion | flops 8610906112 | bytes 16777216 | tf_op jit(solution)/shard_map/dot_general | solution.py:33
  868.2 10.2 fusion.127
  883.0 29.2 %convolution_convert_fusion.1 = bf16[2048,4224]{1,0:T(8,128)(2,1)} fusion(bf16[1024,2048]{1,0:T(8,128)(2,1)} %copy-done.69, bf16[256,128]{1,0:T(8,128)(2,1)S(1)} %fusion.227, bf16[256,2048]{1,0:T(8,128)(2,1)} %copy-done.111, bf16[256,2048]{1,0:T(8,128)(2,1)} %copy-done.110, bf16[256,128]{1,0:T(8,128)(2,1)S(1)} %fusion.230, ...), kind=kOutput, calls=%fused_computation.1 | convolution fusion | flops 17829199872 | bytes 30146560 | tf_op jit(solution)/shard_map/dot_general | solution.py:33
  928.7 16.4 %fusion.23 = f32[128,4096]{1,0:T(8,128)} fusion(bf16[1024,128]{1,0:T(8,128)(2,1)S(1)} %pad_maximum_fusion.15, bf16[256,128]{1,0:T(8,128)(2,1)S(1)} %copy-done.117, bf16[256,2048]{1,0:T(8,128)(2,1)} %copy-done.111, bf16[256,2048]{1,0:T(8,128)(2,1)} %copy-done.110, bf16[256,128]{1,0:T(8,128)(2,1)S(1)} %copy-done.115, bf16[256,2048]{1,0:T(8,128)(2,1)} %copy-done.109, ...), kind=kOutput, calls=%fused_computation.26 | convolution fusion | flops 1174405120 | bytes 11010048 | tf_op jit(solution)/shard_map/dot_general | solution.py:33
  952.7 19.4 %collective-permute-done.40 = bf16[256,2048]{1,0:T(8,128)(2,1)} collective-permute-done((bf16[256,2048]{1,0:T(8,128)(2,1)S(1)}, bf16[256,2048]{1,0:T(8,128)(2,1)}, u32[]{:S(2)}, u32[]{:S(2)}) %collective-permute-start.40) | collective-permute-done | bytes 1048608 | tf_op jit(solution)/shard_map/ppermute | solution.py:682
  979.0 21.3 %collective-permute-done.42 = bf16[256,2048]{1,0:T(8,128)(2,1)} collective-permute-done((bf16[256,2048]{1,0:T(8,128)(2,1)}, bf16[256,2048]{1,0:T(8,128)(2,1)}, u32[]{:S(2)}, u32[]{:S(2)}) %collective-permute-start.42) | collective-permute-done | bytes 1048608 | tf_op jit(solution)/shard_map/ppermute | solution.py:682
  1000.3 8.8 fusion.101
  1013.8 39.2 %attention_backward.1 = bf16[1024,3456]{1,0:T(8,128)(2,1)} custom-call(s32[1]{0:T(128)} %bitcast.place_ref, s32[3]{0:T(128)} %bitcast.258, f32[1024,128]{1,0:T(8,128)} %get-tuple-element.445.cosine_ref, f32[1024,128]{1,0:T(8,128)} %get-tuple-element.446.sine_ref, bf16[1024,1024]{1,0:T(8,128)(2,1)} %get-tuple-element.206.q_ref, ...), custom_call_target="tpu_custom_call" | custom-call | flops 10737418240 | bytes 14680064 | tf_op jit(solution)/shard_map/attention_backward/pallas_call | solution.py:233
  1053.1 48.8 %convolution_convert_fusion = bf16[4096,3456]{1,0:T(8,128)(2,1)} fusion(bf16[1024,3456]{1,0:T(8,128)(2,1)} %attention_backward.1, bf16[256,2048]{1,0:T(8,128)(2,1)} %get-tuple-element.442, bf16[256,2048]{1,0:T(8,128)(2,1)} %get-tuple-element.441, bf16[256,2048]{1,0:T(8,128)(2,1)S(1)} %copy-done.54, bf16[256,2048]{1,0:T(8,128)(2,1)} %get-tuple-element.438, ...), kind=kOutput, calls=%fused_computation | convolution fusion | flops 29072293888 | bytes 43778048 | tf_op jit(solution)/shard_map/dot_general | solution.py:33
  1105.7 20.9 %fusion.104 = f32[512,4096]{1,0:T(8,128)S(1)} fusion(bf16[4096,3456]{1,0:T(8,128)(2,1)} %all-gather.9.cloned.1.call-done, bf16[1024,3456]{1,0:T(8,128)(2,1)} %attention_backward.1), kind=kOutput, calls=%fused_computation.144 | convolution fusion | flops 14495514624 | bytes 40239104 | tf_op jit(solution)/shard_map/dot_general | solution.py:29
  1136.2 18.0 %fusion.216 = f32[256,4096]{1,0:T(8,128)} fusion(bf16[4096,3456]{1,0:T(8,128)(2,1)} %all-gather.9.cloned.1.call-done, bf16[1024,3456]{1,0:T(8,128)(2,1)S(1)} %bitcast.214), kind=kOutput, calls=%fused_computation.321 | convolution fusion | flops 7247757312 | bytes 34275328 | tf_op jit(solution)/shard_map/dot_general | solution.py:29
  1154.2 16.8 %fusion.218 = f32[256,4096]{1,0:T(8,128)} fusion(bf16[4096,3456]{1,0:T(8,128)(2,1)} %all-gather.9.cloned.1.call-done, bf16[1024,3456]{1,0:T(8,128)(2,1)} %attention_backward.1), kind=kOutput, calls=%fused_computation.323 | convolution fusion | flops 7247757312 | bytes 34275328 | tf_op jit(solution)/shard_map/dot_general | solution.py:29
  1189.1 32.4 %collective-permute-done.45 = bf16[256,4096]{1,0:T(8,128)(2,1)S(1)} collective-permute-done((bf16[256,4096]{1,0:T(8,128)(2,1)S(1)}, bf16[256,4096]{1,0:T(8,128)(2,1)S(1)}, u32[]{:S(2)}, u32[]{:S(2)}) %collective-permute-start.45) | collective-permute-done | bytes 2097184 | tf_op jit(solution)/shard_map/ppermute | solution.py:682
  1249.6 46.9 %collective-permute-done.49 = bf16[256,2048]{1,0:T(8,128)(2,1)S(1)} collective-permute-done((bf16[256,2048]{1,0:T(8,128)(2,1)}, bf16[256,2048]{1,0:T(8,128)(2,1)S(1)}, u32[]{:S(2)}, u32[]{:S(2)}) %collective-permute-start.49) | collective-permute-done | bytes 1048608 | tf_op jit(solution)/shard_map/ppermute | solution.py:682
  1342.3 8.9 collective-permute-done.57
  (713 shorter events, 469.2 us)
Async XLA Ops:
  7.2 170.5 %all-gather.9.cloned.1.call-start = ((), (), s32[]{:S(2)}) async-start(), calls=%async_computation.6 | async-start | bytes 31850496 | tf_op jit(solution)/shard_map/all_gather | solution.py:838
  16.2 239.5 %all-gather.11.cloned.1.call-start = ((), (), s32[]{:S(2)}) async-start(), calls=%async_computation.7 | async-start | bytes 4718592 | tf_op jit(solution)/shard_map/all_gather | solution.py:838
  17.0 318.5 %all-gather.13.cloned.1.call-start = ((), (), s32[]{:S(2)}) async-start(), calls=%async_computation.8 | async-start | bytes 19464192 | tf_op jit(solution)/shard_map/all_gather | solution.py:838
  22.9 342.5 %all-gather.15.cloned.1.call-start = ((), (), s32[]{:S(2)}) async-start(), calls=%async_computation.9 | async-start | bytes 9437184 | tf_op jit(solution)/shard_map/all_gather | solution.py:838
  23.5 475.8 %all-gather.17.cloned.1.call-start = ((), (), s32[]{:S(2)}) async-start(), calls=%async_computation.10 | async-start | bytes 11206656 | tf_op jit(solution)/shard_map/all_gather | solution.py:838
  27.4 51.2 %collective-permute-start.4 = (bf16[256,2048]{1,0:T(8,128)(2,1)S(1)}, bf16[256,2048]{1,0:T(8,128)(2,1)}, u32[]{:S(2)}, u32[]{:S(2)}) collective-permute-start(bf16[256,2048]{1,0:T(8,128)(2,1)S(1)} %copy-done.9), channel_id=1, source_target_pairs={{0,1},{1,2},{2,3},{3,0},{4,5},{5,6},{6,7},{7,4},{8,9},{9,10},{10,1... | collective-permute-start | bytes 3145736 | tf_op jit(solution)/shard_map/ppermute | solution.py:682
  30.0 50.2 %collective-permute-start.3 = (bf16[256,2048]{1,0:T(8,128)(2,1)S(1)}, bf16[256,2048]{1,0:T(8,128)(2,1)}, u32[]{:S(2)}, u32[]{:S(2)}) collective-permute-start(bf16[256,2048]{1,0:T(8,128)(2,1)S(1)} %copy-done.7), channel_id=1, source_target_pairs={{0,1},{1,2},{2,3},{3,0},{4,5},{5,6},{6,7},{7,4},{8,9},{9,10},{10,1... | collective-permute-start | bytes 3145736 | tf_op jit(solution)/shard_map/ppermute | solution.py:682
  35.1 472.7 %all-gather.19.cloned.1.call-start = ((), (), s32[]{:S(2)}) async-start(), calls=%async_computation.11 | async-start | bytes 4718592 | tf_op jit(solution)/shard_map/all_gather | solution.py:838
  73.8 30.9 %collective-permute-start.2 = (bf16[64,7168]{1,0:T(8,128)(2,1)S(1)}, bf16[64,7168]{1,0:T(8,128)(2,1)S(1)}, u32[]{:S(2)}, u32[]{:S(2)}) collective-permute-start(bf16[64,7168]{1,0:T(8,128)(2,1)S(1)} %pad_maximum_fusion.9), channel_id=1, source_target_pairs={{0,16},{4,20},{8,24},{12,28},{16,0},{20,4},{24,8},{28,12},{1,17},{... | collective-permute-start | bytes 2752520 | tf_op jit(solution)/shard_map/ppermute | solution.py:824
  78.6 28.1 %collective-permute-start.6 = (bf16[256,2048]{1,0:T(8,128)(2,1)}, bf16[256,2048]{1,0:T(8,128)(2,1)S(1)}, u32[]{:S(2)}, u32[]{:S(2)}) collective-permute-start(bf16[256,2048]{1,0:T(8,128)(2,1)} %collective-permute-done.4), channel_id=1, source_target_pairs={{0,1},{1,2},{2,3},{3,0},{4,5},{5,6},{6,7},{7,4},{8,9},{9,10},{10,1... | collective-permute-start | bytes 3145736 | tf_op jit(solution)/shard_map/ppermute | solution.py:682
  80.2 47.3 %collective-permute-start.5 = (bf16[256,2048]{1,0:T(8,128)(2,1)}, bf16[256,2048]{1,0:T(8,128)(2,1)S(1)}, u32[]{:S(2)}, u32[]{:S(2)}) collective-permute-start(bf16[256,2048]{1,0:T(8,128)(2,1)} %collective-permute-done.3), channel_id=1, source_target_pairs={{0,1},{1,2},{2,3},{3,0},{4,5},{5,6},{6,7},{7,4},{8,9},{9,10},{10,1... | collective-permute-start | bytes 3145736 | tf_op jit(solution)/shard_map/ppermute | solution.py:682
  127.4 27.9 %collective-permute-start.7 = (bf16[256,2048]{1,0:T(8,128)(2,1)S(1)}, bf16[256,2048]{1,0:T(8,128)(2,1)S(1)}, u32[]{:S(2)}, u32[]{:S(2)}) collective-permute-start(bf16[256,2048]{1,0:T(8,128)(2,1)S(1)} %collective-permute-done.5), channel_id=1, source_target_pairs={{0,1},{1,2},{2,3},{3,0},{4,5},{5,6},{6,7},{7,4},{8,9},{9,10},{10,1... | collective-permute-start | bytes 3145736 | tf_op jit(solution)/shard_map/ppermute | solution.py:682
  127.4 47.7 %collective-permute-start.8 = (bf16[256,2048]{1,0:T(8,128)(2,1)S(1)}, bf16[256,2048]{1,0:T(8,128)(2,1)S(1)}, u32[]{:S(2)}, u32[]{:S(2)}) collective-permute-start(bf16[256,2048]{1,0:T(8,128)(2,1)S(1)} %collective-permute-done.6), channel_id=1, source_target_pairs={{0,1},{1,2},{2,3},{3,0},{4,5},{5,6},{6,7},{7,4},{8,9},{9,10},{10,1... | collective-permute-start | bytes 3145736 | tf_op jit(solution)/shard_map/ppermute | solution.py:682
  175.2 24.4 %collective-permute-start.9 = (bf16[256,2048]{1,0:T(8,128)(2,1)S(1)}, bf16[256,2048]{1,0:T(8,128)(2,1)}, u32[]{:S(2)}, u32[]{:S(2)}) collective-permute-start(bf16[256,2048]{1,0:T(8,128)(2,1)S(1)} %copy-done.24), channel_id=1, source_target_pairs={{0,1},{1,2},{2,3},{3,0},{4,5},{5,6},{6,7},{7,4},{8,9},{9,10},{10,1... | collective-permute-start | bytes 3145736 | tf_op jit(solution)/shard_map/ppermute | solution.py:682
  199.6 24.6 %collective-permute-start.10 = (bf16[256,2048]{1,0:T(8,128)(2,1)}, bf16[256,2048]{1,0:T(8,128)(2,1)}, u32[]{:S(2)}, u32[]{:S(2)}) collective-permute-start(bf16[256,2048]{1,0:T(8,128)(2,1)} %collective-permute-done.9), channel_id=1, source_target_pairs={{0,1},{1,2},{2,3},{3,0},{4,5},{5,6},{6,7},{7,4},{8,9},{9,10},{10,1... | collective-permute-start | bytes 3145736 | tf_op jit(solution)/shard_map/ppermute | solution.py:682
  224.1 31.6 %collective-permute-start.11 = (bf16[256,2048]{1,0:T(8,128)(2,1)}, bf16[256,2048]{1,0:T(8,128)(2,1)}, u32[]{:S(2)}, u32[]{:S(2)}) collective-permute-start(bf16[256,2048]{1,0:T(8,128)(2,1)} %collective-permute-done.10), channel_id=1, source_target_pairs={{0,1},{1,2},{2,3},{3,0},{4,5},{5,6},{6,7},{7,4},{8,9},{9,10},{10,1... | collective-permute-start | bytes 3145736 | tf_op jit(solution)/shard_map/ppermute | solution.py:682
  284.9 557.4 %reduce-scatter.7.cloned.1.call-start = ((), (), s32[]{:S(2)}) async-start(), calls=%async_computation.12 | async-start | bytes 4718592 | tf_op jit(solution)/shard_map/reduce_scatter | solution.py:842
  335.3 37.4 %collective-permute-start.15 = (bf16[256,2048]{1,0:T(8,128)(2,1)S(1)}, bf16[256,2048]{1,0:T(8,128)(2,1)}, u32[]{:S(2)}, u32[]{:S(2)}) collective-permute-start(bf16[256,2048]{1,0:T(8,128)(2,1)S(1)} %multiply_convert_fusion.5), channel_id=1, source_target_pairs={{0,1},{1,2},{2,3},{3,0},{4,5},{5,6},{6,7},{7,4},{8,9},{9,10},{10,1... | collective-permute-start | bytes 3145736 | tf_op jit(solution)/shard_map/ppermute | solution.py:682
  372.7 28.2 %collective-permute-start.17 = (bf16[256,2048]{1,0:T(8,128)(2,1)}, bf16[256,2048]{1,0:T(8,128)(2,1)S(1)}, u32[]{:S(2)}, u32[]{:S(2)}) collective-permute-start(bf16[256,2048]{1,0:T(8,128)(2,1)} %collective-permute-done.15), channel_id=1, source_target_pairs={{0,1},{1,2},{2,3},{3,0},{4,5},{5,6},{6,7},{7,4},{8,9},{9,10},{10,1... | collective-permute-start | bytes 3145736 | tf_op jit(solution)/shard_map/ppermute | solution.py:682
  390.6 32.7 %collective-permute-start.16 = (bf16[256,2048]{1,0:T(8,128)(2,1)S(1)}, bf16[256,2048]{1,0:T(8,128)(2,1)S(1)}, u32[]{:S(2)}, u32[]{:S(2)}) collective-permute-start(bf16[256,2048]{1,0:T(8,128)(2,1)S(1)} %convolution_convert_fusion.9), channel_id=1, source_target_pairs={{0,1},{1,2},{2,3},{3,0},{4,5},{5,6},{6,7},{7,4},{8,9},{9,10},{10,1... | collective-permute-start | bytes 3145736 | tf_op jit(solution)/shard_map/ppermute | solution.py:682
  400.8 44.9 %collective-permute-start.19 = (bf16[256,2048]{1,0:T(8,128)(2,1)S(1)}, bf16[256,2048]{1,0:T(8,128)(2,1)S(1)}, u32[]{:S(2)}, u32[]{:S(2)}) collective-permute-start(bf16[256,2048]{1,0:T(8,128)(2,1)S(1)} %collective-permute-done.17), channel_id=1, source_target_pairs={{0,1},{1,2},{2,3},{3,0},{4,5},{5,6},{6,7},{7,4},{8,9},{9,10},{10,1... | collective-permute-start | bytes 3145736 | tf_op jit(solution)/shard_map/ppermute | solution.py:682
  423.7 43.9 %collective-permute-start.18 = (bf16[256,2048]{1,0:T(8,128)(2,1)S(1)}, bf16[256,2048]{1,0:T(8,128)(2,1)S(1)}, u32[]{:S(2)}, u32[]{:S(2)}) collective-permute-start(bf16[256,2048]{1,0:T(8,128)(2,1)S(1)} %add_convert_fusion.8), channel_id=1, source_target_pairs={{0,1},{1,2},{2,3},{3,0},{4,5},{5,6},{6,7},{7,4},{8,9},{9,10},{10,1... | collective-permute-start | bytes 3145736 | tf_op jit(solution)/shard_map/ppermute | solution.py:682
  468.9 26.6 %collective-permute-start.20 = (bf16[256,2048]{1,0:T(8,128)(2,1)}, bf16[256,2048]{1,0:T(8,128)(2,1)}, u32[]{:S(2)}, u32[]{:S(2)}) collective-permute-start(bf16[256,2048]{1,0:T(8,128)(2,1)} %add_convert_fusion.7), channel_id=1, source_target_pairs={{0,1},{1,2},{2,3},{3,0},{4,5},{5,6},{6,7},{7,4},{8,9},{9,10},{10,1... | collective-permute-start | bytes 3145736 | tf_op jit(solution)/shard_map/ppermute | solution.py:682
  498.7 26.2 %collective-permute-start.21 = (bf16[256,2048]{1,0:T(8,128)(2,1)}, bf16[256,2048]{1,0:T(8,128)(2,1)}, u32[]{:S(2)}, u32[]{:S(2)}) collective-permute-start(bf16[256,2048]{1,0:T(8,128)(2,1)} %multiply_convert_fusion.4), channel_id=1, source_target_pairs={{0,1},{1,2},{2,3},{3,0},{4,5},{5,6},{6,7},{7,4},{8,9},{9,10},{10,1... | collective-permute-start | bytes 3145736 | tf_op jit(solution)/shard_map/ppermute | solution.py:682
  524.9 24.7 %collective-permute-start.22 = (bf16[256,2048]{1,0:T(8,128)(2,1)}, bf16[256,2048]{1,0:T(8,128)(2,1)S(1)}, u32[]{:S(2)}, u32[]{:S(2)}) collective-permute-start(bf16[256,2048]{1,0:T(8,128)(2,1)} %collective-permute-done.21), channel_id=1, source_target_pairs={{0,1},{1,2},{2,3},{3,0},{4,5},{5,6},{6,7},{7,4},{8,9},{9,10},{10,1... | collective-permute-start | bytes 3145736 | tf_op jit(solution)/shard_map/ppermute | solution.py:682
  618.4 39.7 %collective-permute-start.24 = (bf16[256,2048]{1,0:T(8,128)(2,1)S(1)}, bf16[256,2048]{1,0:T(8,128)(2,1)S(1)}, u32[]{:S(2)}, u32[]{:S(2)}) collective-permute-start(bf16[256,2048]{1,0:T(8,128)(2,1)S(1)} %slice.569), channel_id=1, source_target_pairs={{0,1},{1,2},{2,3},{3,0},{4,5},{5,6},{6,7},{7,4},{8,9},{9,10},{10,1... | collective-permute-start | bytes 3145736 | tf_op jit(solution)/shard_map/ppermute | solution.py:682
  687.3 240.3 %reduce-scatter.9.cloned.1.call-start = ((), (), s32[]{:S(2)}) async-start(), calls=%async_computation.13 | async-start | bytes 11206656 | tf_op jit(solution)/shard_map/reduce_scatter | solution.py:842
  722.1 256.9 %reduce-scatter.11.cloned.1.call-start = ((), (), s32[]{:S(2)}) async-start(), calls=%async_computation.14 | async-start | bytes 9437184 | tf_op jit(solution)/shard_map/reduce_scatter | solution.py:842
  744.0 34.7 %collective-permute-start.30 = (f32[4,864]{1,0:T(4,128)S(1)}, f32[4,864]{1,0:T(4,128)S(1)}, u32[]{:S(2)}, u32[]{:S(2)}) collective-permute-start(f32[4,864]{1,0:T(4,128)S(1)} %slice_select_fusion.2), channel_id=1, source_target_pairs={{0,16},{4,20},{8,24},{12,28},{16,0},{20,4},{24,8},{28,12},{1,17},{... | collective-permute-start | bytes 41480 | tf_op jit(solution)/shard_map/ppermute | solution.py:699
  778.8 24.5 %collective-permute-start.33 = (f32[2,864]{1,0:T(2,128)S(1)}, f32[2,864]{1,0:T(2,128)S(1)}, u32[]{:S(2)}, u32[]{:S(2)}) collective-permute-start(f32[2,864]{1,0:T(2,128)S(1)} %broadcast_select_fusion.10), channel_id=1, source_target_pairs={{0,8},{4,12},{8,0},{12,4},{16,24},{20,28},{24,16},{28,20},{1,9},{5... | collective-permute-start | bytes 20744 | tf_op jit(solution)/shard_map/ppermute | solution.py:699
  802.7 28.0 %collective-permute-start.31 = (bf16[256,2048]{1,0:T(8,128)(2,1)}, bf16[256,2048]{1,0:T(8,128)(2,1)}, u32[]{:S(2)}, u32[]{:S(2)}) collective-permute-start(bf16[256,2048]{1,0:T(8,128)(2,1)} %convolution_convert_fusion.6), channel_id=1, source_target_pairs={{0,1},{1,2},{2,3},{3,0},{4,5},{5,6},{6,7},{7,4},{8,9},{9,10},{10,1... | collective-permute-start | bytes 3145736 | tf_op jit(solution)/shard_map/ppermute | solution.py:682
  803.4 29.9 %collective-permute-start.36 = (f32[1,864]{1,0:T(1,128)S(1)}, f32[1,864]{1,0:T(1,128)S(1)}, u32[]{:S(2)}, u32[]{:S(2)}) collective-permute-start(f32[1,864]{1,0:T(1,128)S(1)} %broadcast_select_fusion.9), channel_id=1, source_target_pairs={{0,4},{4,0},{8,12},{12,8},{16,20},{20,16},{24,28},{28,24},{1,5},{5... | collective-permute-start | bytes 10376 | tf_op jit(solution)/shard_map/ppermute | solution.py:699
  803.4 38.8 %collective-permute-start.35 = (bf16[256,2048]{1,0:T(8,128)(2,1)}, bf16[256,2048]{1,0:T(8,128)(2,1)}, u32[]{:S(2)}, u32[]{:S(2)}) collective-permute-start(bf16[256,2048]{1,0:T(8,128)(2,1)} %collective-permute-done.32), channel_id=1, source_target_pairs={{0,1},{1,2},{2,3},{3,0},{4,5},{5,6},{6,7},{7,4},{8,9},{9,10},{10,1... | collective-permute-start | bytes 3145736 | tf_op jit(solution)/shard_map/ppermute | solution.py:682
  856.3 196.8 %reduce-scatter.13.cloned.1.call-start = ((), (), s32[]{:S(2)}) async-start(), calls=%async_computation.15 | async-start | bytes 19464192 | tf_op jit(solution)/shard_map/reduce_scatter | solution.py:842
  880.9 31.4 %collective-permute-start.37 = (bf16[256,2048]{1,0:T(8,128)(2,1)}, bf16[256,2048]{1,0:T(8,128)(2,1)S(1)}, u32[]{:S(2)}, u32[]{:S(2)}) collective-permute-start(bf16[256,2048]{1,0:T(8,128)(2,1)} %add_convert_fusion.2), channel_id=1, source_target_pairs={{0,1},{1,2},{2,3},{3,0},{4,5},{5,6},{6,7},{7,4},{8,9},{9,10},{10,1... | collective-permute-start | bytes 3145736 | tf_op jit(solution)/shard_map/ppermute | solution.py:682
  912.3 311.1 %reduce-scatter.15.cloned.1.call-start = ((), (), s32[]{:S(2)}) async-start(), calls=%async_computation.16 | async-start | bytes 4718592 | tf_op jit(solution)/shard_map/reduce_scatter | solution.py:842
  972.1 28.2 %collective-permute-start.42 = (bf16[256,2048]{1,0:T(8,128)(2,1)}, bf16[256,2048]{1,0:T(8,128)(2,1)}, u32[]{:S(2)}, u32[]{:S(2)}) collective-permute-start(bf16[256,2048]{1,0:T(8,128)(2,1)} %collective-permute-done.40), channel_id=1, source_target_pairs={{0,1},{1,2},{2,3},{3,0},{4,5},{5,6},{6,7},{7,4},{8,9},{9,10},{10,1... | collective-permute-start | bytes 3145736 | tf_op jit(solution)/shard_map/ppermute | solution.py:682
  974.7 78.4 %collective-permute-start.25 = (bf16[256,2048]{1,0:T(8,128)(2,1)}, bf16[256,2048]{1,0:T(8,128)(2,1)}, u32[]{:S(2)}, u32[]{:S(2)}) collective-permute-start(bf16[256,2048]{1,0:T(8,128)(2,1)} %add_convert_fusion.6), channel_id=1, source_target_pairs={{0,1},{1,2},{2,3},{3,0},{4,5},{5,6},{6,7},{7,4},{8,9},{9,10},{10,1... | collective-permute-start | bytes 3145736 | tf_op jit(solution)/shard_map/ppermute | solution.py:682
  1009.1 325.6 %reduce-scatter.17.cloned.1.call-start = ((), (), s32[]{:S(2)}) async-start(), calls=%async_computation.17 | async-start | bytes 31850496 | tf_op jit(solution)/shard_map/reduce_scatter | solution.py:842
  1105.7 83.4 %collective-permute-start.47 = (f32[576]{0:T(1024)S(1)}, f32[576]{0:T(1024)S(1)}, u32[]{:S(2)}, u32[]{:S(2)}) collective-permute-start(f32[576]{0:T(1024)S(1)} %pad_maximum_fusion.18), channel_id=1, source_target_pairs={{0,1},{1,0},{2,3},{3,2},{4,5},{5,4},{6,7},{7,6},{8,9},{9,8},{10,11... | collective-permute-start | bytes 6920 | tf_op jit(solution)/shard_map/ppermute | solution.py:722
  1128.2 45.9 %collective-permute-start.44 = (bf16[256,4096]{1,0:T(8,128)(2,1)}, bf16[256,4096]{1,0:T(8,128)(2,1)}, u32[]{:S(2)}, u32[]{:S(2)}) collective-permute-start(bf16[256,4096]{1,0:T(8,128)(2,1)} %slice.924), channel_id=1, source_target_pairs={{0,1},{1,2},{2,3},{3,0},{4,5},{5,6},{6,7},{7,4},{8,9},{9,10},{10,1... | collective-permute-start | bytes 6291464 | tf_op jit(solution)/shard_map/ppermute | solution.py:682
  1135.3 53.8 %collective-permute-start.46 = (bf16[4,16,7168]{2,1,0:T(8,128)(2,1)}, bf16[4,16,7168]{2,1,0:T(8,128)(2,1)}, u32[]{:S(2)}, u32[]{:S(2)}) collective-permute-start(bf16[4,16,7168]{2,1,0:T(8,128)(2,1)} %bitcast.36), channel_id=1, source_target_pairs={{0,16},{4,20},{8,24},{12,28},{16,0},{20,4},{24,8},{28,12},{1,17},{... | collective-permute-start | bytes 2752520 | tf_op jit(solution)/shard_map/ppermute | solution.py:699
  1176.3 45.2 %collective-permute-start.45 = (bf16[256,4096]{1,0:T(8,128)(2,1)S(1)}, bf16[256,4096]{1,0:T(8,128)(2,1)S(1)}, u32[]{:S(2)}, u32[]{:S(2)}) collective-permute-start(bf16[256,4096]{1,0:T(8,128)(2,1)S(1)} %add_convert_fusion.1), channel_id=1, source_target_pairs={{0,1},{1,2},{2,3},{3,0},{4,5},{5,6},{6,7},{7,4},{8,9},{9,10},{10,1... | collective-permute-start | bytes 6291464 | tf_op jit(solution)/shard_map/ppermute | solution.py:682
  1225.0 74.6 %collective-permute-start.48 = (bf16[256,4096]{1,0:T(8,128)(2,1)}, bf16[256,4096]{1,0:T(8,128)(2,1)}, u32[]{:S(2)}, u32[]{:S(2)}) collective-permute-start(bf16[256,4096]{1,0:T(8,128)(2,1)} %add_convert_fusion), channel_id=1, source_target_pairs={{0,1},{1,2},{2,3},{3,0},{4,5},{5,6},{6,7},{7,4},{8,9},{9,10},{10,1... | collective-permute-start | bytes 6291464 | tf_op jit(solution)/shard_map/ppermute | solution.py:682
  1227.4 72.2 %collective-permute-start.51 = (f32[576]{0:T(1024)S(1)}, f32[576]{0:T(1024)S(1)}, u32[]{:S(2)}, u32[]{:S(2)}) collective-permute-start(f32[576]{0:T(1024)S(1)} %fusion.270), channel_id=1, source_target_pairs={{0,2},{1,3},{2,0},{3,1},{4,6},{5,7},{6,4},{7,5},{8,10},{9,11},{10,... | collective-permute-start | bytes 6920 | tf_op jit(solution)/shard_map/ppermute | solution.py:722
  1230.4 83.6 %collective-permute-start.60 = (bf16[256,384]{1,0:T(8,128)(2,1)S(1)}, bf16[256,384]{1,0:T(8,128)(2,1)S(1)}, u32[]{:S(2)}, u32[]{:S(2)}) collective-permute-start(bf16[256,384]{1,0:T(8,128)(2,1)S(1)} %fusion.249), channel_id=1, source_target_pairs={{0,1},{1,0},{2,3},{3,2},{4,5},{5,4},{6,7},{7,6},{8,9},{9,8},{10,11... | collective-permute-start | bytes 589832 | tf_op jit(solution)/shard_map/ppermute | solution.py:722
  1232.5 64.0 %collective-permute-start.49 = (bf16[256,2048]{1,0:T(8,128)(2,1)}, bf16[256,2048]{1,0:T(8,128)(2,1)S(1)}, u32[]{:S(2)}, u32[]{:S(2)}) collective-permute-start(bf16[256,2048]{1,0:T(8,128)(2,1)} %convert_add_fusion.6), channel_id=1, source_target_pairs={{0,1},{1,2},{2,3},{3,0},{4,5},{5,6},{6,7},{7,4},{8,9},{9,10},{10,1... | collective-permute-start | bytes 3145736 | tf_op jit(solution)/shard_map/ppermute | solution.py:682
  1235.3 64.3 %collective-permute-start.50 = (bf16[2,16,7168]{2,1,0:T(8,128)(2,1)S(1)}, bf16[2,16,7168]{2,1,0:T(8,128)(2,1)S(1)}, u32[]{:S(2)}, u32[]{:S(2)}) collective-permute-start(bf16[2,16,7168]{2,1,0:T(8,128)(2,1)S(1)} %select_convert_fusion.1), channel_id=1, source_target_pairs={{0,8},{4,12},{8,0},{12,4},{16,24},{20,28},{24,16},{28,20},{1,9},{5... | collective-permute-start | bytes 1376264 | tf_op jit(solution)/shard_map/ppermute | solution.py:699
  (154 other events, 1956.5 us)
Sparse Core Ops, SparseCore 0:
  16.4 158.4 all-gather.8
  176.8 36.3 all-gather.10
  215.6 92.0 all-gather.12
  309.5 55.9 all-gather.14
  367.2 61.0 all-gather.16
  430.0 37.4 all-gather.18
  687.4 48.5 reduce-scatter.6
  740.0 79.0 reduce-scatter.8
  856.5 70.3 reduce-scatter.10
  930.3 118.6 reduce-scatter.12
  1053.3 51.2 reduce-scatter.14
  1108.2 175.4 reduce-scatter.16

commit v4 on v3

--- a/solution.py
+++ b/solution.py
@@ -611,17 +611,18 @@
     )(place, lengths, zx, zx, sd, sd, grad_scaled, stats, states, wide, narrow, rates)
 
 
-def norm_back_kernel(parts, with_base, with_low, *refs):
+def norm_back_kernel(parts, with_base, with_low, with_gain, *refs):
     values, refs = refs[:parts], refs[parts:]
     grad, gain, refs = refs[0], refs[1], refs[2:]
     base, refs = (refs[0], refs[1:]) if with_base else (None, refs)
     outs, refs = refs[:parts], refs[parts:]
     low, refs = (refs[0], refs[1:]) if with_low else (None, refs)
-    grad_gain = refs[0]
-
-    @pl.when(pl.program_id(0) == 0)
-    def _():
-        grad_gain[...] = jnp.zeros_like(grad_gain)
+    if with_gain:
+        grad_gain = refs[0]
+
+        @pl.when(pl.program_id(0) == 0)
+        def _():
+            grad_gain[...] = jnp.zeros_like(grad_gain)
 
     width = grad.shape[1]
     each = width // parts
@@ -634,7 +635,8 @@
     cross = sum(jnp.sum(g * u, axis=1, keepdims=True) for g, u in zip(grad_units, units)) / width
     for i in range(parts):
         cols = slice(i * each, (i + 1) * each)
-        grad_gain[0:1, cols] += jnp.sum(grads[i] * units[i], axis=0, keepdims=True)
+        if with_gain:
+            grad_gain[0:1, cols] += jnp.sum(grads[i] * units[i], axis=0, keepdims=True)
         result = inv_root * (grad_units[i] - units[i] * cross)
         if with_base and i == 0:
             result = result + base[...].astype(f32)
@@ -643,7 +645,7 @@
             low[...] = result.astype(bf16)
 
 
-def norm_back(values, grad, gain, base=None, with_low=False):
+def norm_back(values, grad, gain, base=None, with_low=False, with_gain=True):
     rows, width = grad.shape
     parts = len(values)
     block = math.gcd(rows, 64)
@@ -653,24 +655,29 @@
     shapes = [jax.ShapeDtypeStruct((rows, width // parts), f32)] * parts
     shapes += [jax.ShapeDtypeStruct((rows, width // parts), bf16)] if with_low else []
     results = pl.pallas_call(
-        functools.partial(norm_back_kernel, parts, base is not None, with_low),
-        out_shape=shapes + [jax.ShapeDtypeStruct((8, width), f32)],
+        functools.partial(norm_back_kernel, parts, base is not None, with_low, with_gain),
+        out_shape=shapes + [jax.ShapeDtypeStruct((8, width), f32)] * int(with_gain),
         grid=(rows // block,),
         in_specs=[row_spec] * parts
         + [full_spec, pl.BlockSpec((1, width), lambda i: (0, 0))]
         + ([row_spec] if base is not None else []),
-        out_specs=[row_spec] * (parts + int(with_low)) + [pl.BlockSpec((8, width), lambda i: (0, 0))],
+        out_specs=[row_spec] * (parts + int(with_low))
+        + [pl.BlockSpec((8, width), lambda i: (0, 0))] * int(with_gain),
         compiler_params=pltpu.CompilerParams(vmem_limit_bytes=VMEM_LIMIT),
         cost_estimate=pl.CostEstimate(
             flops=20 * rows * width, bytes_accessed=14 * rows * width, transcendentals=rows
         ),
         name="norm_back",
     )(*operands)
-    return list(results[:-1]) + [results[-1][0]]
+    return list(results[:-1]) + [results[-1][0]] if with_gain else list(results)
 
 
 def tie(value, others):
     return lax.optimization_barrier((value, others))[0]
+
+
+def after(value, token):
+    return value if token is None else tie(value, token)
 
 
 def ring_pairs():
@@ -768,12 +775,12 @@
     tp = lax.axis_size("tp")
     fill = list(fill)
     filled = []
-    total = part(1 % tp)
+    total = part(1 % tp, None)
     for p in range(2, tp + 1):
         low = total.astype(bf16)
         moved = hop(low)
         live = begin(tasks)
-        term = part(p % tp)
+        term = part(p % tp, low)
         extra = [fill.pop(0)(low, tasks)] if fill else []
         moved, (term, extra) = settle(moved, (term, extra), live)
         filled += extra
@@ -789,7 +796,7 @@
     moved = hop(own)
     live = begin(tasks)
     first = work(0, own)
-    moved, first = settle(moved, first, live)
+    moved, _ = settle(moved, (), live)
     total, ahead = None, None
     for p in range(1, tp):
         pieces.append(moved)
@@ -807,7 +814,7 @@
         low = total.astype(bf16)
         ahead = hop(low)
         if p < tp - 1:
-            moved, low = settle(moved, low, live)
+            moved, (low, first) = settle(moved, (low, first), live)
         elif fill is not None:
             ahead, result = settle(ahead, fill(low), live)
             filled.append(result)
@@ -888,39 +895,13 @@
     def piece(values, p):
         return values[p * share : (p + 1) * share]
 
-    weight_qkv = gather(
-        jnp.concatenate(
-            [query_key_value_weight[:, j, :] for j in range(3)]
-            + [attention_adapter_down[:, j, :] for j in range(3)],
-            axis=1,
-        )
-    )
-    ups = doubling_gather(
-        jnp.concatenate(
-            [attention_adapter_up[:, j, :] for j in range(3)]
-            + [feedforward_adapter_up[:, j, :] for j in range(2)],
-            axis=1,
-        ),
-        "fsdp",
-    )
-    fc_up = ups[:, 3 * head_cols :]
-    weight_o = gather(attention_output_weight, 1)
-    weight_fc1 = gather(
-        jnp.concatenate(
-            [gate_up_weight[:, j, :] for j in range(2)] + [feedforward_adapter_down], axis=1
-        )
-    )
-    weight_fc2 = gather(down_weight, 1)
-    weight_zx = gather(
-        jnp.concatenate(
-            [gate_inner_weight[:, j, :] for j in range(2)]
-            + [jnp.pad(state_input_weight[:, j, :], ((0, 0), (0, LANES - states))) for j in range(2)]
-            + [jnp.pad(step_projection, ((0, 0), (0, LANES - mixer_heads)))],
-            axis=1,
-        )
-    )
-
-    weight_out = gather(mixer_output_weight, 1)
+    own_qkv = jnp.concatenate(
+        [query_key_value_weight[:, j, :] for j in range(3)]
+        + [attention_adapter_down[:, j, :] for j in range(3)],
+        axis=1,
+    )
+    weight_qkv = gather(own_qkv)
+    first_hop = tuple(hop(v) for v in (hidden, embed))
 
     small = [
         attention_norm_gain,
@@ -960,6 +941,21 @@
     cosine = jnp.concatenate([cosine, cosine], axis=1)
     sine = jnp.concatenate([-sine, sine], axis=1)
 
+    own_fc1 = jnp.concatenate(
+        [gate_up_weight[:, j, :] for j in range(2)] + [feedforward_adapter_down], axis=1
+    )
+    own_zx = jnp.concatenate(
+        [gate_inner_weight[:, j, :] for j in range(2)]
+        + [jnp.pad(state_input_weight[:, j, :], ((0, 0), (0, LANES - states))) for j in range(2)]
+        + [jnp.pad(step_projection, ((0, 0), (0, LANES - mixer_heads)))],
+        axis=1,
+    )
+    weight_o = gather(attention_output_weight, 1)
+    weight_fc1 = gather(own_fc1)
+    weight_fc2 = gather(down_weight, 1)
+    weight_zx = gather(own_zx)
+    weight_out = gather(mixer_output_weight, 1)
+
     def norm_rows(pair):
         pair = [v.astype(f32) for v in pair]
         squares = sum(jnp.sum(v * v, axis=1, keepdims=True) for v in pair)
@@ -969,16 +965,21 @@
             for i, v in enumerate(pair)
         ]
 
-    raw, normed = [(hidden, embed)], []
-    for p in range(1, tp):
+    raw, normed = [(hidden, embed), first_hop], []
+    for p in range(2, tp):
         moved = tuple(hop(v) for v in raw[-1])
-        if p > 1:
-            normed.append(norm_rows(raw[p - 2]))
-            moved = tie(moved, normed[-1])
-        raw.append(moved)
+        normed.append(norm_rows(raw[p - 2]))
+        raw.append(tie(moved, normed[-1]))
     normed += [norm_rows(v) for v in raw[len(normed) :]]
 
-    out_grad = [tie(output_cotangent, raw[-1][0])]
+    own_ups = jnp.concatenate(
+        [attention_adapter_up[:, j, :] for j in range(3)]
+        + [feedforward_adapter_up[:, j, :] for j in range(2)],
+        axis=1,
+    )
+    ups = doubling_gather(tie(own_ups, raw[-2]), "fsdp")
+    fc_up = ups[:, 3 * head_cols :]
+    out_grad = [tie(output_cotangent, raw[-1])]
     normed_parts, projected = [], []
     for i in range(tp - 1):
         moved = hop(out_grad[-1])
@@ -997,7 +998,7 @@
     attended, lora_rows, out_grad[-1] = lax.optimization_barrier((attended, lora_rows, moved))
     out_grad_rows = jnp.concatenate(out_grad, axis=0)
     normed_rows = jnp.concatenate(normed_parts, axis=0)
-    mixed, _ = ring_scatter(lambda p: mm(piece(attended, p), weight_o))
+    mixed, _ = ring_scatter(lambda p, t: mm(piece(after(attended, t), p), weight_o))
 
     mlp_root = inverse_root(mixed)
     gate_up, fc_mid, units = [], [], []
@@ -1075,7 +1076,7 @@
         ]
 
     grad_mixer_in, (sum_w_out, sum_w_zx, small) = ring_scatter(
-        lambda p: mm_nt(piece(grad_all, p), weight_zx),
+        lambda p, t: mm_nt(piece(after(grad_all, t), p), weight_zx),
         [
             lambda t, _: mm_tn(tie(scaled, t), out_grad_rows).astype(bf16),
             lambda t, _: mm_tn(tie(mixer_rows, t), grad_all).astype(bf16),
@@ -1141,15 +1142,16 @@
     )
     out, grad_projected, sum_w_fc1 = lax.optimization_barrier((out, grad_projected, sum_w_fc1))
     out = out.astype(f32) + out_terms[3 % tp].astype(f32)
+    out = hop(out.astype(bf16))
     sum_w_qkv = mm_tn(normed_rows, grad_projected).astype(bf16)
-    grad_projected = tie(grad_projected, sum_w_qkv)
+    out, sum_w_qkv, grad_projected = lax.optimization_barrier((out, sum_w_qkv, grad_projected))
     sum_w_qkv = scatter(sum_w_qkv)
 
     at_t = 2 * inner_cols + 2 * LANES
 
     def finish_out(token):
-        total = tie(out, token)
-        for p in range(4, tp + 1):
+        total = tie(out, token).astype(f32) + out_terms[4 % tp].astype(f32)
+        for p in range(5, tp + 1):
             total = hop(total.astype(bf16)).astype(f32) + out_terms[p % tp].astype(f32)
         return residual + total
 
@@ -1198,18 +1200,25 @@
     tasks, bc_sums = [], []
     pair = mm_nt(grad_projected[share : 3 * share], weight_qkv)
     grad_normed, (_, mixer_sums, feed_sums) = ring_scatter(
-        lambda p: piece(pair, p - 1) if p in (1, 2) else mm_nt(piece(grad_projected, p), weight_qkv),
+        lambda p, t: piece(pair, p - 1)
+        if p in (1, 2)
+        else mm_nt(piece(after(grad_projected, t), p), weight_qkv),
         [finish_adapters, finish_mixer, finish_feed],
         tasks,
     )
     grad_w_zx, grad_w_dt, grad_w_out, grad_w_fc2 = mixer_sums
     grad_w_fc1, grad_w_o, out = feed_sums
-    grad_hidden, grad_embed, grad_gain_attn = norm_back([hidden, embed], grad_normed, gain_attn, grad_residual)
-    gain_first = Halving(grad_gain_attn.reshape(fsdp, -1), "fsdp")
-    grad_gain_attn = Halving(gain_first.result().reshape(tp, -1), "tp").result()
-    grad_down = Halving(
-        sum_w_qkv[:, 3 * head_cols :].astype(f32).reshape(tp, -1, 3 * rank), "tp", bf16
-    ).result()
+    grad_hidden, grad_embed = norm_back(
+        [hidden, embed], grad_normed, gain_attn, grad_residual, with_gain=False
+    )
+    gain_rows = jnp.sum(sum_w_qkv.astype(f32) * own_qkv.astype(f32), axis=1)
+    gain_rows = gain_rows / attention_norm_gain.astype(f32)
+    down_task = Halving(sum_w_qkv[:, 3 * head_cols :].astype(f32).reshape(tp, -1, 3 * rank), "tp", bf16)
+    gain_last = Halving(gain_rows.reshape(tp, -1), "tp")
+    while down_task.live():
+        for t in begin([down_task, gain_last]):
+            t.finish()
+    grad_down, grad_gain_attn = down_task.result(), gain_last.result()
     grad_w_qkv = jnp.stack(
         [sum_w_qkv[:, j * head_cols : (j + 1) * head_cols].astype(f32) for j in range(3)], axis=1
     )

time: 1370 us -> 1340 us (0.978)
  waiting for transfers between devices: 467 us -> 434 us
    ppermute x3, waiting for transfers between devices: 39.4 us -> 17 us  [doubling_gather(): moved = lax.ppermute(values, name, [(i, i ^ step) for i in range(count)])]
    unnamed x290 -> x298, local copies, waits for them, and re-layouts: 52.8 us -> 55.8 us
  transfers between devices with their start and end apart: 74 -> 71, of which waited for: 39 -> 34; matrix products, arithmetic and copies ran while one was open for 44% -> 46% of each run, Pallas kernels for 9% -> 9%
where the time goes in v4:
time: 1340 us; the launch traced here: 1330 us
  matrix products  462 us (34%)
  waiting for transfers between devices  434 us (32%)
  Pallas kernels  139 us (10%)
  other arithmetic  113 us (8%)
  local copies, waits for them, and re-layouts  101 us (8%)
  starting transfers between devices  47.2 us (4%)
  blocking collectives  17.8 us (1%)
  between operations  17.2 us (1%)
    ppermute x39, waiting for transfers between devices, hop(): return lax.ppermute(values, 'tp', ring_pairs())  388 us
    dot_general x24, matrix products, mm_nt(): lax.dot_general(left, right, (((1,), (1,)), ((), ())), preferred_element_...  185 us
    dot_general x10, matrix products, mm_tn(): lax.dot_general(left, right, (((0,), (0,)), ((), ())), preferred_element_...  141 us
    dot_general x23, matrix products, mm(): return jnp.dot(left, right, preferred_element_type=f32)  136 us
    unnamed x298, local copies, waits for them, and re-layouts  55.8 us
    pallas_call x1, Pallas kernels, attention_backward(): pl.pallas_call(functools.partial(attention_backward_kernel, tp, heads), o...  39.2 us
    pallas_call x1, Pallas kernels, mixer_backward(): pl.pallas_call(functools.partial(mixer_backward_kernel, chunks), out_shap...  36.4 us
    ppermute x39, starting transfers between devices, hop(): return lax.ppermute(values, 'tp', ring_pairs())  28.3 us
  transfers between devices with their start and end apart: 71, of which 34 were waited for; matrix products, arithmetic and copies ran while one was open for 46% of the time, Pallas kernels for 9%

profile of v4, /device:TPU:0, one launch (start us, length us, event | category | flops | bytes accessed | tf_op | source)
XLA Modules:
  0.0 1331.7 jit_solution(1725174646149513893)
XLA Ops:
  40.3 9.3 all-gather.1
  59.6 17.9 %collective-permute-done = bf16[256,2048]{1,0:T(8,128)(2,1)} collective-permute-done((bf16[256,2048]{1,0:T(8,128)(2,1)S(1)}, bf16[256,2048]{1,0:T(8,128)(2,1)}, u32[]{:S(2)}, u32[]{:S(2)}) %collective-permute-start) | collective-permute-done | bytes 1048608 | tf_op jit(solution)/shard_map/ppermute | solution.py:689
  81.6 18.2 %collective-permute-done.3 = bf16[256,2048]{1,0:T(8,128)(2,1)S(1)} collective-permute-done((bf16[256,2048]{1,0:T(8,128)(2,1)S(1)}, bf16[256,2048]{1,0:T(8,128)(2,1)S(1)}, u32[]{:S(2)}, u32[]{:S(2)}) %collective-permute-start.3) | collective-permute-done | bytes 1048608 | tf_op jit(solution)/shard_map/ppermute | solution.py:689
  99.8 21.6 %collective-permute-done.1 = bf16[256,2048]{1,0:T(8,128)(2,1)S(1)} collective-permute-done((bf16[256,2048]{1,0:T(8,128)(2,1)}, bf16[256,2048]{1,0:T(8,128)(2,1)S(1)}, u32[]{:S(2)}, u32[]{:S(2)}) %collective-permute-start.1) | collective-permute-done | bytes 1048608 | tf_op jit(solution)/shard_map/ppermute | solution.py:689
  129.7 17.0 %collective-permute-done.5 = bf16[32,7168]{1,0:T(8,128)(2,1)S(1)} collective-permute-done((bf16[32,7168]{1,0:T(8,128)(2,1)S(1)}, bf16[32,7168]{1,0:T(8,128)(2,1)S(1)}, u32[]{:S(2)}, u32[]{:S(2)}) %collective-permute-start.5) | collective-permute-done | bytes 458784 | tf_op jit(solution)/shard_map/ppermute | solution.py:831
  149.8 22.1 %collective-permute-done.8 = bf16[256,2048]{1,0:T(8,128)(2,1)S(1)} collective-permute-done((bf16[256,2048]{1,0:T(8,128)(2,1)S(1)}, bf16[256,2048]{1,0:T(8,128)(2,1)S(1)}, u32[]{:S(2)}, u32[]{:S(2)}) %collective-permute-start.8) | collective-permute-done | bytes 1048608 | tf_op jit(solution)/shard_map/ppermute | solution.py:689
  175.8 22.1 %fusion.70.refs_0_.refs_1_.refs_2_.refs_3_ = f32[512,3456]{1,0:T(8,128)S(1)} fusion(bf16[4096,3456]{1,0:T(8,128)(2,1)} %all-gather.9.cloned.1.call-done, bf16[256,2048]{1,0:T(8,128)(2,1)} %get-tuple-element.447, bf16[256,2048]{1,0:T(8,128)(2,1)} %get-tuple-element.457, bf16[256,2048]{1,0:T(8,128)(2,1)} %get-tuple-element.461, ...), kind=kOutput, calls=%fused_computation.83 | convolution fusion | flops 14512291840 | bytes 39583744 | tf_op jit(solution)/shard_map/dot_general | solution.py:25
  198.9 23.2 %fusion.78.refs_4_.refs_5_.refs_6_.refs_7_ = f32[512,3456]{1,0:T(8,128)S(1)} fusion(bf16[4096,3456]{1,0:T(8,128)(2,1)} %all-gather.9.cloned.1.call-done, bf16[256,2048]{1,0:T(8,128)(2,1)} %get-tuple-element.460, bf16[256,2048]{1,0:T(8,128)(2,1)} %get-tuple-element.459, bf16[256,2048]{1,0:T(8,128)(2,1)S(1)} %copy-done.54, ...), kind=kOutput, calls=%fused_computation.91 | convolution fusion | flops 14512291840 | bytes 39583744 | tf_op jit(solution)/shard_map/dot_general | solution.py:25
  227.5 26.9 %attention_forward.1 = (bf16[1024,1024]{1,0:T(8,128)(2,1)}, bf16[1024,1024]{1,0:T(8,128)(2,1)}, bf16[1024,1024]{1,0:T(8,128)(2,1)}, bf16[1024,1024]{1,0:T(8,128)(2,1)}) custom-call(s32[1]{0:T(128)} %bitcast.place_ref, s32[3]{0:T(128)} %bitcast.257, f32[1024,128]{1,0:T(8,128)} %get-tuple-element.463.cosine_ref, f32[1024,128]{1,0:T(8,128)} %get-tuple-element.464.sine_ref, ...), custom_call_target="tpu_custom_call" | custom-call | flops 4294967296 | bytes 20971520 | tf_op jit(solution)/shard_map/attention_forward/pallas_call | solution.py:119
  261.2 22.9 %collective-permute-done.12 = bf16[256,2048]{1,0:T(8,128)(2,1)S(1)} collective-permute-done((bf16[256,2048]{1,0:T(8,128)(2,1)S(1)}, bf16[256,2048]{1,0:T(8,128)(2,1)S(1)}, u32[]{:S(2)}, u32[]{:S(2)}) %collective-permute-start.12) | collective-permute-done | bytes 1048608 | tf_op jit(solution)/shard_map/ppermute | solution.py:689
  288.8 20.7 %collective-permute-done.13 = bf16[256,2048]{1,0:T(8,128)(2,1)} collective-permute-done((bf16[256,2048]{1,0:T(8,128)(2,1)S(1)}, bf16[256,2048]{1,0:T(8,128)(2,1)}, u32[]{:S(2)}, u32[]{:S(2)}) %collective-permute-start.13) | collective-permute-done | bytes 1048608 | tf_op jit(solution)/shard_map/ppermute | solution.py:689
  316.7 19.7 %collective-permute-done.14 = bf16[256,2048]{1,0:T(8,128)(2,1)} collective-permute-done((bf16[256,2048]{1,0:T(8,128)(2,1)}, bf16[256,2048]{1,0:T(8,128)(2,1)}, u32[]{:S(2)}, u32[]{:S(2)}) %collective-permute-start.14) | collective-permute-done | bytes 1048608 | tf_op jit(solution)/shard_map/ppermute | solution.py:689
  339.7 9.2 fusion.298
  384.0 9.2 collective-permute-done.17
  416.5 21.6 %collective-permute-done.19 = bf16[256,2048]{1,0:T(8,128)(2,1)S(1)} collective-permute-done((bf16[256,2048]{1,0:T(8,128)(2,1)S(1)}, bf16[256,2048]{1,0:T(8,128)(2,1)S(1)}, u32[]{:S(2)}, u32[]{:S(2)}) %collective-permute-start.19) | collective-permute-done | bytes 1048608 | tf_op jit(solution)/shard_map/ppermute | solution.py:689
  438.1 9.3 fusion.302
  469.8 16.9 %collective-permute-done.20 = bf16[256,2048]{1,0:T(8,128)(2,1)} collective-permute-done((bf16[256,2048]{1,0:T(8,128)(2,1)S(1)}, bf16[256,2048]{1,0:T(8,128)(2,1)}, u32[]{:S(2)}, u32[]{:S(2)}) %collective-permute-start.20) | collective-permute-done | bytes 1048608 | tf_op jit(solution)/shard_map/ppermute | solution.py:689
  490.2 8.5 fusion.304
  506.9 9.0 collective-permute-done.21
  522.9 17.6 %collective-permute-done.22 = bf16[256,2048]{1,0:T(8,128)(2,1)S(1)} collective-permute-done((bf16[256,2048]{1,0:T(8,128)(2,1)}, bf16[256,2048]{1,0:T(8,128)(2,1)S(1)}, u32[]{:S(2)}, u32[]{:S(2)}) %collective-permute-start.22) | collective-permute-done | bytes 1048608 | tf_op jit(solution)/shard_map/ppermute | solution.py:689
  544.8 19.5 %collective-permute-done.23 = bf16[256,2048]{1,0:T(8,128)(2,1)S(1)} collective-permute-done((bf16[256,2048]{1,0:T(8,128)(2,1)S(1)}, bf16[256,2048]{1,0:T(8,128)(2,1)S(1)}, u32[]{:S(2)}, u32[]{:S(2)}) %collective-permute-start.23) | collective-permute-done | bytes 1048608 | tf_op jit(solution)/shard_map/ppermute | solution.py:689
  571.2 17.6 %mixer_forward.1 = (bf16[1024,1024]{1,0:T(8,128)(2,1)}, bf16[8,64,1024]{2,1,0:T(8,128)(2,1)}) custom-call(s32[1]{0:T(128)} %bitcast.place_ref, s32[3]{0:T(128)} %bitcast.258, bf16[1024,2048]{1,0:T(8,128)(2,1)} %pad_maximum_fusion.zx.before, bf16[1024,2048]{1,0:T(8,128)(2,1)} %pad_maximum_fusion.zx.before, f32[1024,384]{1,0:T(8,128)} %pad_maximum_fusion.8.sd.sd_before, ...), custom_call_target="tpu_custom_call" | custom-call | flops 1073741824 | bytes 8388608 | tf_op jit(solution)/shard_map/mixer_forward/pallas_call | solution.py:530
  591.7 8.5 psum.7
  612.9 36.4 %mixer_backward.1 = (bf16[1024,2432]{1,0:T(8,128)(2,1)}, f32[8,1024]{1,0:T(8,128)}, f32[8,256]{1,0:T(8,128)}, f32[8,128]{1,0:T(8,128)}) custom-call(s32[1]{0:T(128)} %bitcast.place_ref, s32[3]{0:T(128)} %bitcast.259, bf16[1024,2048]{1,0:T(8,128)(2,1)} %pad_maximum_fusion.zx.before, bf16[1024,2048]{1,0:T(8,128)(2,1)} %pad_maximum_fusion.zx.before, ...), custom_call_target="tpu_custom_call" | custom-call | flops 3221225472 | bytes 12582912 | tf_op jit(solution)/shard_map/mixer_backward/pallas_call | solution.py:567
  649.4 8.5 convolution_convert_fusion.7
  683.8 16.2 %convolution_convert_fusion.2 = bf16[2048,2432]{1,0:T(8,128)(2,1)} fusion(bf16[1024,2048]{1,0:T(8,128)(2,1)S(1)} %pad_maximum_fusion.1, bf16[1024,2432]{1,0:T(8,128)(2,1)} %get-tuple-element.233), kind=kOutput, calls=%fused_computation.2 | convolution fusion | flops 10205528064 | bytes 19136512 | tf_op jit(solution)/shard_map/dot_general | solution.py:33
  700.0 8.4 fusion.222
  724.0 8.9 collective-permute-done.28
  743.1 9.3 fusion.166
  754.4 13.6 %fusion.115 = f32[256,2048]{1,0:T(8,128)} fusion(bf16[2048,4224]{1,0:T(8,128)(2,1)} %all-gather.13.cloned.1.call-done, bf16[256,128]{1,0:T(8,128)(2,1)S(1)} %fusion.233, bf16[256,2048]{1,0:T(8,128)(2,1)} %copy-done.111, bf16[256,2048]{1,0:T(8,128)(2,1)} %copy-done.110), kind=kOutput, calls=%fused_computation.187 | convolution fusion | flops 4435673088 | bytes 21561344 | tf_op jit(solution)/shard_map/dot_general | solution.py:29
  780.1 12.7 convolution_convert_fusion.6
  807.9 9.2 fusion.121
  821.4 10.7 collective-permute-done.35
  832.1 14.0 %convolution_convert_fusion.3 = bf16[2048,2048]{1,0:T(8,128)(2,1)} fusion(bf16[1024,2048]{1,0:T(8,128)(2,1)} %pad_maximum_fusion.2, bf16[256,2048]{1,0:T(8,128)(2,1)} %collective-permute-done.35, bf16[256,2048]{1,0:T(8,128)(2,1)} %collective-permute-done.32, bf16[256,2048]{1,0:T(8,128)(2,1)} %collective-permute-done.29, ...), kind=kOutput, calls=%fused_computation.65 | convolution fusion | flops 8610906112 | bytes 16777216 | tf_op jit(solution)/shard_map/dot_general | solution.py:33
  857.9 10.3 fusion.127
  872.6 29.2 %convolution_convert_fusion.1 = bf16[2048,4224]{1,0:T(8,128)(2,1)} fusion(bf16[1024,2048]{1,0:T(8,128)(2,1)} %copy-done.71, bf16[256,128]{1,0:T(8,128)(2,1)S(1)} %fusion.227, bf16[256,2048]{1,0:T(8,128)(2,1)} %copy-done.117, bf16[256,2048]{1,0:T(8,128)(2,1)} %copy-done.116, bf16[256,128]{1,0:T(8,128)(2,1)S(1)} %fusion.230, ...), kind=kOutput, calls=%fused_computation.1 | convolution fusion | flops 17829199872 | bytes 30146560 | tf_op jit(solution)/shard_map/dot_general | solution.py:33
  918.9 15.9 %fusion.23 = f32[128,4096]{1,0:T(8,128)} fusion(bf16[1024,128]{1,0:T(8,128)(2,1)S(1)} %pad_maximum_fusion.15, bf16[256,128]{1,0:T(8,128)(2,1)S(1)} %copy-done.123, bf16[256,2048]{1,0:T(8,128)(2,1)} %copy-done.117, bf16[256,2048]{1,0:T(8,128)(2,1)} %copy-done.116, bf16[256,128]{1,0:T(8,128)(2,1)S(1)} %copy-done.121, bf16[256,2048]{1,0:T(8,128)(2,1)} %copy-done.115, ...), kind=kOutput, calls=%fused_computation.26 | convolution fusion | flops 1174405120 | bytes 11010048 | tf_op jit(solution)/shard_map/dot_general | solution.py:33
  942.8 19.4 %collective-permute-done.40 = bf16[256,2048]{1,0:T(8,128)(2,1)} collective-permute-done((bf16[256,2048]{1,0:T(8,128)(2,1)S(1)}, bf16[256,2048]{1,0:T(8,128)(2,1)}, u32[]{:S(2)}, u32[]{:S(2)}) %collective-permute-start.40) | collective-permute-done | bytes 1048608 | tf_op jit(solution)/shard_map/ppermute | solution.py:689
  969.0 21.4 %collective-permute-done.42 = bf16[256,2048]{1,0:T(8,128)(2,1)} collective-permute-done((bf16[256,2048]{1,0:T(8,128)(2,1)}, bf16[256,2048]{1,0:T(8,128)(2,1)}, u32[]{:S(2)}, u32[]{:S(2)}) %collective-permute-start.42) | collective-permute-done | bytes 1048608 | tf_op jit(solution)/shard_map/ppermute | solution.py:689
  990.4 8.8 fusion.101
  1004.0 39.2 %attention_backward.1 = bf16[1024,3456]{1,0:T(8,128)(2,1)} custom-call(s32[1]{0:T(128)} %bitcast.place_ref, s32[3]{0:T(128)} %bitcast.260, f32[1024,128]{1,0:T(8,128)} %get-tuple-element.463.cosine_ref, f32[1024,128]{1,0:T(8,128)} %get-tuple-element.464.sine_ref, bf16[1024,1024]{1,0:T(8,128)(2,1)} %get-tuple-element.221.q_ref, ...), custom_call_target="tpu_custom_call" | custom-call | flops 10737418240 | bytes 14680064 | tf_op jit(solution)/shard_map/attention_backward/pallas_call | solution.py:233
  1046.3 48.9 %convolution_convert_fusion = bf16[4096,3456]{1,0:T(8,128)(2,1)} fusion(bf16[1024,3456]{1,0:T(8,128)(2,1)} %attention_backward.1, bf16[256,2048]{1,0:T(8,128)(2,1)} %get-tuple-element.460, bf16[256,2048]{1,0:T(8,128)(2,1)} %get-tuple-element.459, bf16[256,2048]{1,0:T(8,128)(2,1)S(1)} %copy-done.55, bf16[256,2048]{1,0:T(8,128)(2,1)} %get-tuple-element.458, ...), kind=kOutput, calls=%fused_computation | convolution fusion | flops 29072293888 | bytes 43778048 | tf_op jit(solution)/shard_map/dot_general | solution.py:33
  1099.1 21.3 %fusion.104 = f32[512,4096]{1,0:T(8,128)S(1)} fusion(bf16[4096,3456]{1,0:T(8,128)(2,1)} %all-gather.9.cloned.1.call-done, bf16[1024,3456]{1,0:T(8,128)(2,1)} %attention_backward.1), kind=kOutput, calls=%fused_computation.145 | convolution fusion | flops 14495514624 | bytes 40239104 | tf_op jit(solution)/shard_map/dot_general | solution.py:29
  1129.3 37.9 %collective-permute-done.45 = bf16[256,4096]{1,0:T(8,128)(2,1)S(1)} collective-permute-done((bf16[256,4096]{1,0:T(8,128)(2,1)S(1)}, bf16[256,4096]{1,0:T(8,128)(2,1)S(1)}, u32[]{:S(2)}, u32[]{:S(2)}) %collective-permute-start.45) | collective-permute-done | bytes 2097184 | tf_op jit(solution)/shard_map/ppermute | solution.py:689
  1169.2 16.0 %fusion.218 = f32[256,4096]{1,0:T(8,128)} fusion(bf16[4096,3456]{1,0:T(8,128)(2,1)} %all-gather.9.cloned.1.call-done, bf16[1024,3456]{1,0:T(8,128)(2,1)S(1)} %bitcast.216), kind=kOutput, calls=%fused_computation.324 | convolution fusion | flops 7247757312 | bytes 34275328 | tf_op jit(solution)/shard_map/dot_general | solution.py:29
  1193.3 21.8 %collective-permute-done.46 = bf16[256,4096]{1,0:T(8,128)(2,1)} collective-permute-done((bf16[256,4096]{1,0:T(8,128)(2,1)}, bf16[256,4096]{1,0:T(8,128)(2,1)}, u32[]{:S(2)}, u32[]{:S(2)}) %collective-permute-start.46) | collective-permute-done | bytes 2097184 | tf_op jit(solution)/shard_map/ppermute | solution.py:689
  1230.6 16.8 %fusion.216 = f32[256,4096]{1,0:T(8,128)} fusion(bf16[4096,3456]{1,0:T(8,128)(2,1)} %all-gather.9.cloned.1.call-done, bf16[1024,3456]{1,0:T(8,128)(2,1)} %attention_backward.1), kind=kOutput, calls=%fused_computation.322 | convolution fusion | flops 7247757312 | bytes 34275328 | tf_op jit(solution)/shard_map/dot_general | solution.py:29
  1259.2 8.6 collective-permute-done.57
  (708 shorter events, 462.6 us)
Async XLA Ops:
  7.2 168.6 %all-gather.9.cloned.1.call-start = ((), (), s32[]{:S(2)}) async-start(), calls=%async_computation.6 | async-start | bytes 31850496 | tf_op jit(solution)/shard_map/all_gather | solution.py:845
  15.8 238.6 %all-gather.11.cloned.1.call-start = ((), (), s32[]{:S(2)}) async-start(), calls=%async_computation.7 | async-start | bytes 4718592 | tf_op jit(solution)/shard_map/all_gather | solution.py:845
  16.6 323.1 %all-gather.13.cloned.1.call-start = ((), (), s32[]{:S(2)}) async-start(), calls=%async_computation.8 | async-start | bytes 19464192 | tf_op jit(solution)/shard_map/all_gather | solution.py:845
  25.2 332.6 %all-gather.15.cloned.1.call-start = ((), (), s32[]{:S(2)}) async-start(), calls=%async_computation.9 | async-start | bytes 9437184 | tf_op jit(solution)/shard_map/all_gather | solution.py:845
  25.7 464.5 %all-gather.17.cloned.1.call-start = ((), (), s32[]{:S(2)}) async-start(), calls=%async_computation.10 | async-start | bytes 11206656 | tf_op jit(solution)/shard_map/all_gather | solution.py:845
  25.8 32.2 %collective-permute-start.2 = (bf16[256,2048]{1,0:T(8,128)(2,1)S(1)}, bf16[256,2048]{1,0:T(8,128)(2,1)S(1)}, u32[]{:S(2)}, u32[]{:S(2)}) collective-permute-start(bf16[256,2048]{1,0:T(8,128)(2,1)S(1)} %copy-done.11), channel_id=1, source_target_pairs={{0,1},{1,2},{2,3},{3,0},{4,5},{5,6},{6,7},{7,4},{8,9},{9,10},{10,1... | collective-permute-start | bytes 3145736 | tf_op jit(solution)/shard_map/ppermute | solution.py:689
  28.9 48.6 %collective-permute-start = (bf16[256,2048]{1,0:T(8,128)(2,1)S(1)}, bf16[256,2048]{1,0:T(8,128)(2,1)}, u32[]{:S(2)}, u32[]{:S(2)}) collective-permute-start(bf16[256,2048]{1,0:T(8,128)(2,1)S(1)} %copy-done.9), channel_id=1, source_target_pairs={{0,1},{1,2},{2,3},{3,0},{4,5},{5,6},{6,7},{7,4},{8,9},{9,10},{10,1... | collective-permute-start | bytes 3145736 | tf_op jit(solution)/shard_map/ppermute | solution.py:689
  38.2 460.5 %all-gather.19.cloned.1.call-start = ((), (), s32[]{:S(2)}) async-start(), calls=%async_computation.11 | async-start | bytes 4718592 | tf_op jit(solution)/shard_map/all_gather | solution.py:845
  58.0 41.8 %collective-permute-start.3 = (bf16[256,2048]{1,0:T(8,128)(2,1)S(1)}, bf16[256,2048]{1,0:T(8,128)(2,1)S(1)}, u32[]{:S(2)}, u32[]{:S(2)}) collective-permute-start(bf16[256,2048]{1,0:T(8,128)(2,1)S(1)} %collective-permute-done.2), channel_id=1, source_target_pairs={{0,1},{1,2},{2,3},{3,0},{4,5},{5,6},{6,7},{7,4},{8,9},{9,10},{10,1... | collective-permute-start | bytes 3145736 | tf_op jit(solution)/shard_map/ppermute | solution.py:689
  77.5 44.0 %collective-permute-start.1 = (bf16[256,2048]{1,0:T(8,128)(2,1)}, bf16[256,2048]{1,0:T(8,128)(2,1)S(1)}, u32[]{:S(2)}, u32[]{:S(2)}) collective-permute-start(bf16[256,2048]{1,0:T(8,128)(2,1)} %collective-permute-done), channel_id=1, source_target_pairs={{0,1},{1,2},{2,3},{3,0},{4,5},{5,6},{6,7},{7,4},{8,9},{9,10},{10,1... | collective-permute-start | bytes 3145736 | tf_op jit(solution)/shard_map/ppermute | solution.py:689
  122.0 27.8 %collective-permute-start.7 = (bf16[256,2048]{1,0:T(8,128)(2,1)S(1)}, bf16[256,2048]{1,0:T(8,128)(2,1)S(1)}, u32[]{:S(2)}, u32[]{:S(2)}) collective-permute-start(bf16[256,2048]{1,0:T(8,128)(2,1)S(1)} %collective-permute-done.1), channel_id=1, source_target_pairs={{0,1},{1,2},{2,3},{3,0},{4,5},{5,6},{6,7},{7,4},{8,9},{9,10},{10,1... | collective-permute-start | bytes 3145736 | tf_op jit(solution)/shard_map/ppermute | solution.py:689
  122.0 49.8 %collective-permute-start.8 = (bf16[256,2048]{1,0:T(8,128)(2,1)S(1)}, bf16[256,2048]{1,0:T(8,128)(2,1)S(1)}, u32[]{:S(2)}, u32[]{:S(2)}) collective-permute-start(bf16[256,2048]{1,0:T(8,128)(2,1)S(1)} %collective-permute-done.3), channel_id=1, source_target_pairs={{0,1},{1,2},{2,3},{3,0},{4,5},{5,6},{6,7},{7,4},{8,9},{9,10},{10,1... | collective-permute-start | bytes 3145736 | tf_op jit(solution)/shard_map/ppermute | solution.py:689
  147.0 27.5 %collective-permute-start.6 = (bf16[64,7168]{1,0:T(8,128)(2,1)S(1)}, bf16[64,7168]{1,0:T(8,128)(2,1)S(1)}, u32[]{:S(2)}, u32[]{:S(2)}) collective-permute-start(bf16[64,7168]{1,0:T(8,128)(2,1)S(1)} %pad_maximum_fusion.9), channel_id=1, source_target_pairs={{0,16},{4,20},{8,24},{12,28},{16,0},{20,4},{24,8},{28,12},{1,17},{... | collective-permute-start | bytes 2752520 | tf_op jit(solution)/shard_map/ppermute | solution.py:831
  171.8 26.9 %collective-permute-start.9 = (bf16[256,2048]{1,0:T(8,128)(2,1)}, bf16[256,2048]{1,0:T(8,128)(2,1)}, u32[]{:S(2)}, u32[]{:S(2)}) collective-permute-start(bf16[256,2048]{1,0:T(8,128)(2,1)} %refs_3_.1), channel_id=1, source_target_pairs={{0,1},{1,2},{2,3},{3,0},{4,5},{5,6},{6,7},{7,4},{8,9},{9,10},{10,1... | collective-permute-start | bytes 3145736 | tf_op jit(solution)/shard_map/ppermute | solution.py:689
  198.7 26.1 %collective-permute-start.10 = (bf16[256,2048]{1,0:T(8,128)(2,1)}, bf16[256,2048]{1,0:T(8,128)(2,1)}, u32[]{:S(2)}, u32[]{:S(2)}) collective-permute-start(bf16[256,2048]{1,0:T(8,128)(2,1)} %collective-permute-done.9), channel_id=1, source_target_pairs={{0,1},{1,2},{2,3},{3,0},{4,5},{5,6},{6,7},{7,4},{8,9},{9,10},{10,1... | collective-permute-start | bytes 3145736 | tf_op jit(solution)/shard_map/ppermute | solution.py:689
  224.8 29.5 %collective-permute-start.11 = (bf16[256,2048]{1,0:T(8,128)(2,1)}, bf16[256,2048]{1,0:T(8,128)(2,1)}, u32[]{:S(2)}, u32[]{:S(2)}) collective-permute-start(bf16[256,2048]{1,0:T(8,128)(2,1)} %collective-permute-done.10), channel_id=1, source_target_pairs={{0,1},{1,2},{2,3},{3,0},{4,5},{5,6},{6,7},{7,4},{8,9},{9,10},{10,1... | collective-permute-start | bytes 3145736 | tf_op jit(solution)/shard_map/ppermute | solution.py:689
  258.2 25.9 %collective-permute-start.12 = (bf16[256,2048]{1,0:T(8,128)(2,1)S(1)}, bf16[256,2048]{1,0:T(8,128)(2,1)S(1)}, u32[]{:S(2)}, u32[]{:S(2)}) collective-permute-start(bf16[256,2048]{1,0:T(8,128)(2,1)S(1)} %convolution_convert_fusion.8), channel_id=1, source_target_pairs={{0,1},{1,2},{2,3},{3,0},{4,5},{5,6},{6,7},{7,4},{8,9},{9,10},{10,1... | collective-permute-start | bytes 3145736 | tf_op jit(solution)/shard_map/ppermute | solution.py:689
  284.5 547.7 %reduce-scatter.7.cloned.1.call-start = ((), (), s32[]{:S(2)}) async-start(), calls=%async_computation.12 | async-start | bytes 4718592 | tf_op jit(solution)/shard_map/reduce_scatter | solution.py:849
  339.6 25.4 %collective-permute-start.15 = (bf16[256,2048]{1,0:T(8,128)(2,1)S(1)}, bf16[256,2048]{1,0:T(8,128)(2,1)}, u32[]{:S(2)}, u32[]{:S(2)}) collective-permute-start(bf16[256,2048]{1,0:T(8,128)(2,1)S(1)} %multiply_convert_fusion.5), channel_id=1, source_target_pairs={{0,1},{1,2},{2,3},{3,0},{4,5},{5,6},{6,7},{7,4},{8,9},{9,10},{10,1... | collective-permute-start | bytes 3145736 | tf_op jit(solution)/shard_map/ppermute | solution.py:689
  365.0 28.2 %collective-permute-start.17 = (bf16[256,2048]{1,0:T(8,128)(2,1)}, bf16[256,2048]{1,0:T(8,128)(2,1)S(1)}, u32[]{:S(2)}, u32[]{:S(2)}) collective-permute-start(bf16[256,2048]{1,0:T(8,128)(2,1)} %collective-permute-done.15), channel_id=1, source_target_pairs={{0,1},{1,2},{2,3},{3,0},{4,5},{5,6},{6,7},{7,4},{8,9},{9,10},{10,1... | collective-permute-start | bytes 3145736 | tf_op jit(solution)/shard_map/ppermute | solution.py:689
  382.6 33.0 %collective-permute-start.16 = (bf16[256,2048]{1,0:T(8,128)(2,1)S(1)}, bf16[256,2048]{1,0:T(8,128)(2,1)S(1)}, u32[]{:S(2)}, u32[]{:S(2)}) collective-permute-start(bf16[256,2048]{1,0:T(8,128)(2,1)S(1)} %convolution_convert_fusion.9), channel_id=1, source_target_pairs={{0,1},{1,2},{2,3},{3,0},{4,5},{5,6},{6,7},{7,4},{8,9},{9,10},{10,1... | collective-permute-start | bytes 3145736 | tf_op jit(solution)/shard_map/ppermute | solution.py:689
  393.2 44.9 %collective-permute-start.19 = (bf16[256,2048]{1,0:T(8,128)(2,1)S(1)}, bf16[256,2048]{1,0:T(8,128)(2,1)S(1)}, u32[]{:S(2)}, u32[]{:S(2)}) collective-permute-start(bf16[256,2048]{1,0:T(8,128)(2,1)S(1)} %collective-permute-done.17), channel_id=1, source_target_pairs={{0,1},{1,2},{2,3},{3,0},{4,5},{5,6},{6,7},{7,4},{8,9},{9,10},{10,1... | collective-permute-start | bytes 3145736 | tf_op jit(solution)/shard_map/ppermute | solution.py:689
  416.0 43.9 %collective-permute-start.18 = (bf16[256,2048]{1,0:T(8,128)(2,1)S(1)}, bf16[256,2048]{1,0:T(8,128)(2,1)S(1)}, u32[]{:S(2)}, u32[]{:S(2)}) collective-permute-start(bf16[256,2048]{1,0:T(8,128)(2,1)S(1)} %add_convert_fusion.9), channel_id=1, source_target_pairs={{0,1},{1,2},{2,3},{3,0},{4,5},{5,6},{6,7},{7,4},{8,9},{9,10},{10,1... | collective-permute-start | bytes 3145736 | tf_op jit(solution)/shard_map/ppermute | solution.py:689
  460.2 26.5 %collective-permute-start.20 = (bf16[256,2048]{1,0:T(8,128)(2,1)S(1)}, bf16[256,2048]{1,0:T(8,128)(2,1)}, u32[]{:S(2)}, u32[]{:S(2)}) collective-permute-start(bf16[256,2048]{1,0:T(8,128)(2,1)S(1)} %add_convert_fusion.8), channel_id=1, source_target_pairs={{0,1},{1,2},{2,3},{3,0},{4,5},{5,6},{6,7},{7,4},{8,9},{9,10},{10,1... | collective-permute-start | bytes 3145736 | tf_op jit(solution)/shard_map/ppermute | solution.py:689
  490.0 25.9 %collective-permute-start.21 = (bf16[256,2048]{1,0:T(8,128)(2,1)}, bf16[256,2048]{1,0:T(8,128)(2,1)}, u32[]{:S(2)}, u32[]{:S(2)}) collective-permute-start(bf16[256,2048]{1,0:T(8,128)(2,1)} %multiply_convert_fusion.4), channel_id=1, source_target_pairs={{0,1},{1,2},{2,3},{3,0},{4,5},{5,6},{6,7},{7,4},{8,9},{9,10},{10,1... | collective-permute-start | bytes 3145736 | tf_op jit(solution)/shard_map/ppermute | solution.py:689
  609.5 39.8 %collective-permute-start.24 = (bf16[256,2048]{1,0:T(8,128)(2,1)S(1)}, bf16[256,2048]{1,0:T(8,128)(2,1)S(1)}, u32[]{:S(2)}, u32[]{:S(2)}) collective-permute-start(bf16[256,2048]{1,0:T(8,128)(2,1)S(1)} %slice.562), channel_id=1, source_target_pairs={{0,1},{1,2},{2,3},{3,0},{4,5},{5,6},{6,7},{7,4},{8,9},{9,10},{10,1... | collective-permute-start | bytes 3145736 | tf_op jit(solution)/shard_map/ppermute | solution.py:689
  678.6 238.9 %reduce-scatter.9.cloned.1.call-start = ((), (), s32[]{:S(2)}) async-start(), calls=%async_computation.13 | async-start | bytes 11206656 | tf_op jit(solution)/shard_map/reduce_scatter | solution.py:849
  709.5 259.5 %reduce-scatter.11.cloned.1.call-start = ((), (), s32[]{:S(2)}) async-start(), calls=%async_computation.14 | async-start | bytes 9437184 | tf_op jit(solution)/shard_map/reduce_scatter | solution.py:849
  733.0 35.0 %collective-permute-start.30 = (f32[4,864]{1,0:T(4,128)S(1)}, f32[4,864]{1,0:T(4,128)S(1)}, u32[]{:S(2)}, u32[]{:S(2)}) collective-permute-start(f32[4,864]{1,0:T(4,128)S(1)} %slice_select_fusion.2), channel_id=1, source_target_pairs={{0,16},{4,20},{8,24},{12,28},{16,0},{20,4},{24,8},{28,12},{1,17},{... | collective-permute-start | bytes 41480 | tf_op jit(solution)/shard_map/ppermute | solution.py:706
  768.1 26.5 %collective-permute-start.33 = (f32[2,864]{1,0:T(2,128)S(1)}, f32[2,864]{1,0:T(2,128)S(1)}, u32[]{:S(2)}, u32[]{:S(2)}) collective-permute-start(f32[2,864]{1,0:T(2,128)S(1)} %broadcast_select_fusion.8), channel_id=1, source_target_pairs={{0,8},{4,12},{8,0},{12,4},{16,24},{20,28},{24,16},{28,20},{1,9},{5... | collective-permute-start | bytes 20744 | tf_op jit(solution)/shard_map/ppermute | solution.py:706
  792.8 26.1 %collective-permute-start.31 = (bf16[256,2048]{1,0:T(8,128)(2,1)}, bf16[256,2048]{1,0:T(8,128)(2,1)}, u32[]{:S(2)}, u32[]{:S(2)}) collective-permute-start(bf16[256,2048]{1,0:T(8,128)(2,1)} %convolution_convert_fusion.6), channel_id=1, source_target_pairs={{0,1},{1,2},{2,3},{3,0},{4,5},{5,6},{6,7},{7,4},{8,9},{9,10},{10,1... | collective-permute-start | bytes 3145736 | tf_op jit(solution)/shard_map/ppermute | solution.py:689
  794.6 26.8 %collective-permute-start.36 = (f32[1,864]{1,0:T(1,128)S(1)}, f32[1,864]{1,0:T(1,128)S(1)}, u32[]{:S(2)}, u32[]{:S(2)}) collective-permute-start(f32[1,864]{1,0:T(1,128)S(1)} %broadcast_select_fusion.7), channel_id=1, source_target_pairs={{0,4},{4,0},{8,12},{12,8},{16,20},{20,16},{24,28},{28,24},{1,5},{5... | collective-permute-start | bytes 10376 | tf_op jit(solution)/shard_map/ppermute | solution.py:706
  794.7 37.4 %collective-permute-start.35 = (bf16[256,2048]{1,0:T(8,128)(2,1)}, bf16[256,2048]{1,0:T(8,128)(2,1)}, u32[]{:S(2)}, u32[]{:S(2)}) collective-permute-start(bf16[256,2048]{1,0:T(8,128)(2,1)} %collective-permute-done.32), channel_id=1, source_target_pairs={{0,1},{1,2},{2,3},{3,0},{4,5},{5,6},{6,7},{7,4},{8,9},{9,10},{10,1... | collective-permute-start | bytes 3145736 | tf_op jit(solution)/shard_map/ppermute | solution.py:689
  846.2 197.0 %reduce-scatter.13.cloned.1.call-start = ((), (), s32[]{:S(2)}) async-start(), calls=%async_computation.15 | async-start | bytes 19464192 | tf_op jit(solution)/shard_map/reduce_scatter | solution.py:849
  870.8 31.1 %collective-permute-start.37 = (bf16[256,2048]{1,0:T(8,128)(2,1)}, bf16[256,2048]{1,0:T(8,128)(2,1)S(1)}, u32[]{:S(2)}, u32[]{:S(2)}) collective-permute-start(bf16[256,2048]{1,0:T(8,128)(2,1)} %add_convert_fusion.3), channel_id=1, source_target_pairs={{0,1},{1,2},{2,3},{3,0},{4,5},{5,6},{6,7},{7,4},{8,9},{9,10},{10,1... | collective-permute-start | bytes 3145736 | tf_op jit(solution)/shard_map/ppermute | solution.py:689
  901.9 316.8 %reduce-scatter.15.cloned.1.call-start = ((), (), s32[]{:S(2)}) async-start(), calls=%async_computation.16 | async-start | bytes 4718592 | tf_op jit(solution)/shard_map/reduce_scatter | solution.py:849
  962.2 28.2 %collective-permute-start.42 = (bf16[256,2048]{1,0:T(8,128)(2,1)}, bf16[256,2048]{1,0:T(8,128)(2,1)}, u32[]{:S(2)}, u32[]{:S(2)}) collective-permute-start(bf16[256,2048]{1,0:T(8,128)(2,1)} %collective-permute-done.40), channel_id=1, source_target_pairs={{0,1},{1,2},{2,3},{3,0},{4,5},{5,6},{6,7},{7,4},{8,9},{9,10},{10,1... | collective-permute-start | bytes 3145736 | tf_op jit(solution)/shard_map/ppermute | solution.py:689
  964.8 78.4 %collective-permute-start.25 = (bf16[256,2048]{1,0:T(8,128)(2,1)}, bf16[256,2048]{1,0:T(8,128)(2,1)}, u32[]{:S(2)}, u32[]{:S(2)}) collective-permute-start(bf16[256,2048]{1,0:T(8,128)(2,1)} %add_convert_fusion.7), channel_id=1, source_target_pairs={{0,1},{1,2},{2,3},{3,0},{4,5},{5,6},{6,7},{7,4},{8,9},{9,10},{10,1... | collective-permute-start | bytes 3145736 | tf_op jit(solution)/shard_map/ppermute | solution.py:689
  1003.9 298.2 %reduce-scatter.17.cloned.1.call-start = ((), (), s32[]{:S(2)}) async-start(), calls=%async_computation.17 | async-start | bytes 31850496 | tf_op jit(solution)/shard_map/reduce_scatter | solution.py:849
  1046.1 49.1 %collective-permute-start.44 = (bf16[256,2048]{1,0:T(8,128)(2,1)}, bf16[256,2048]{1,0:T(8,128)(2,1)}, u32[]{:S(2)}, u32[]{:S(2)}) collective-permute-start(bf16[256,2048]{1,0:T(8,128)(2,1)} %add_convert_fusion.2), channel_id=1, source_target_pairs={{0,1},{1,2},{2,3},{3,0},{4,5},{5,6},{6,7},{7,4},{8,9},{9,10},{10,1... | collective-permute-start | bytes 3145736 | tf_op jit(solution)/shard_map/ppermute | solution.py:689
  1099.0 94.3 %collective-permute-start.48 = (f32[576]{0:T(1024)S(1)}, f32[576]{0:T(1024)S(1)}, u32[]{:S(2)}, u32[]{:S(2)}) collective-permute-start(f32[576]{0:T(1024)S(1)} %pad_maximum_fusion.18), channel_id=1, source_target_pairs={{0,1},{1,0},{2,3},{3,2},{4,5},{5,4},{6,7},{7,6},{8,9},{9,8},{10,11... | collective-permute-start | bytes 6920 | tf_op jit(solution)/shard_map/ppermute | solution.py:729
  1120.6 46.6 %collective-permute-start.45 = (bf16[256,4096]{1,0:T(8,128)(2,1)S(1)}, bf16[256,4096]{1,0:T(8,128)(2,1)S(1)}, u32[]{:S(2)}, u32[]{:S(2)}) collective-permute-start(bf16[256,4096]{1,0:T(8,128)(2,1)S(1)} %slice.893), channel_id=1, source_target_pairs={{0,1},{1,2},{2,3},{3,0},{4,5},{5,6},{6,7},{7,4},{8,9},{9,10},{10,1... | collective-permute-start | bytes 6291464 | tf_op jit(solution)/shard_map/ppermute | solution.py:689
  1127.9 65.4 %collective-permute-start.47 = (bf16[4,16,7168]{2,1,0:T(8,128)(2,1)}, bf16[4,16,7168]{2,1,0:T(8,128)(2,1)}, u32[]{:S(2)}, u32[]{:S(2)}) collective-permute-start(bf16[4,16,7168]{2,1,0:T(8,128)(2,1)} %bitcast.36), channel_id=1, source_target_pairs={{0,16},{4,20},{8,24},{12,28},{16,0},{20,4},{24,8},{28,12},{1,17},{... | collective-permute-start | bytes 2752520 | tf_op jit(solution)/shard_map/ppermute | solution.py:706
  1169.2 45.9 %collective-permute-start.46 = (bf16[256,4096]{1,0:T(8,128)(2,1)}, bf16[256,4096]{1,0:T(8,128)(2,1)}, u32[]{:S(2)}, u32[]{:S(2)}) collective-permute-start(bf16[256,4096]{1,0:T(8,128)(2,1)} %add_convert_fusion.1), channel_id=1, source_target_pairs={{0,1},{1,2},{2,3},{3,0},{4,5},{5,6},{6,7},{7,4},{8,9},{9,10},{10,1... | collective-permute-start | bytes 6291464 | tf_op jit(solution)/shard_map/ppermute | solution.py:689
  1218.7 61.7 %collective-permute-start.49 = (bf16[256,4096]{1,0:T(8,128)(2,1)}, bf16[256,4096]{1,0:T(8,128)(2,1)}, u32[]{:S(2)}, u32[]{:S(2)}) collective-permute-start(bf16[256,4096]{1,0:T(8,128)(2,1)} %add_convert_fusion), channel_id=1, source_target_pairs={{0,1},{1,2},{2,3},{3,0},{4,5},{5,6},{6,7},{7,4},{8,9},{9,10},{10,1... | collective-permute-start | bytes 6291464 | tf_op jit(solution)/shard_map/ppermute | solution.py:689
  1221.1 59.3 %collective-permute-start.51 = (f32[576]{0:T(1024)S(1)}, f32[576]{0:T(1024)S(1)}, u32[]{:S(2)}, u32[]{:S(2)}) collective-permute-start(f32[576]{0:T(1024)S(1)} %fusion.267), channel_id=1, source_target_pairs={{0,2},{1,3},{2,0},{3,1},{4,6},{5,7},{6,4},{7,5},{8,10},{9,11},{10,... | collective-permute-start | bytes 6920 | tf_op jit(solution)/shard_map/ppermute | solution.py:729
  1221.9 45.9 %collective-permute-start.57 = (bf16[256,384]{1,0:T(8,128)(2,1)S(1)}, bf16[256,384]{1,0:T(8,128)(2,1)S(1)}, u32[]{:S(2)}, u32[]{:S(2)}) collective-permute-start(bf16[256,384]{1,0:T(8,128)(2,1)S(1)} %fusion.249), channel_id=1, source_target_pairs={{0,1},{1,0},{2,3},{3,2},{4,5},{5,4},{6,7},{7,6},{8,9},{9,8},{10,11... | collective-permute-start | bytes 589832 | tf_op jit(solution)/shard_map/ppermute | solution.py:729
  1228.2 52.2 %collective-permute-start.50 = (bf16[2,16,7168]{2,1,0:T(8,128)(2,1)S(1)}, bf16[2,16,7168]{2,1,0:T(8,128)(2,1)S(1)}, u32[]{:S(2)}, u32[]{:S(2)}) collective-permute-start(bf16[2,16,7168]{2,1,0:T(8,128)(2,1)S(1)} %select_convert_fusion.1), channel_id=1, source_target_pairs={{0,8},{4,12},{8,0},{12,4},{16,24},{20,28},{24,16},{28,20},{1,9},{5... | collective-permute-start | bytes 1376264 | tf_op jit(solution)/shard_map/ppermute | solution.py:706
  (155 other events, 1985.9 us)
Sparse Core Ops, SparseCore 0:
  15.9 150.1 all-gather.8
  168.0 37.4 all-gather.10
  207.9 92.0 all-gather.12
  301.8 55.9 all-gather.14
  360.1 61.0 all-gather.16
  422.9 37.4 all-gather.18
  678.7 48.5 reduce-scatter.6
  731.3 79.0 reduce-scatter.8
  846.3 70.3 reduce-scatter.10
  920.3 118.5 reduce-scatter.12
  1043.2 51.3 reduce-scatter.14
  1098.1 178.5 reduce-scatter.16

commit v5 on v4

--- a/solution.py
+++ b/solution.py
@@ -997,8 +997,10 @@
     lora_rows = jnp.concatenate([v[:, 3 * head_cols :].astype(bf16) for v in projected], axis=0)
     attended, lora_rows, out_grad[-1] = lax.optimization_barrier((attended, lora_rows, moved))
     out_grad_rows = jnp.concatenate(out_grad, axis=0)
-    normed_rows = jnp.concatenate(normed_parts, axis=0)
-    mixed, _ = ring_scatter(lambda p, t: mm(piece(after(attended, t), p), weight_o))
+    mixed, (normed_rows,) = ring_scatter(
+        lambda p, t: mm(piece(after(attended, t), p), weight_o),
+        [lambda t, _: jnp.concatenate(tie(normed_parts, t), axis=0)],
+    )
 
     mlp_root = inverse_root(mixed)
     gate_up, fc_mid, units = [], [], []
@@ -1106,13 +1108,21 @@
         grad_gate_up.append(both)
         return mm_nt(both, weight_fc1)
 
-    grad_branch, grad_mlp_in, (sum_w_fc2, sum_w_fc1) = ring_both(
-        grad_residual_low,
-        feed_back,
-        lambda pieces: mm_tn(tie(units_rows, sum_w_out), jnp.concatenate(pieces, axis=0)).astype(bf16),
-        lambda t: mm_tn(tie(mlp_rows, t), jnp.concatenate(grad_gate_up, axis=0)).astype(bf16),
-        [small_task],
-    )
+    def fc2_fill(token, _):
+        rows_in = tie(units_rows, (sum_w_out, token))
+        return mm_tn(rows_in, jnp.concatenate(grad_branch, axis=0)).astype(bf16)
+
+    def fc1_fill(token, _):
+        return mm_tn(tie(mlp_rows, token), jnp.concatenate(grad_gate_up, axis=0)).astype(bf16)
+
+    grad_branch, back_terms = ring_gather(
+        grad_residual_low, lambda p, v: feed_back(p, v) if p < tp - 1 else (), [small_task]
+    )
+    grad_mlp_in, filled = ring_scatter(
+        lambda p, t: back_terms[p] if p < tp - 1 else feed_back(p, after(grad_branch[p], t)),
+        [fc2_fill] + [lambda t, _: ()] * (tp - 3) + [fc1_fill],
+    )
+    sum_w_fc2, sum_w_fc1 = filled[0], filled[-1]
     sum_w_fc2 = scatter(sum_w_fc2, 1)
     sum_w_fc1 = scatter(sum_w_fc1)
     grad_gate_up_rows = jnp.concatenate(grad_gate_up, axis=0)
@@ -1198,12 +1208,18 @@
         return with_layout_constraint(values, Layout(major_to_minor=(0, 1, 2)))
 
     tasks, bc_sums = [], []
+    normed_terms = {}
     pair = mm_nt(grad_projected[share : 3 * share], weight_qkv)
-    grad_normed, (_, mixer_sums, feed_sums) = ring_scatter(
-        lambda p, t: piece(pair, p - 1)
-        if p in (1, 2)
-        else mm_nt(piece(after(grad_projected, t), p), weight_qkv),
-        [finish_adapters, finish_mixer, finish_feed],
+    normed_terms[1], normed_terms[2] = piece(pair, 0), piece(pair, 1)
+
+    def normed_back(p, token):
+        if p not in normed_terms:
+            normed_terms[p] = mm_nt(piece(after(grad_projected, token), p), weight_qkv)
+        return normed_terms[p]
+
+    grad_normed, ((_, mixer_sums, _), feed_sums) = ring_scatter(
+        normed_back,
+        [lambda t, k: (finish_adapters(t, k), finish_mixer(t, k), normed_back(3 % tp, t)), finish_feed],
         tasks,
     )
     grad_w_zx, grad_w_dt, grad_w_out, grad_w_fc2 = mixer_sums

time: 1340 us -> 1340 us (level)
  waiting for transfers between devices: 434 us -> 380 us
  other arithmetic: 113 us -> 155 us
    ppermute x39, waiting for transfers between devices: 388 us -> 340 us  [hop(): return lax.ppermute(values, 'tp', ring_pairs())]
    concatenate x0 -> x3, other arithmetic: none -> 45.8 us  [the longest x2 37.9 us: local(): jnp.concatenate([jnp.concatenate(v, axis=1) for v in normed[low:high]], a...]
    ppermute x3, waiting for transfers between devices: 17 us -> 2.62 us  [doubling_gather(): moved = lax.ppermute(values, name, [(i, i ^ step) for i in range(count)])]
    unnamed x298 -> x320, local copies, waits for them, and re-layouts: 55.8 us -> 57.1 us
  transfers between devices with their start and end apart: 71 -> 71, of which waited for: 34 -> 33; matrix products, arithmetic and copies ran while one was open for 46% -> 50% of each run, Pallas kernels for 9% -> 9%
where the time goes in v5:
time: 1340 us; the launch traced here: 1330 us
  matrix products  461 us (34%)
  waiting for transfers between devices  380 us (28%)
  other arithmetic  155 us (12%)
  Pallas kernels  138 us (10%)
  local copies, waits for them, and re-layouts  111 us (8%)
  starting transfers between devices  48.9 us (4%)
  blocking collectives  17.7 us (1%)
  between operations  17.3 us (1%)
    ppermute x39, waiting for transfers between devices, hop(): return lax.ppermute(values, 'tp', ring_pairs())  340 us
    dot_general x24, matrix products, mm_nt(): lax.dot_general(left, right, (((1,), (1,)), ((), ())), preferred_element_...  189 us
    dot_general x23, matrix products, mm(): return jnp.dot(left, right, preferred_element_type=f32)  139 us
    dot_general x10, matrix products, mm_tn(): lax.dot_general(left, right, (((0,), (0,)), ((), ())), preferred_element_...  133 us
    unnamed x320, local copies, waits for them, and re-layouts  57.1 us
    pallas_call x1, Pallas kernels, attention_backward(): pl.pallas_call(functools.partial(attention_backward_kernel, tp, heads), o...  39 us
    concatenate x2, other arithmetic, local(): jnp.concatenate([jnp.concatenate(v, axis=1) for v in normed[low:high]], a...  37.9 us
    pallas_call x1, Pallas kernels, mixer_backward(): pl.pallas_call(functools.partial(mixer_backward_kernel, chunks), out_shap...  36.4 us
  transfers between devices with their start and end apart: 71, of which 33 were waited for; matrix products, arithmetic and copies ran while one was open for 50% of the time, Pallas kernels for 9%

profile of v5, /device:TPU:0, one launch (start us, length us, event | category | flops | bytes accessed | tf_op | source)
XLA Modules:
  0.0 1328.8 jit_solution(11149609411729646521)
XLA Ops:
  37.8 9.2 all-gather.1
  57.1 17.8 %collective-permute-done = bf16[256,2048]{1,0:T(8,128)(2,1)} collective-permute-done((bf16[256,2048]{1,0:T(8,128)(2,1)S(1)}, bf16[256,2048]{1,0:T(8,128)(2,1)}, u32[]{:S(2)}, u32[]{:S(2)}) %collective-permute-start) | collective-permute-done | bytes 1048608 | tf_op jit(solution)/shard_map/ppermute | solution.py:689
  79.0 18.2 %collective-permute-done.3 = bf16[256,2048]{1,0:T(8,128)(2,1)S(1)} collective-permute-done((bf16[256,2048]{1,0:T(8,128)(2,1)S(1)}, bf16[256,2048]{1,0:T(8,128)(2,1)S(1)}, u32[]{:S(2)}, u32[]{:S(2)}) %collective-permute-start.3) | collective-permute-done | bytes 1048608 | tf_op jit(solution)/shard_map/ppermute | solution.py:689
  97.2 21.6 %collective-permute-done.1 = bf16[256,2048]{1,0:T(8,128)(2,1)S(1)} collective-permute-done((bf16[256,2048]{1,0:T(8,128)(2,1)}, bf16[256,2048]{1,0:T(8,128)(2,1)S(1)}, u32[]{:S(2)}, u32[]{:S(2)}) %collective-permute-start.1) | collective-permute-done | bytes 1048608 | tf_op jit(solution)/shard_map/ppermute | solution.py:689
  125.3 18.9 %maximum_maximum_fusion = bf16[512,4096]{1,0:T(8,128)(2,1)} fusion(bf16[256,2048]{1,0:T(8,128)(2,1)S(1)} %get-tuple-element.459, bf16[256,2048]{1,0:T(8,128)(2,1)S(1)} %get-tuple-element.469, bf16[256,2048]{1,0:T(8,128)(2,1)S(1)} %copy-done.41, bf16[256,2048]{1,0:T(8,128)(2,1)S(1)} %copy-done.43), kind=kLoop, calls=%fused_computation.69 | loop fusion | flops 16777216 | bytes 8388608 | tf_op jit(solution)/shard_map/concatenate | solution.py:988
  148.7 18.8 %collective-permute-done.8 = bf16[256,2048]{1,0:T(8,128)(2,1)S(1)} collective-permute-done((bf16[256,2048]{1,0:T(8,128)(2,1)S(1)}, bf16[256,2048]{1,0:T(8,128)(2,1)S(1)}, u32[]{:S(2)}, u32[]{:S(2)}) %collective-permute-start.8) | collective-permute-done | bytes 1048608 | tf_op jit(solution)/shard_map/ppermute | solution.py:689
  169.1 19.0 %maximum_maximum_fusion.1 = bf16[512,4096]{1,0:T(8,128)(2,1)} fusion(bf16[256,2048]{1,0:T(8,128)(2,1)S(1)} %get-tuple-element.472, bf16[256,2048]{1,0:T(8,128)(2,1)S(1)} %get-tuple-element.471, bf16[256,2048]{1,0:T(8,128)(2,1)S(1)} %get-tuple-element.458, bf16[256,2048]{1,0:T(8,128)(2,1)S(1)} %get-tuple-element.470), kind=kLoop, calls=%fused_computation.70 | loop fusion | flops 16777216 | bytes 8388608 | tf_op jit(solution)/shard_map/concatenate | solution.py:988
  189.3 21.7 %fusion.251.refs_0_.refs_1_.refs_2_.refs_3_ = f32[512,3456]{1,0:T(8,128)S(1)} fusion(bf16[4096,3456]{1,0:T(8,128)(2,1)} %all-gather.9.cloned.1.call-done, bf16[256,2048]{1,0:T(8,128)(2,1)} %copy-done.46, bf16[256,2048]{1,0:T(8,128)(2,1)} %copy-done.47, bf16[256,2048]{1,0:T(8,128)(2,1)S(1)} %copy-done.42, bf16[256,2048]{1,0:T(8,128)(2,1)} %get-tuple-element.474), kind=kOutput, calls=%fused_computation.482 | convolution fusion | flops 14512291840 | bytes 39583744 | tf_op jit(solution)/shard_map/dot_general | solution.py:25
  211.1 25.0 %fusion.250.refs_4_.refs_5_.refs_6_.refs_7_ = f32[512,3456]{1,0:T(8,128)S(1)} fusion(bf16[4096,3456]{1,0:T(8,128)(2,1)} %all-gather.9.cloned.1.call-done, bf16[256,2048]{1,0:T(8,128)(2,1)} %copy-done.49, bf16[256,2048]{1,0:T(8,128)(2,1)} %copy-done.48, bf16[256,2048]{1,0:T(8,128)(2,1)} %copy-done.44, bf16[256,2048]{1,0:T(8,128)(2,1)} %copy-done.45), kind=kOutput, calls=%fused_computation.481 | convolution fusion | flops 14512291840 | bytes 39583744 | tf_op jit(solution)/shard_map/dot_general | solution.py:25
  240.5 27.1 %attention_forward.1 = (bf16[1024,1024]{1,0:T(8,128)(2,1)}, bf16[1024,1024]{1,0:T(8,128)(2,1)}, bf16[1024,1024]{1,0:T(8,128)(2,1)}, bf16[1024,1024]{1,0:T(8,128)(2,1)}) custom-call(s32[1]{0:T(128)} %bitcast.place_ref, s32[3]{0:T(128)} %bitcast.257, f32[1024,128]{1,0:T(8,128)} %get-tuple-element.475.cosine_ref, f32[1024,128]{1,0:T(8,128)} %get-tuple-element.476.sine_ref, ...), custom_call_target="tpu_custom_call" | custom-call | flops 4294967296 | bytes 20971520 | tf_op jit(solution)/shard_map/attention_forward/pallas_call | solution.py:119
  283.9 13.5 %collective-permute-done.12 = bf16[256,2048]{1,0:T(8,128)(2,1)} collective-permute-done((bf16[256,2048]{1,0:T(8,128)(2,1)S(1)}, bf16[256,2048]{1,0:T(8,128)(2,1)}, u32[]{:S(2)}, u32[]{:S(2)}) %collective-permute-start.12) | collective-permute-done | bytes 1048608 | tf_op jit(solution)/shard_map/ppermute | solution.py:689
  304.0 20.7 %collective-permute-done.13 = bf16[256,2048]{1,0:T(8,128)(2,1)} collective-permute-done((bf16[256,2048]{1,0:T(8,128)(2,1)S(1)}, bf16[256,2048]{1,0:T(8,128)(2,1)}, u32[]{:S(2)}, u32[]{:S(2)}) %collective-permute-start.13) | collective-permute-done | bytes 1048608 | tf_op jit(solution)/shard_map/ppermute | solution.py:689
  332.0 19.6 %collective-permute-done.14 = bf16[256,2048]{1,0:T(8,128)(2,1)} collective-permute-done((bf16[256,2048]{1,0:T(8,128)(2,1)}, bf16[256,2048]{1,0:T(8,128)(2,1)}, u32[]{:S(2)}, u32[]{:S(2)}) %collective-permute-start.14) | collective-permute-done | bytes 1048608 | tf_op jit(solution)/shard_map/ppermute | solution.py:689
  355.1 9.1 fusion.267
  393.9 11.1 collective-permute-done.17
  428.1 21.9 %collective-permute-done.19 = bf16[256,2048]{1,0:T(8,128)(2,1)S(1)} collective-permute-done((bf16[256,2048]{1,0:T(8,128)(2,1)S(1)}, bf16[256,2048]{1,0:T(8,128)(2,1)S(1)}, u32[]{:S(2)}, u32[]{:S(2)}) %collective-permute-start.19) | collective-permute-done | bytes 1048608 | tf_op jit(solution)/shard_map/ppermute | solution.py:689
  450.0 9.3 fusion.271
  477.8 12.8 collective-permute-done.20
  494.0 8.5 fusion.273
  524.3 16.1 %collective-permute-done.22 = bf16[256,2048]{1,0:T(8,128)(2,1)S(1)} collective-permute-done((bf16[256,2048]{1,0:T(8,128)(2,1)}, bf16[256,2048]{1,0:T(8,128)(2,1)S(1)}, u32[]{:S(2)}, u32[]{:S(2)}) %collective-permute-start.22) | collective-permute-done | bytes 1048608 | tf_op jit(solution)/shard_map/ppermute | solution.py:689
  544.8 15.7 %collective-permute-done.23 = bf16[256,2048]{1,0:T(8,128)(2,1)S(1)} collective-permute-done((bf16[256,2048]{1,0:T(8,128)(2,1)S(1)}, bf16[256,2048]{1,0:T(8,128)(2,1)S(1)}, u32[]{:S(2)}, u32[]{:S(2)}) %collective-permute-start.23) | collective-permute-done | bytes 1048608 | tf_op jit(solution)/shard_map/ppermute | solution.py:689
  567.4 17.6 %mixer_forward.1 = (bf16[1024,1024]{1,0:T(8,128)(2,1)}, bf16[8,64,1024]{2,1,0:T(8,128)(2,1)}) custom-call(s32[1]{0:T(128)} %bitcast.place_ref, s32[3]{0:T(128)} %bitcast.258, bf16[1024,2048]{1,0:T(8,128)(2,1)} %pad_maximum_fusion.1.zx.before, bf16[1024,2048]{1,0:T(8,128)(2,1)} %pad_maximum_fusion.1.zx.before, f32[1024,384]{1,0:T(8,128)} %pad_maximum_fusion.9.sd.sd_before, ...), custom_call_target="tpu_custom_call" | custom-call | flops 1073741824 | bytes 8388608 | tf_op jit(solution)/shard_map/mixer_forward/pallas_call | solution.py:530
  587.9 8.5 psum.7
  609.0 36.4 %mixer_backward.1 = (bf16[1024,2432]{1,0:T(8,128)(2,1)}, f32[8,1024]{1,0:T(8,128)}, f32[8,256]{1,0:T(8,128)}, f32[8,128]{1,0:T(8,128)}) custom-call(s32[1]{0:T(128)} %bitcast.place_ref, s32[3]{0:T(128)} %bitcast.259, bf16[1024,2048]{1,0:T(8,128)(2,1)} %pad_maximum_fusion.1.zx.before, bf16[1024,2048]{1,0:T(8,128)(2,1)} %pad_maximum_fusion.1.zx.before, ...), custom_call_target="tpu_custom_call" | custom-call | flops 3221225472 | bytes 12582912 | tf_op jit(solution)/shard_map/mixer_backward/pallas_call | solution.py:567
  645.5 8.5 convolution_convert_fusion.6
  677.8 16.2 %convolution_convert_fusion.2 = bf16[2048,2432]{1,0:T(8,128)(2,1)} fusion(bf16[1024,2048]{1,0:T(8,128)(2,1)S(1)} %pad_maximum_fusion.2, bf16[1024,2432]{1,0:T(8,128)(2,1)} %get-tuple-element.241), kind=kOutput, calls=%fused_computation.2 | convolution fusion | flops 10205528064 | bytes 19136512 | tf_op jit(solution)/shard_map/dot_general | solution.py:33
  694.1 8.4 fusion.192
  734.6 9.6 fusion.136
  746.2 13.4 %fusion.79 = f32[256,2048]{1,0:T(8,128)} fusion(bf16[2048,4224]{1,0:T(8,128)(2,1)} %all-gather.13.cloned.1.call-done, bf16[256,128]{1,0:T(8,128)(2,1)S(1)} %fusion.206, bf16[256,2048]{1,0:T(8,128)(2,1)} %copy-done.122, bf16[256,2048]{1,0:T(8,128)(2,1)} %copy-done.120), kind=kOutput, calls=%fused_computation.153 | convolution fusion | flops 4435673088 | bytes 21561344 | tf_op jit(solution)/shard_map/dot_general | solution.py:29
  775.1 12.7 fusion.85
  800.1 13.0 fusion.91
  813.1 25.0 %collective-permute-done.34 = bf16[256,2048]{1,0:T(8,128)(2,1)} collective-permute-done((bf16[256,2048]{1,0:T(8,128)(2,1)}, bf16[256,2048]{1,0:T(8,128)(2,1)}, u32[]{:S(2)}, u32[]{:S(2)}) %collective-permute-start.34) | collective-permute-done | bytes 1048608 | tf_op jit(solution)/shard_map/ppermute | solution.py:689
  838.1 14.1 %convolution_convert_fusion.3 = bf16[2048,2048]{1,0:T(8,128)(2,1)} fusion(bf16[1024,2048]{1,0:T(8,128)(2,1)} %pad_maximum_fusion.3, bf16[256,2048]{1,0:T(8,128)(2,1)} %collective-permute-done.34, bf16[256,2048]{1,0:T(8,128)(2,1)} %collective-permute-done.31, bf16[256,2048]{1,0:T(8,128)(2,1)} %collective-permute-done.29, bf16[256,2048]{1,0:T(8,128)(2,1)S(1)} %copy-done.118), kind=kOutput, calls=%fused_computation.51 | convolution fusion | flops 8610906112 | bytes 16777216 | tf_op jit(solution)/shard_map/dot_general | solution.py:33
  855.5 9.1 fusion.130
  866.7 9.1 fusion.97
  884.9 30.0 %convolution_convert_fusion.1 = bf16[2048,4224]{1,0:T(8,128)(2,1)} fusion(bf16[1024,2048]{1,0:T(8,128)(2,1)} %copy-done.80, bf16[256,128]{1,0:T(8,128)(2,1)S(1)} %fusion.197, bf16[256,2048]{1,0:T(8,128)(2,1)} %copy-done.128, bf16[256,2048]{1,0:T(8,128)(2,1)} %copy-done.127, bf16[256,128]{1,0:T(8,128)(2,1)S(1)} %fusion.200, ...), kind=kOutput, calls=%fused_computation.1 | convolution fusion | flops 17829199872 | bytes 30146560 | tf_op jit(solution)/shard_map/dot_general | solution.py:33
  930.0 17.4 %fusion.23 = f32[128,4096]{1,0:T(8,128)} fusion(bf16[1024,128]{1,0:T(8,128)(2,1)S(1)} %pad_maximum_fusion.16, bf16[256,128]{1,0:T(8,128)(2,1)S(1)} %copy-done.134, bf16[256,2048]{1,0:T(8,128)(2,1)} %copy-done.128, bf16[256,2048]{1,0:T(8,128)(2,1)} %copy-done.127, bf16[256,128]{1,0:T(8,128)(2,1)S(1)} %copy-done.132, bf16[256,2048]{1,0:T(8,128)(2,1)} %copy-done.126, ...), kind=kOutput, calls=%fused_computation.26 | convolution fusion | flops 1174405120 | bytes 11010048 | tf_op jit(solution)/shard_map/dot_general | solution.py:33
  959.2 20.8 %collective-permute-done.40 = bf16[256,2048]{1,0:T(8,128)(2,1)} collective-permute-done((bf16[256,2048]{1,0:T(8,128)(2,1)S(1)}, bf16[256,2048]{1,0:T(8,128)(2,1)}, u32[]{:S(2)}, u32[]{:S(2)}) %collective-permute-start.40) | collective-permute-done | bytes 1048608 | tf_op jit(solution)/shard_map/ppermute | solution.py:689
  985.4 22.8 %collective-permute-done.42 = bf16[256,2048]{1,0:T(8,128)(2,1)} collective-permute-done((bf16[256,2048]{1,0:T(8,128)(2,1)}, bf16[256,2048]{1,0:T(8,128)(2,1)}, u32[]{:S(2)}, u32[]{:S(2)}) %collective-permute-start.42) | collective-permute-done | bytes 1048608 | tf_op jit(solution)/shard_map/ppermute | solution.py:689
  1008.2 9.1 fusion.70
  1022.0 39.0 %attention_backward.1 = bf16[1024,3456]{1,0:T(8,128)(2,1)} custom-call(s32[1]{0:T(128)} %bitcast.place_ref, s32[3]{0:T(128)} %bitcast.260, f32[1024,128]{1,0:T(8,128)} %get-tuple-element.475.cosine_ref, f32[1024,128]{1,0:T(8,128)} %get-tuple-element.476.sine_ref, bf16[1024,1024]{1,0:T(8,128)(2,1)} %get-tuple-element.229.q_ref, ...), custom_call_target="tpu_custom_call" | custom-call | flops 10737418240 | bytes 14680064 | tf_op jit(solution)/shard_map/attention_backward/pallas_call | solution.py:233
  1062.9 37.9 %convolution_convert_fusion = bf16[4096,3456]{1,0:T(8,128)(2,1)} fusion(bf16[1024,4096]{1,0:T(8,128)(2,1)} %pad_maximum_fusion, bf16[1024,3456]{1,0:T(8,128)(2,1)} %attention_backward.1), kind=kOutput, calls=%fused_computation | convolution fusion | flops 29005185024 | bytes 43778048 | tf_op jit(solution)/shard_map/dot_general | solution.py:33
  1105.0 22.1 %fusion.73 = f32[512,4096]{1,0:T(8,128)S(1)} fusion(bf16[4096,3456]{1,0:T(8,128)(2,1)} %all-gather.9.cloned.1.call-done, bf16[1024,3456]{1,0:T(8,128)(2,1)} %attention_backward.1), kind=kOutput, calls=%fused_computation.117 | convolution fusion | flops 14495514624 | bytes 40239104 | tf_op jit(solution)/shard_map/dot_general | solution.py:29
  1148.0 16.7 %fusion.188 = f32[256,4096]{1,0:T(8,128)} fusion(bf16[4096,3456]{1,0:T(8,128)(2,1)} %all-gather.9.cloned.1.call-done, bf16[1024,3456]{1,0:T(8,128)(2,1)} %attention_backward.1), kind=kOutput, calls=%fused_computation.296 | convolution fusion | flops 7247757312 | bytes 34275328 | tf_op jit(solution)/shard_map/dot_general | solution.py:29
  1164.7 10.8 collective-permute-done.45
  1211.0 11.2 collective-permute-done.47
  1236.2 15.8 %fusion.186 = f32[256,4096]{1,0:T(8,128)} fusion(bf16[4096,3456]{1,0:T(8,128)(2,1)} %all-gather.9.cloned.1.call-done, bf16[1024,3456]{1,0:T(8,128)(2,1)} %attention_backward.1), kind=kOutput, calls=%fused_computation.294 | convolution fusion | flops 7247757312 | bytes 34275328 | tf_op jit(solution)/shard_map/dot_general | solution.py:29
  1252.0 15.5 %collective-permute-done.51 = f32[576]{0:T(1024)S(1)} collective-permute-done((f32[576]{0:T(1024)S(1)}, f32[576]{0:T(1024)S(1)}, u32[]{:S(2)}, u32[]{:S(2)}) %collective-permute-start.51) | collective-permute-done | bytes 2336 | tf_op jit(solution)/shard_map/ppermute | solution.py:729
  (733 shorter events, 485.1 us)
Async XLA Ops:
  7.2 181.2 %all-gather.9.cloned.1.call-start = ((), (), s32[]{:S(2)}) async-start(), calls=%async_computation.6 | async-start | bytes 31850496 | tf_op jit(solution)/shard_map/all_gather | solution.py:845
  13.2 254.5 %all-gather.11.cloned.1.call-start = ((), (), s32[]{:S(2)}) async-start(), calls=%async_computation.7 | async-start | bytes 4718592 | tf_op jit(solution)/shard_map/all_gather | solution.py:845
  13.9 341.2 %all-gather.13.cloned.1.call-start = ((), (), s32[]{:S(2)}) async-start(), calls=%async_computation.8 | async-start | bytes 19464192 | tf_op jit(solution)/shard_map/all_gather | solution.py:845
  22.6 346.0 %all-gather.15.cloned.1.call-start = ((), (), s32[]{:S(2)}) async-start(), calls=%async_computation.9 | async-start | bytes 9437184 | tf_op jit(solution)/shard_map/all_gather | solution.py:845
  23.1 470.9 %all-gather.17.cloned.1.call-start = ((), (), s32[]{:S(2)}) async-start(), calls=%async_computation.10 | async-start | bytes 11206656 | tf_op jit(solution)/shard_map/all_gather | solution.py:845
  23.2 32.3 %collective-permute-start.2 = (bf16[256,2048]{1,0:T(8,128)(2,1)S(1)}, bf16[256,2048]{1,0:T(8,128)(2,1)S(1)}, u32[]{:S(2)}, u32[]{:S(2)}) collective-permute-start(bf16[256,2048]{1,0:T(8,128)(2,1)S(1)} %copy-done.11), channel_id=1, source_target_pairs={{0,1},{1,2},{2,3},{3,0},{4,5},{5,6},{6,7},{7,4},{8,9},{9,10},{10,1... | collective-permute-start | bytes 3145736 | tf_op jit(solution)/shard_map/ppermute | solution.py:689
  26.3 48.6 %collective-permute-start = (bf16[256,2048]{1,0:T(8,128)(2,1)S(1)}, bf16[256,2048]{1,0:T(8,128)(2,1)}, u32[]{:S(2)}, u32[]{:S(2)}) collective-permute-start(bf16[256,2048]{1,0:T(8,128)(2,1)S(1)} %copy-done.9), channel_id=1, source_target_pairs={{0,1},{1,2},{2,3},{3,0},{4,5},{5,6},{6,7},{7,4},{8,9},{9,10},{10,1... | collective-permute-start | bytes 3145736 | tf_op jit(solution)/shard_map/ppermute | solution.py:689
  35.7 466.8 %all-gather.19.cloned.1.call-start = ((), (), s32[]{:S(2)}) async-start(), calls=%async_computation.11 | async-start | bytes 4718592 | tf_op jit(solution)/shard_map/all_gather | solution.py:845
  55.5 41.8 %collective-permute-start.3 = (bf16[256,2048]{1,0:T(8,128)(2,1)S(1)}, bf16[256,2048]{1,0:T(8,128)(2,1)S(1)}, u32[]{:S(2)}, u32[]{:S(2)}) collective-permute-start(bf16[256,2048]{1,0:T(8,128)(2,1)S(1)} %collective-permute-done.2), channel_id=1, source_target_pairs={{0,1},{1,2},{2,3},{3,0},{4,5},{5,6},{6,7},{7,4},{8,9},{9,10},{10,1... | collective-permute-start | bytes 3145736 | tf_op jit(solution)/shard_map/ppermute | solution.py:689
  74.9 44.0 %collective-permute-start.1 = (bf16[256,2048]{1,0:T(8,128)(2,1)}, bf16[256,2048]{1,0:T(8,128)(2,1)S(1)}, u32[]{:S(2)}, u32[]{:S(2)}) collective-permute-start(bf16[256,2048]{1,0:T(8,128)(2,1)} %collective-permute-done), channel_id=1, source_target_pairs={{0,1},{1,2},{2,3},{3,0},{4,5},{5,6},{6,7},{7,4},{8,9},{9,10},{10,1... | collective-permute-start | bytes 3145736 | tf_op jit(solution)/shard_map/ppermute | solution.py:689
  118.9 29.8 %collective-permute-start.7 = (bf16[256,2048]{1,0:T(8,128)(2,1)S(1)}, bf16[256,2048]{1,0:T(8,128)(2,1)S(1)}, u32[]{:S(2)}, u32[]{:S(2)}) collective-permute-start(bf16[256,2048]{1,0:T(8,128)(2,1)S(1)} %collective-permute-done.1), channel_id=1, source_target_pairs={{0,1},{1,2},{2,3},{3,0},{4,5},{5,6},{6,7},{7,4},{8,9},{9,10},{10,1... | collective-permute-start | bytes 3145736 | tf_op jit(solution)/shard_map/ppermute | solution.py:689
  119.4 48.1 %collective-permute-start.8 = (bf16[256,2048]{1,0:T(8,128)(2,1)S(1)}, bf16[256,2048]{1,0:T(8,128)(2,1)S(1)}, u32[]{:S(2)}, u32[]{:S(2)}) collective-permute-start(bf16[256,2048]{1,0:T(8,128)(2,1)S(1)} %collective-permute-done.3), channel_id=1, source_target_pairs={{0,1},{1,2},{2,3},{3,0},{4,5},{5,6},{6,7},{7,4},{8,9},{9,10},{10,1... | collective-permute-start | bytes 3145736 | tf_op jit(solution)/shard_map/ppermute | solution.py:689
  147.1 41.0 %collective-permute-start.6 = (bf16[64,7168]{1,0:T(8,128)(2,1)S(1)}, bf16[64,7168]{1,0:T(8,128)(2,1)S(1)}, u32[]{:S(2)}, u32[]{:S(2)}) collective-permute-start(bf16[64,7168]{1,0:T(8,128)(2,1)S(1)} %pad_maximum_fusion.10), channel_id=1, source_target_pairs={{0,16},{4,20},{8,24},{12,28},{16,0},{20,4},{24,8},{28,12},{1,17},{... | collective-permute-start | bytes 2752520 | tf_op jit(solution)/shard_map/ppermute | solution.py:831
  167.5 43.6 %collective-permute-start.9 = (bf16[256,2048]{1,0:T(8,128)(2,1)}, bf16[256,2048]{1,0:T(8,128)(2,1)}, u32[]{:S(2)}, u32[]{:S(2)}) collective-permute-start(bf16[256,2048]{1,0:T(8,128)(2,1)} %refs_3_.1), channel_id=1, source_target_pairs={{0,1},{1,2},{2,3},{3,0},{4,5},{5,6},{6,7},{7,4},{8,9},{9,10},{10,1... | collective-permute-start | bytes 3145736 | tf_op jit(solution)/shard_map/ppermute | solution.py:689
  211.1 25.9 %collective-permute-start.10 = (bf16[256,2048]{1,0:T(8,128)(2,1)}, bf16[256,2048]{1,0:T(8,128)(2,1)}, u32[]{:S(2)}, u32[]{:S(2)}) collective-permute-start(bf16[256,2048]{1,0:T(8,128)(2,1)} %collective-permute-done.9), channel_id=1, source_target_pairs={{0,1},{1,2},{2,3},{3,0},{4,5},{5,6},{6,7},{7,4},{8,9},{9,10},{10,1... | collective-permute-start | bytes 3145736 | tf_op jit(solution)/shard_map/ppermute | solution.py:689
  237.0 30.6 %collective-permute-start.11 = (bf16[256,2048]{1,0:T(8,128)(2,1)}, bf16[256,2048]{1,0:T(8,128)(2,1)}, u32[]{:S(2)}, u32[]{:S(2)}) collective-permute-start(bf16[256,2048]{1,0:T(8,128)(2,1)} %collective-permute-done.10), channel_id=1, source_target_pairs={{0,1},{1,2},{2,3},{3,0},{4,5},{5,6},{6,7},{7,4},{8,9},{9,10},{10,1... | collective-permute-start | bytes 3145736 | tf_op jit(solution)/shard_map/ppermute | solution.py:689
  271.4 26.0 %collective-permute-start.12 = (bf16[256,2048]{1,0:T(8,128)(2,1)S(1)}, bf16[256,2048]{1,0:T(8,128)(2,1)}, u32[]{:S(2)}, u32[]{:S(2)}) collective-permute-start(bf16[256,2048]{1,0:T(8,128)(2,1)S(1)} %convolution_convert_fusion.7), channel_id=1, source_target_pairs={{0,1},{1,2},{2,3},{3,0},{4,5},{5,6},{6,7},{7,4},{8,9},{9,10},{10,1... | collective-permute-start | bytes 3145736 | tf_op jit(solution)/shard_map/ppermute | solution.py:689
  299.7 538.4 %reduce-scatter.7.cloned.1.call-start = ((), (), s32[]{:S(2)}) async-start(), calls=%async_computation.12 | async-start | bytes 4718592 | tf_op jit(solution)/shard_map/reduce_scatter | solution.py:849
  378.0 27.1 %collective-permute-start.17 = (bf16[256,2048]{1,0:T(8,128)(2,1)}, bf16[256,2048]{1,0:T(8,128)(2,1)S(1)}, u32[]{:S(2)}, u32[]{:S(2)}) collective-permute-start(bf16[256,2048]{1,0:T(8,128)(2,1)} %collective-permute-done.15), channel_id=1, source_target_pairs={{0,1},{1,2},{2,3},{3,0},{4,5},{5,6},{6,7},{7,4},{8,9},{9,10},{10,1... | collective-permute-start | bytes 3145736 | tf_op jit(solution)/shard_map/ppermute | solution.py:689
  393.9 33.6 %collective-permute-start.16 = (bf16[256,2048]{1,0:T(8,128)(2,1)S(1)}, bf16[256,2048]{1,0:T(8,128)(2,1)S(1)}, u32[]{:S(2)}, u32[]{:S(2)}) collective-permute-start(bf16[256,2048]{1,0:T(8,128)(2,1)S(1)} %convolution_convert_fusion.8), channel_id=1, source_target_pairs={{0,1},{1,2},{2,3},{3,0},{4,5},{5,6},{6,7},{7,4},{8,9},{9,10},{10,1... | collective-permute-start | bytes 3145736 | tf_op jit(solution)/shard_map/ppermute | solution.py:689
  405.0 44.9 %collective-permute-start.19 = (bf16[256,2048]{1,0:T(8,128)(2,1)S(1)}, bf16[256,2048]{1,0:T(8,128)(2,1)S(1)}, u32[]{:S(2)}, u32[]{:S(2)}) collective-permute-start(bf16[256,2048]{1,0:T(8,128)(2,1)S(1)} %collective-permute-done.17), channel_id=1, source_target_pairs={{0,1},{1,2},{2,3},{3,0},{4,5},{5,6},{6,7},{7,4},{8,9},{9,10},{10,1... | collective-permute-start | bytes 3145736 | tf_op jit(solution)/shard_map/ppermute | solution.py:689
  427.8 39.9 %collective-permute-start.18 = (bf16[256,2048]{1,0:T(8,128)(2,1)S(1)}, bf16[256,2048]{1,0:T(8,128)(2,1)S(1)}, u32[]{:S(2)}, u32[]{:S(2)}) collective-permute-start(bf16[256,2048]{1,0:T(8,128)(2,1)S(1)} %add_convert_fusion.9), channel_id=1, source_target_pairs={{0,1},{1,2},{2,3},{3,0},{4,5},{5,6},{6,7},{7,4},{8,9},{9,10},{10,1... | collective-permute-start | bytes 3145736 | tf_op jit(solution)/shard_map/ppermute | solution.py:689
  605.8 39.6 %collective-permute-start.24 = (bf16[256,2048]{1,0:T(8,128)(2,1)S(1)}, bf16[256,2048]{1,0:T(8,128)(2,1)S(1)}, u32[]{:S(2)}, u32[]{:S(2)}) collective-permute-start(bf16[256,2048]{1,0:T(8,128)(2,1)S(1)} %slice.562), channel_id=1, source_target_pairs={{0,1},{1,2},{2,3},{3,0},{4,5},{5,6},{6,7},{7,4},{8,9},{9,10},{10,1... | collective-permute-start | bytes 3145736 | tf_op jit(solution)/shard_map/ppermute | solution.py:689
  672.6 257.3 %reduce-scatter.9.cloned.1.call-start = ((), (), s32[]{:S(2)}) async-start(), calls=%async_computation.13 | async-start | bytes 11206656 | tf_op jit(solution)/shard_map/reduce_scatter | solution.py:849
  703.5 281.8 %reduce-scatter.11.cloned.1.call-start = ((), (), s32[]{:S(2)}) async-start(), calls=%async_computation.14 | async-start | bytes 9437184 | tf_op jit(solution)/shard_map/reduce_scatter | solution.py:849
  725.4 34.2 %collective-permute-start.30 = (f32[4,864]{1,0:T(4,128)S(1)}, f32[4,864]{1,0:T(4,128)S(1)}, u32[]{:S(2)}, u32[]{:S(2)}) collective-permute-start(f32[4,864]{1,0:T(4,128)S(1)} %slice_select_fusion.2), channel_id=1, source_target_pairs={{0,16},{4,20},{8,24},{12,28},{16,0},{20,4},{24,8},{28,12},{1,17},{... | collective-permute-start | bytes 41480 | tf_op jit(solution)/shard_map/ppermute | solution.py:706
  734.3 25.3 %collective-permute-start.29 = (bf16[256,2048]{1,0:T(8,128)(2,1)}, bf16[256,2048]{1,0:T(8,128)(2,1)}, u32[]{:S(2)}, u32[]{:S(2)}) collective-permute-start(bf16[256,2048]{1,0:T(8,128)(2,1)} %get-tuple-element.250), channel_id=1, source_target_pairs={{0,1},{1,2},{2,3},{3,0},{4,5},{5,6},{6,7},{7,4},{8,9},{9,10},{10,1... | collective-permute-start | bytes 3145736 | tf_op jit(solution)/shard_map/ppermute | solution.py:689
  759.7 28.1 %collective-permute-start.32 = (f32[2,864]{1,0:T(2,128)S(1)}, f32[2,864]{1,0:T(2,128)S(1)}, u32[]{:S(2)}, u32[]{:S(2)}) collective-permute-start(f32[2,864]{1,0:T(2,128)S(1)} %broadcast_select_fusion.8), channel_id=1, source_target_pairs={{0,8},{4,12},{8,0},{12,4},{16,24},{20,28},{24,16},{28,20},{1,9},{5... | collective-permute-start | bytes 20744 | tf_op jit(solution)/shard_map/ppermute | solution.py:706
  762.1 25.7 %collective-permute-start.31 = (bf16[256,2048]{1,0:T(8,128)(2,1)}, bf16[256,2048]{1,0:T(8,128)(2,1)}, u32[]{:S(2)}, u32[]{:S(2)}) collective-permute-start(bf16[256,2048]{1,0:T(8,128)(2,1)} %collective-permute-done.29), channel_id=1, source_target_pairs={{0,1},{1,2},{2,3},{3,0},{4,5},{5,6},{6,7},{7,4},{8,9},{9,10},{10,1... | collective-permute-start | bytes 3145736 | tf_op jit(solution)/shard_map/ppermute | solution.py:689
  787.9 64.3 %collective-permute-start.33 = (bf16[256,2048]{1,0:T(8,128)(2,1)}, bf16[256,2048]{1,0:T(8,128)(2,1)}, u32[]{:S(2)}, u32[]{:S(2)}) collective-permute-start(bf16[256,2048]{1,0:T(8,128)(2,1)} %fusion.85), channel_id=1, source_target_pairs={{0,1},{1,2},{2,3},{3,0},{4,5},{5,6},{6,7},{7,4},{8,9},{9,10},{10,1... | collective-permute-start | bytes 3145736 | tf_op jit(solution)/shard_map/ppermute | solution.py:689
  789.7 48.4 %collective-permute-start.34 = (bf16[256,2048]{1,0:T(8,128)(2,1)}, bf16[256,2048]{1,0:T(8,128)(2,1)}, u32[]{:S(2)}, u32[]{:S(2)}) collective-permute-start(bf16[256,2048]{1,0:T(8,128)(2,1)} %collective-permute-done.31), channel_id=1, source_target_pairs={{0,1},{1,2},{2,3},{3,0},{4,5},{5,6},{6,7},{7,4},{8,9},{9,10},{10,1... | collective-permute-start | bytes 3145736 | tf_op jit(solution)/shard_map/ppermute | solution.py:689
  852.2 208.8 %reduce-scatter.13.cloned.1.call-start = ((), (), s32[]{:S(2)}) async-start(), calls=%async_computation.15 | async-start | bytes 19464192 | tf_op jit(solution)/shard_map/reduce_scatter | solution.py:849
  855.5 26.8 %collective-permute-start.36 = (bf16[256,2048]{1,0:T(8,128)(2,1)}, bf16[256,2048]{1,0:T(8,128)(2,1)}, u32[]{:S(2)}, u32[]{:S(2)}) collective-permute-start(bf16[256,2048]{1,0:T(8,128)(2,1)} %add_convert_fusion.4), channel_id=1, source_target_pairs={{0,1},{1,2},{2,3},{3,0},{4,5},{5,6},{6,7},{7,4},{8,9},{9,10},{10,1... | collective-permute-start | bytes 3145736 | tf_op jit(solution)/shard_map/ppermute | solution.py:689
  884.9 30.0 %collective-permute-start.37 = (bf16[256,2048]{1,0:T(8,128)(2,1)}, bf16[256,2048]{1,0:T(8,128)(2,1)S(1)}, u32[]{:S(2)}, u32[]{:S(2)}) collective-permute-start(bf16[256,2048]{1,0:T(8,128)(2,1)} %add_convert_fusion.3), channel_id=1, source_target_pairs={{0,1},{1,2},{2,3},{3,0},{4,5},{5,6},{6,7},{7,4},{8,9},{9,10},{10,1... | collective-permute-start | bytes 3145736 | tf_op jit(solution)/shard_map/ppermute | solution.py:689
  914.9 271.0 %reduce-scatter.15.cloned.1.call-start = ((), (), s32[]{:S(2)}) async-start(), calls=%async_computation.16 | async-start | bytes 4718592 | tf_op jit(solution)/shard_map/reduce_scatter | solution.py:849
  929.9 25.6 %collective-permute-start.38 = (bf16[256,2048]{1,0:T(8,128)(2,1)}, bf16[256,2048]{1,0:T(8,128)(2,1)S(1)}, u32[]{:S(2)}, u32[]{:S(2)}) collective-permute-start(bf16[256,2048]{1,0:T(8,128)(2,1)} %get-tuple-element.281), channel_id=1, source_target_pairs={{0,1},{1,2},{2,3},{3,0},{4,5},{5,6},{6,7},{7,4},{8,9},{9,10},{10,1... | collective-permute-start | bytes 3145736 | tf_op jit(solution)/shard_map/ppermute | solution.py:689
  980.0 28.2 %collective-permute-start.42 = (bf16[256,2048]{1,0:T(8,128)(2,1)}, bf16[256,2048]{1,0:T(8,128)(2,1)}, u32[]{:S(2)}, u32[]{:S(2)}) collective-permute-start(bf16[256,2048]{1,0:T(8,128)(2,1)} %collective-permute-done.40), channel_id=1, source_target_pairs={{0,1},{1,2},{2,3},{3,0},{4,5},{5,6},{6,7},{7,4},{8,9},{9,10},{10,1... | collective-permute-start | bytes 3145736 | tf_op jit(solution)/shard_map/ppermute | solution.py:689
  981.6 79.4 %collective-permute-start.25 = (bf16[256,2048]{1,0:T(8,128)(2,1)S(1)}, bf16[256,2048]{1,0:T(8,128)(2,1)S(1)}, u32[]{:S(2)}, u32[]{:S(2)}) collective-permute-start(bf16[256,2048]{1,0:T(8,128)(2,1)S(1)} %add_convert_fusion.7), channel_id=1, source_target_pairs={{0,1},{1,2},{2,3},{3,0},{4,5},{5,6},{6,7},{7,4},{8,9},{9,10},{10,1... | collective-permute-start | bytes 3145736 | tf_op jit(solution)/shard_map/ppermute | solution.py:689
  1021.9 275.6 %reduce-scatter.17.cloned.1.call-start = ((), (), s32[]{:S(2)}) async-start(), calls=%async_computation.17 | async-start | bytes 31850496 | tf_op jit(solution)/shard_map/reduce_scatter | solution.py:849
  1062.7 38.2 %collective-permute-start.44 = (bf16[256,2048]{1,0:T(8,128)(2,1)S(1)}, bf16[256,2048]{1,0:T(8,128)(2,1)S(1)}, u32[]{:S(2)}, u32[]{:S(2)}) collective-permute-start(bf16[256,2048]{1,0:T(8,128)(2,1)S(1)} %add_convert_fusion.2), channel_id=1, source_target_pairs={{0,1},{1,2},{2,3},{3,0},{4,5},{5,6},{6,7},{7,4},{8,9},{9,10},{10,1... | collective-permute-start | bytes 3145736 | tf_op jit(solution)/shard_map/ppermute | solution.py:689
  1105.0 106.0 %collective-permute-start.48 = (f32[576]{0:T(1024)S(1)}, f32[576]{0:T(1024)S(1)}, u32[]{:S(2)}, u32[]{:S(2)}) collective-permute-start(f32[576]{0:T(1024)S(1)} %pad_maximum_fusion.19), channel_id=1, source_target_pairs={{0,1},{1,0},{2,3},{3,2},{4,5},{5,4},{6,7},{7,6},{8,9},{9,8},{10,11... | collective-permute-start | bytes 6920 | tf_op jit(solution)/shard_map/ppermute | solution.py:729
  1133.1 42.5 %collective-permute-start.45 = (bf16[256,4096]{1,0:T(8,128)(2,1)}, bf16[256,4096]{1,0:T(8,128)(2,1)}, u32[]{:S(2)}, u32[]{:S(2)}) collective-permute-start(bf16[256,4096]{1,0:T(8,128)(2,1)} %slice.893), channel_id=1, source_target_pairs={{0,1},{1,2},{2,3},{3,0},{4,5},{5,6},{6,7},{7,4},{8,9},{9,10},{10,1... | collective-permute-start | bytes 6291464 | tf_op jit(solution)/shard_map/ppermute | solution.py:689
  1179.5 48.3 %collective-permute-start.46 = (bf16[256,4096]{1,0:T(8,128)(2,1)}, bf16[256,4096]{1,0:T(8,128)(2,1)}, u32[]{:S(2)}, u32[]{:S(2)}) collective-permute-start(bf16[256,4096]{1,0:T(8,128)(2,1)} %add_convert_fusion.1), channel_id=1, source_target_pairs={{0,1},{1,2},{2,3},{3,0},{4,5},{5,6},{6,7},{7,4},{8,9},{9,10},{10,1... | collective-permute-start | bytes 6291464 | tf_op jit(solution)/shard_map/ppermute | solution.py:689
  1184.4 37.8 %collective-permute-start.47 = (bf16[4,16,7168]{2,1,0:T(8,128)(2,1)}, bf16[4,16,7168]{2,1,0:T(8,128)(2,1)S(1)}, u32[]{:S(2)}, u32[]{:S(2)}) collective-permute-start(bf16[4,16,7168]{2,1,0:T(8,128)(2,1)} %bitcast.37), channel_id=1, source_target_pairs={{0,16},{4,20},{8,24},{12,28},{16,0},{20,4},{24,8},{28,12},{1,17},{... | collective-permute-start | bytes 2752520 | tf_op jit(solution)/shard_map/ppermute | solution.py:706
  1191.4 60.6 %collective-permute-start.52 = (bf16[256,384]{1,0:T(8,128)(2,1)S(1)}, bf16[256,384]{1,0:T(8,128)(2,1)S(1)}, u32[]{:S(2)}, u32[]{:S(2)}) collective-permute-start(bf16[256,384]{1,0:T(8,128)(2,1)S(1)} %fusion.219), channel_id=1, source_target_pairs={{0,1},{1,0},{2,3},{3,2},{4,5},{5,4},{6,7},{7,6},{8,9},{9,8},{10,11... | collective-permute-start | bytes 589832 | tf_op jit(solution)/shard_map/ppermute | solution.py:729
  1230.4 39.9 %collective-permute-start.49 = (bf16[256,4096]{1,0:T(8,128)(2,1)S(1)}, bf16[256,4096]{1,0:T(8,128)(2,1)}, u32[]{:S(2)}, u32[]{:S(2)}) collective-permute-start(bf16[256,4096]{1,0:T(8,128)(2,1)S(1)} %add_convert_fusion), channel_id=1, source_target_pairs={{0,1},{1,2},{2,3},{3,0},{4,5},{5,6},{6,7},{7,4},{8,9},{9,10},{10,1... | collective-permute-start | bytes 6291464 | tf_op jit(solution)/shard_map/ppermute | solution.py:689
  1231.8 35.7 %collective-permute-start.51 = (f32[576]{0:T(1024)S(1)}, f32[576]{0:T(1024)S(1)}, u32[]{:S(2)}, u32[]{:S(2)}) collective-permute-start(f32[576]{0:T(1024)S(1)} %fusion.237), channel_id=1, source_target_pairs={{0,2},{1,3},{2,0},{3,1},{4,6},{5,7},{6,4},{7,5},{8,10},{9,11},{10,... | collective-permute-start | bytes 6920 | tf_op jit(solution)/shard_map/ppermute | solution.py:729
  1233.2 34.3 %collective-permute-start.50 = (bf16[2,16,7168]{2,1,0:T(8,128)(2,1)S(1)}, bf16[2,16,7168]{2,1,0:T(8,128)(2,1)S(1)}, u32[]{:S(2)}, u32[]{:S(2)}) collective-permute-start(bf16[2,16,7168]{2,1,0:T(8,128)(2,1)S(1)} %select_convert_fusion.1), channel_id=1, source_target_pairs={{0,8},{4,12},{8,0},{12,4},{16,24},{20,28},{24,16},{28,20},{1,9},{5... | collective-permute-start | bytes 1376264 | tf_op jit(solution)/shard_map/ppermute | solution.py:706
  (166 other events, 2022.6 us)
Sparse Core Ops, SparseCore 0:
  13.3 150.1 all-gather.8
  165.3 37.4 all-gather.10
  204.7 92.0 all-gather.12
  298.6 55.9 all-gather.14
  356.3 61.0 all-gather.16
  419.1 37.4 all-gather.18
  672.7 49.4 reduce-scatter.6
  726.1 78.9 reduce-scatter.8
  852.3 68.1 reduce-scatter.10
  924.0 118.5 reduce-scatter.12
  1046.9 51.2 reduce-scatter.14
  1101.8 192.7 reduce-scatter.16

commit v6 on v5

--- a/solution.py
+++ b/solution.py
@@ -92,14 +92,14 @@
     scale = HDA ** (-0.5)
     for at in range(0, rows, block):
         upto = at + block
-        scores = mm_nt(q_ref[at:upto, :], k_ref[:upto, :]) * scale
-        query = at + iota((block, 1), 0)
-        key = iota((1, upto), 1)
+        scores = mm_nt(k_ref[:upto, :], q_ref[at:upto, :]) * scale
+        query = at + iota((1, block), 1)
+        key = iota((upto, 1), 0)
         seen = (key <= query) & (key >= starts_of(query, ends))
         scores = jnp.where(seen, scores, -1e30)
-        raised = jnp.exp(scores - jnp.max(scores, axis=1, keepdims=True))
-        probs = (raised * (1.0 / jnp.sum(raised, axis=1, keepdims=True))).astype(bf16)
-        held[at:upto, :] = mm(probs, v_ref[:upto, :]).astype(bf16)
+        raised = jnp.exp(scores - jnp.max(scores, axis=0, keepdims=True))
+        probs = (raised * (1.0 / jnp.sum(raised, axis=0, keepdims=True))).astype(bf16)
+        held[at:upto, :] = mm_tn(probs, v_ref[:upto, :]).astype(bf16)
     for p in range(tp):
         owner = lax.rem(here - p + tp, tp)
         part = pl.ds(pl.multiple_of(owner * share, share), share)
@@ -496,9 +496,13 @@
     grad_all[:, 2 * width + 2 * LANES :] = grad_raw.astype(bf16)
 
 
-def mixer_specs(tp, rows, width, order):
+def chunk_of(tp, rows):
+    return math.gcd(rows // tp, CHUNK)
+
+
+def mixer_specs(tp, rows, chunk, order):
     share = rows // tp
-    per_share = share // CHUNK
+    per_share = share // chunk
 
     def here(place, c):
         owner = lax.div(c, per_share)
@@ -512,7 +516,7 @@
         def index(i, place, lengths):
             c = order(i)
             previous = jnp.maximum(c - 1, 0)
-            return (here(place, previous) * (CHUNK // unit) + CHUNK // unit - 1, column)
+            return (here(place, previous) * (chunk // unit) + chunk // unit - 1, column)
 
         return index
 
@@ -524,9 +528,10 @@
 
 def mixer_forward(place, lengths, tp, zx, sd, wide, narrow, rates):
     rows, width = zx.shape[0], zx.shape[1] // 2
-    chunks = rows // CHUNK
-    chunk_map, before_map, fixed = mixer_specs(tp, rows, width, lambda i: i)
-    work = rows * width * CHUNK
+    chunk = chunk_of(tp, rows)
+    chunks = rows // chunk
+    chunk_map, before_map, fixed = mixer_specs(tp, rows, chunk, lambda i: i)
+    work = rows * width * chunk
     return pl.pallas_call(
         mixer_forward_kernel,
         out_shape=[
@@ -537,16 +542,16 @@
             num_scalar_prefetch=2,
             grid=(chunks,),
             in_specs=[
-                pl.BlockSpec((CHUNK, 2 * width), chunk_map),
+                pl.BlockSpec((chunk, 2 * width), chunk_map),
                 pl.BlockSpec((16, width), before_map(16, 1)),
-                pl.BlockSpec((CHUNK, 3 * LANES), chunk_map),
+                pl.BlockSpec((chunk, 3 * LANES), chunk_map),
                 pl.BlockSpec((8, 3 * LANES), before_map(8, 0)),
                 pl.BlockSpec((8, width), fixed),
                 pl.BlockSpec((8, 2 * LANES), fixed),
                 pl.BlockSpec((8, LANES), fixed),
             ],
             out_specs=[
-                pl.BlockSpec((CHUNK, width), chunk_map),
+                pl.BlockSpec((chunk, width), chunk_map),
                 pl.BlockSpec((None, HD, width), lambda i, *_: (i, 0, 0)),
             ],
             scratch_shapes=[pltpu.VMEM((HD, width), f32)],
@@ -561,9 +566,10 @@
 
 def mixer_backward(place, lengths, tp, zx, sd, grad_scaled, stats, states, wide, narrow, rates):
     rows, width = zx.shape[0], zx.shape[1] // 2
-    chunks = rows // CHUNK
-    chunk_map, before_map, fixed = mixer_specs(tp, rows, width, lambda i: chunks - 1 - i)
-    work = rows * width * CHUNK
+    chunk = chunk_of(tp, rows)
+    chunks = rows // chunk
+    chunk_map, before_map, fixed = mixer_specs(tp, rows, chunk, lambda i: chunks - 1 - i)
+    work = rows * width * chunk
     return pl.pallas_call(
         functools.partial(mixer_backward_kernel, chunks),
         out_shape=[
@@ -576,19 +582,19 @@
             num_scalar_prefetch=2,
             grid=(chunks,),
             in_specs=[
-                pl.BlockSpec((CHUNK, 2 * width), chunk_map),
+                pl.BlockSpec((chunk, 2 * width), chunk_map),
                 pl.BlockSpec((16, width), before_map(16, 1)),
-                pl.BlockSpec((CHUNK, 3 * LANES), chunk_map),
+                pl.BlockSpec((chunk, 3 * LANES), chunk_map),
                 pl.BlockSpec((8, 3 * LANES), before_map(8, 0)),
-                pl.BlockSpec((CHUNK, width), chunk_map),
-                pl.BlockSpec((CHUNK, 2), chunk_map),
+                pl.BlockSpec((chunk, width), chunk_map),
+                pl.BlockSpec((chunk, 2), chunk_map),
                 pl.BlockSpec((None, HD, width), lambda i, *_: (chunks - 1 - i, 0, 0)),
                 pl.BlockSpec((8, width), fixed),
                 pl.BlockSpec((8, 2 * LANES), fixed),
                 pl.BlockSpec((8, LANES), fixed),
             ],
             out_specs=[
-                pl.BlockSpec((CHUNK, 2 * width + 3 * LANES), chunk_map),
+                pl.BlockSpec((chunk, 2 * width + 3 * LANES), chunk_map),
                 pl.BlockSpec((8, width), fixed),
                 pl.BlockSpec((8, 2 * LANES), fixed),
                 pl.BlockSpec((8, LANES), fixed),
@@ -598,9 +604,9 @@
                 pltpu.VMEM((8, width), f32),
                 pltpu.VMEM((8, 2 * LANES), f32),
                 pltpu.VMEM((8, LANES), f32),
-                pltpu.VMEM((CHUNK, width), f32),
-                pltpu.VMEM((CHUNK, width), f32),
-                pltpu.VMEM((CHUNK, width), f32),
+                pltpu.VMEM((chunk, width), f32),
+                pltpu.VMEM((chunk, width), f32),
+                pltpu.VMEM((chunk, width), f32),
             ],
         ),
         compiler_params=pltpu.CompilerParams(vmem_limit_bytes=VMEM_LIMIT),
@@ -739,6 +745,21 @@
             self.start()
             self.finish()
         return self.values
+
+
+def direct(values, name, sent_as=f32):
+    count = lax.axis_size(name)
+    here = lax.axis_index(name)
+
+    def block(at):
+        return lax.dynamic_index_in_dim(values, lax.rem(at, count), 0, keepdims=False)
+
+    total = block(here)
+    for step in range(1, count):
+        sent = block(here + step).astype(sent_as)
+        moved = lax.ppermute(sent, name, [(i, (i + step) % count) for i in range(count)])
+        total = total + moved.astype(f32)
+    return total
 
 
 def begin(tasks):
@@ -1119,7 +1140,9 @@
         grad_residual_low, lambda p, v: feed_back(p, v) if p < tp - 1 else (), [small_task]
     )
     grad_mlp_in, filled = ring_scatter(
-        lambda p, t: back_terms[p] if p < tp - 1 else feed_back(p, after(grad_branch[p], t)),
+        lambda p, t: feed_back(p, after(grad_branch[p], t))
+        if p == tp - 1
+        else tie(back_terms[p], grad_branch[-1]),
         [fc2_fill] + [lambda t, _: ()] * (tp - 3) + [fc1_fill],
     )
     sum_w_fc2, sum_w_fc1 = filled[0], filled[-1]
@@ -1229,12 +1252,8 @@
     )
     gain_rows = jnp.sum(sum_w_qkv.astype(f32) * own_qkv.astype(f32), axis=1)
     gain_rows = gain_rows / attention_norm_gain.astype(f32)
-    down_task = Halving(sum_w_qkv[:, 3 * head_cols :].astype(f32).reshape(tp, -1, 3 * rank), "tp", bf16)
-    gain_last = Halving(gain_rows.reshape(tp, -1), "tp")
-    while down_task.live():
-        for t in begin([down_task, gain_last]):
-            t.finish()
-    grad_down, grad_gain_attn = down_task.result(), gain_last.result()
+    grad_down = direct(sum_w_qkv[:, 3 * head_cols :].astype(f32).reshape(tp, -1, 3 * rank), "tp", bf16)
+    grad_gain_attn = direct(gain_rows.reshape(tp, -1), "tp")
     grad_w_qkv = jnp.stack(
         [sum_w_qkv[:, j * head_cols : (j + 1) * head_cols].astype(f32) for j in range(3)], axis=1
     )

time: 1340 us -> 1320 us (0.985)
  waiting for transfers between devices: 380 us -> 364 us
    unnamed x320 -> x325, local copies, waits for them, and re-layouts: 57.1 us -> 59.8 us
  transfers between devices with their start and end apart: 71 -> 73, of which waited for: 33 -> 35; matrix products, arithmetic and copies ran while one was open for 50% -> 50% of each run, Pallas kernels for 9% -> 9%
where the time goes in v6:
time: 1320 us; the launch traced here: 1310 us
  matrix products  462 us (35%)
  waiting for transfers between devices  364 us (28%)
  other arithmetic  153 us (12%)
  Pallas kernels  133 us (10%)
  local copies, waits for them, and re-layouts  113 us (9%)
  starting transfers between devices  51.7 us (4%)
  blocking collectives  17.7 us (1%)
  between operations  17.3 us (1%)
    ppermute x39, waiting for transfers between devices, hop(): return lax.ppermute(values, 'tp', ring_pairs())  327 us
    dot_general x24, matrix products, mm_nt(): lax.dot_general(left, right, (((1,), (1,)), ((), ())), preferred_element_...  190 us
    dot_general x23, matrix products, mm(): return jnp.dot(left, right, preferred_element_type=f32)  140 us
    dot_general x10, matrix products, mm_tn(): lax.dot_general(left, right, (((0,), (0,)), ((), ())), preferred_element_...  132 us
    unnamed x325, local copies, waits for them, and re-layouts  59.8 us
    pallas_call x1, Pallas kernels, attention_backward(): pl.pallas_call(functools.partial(attention_backward_kernel, tp, heads), o...  39.3 us
    concatenate x2, other arithmetic, local(): jnp.concatenate([jnp.concatenate(v, axis=1) for v in normed[low:high]], a...  37.9 us
    pallas_call x1, Pallas kernels, mixer_backward(): pl.pallas_call(functools.partial(mixer_backward_kernel, chunks), out_shap...  36.4 us
  transfers between devices with their start and end apart: 73, of which 35 were waited for; matrix products, arithmetic and copies ran while one was open for 50% of the time, Pallas kernels for 9%

profile of v6, /device:TPU:0, one launch (start us, length us, event | category | flops | bytes accessed | tf_op | source)
XLA Modules:
  0.0 1312.6 jit_solution(2387637157129552860)
XLA Ops:
  37.8 9.2 all-gather.1
  57.0 17.8 %collective-permute-done = bf16[256,2048]{1,0:T(8,128)(2,1)} collective-permute-done((bf16[256,2048]{1,0:T(8,128)(2,1)S(1)}, bf16[256,2048]{1,0:T(8,128)(2,1)}, u32[]{:S(2)}, u32[]{:S(2)}) %collective-permute-start) | collective-permute-done | bytes 1048608 | tf_op jit(solution)/shard_map/ppermute | solution.py:695
  79.0 18.2 %collective-permute-done.3 = bf16[256,2048]{1,0:T(8,128)(2,1)S(1)} collective-permute-done((bf16[256,2048]{1,0:T(8,128)(2,1)S(1)}, bf16[256,2048]{1,0:T(8,128)(2,1)S(1)}, u32[]{:S(2)}, u32[]{:S(2)}) %collective-permute-start.3) | collective-permute-done | bytes 1048608 | tf_op jit(solution)/shard_map/ppermute | solution.py:695
  97.2 21.6 %collective-permute-done.1 = bf16[256,2048]{1,0:T(8,128)(2,1)S(1)} collective-permute-done((bf16[256,2048]{1,0:T(8,128)(2,1)}, bf16[256,2048]{1,0:T(8,128)(2,1)S(1)}, u32[]{:S(2)}, u32[]{:S(2)}) %collective-permute-start.1) | collective-permute-done | bytes 1048608 | tf_op jit(solution)/shard_map/ppermute | solution.py:695
  125.3 18.9 %maximum_maximum_fusion = bf16[512,4096]{1,0:T(8,128)(2,1)} fusion(bf16[256,2048]{1,0:T(8,128)(2,1)S(1)} %get-tuple-element.468, bf16[256,2048]{1,0:T(8,128)(2,1)S(1)} %get-tuple-element.478, bf16[256,2048]{1,0:T(8,128)(2,1)S(1)} %copy-done.41, bf16[256,2048]{1,0:T(8,128)(2,1)S(1)} %copy-done.43), kind=kLoop, calls=%fused_computation.69 | loop fusion | flops 16777216 | bytes 8388608 | tf_op jit(solution)/shard_map/concatenate | solution.py:1009
  148.7 18.8 %collective-permute-done.8 = bf16[256,2048]{1,0:T(8,128)(2,1)S(1)} collective-permute-done((bf16[256,2048]{1,0:T(8,128)(2,1)S(1)}, bf16[256,2048]{1,0:T(8,128)(2,1)S(1)}, u32[]{:S(2)}, u32[]{:S(2)}) %collective-permute-start.8) | collective-permute-done | bytes 1048608 | tf_op jit(solution)/shard_map/ppermute | solution.py:695
  169.0 19.0 %maximum_maximum_fusion.1 = bf16[512,4096]{1,0:T(8,128)(2,1)} fusion(bf16[256,2048]{1,0:T(8,128)(2,1)S(1)} %get-tuple-element.484, bf16[256,2048]{1,0:T(8,128)(2,1)S(1)} %get-tuple-element.483, bf16[256,2048]{1,0:T(8,128)(2,1)S(1)} %get-tuple-element.467, bf16[256,2048]{1,0:T(8,128)(2,1)S(1)} %get-tuple-element.479), kind=kLoop, calls=%fused_computation.70 | loop fusion | flops 16777216 | bytes 8388608 | tf_op jit(solution)/shard_map/concatenate | solution.py:1009
  189.3 21.7 %fusion.259.refs_0_.refs_1_.refs_2_.refs_3_ = f32[512,3456]{1,0:T(8,128)S(1)} fusion(bf16[4096,3456]{1,0:T(8,128)(2,1)} %all-gather.9.cloned.1.call-done, bf16[256,2048]{1,0:T(8,128)(2,1)} %copy-done.46, bf16[256,2048]{1,0:T(8,128)(2,1)} %copy-done.47, bf16[256,2048]{1,0:T(8,128)(2,1)S(1)} %copy-done.42, bf16[256,2048]{1,0:T(8,128)(2,1)} %get-tuple-element.486), kind=kOutput, calls=%fused_computation.492 | convolution fusion | flops 14512291840 | bytes 39583744 | tf_op jit(solution)/shard_map/dot_general | solution.py:25
  211.2 25.0 %fusion.258.refs_4_.refs_5_.refs_6_.refs_7_ = f32[512,3456]{1,0:T(8,128)S(1)} fusion(bf16[4096,3456]{1,0:T(8,128)(2,1)} %all-gather.9.cloned.1.call-done, bf16[256,2048]{1,0:T(8,128)(2,1)} %copy-done.49, bf16[256,2048]{1,0:T(8,128)(2,1)} %copy-done.48, bf16[256,2048]{1,0:T(8,128)(2,1)} %copy-done.44, bf16[256,2048]{1,0:T(8,128)(2,1)} %copy-done.45), kind=kOutput, calls=%fused_computation.491 | convolution fusion | flops 14512291840 | bytes 39583744 | tf_op jit(solution)/shard_map/dot_general | solution.py:25
  240.5 21.6 %attention_forward.1 = (bf16[1024,1024]{1,0:T(8,128)(2,1)}, bf16[1024,1024]{1,0:T(8,128)(2,1)}, bf16[1024,1024]{1,0:T(8,128)(2,1)}, bf16[1024,1024]{1,0:T(8,128)(2,1)}) custom-call(s32[1]{0:T(128)} %bitcast.place_ref, s32[3]{0:T(128)} %bitcast.284, f32[1024,128]{1,0:T(8,128)} %get-tuple-element.487.cosine_ref, f32[1024,128]{1,0:T(8,128)} %get-tuple-element.488.sine_ref, ...), custom_call_target="tpu_custom_call" | custom-call | flops 4294967296 | bytes 20971520 | tf_op jit(solution)/shard_map/attention_forward/pallas_call | solution.py:119
  278.8 13.5 %collective-permute-done.12 = bf16[256,2048]{1,0:T(8,128)(2,1)} collective-permute-done((bf16[256,2048]{1,0:T(8,128)(2,1)S(1)}, bf16[256,2048]{1,0:T(8,128)(2,1)}, u32[]{:S(2)}, u32[]{:S(2)}) %collective-permute-start.12) | collective-permute-done | bytes 1048608 | tf_op jit(solution)/shard_map/ppermute | solution.py:695
  298.8 20.6 %collective-permute-done.13 = bf16[256,2048]{1,0:T(8,128)(2,1)} collective-permute-done((bf16[256,2048]{1,0:T(8,128)(2,1)S(1)}, bf16[256,2048]{1,0:T(8,128)(2,1)}, u32[]{:S(2)}, u32[]{:S(2)}) %collective-permute-start.13) | collective-permute-done | bytes 1048608 | tf_op jit(solution)/shard_map/ppermute | solution.py:695
  326.5 19.6 %collective-permute-done.14 = bf16[256,2048]{1,0:T(8,128)(2,1)} collective-permute-done((bf16[256,2048]{1,0:T(8,128)(2,1)}, bf16[256,2048]{1,0:T(8,128)(2,1)}, u32[]{:S(2)}, u32[]{:S(2)}) %collective-permute-start.14) | collective-permute-done | bytes 1048608 | tf_op jit(solution)/shard_map/ppermute | solution.py:695
  349.4 9.7 fusion.275
  389.1 11.3 collective-permute-done.17
  423.8 21.6 %collective-permute-done.19 = bf16[256,2048]{1,0:T(8,128)(2,1)S(1)} collective-permute-done((bf16[256,2048]{1,0:T(8,128)(2,1)S(1)}, bf16[256,2048]{1,0:T(8,128)(2,1)S(1)}, u32[]{:S(2)}, u32[]{:S(2)}) %collective-permute-start.19) | collective-permute-done | bytes 1048608 | tf_op jit(solution)/shard_map/ppermute | solution.py:695
  445.4 9.3 fusion.279
  472.9 12.0 collective-permute-done.20
  488.4 8.5 fusion.281
  518.7 16.3 %collective-permute-done.22 = bf16[256,2048]{1,0:T(8,128)(2,1)S(1)} collective-permute-done((bf16[256,2048]{1,0:T(8,128)(2,1)}, bf16[256,2048]{1,0:T(8,128)(2,1)S(1)}, u32[]{:S(2)}, u32[]{:S(2)}) %collective-permute-start.22) | collective-permute-done | bytes 1048608 | tf_op jit(solution)/shard_map/ppermute | solution.py:695
  539.2 15.0 %collective-permute-done.23 = bf16[256,2048]{1,0:T(8,128)(2,1)S(1)} collective-permute-done((bf16[256,2048]{1,0:T(8,128)(2,1)S(1)}, bf16[256,2048]{1,0:T(8,128)(2,1)S(1)}, u32[]{:S(2)}, u32[]{:S(2)}) %collective-permute-start.23) | collective-permute-done | bytes 1048608 | tf_op jit(solution)/shard_map/ppermute | solution.py:695
  561.0 17.6 %mixer_forward.1 = (bf16[1024,1024]{1,0:T(8,128)(2,1)}, bf16[8,64,1024]{2,1,0:T(8,128)(2,1)}) custom-call(s32[1]{0:T(128)} %bitcast.place_ref, s32[3]{0:T(128)} %bitcast.285, bf16[1024,2048]{1,0:T(8,128)(2,1)} %pad_maximum_fusion.1.zx.before, bf16[1024,2048]{1,0:T(8,128)(2,1)} %pad_maximum_fusion.1.zx.before, f32[1024,384]{1,0:T(8,128)} %pad_maximum_fusion.9.sd.sd_before, ...), custom_call_target="tpu_custom_call" | custom-call | flops 1073741824 | bytes 8388608 | tf_op jit(solution)/shard_map/mixer_forward/pallas_call | solution.py:535
  581.5 8.5 psum.7
  602.9 36.4 %mixer_backward.1 = (bf16[1024,2432]{1,0:T(8,128)(2,1)}, f32[8,1024]{1,0:T(8,128)}, f32[8,256]{1,0:T(8,128)}, f32[8,128]{1,0:T(8,128)}) custom-call(s32[1]{0:T(128)} %bitcast.place_ref, s32[3]{0:T(128)} %bitcast.286, bf16[1024,2048]{1,0:T(8,128)(2,1)} %pad_maximum_fusion.1.zx.before, bf16[1024,2048]{1,0:T(8,128)(2,1)} %pad_maximum_fusion.1.zx.before, ...), custom_call_target="tpu_custom_call" | custom-call | flops 3221225472 | bytes 12582912 | tf_op jit(solution)/shard_map/mixer_backward/pallas_call | solution.py:573
  639.4 8.5 convolution_convert_fusion.6
  672.3 16.3 %convolution_convert_fusion.2 = bf16[2048,2432]{1,0:T(8,128)(2,1)} fusion(bf16[1024,2048]{1,0:T(8,128)(2,1)S(1)} %pad_maximum_fusion.2, bf16[1024,2432]{1,0:T(8,128)(2,1)} %get-tuple-element.244), kind=kOutput, calls=%fused_computation.2 | convolution fusion | flops 10205528064 | bytes 19136512 | tf_op jit(solution)/shard_map/dot_general | solution.py:33
  688.6 8.4 fusion.192
  730.3 9.6 fusion.136
  741.9 13.6 %fusion.79 = f32[256,2048]{1,0:T(8,128)} fusion(bf16[2048,4224]{1,0:T(8,128)(2,1)} %all-gather.13.cloned.1.call-done, bf16[256,128]{1,0:T(8,128)(2,1)S(1)} %fusion.206, bf16[256,2048]{1,0:T(8,128)(2,1)} %copy-done.123, bf16[256,2048]{1,0:T(8,128)(2,1)} %copy-done.121), kind=kOutput, calls=%fused_computation.153 | convolution fusion | flops 4435673088 | bytes 21561344 | tf_op jit(solution)/shard_map/dot_general | solution.py:29
  769.8 12.7 fusion.85
  794.7 13.0 fusion.91
  811.0 13.9 %convolution_convert_fusion.3 = bf16[2048,2048]{1,0:T(8,128)(2,1)} fusion(bf16[1024,2048]{1,0:T(8,128)(2,1)} %pad_maximum_fusion.3, bf16[256,2048]{1,0:T(8,128)(2,1)} %collective-permute-done.33, bf16[256,2048]{1,0:T(8,128)(2,1)} %collective-permute-done.31, bf16[256,2048]{1,0:T(8,128)(2,1)} %collective-permute-done.29, bf16[256,2048]{1,0:T(8,128)(2,1)S(1)} %copy-done.119), kind=kOutput, calls=%fused_computation.51 | convolution fusion | flops 8610906112 | bytes 16777216 | tf_op jit(solution)/shard_map/dot_general | solution.py:33
  825.0 12.7 collective-permute-done.35
  842.0 9.2 fusion.130
  853.2 9.1 fusion.97
  870.8 29.5 %convolution_convert_fusion.1 = bf16[2048,4224]{1,0:T(8,128)(2,1)} fusion(bf16[1024,2048]{1,0:T(8,128)(2,1)} %copy-done.81, bf16[256,128]{1,0:T(8,128)(2,1)S(1)} %fusion.197, bf16[256,2048]{1,0:T(8,128)(2,1)} %copy-done.129, bf16[256,2048]{1,0:T(8,128)(2,1)} %copy-done.128, bf16[256,128]{1,0:T(8,128)(2,1)S(1)} %fusion.200, ...), kind=kOutput, calls=%fused_computation.1 | convolution fusion | flops 17829199872 | bytes 30146560 | tf_op jit(solution)/shard_map/dot_general | solution.py:33
  914.6 17.8 %fusion.23 = f32[128,4096]{1,0:T(8,128)} fusion(bf16[1024,128]{1,0:T(8,128)(2,1)S(1)} %pad_maximum_fusion.16, bf16[256,128]{1,0:T(8,128)(2,1)S(1)} %copy-done.135, bf16[256,2048]{1,0:T(8,128)(2,1)} %copy-done.129, bf16[256,2048]{1,0:T(8,128)(2,1)} %copy-done.128, bf16[256,128]{1,0:T(8,128)(2,1)S(1)} %copy-done.133, bf16[256,2048]{1,0:T(8,128)(2,1)} %copy-done.127, ...), kind=kOutput, calls=%fused_computation.26 | convolution fusion | flops 1174405120 | bytes 11010048 | tf_op jit(solution)/shard_map/dot_general | solution.py:33
  943.2 20.2 %collective-permute-done.40 = bf16[256,2048]{1,0:T(8,128)(2,1)} collective-permute-done((bf16[256,2048]{1,0:T(8,128)(2,1)S(1)}, bf16[256,2048]{1,0:T(8,128)(2,1)}, u32[]{:S(2)}, u32[]{:S(2)}) %collective-permute-start.40) | collective-permute-done | bytes 1048608 | tf_op jit(solution)/shard_map/ppermute | solution.py:695
  968.9 22.7 %collective-permute-done.42 = bf16[256,2048]{1,0:T(8,128)(2,1)} collective-permute-done((bf16[256,2048]{1,0:T(8,128)(2,1)}, bf16[256,2048]{1,0:T(8,128)(2,1)}, u32[]{:S(2)}, u32[]{:S(2)}) %collective-permute-start.42) | collective-permute-done | bytes 1048608 | tf_op jit(solution)/shard_map/ppermute | solution.py:695
  991.7 9.1 fusion.70
  1006.1 39.3 %attention_backward.1 = bf16[1024,3456]{1,0:T(8,128)(2,1)} custom-call(s32[1]{0:T(128)} %bitcast.place_ref, s32[3]{0:T(128)} %bitcast.287, f32[1024,128]{1,0:T(8,128)} %get-tuple-element.487.cosine_ref, f32[1024,128]{1,0:T(8,128)} %get-tuple-element.488.sine_ref, bf16[1024,1024]{1,0:T(8,128)(2,1)} %get-tuple-element.232.q_ref, ...), custom_call_target="tpu_custom_call" | custom-call | flops 10737418240 | bytes 14680064 | tf_op jit(solution)/shard_map/attention_backward/pallas_call | solution.py:233
  1047.4 38.0 %convolution_convert_fusion = bf16[4096,3456]{1,0:T(8,128)(2,1)} fusion(bf16[1024,4096]{1,0:T(8,128)(2,1)} %pad_maximum_fusion, bf16[1024,3456]{1,0:T(8,128)(2,1)} %attention_backward.1), kind=kOutput, calls=%fused_computation | convolution fusion | flops 29005185024 | bytes 43778048 | tf_op jit(solution)/shard_map/dot_general | solution.py:33
  1089.5 21.0 %fusion.73 = f32[512,4096]{1,0:T(8,128)S(1)} fusion(bf16[4096,3456]{1,0:T(8,128)(2,1)} %all-gather.9.cloned.1.call-done, bf16[1024,3456]{1,0:T(8,128)(2,1)} %attention_backward.1), kind=kOutput, calls=%fused_computation.117 | convolution fusion | flops 14495514624 | bytes 40239104 | tf_op jit(solution)/shard_map/dot_general | solution.py:29
  1131.7 17.7 %fusion.188 = f32[256,4096]{1,0:T(8,128)} fusion(bf16[4096,3456]{1,0:T(8,128)(2,1)} %all-gather.9.cloned.1.call-done, bf16[1024,3456]{1,0:T(8,128)(2,1)} %attention_backward.1), kind=kOutput, calls=%fused_computation.296 | convolution fusion | flops 7247757312 | bytes 34275328 | tf_op jit(solution)/shard_map/dot_general | solution.py:29
  1149.4 9.5 collective-permute-done.45
  1194.3 9.9 collective-permute-done.47
  1218.0 15.8 %fusion.186 = f32[256,4096]{1,0:T(8,128)} fusion(bf16[4096,3456]{1,0:T(8,128)(2,1)} %all-gather.9.cloned.1.call-done, bf16[1024,3456]{1,0:T(8,128)(2,1)} %attention_backward.1), kind=kOutput, calls=%fused_computation.294 | convolution fusion | flops 7247757312 | bytes 34275328 | tf_op jit(solution)/shard_map/dot_general | solution.py:29
  1233.9 14.8 %collective-permute-done.51 = f32[576]{0:T(1024)S(1)} collective-permute-done((f32[576]{0:T(1024)S(1)}, f32[576]{0:T(1024)S(1)}, u32[]{:S(2)}, u32[]{:S(2)}) %collective-permute-start.51) | collective-permute-done | bytes 2336 | tf_op jit(solution)/shard_map/ppermute | solution.py:735
  (739 shorter events, 491.2 us)
Async XLA Ops:
  7.2 181.2 %all-gather.9.cloned.1.call-start = ((), (), s32[]{:S(2)}) async-start(), calls=%async_computation.6 | async-start | bytes 31850496 | tf_op jit(solution)/shard_map/all_gather | solution.py:866
  13.2 249.2 %all-gather.11.cloned.1.call-start = ((), (), s32[]{:S(2)}) async-start(), calls=%async_computation.7 | async-start | bytes 4718592 | tf_op jit(solution)/shard_map/all_gather | solution.py:866
  13.9 335.5 %all-gather.13.cloned.1.call-start = ((), (), s32[]{:S(2)}) async-start(), calls=%async_computation.8 | async-start | bytes 19464192 | tf_op jit(solution)/shard_map/all_gather | solution.py:866
  22.6 340.9 %all-gather.15.cloned.1.call-start = ((), (), s32[]{:S(2)}) async-start(), calls=%async_computation.9 | async-start | bytes 9437184 | tf_op jit(solution)/shard_map/all_gather | solution.py:866
  23.1 465.2 %all-gather.17.cloned.1.call-start = ((), (), s32[]{:S(2)}) async-start(), calls=%async_computation.10 | async-start | bytes 11206656 | tf_op jit(solution)/shard_map/all_gather | solution.py:866
  23.2 32.2 %collective-permute-start.2 = (bf16[256,2048]{1,0:T(8,128)(2,1)S(1)}, bf16[256,2048]{1,0:T(8,128)(2,1)S(1)}, u32[]{:S(2)}, u32[]{:S(2)}) collective-permute-start(bf16[256,2048]{1,0:T(8,128)(2,1)S(1)} %copy-done.11), channel_id=1, source_target_pairs={{0,1},{1,2},{2,3},{3,0},{4,5},{5,6},{6,7},{7,4},{8,9},{9,10},{10,1... | collective-permute-start | bytes 3145736 | tf_op jit(solution)/shard_map/ppermute | solution.py:695
  26.3 48.6 %collective-permute-start = (bf16[256,2048]{1,0:T(8,128)(2,1)S(1)}, bf16[256,2048]{1,0:T(8,128)(2,1)}, u32[]{:S(2)}, u32[]{:S(2)}) collective-permute-start(bf16[256,2048]{1,0:T(8,128)(2,1)S(1)} %copy-done.9), channel_id=1, source_target_pairs={{0,1},{1,2},{2,3},{3,0},{4,5},{5,6},{6,7},{7,4},{8,9},{9,10},{10,1... | collective-permute-start | bytes 3145736 | tf_op jit(solution)/shard_map/ppermute | solution.py:695
  35.7 461.2 %all-gather.19.cloned.1.call-start = ((), (), s32[]{:S(2)}) async-start(), calls=%async_computation.11 | async-start | bytes 4718592 | tf_op jit(solution)/shard_map/all_gather | solution.py:866
  55.4 41.8 %collective-permute-start.3 = (bf16[256,2048]{1,0:T(8,128)(2,1)S(1)}, bf16[256,2048]{1,0:T(8,128)(2,1)S(1)}, u32[]{:S(2)}, u32[]{:S(2)}) collective-permute-start(bf16[256,2048]{1,0:T(8,128)(2,1)S(1)} %collective-permute-done.2), channel_id=1, source_target_pairs={{0,1},{1,2},{2,3},{3,0},{4,5},{5,6},{6,7},{7,4},{8,9},{9,10},{10,1... | collective-permute-start | bytes 3145736 | tf_op jit(solution)/shard_map/ppermute | solution.py:695
  74.9 44.0 %collective-permute-start.1 = (bf16[256,2048]{1,0:T(8,128)(2,1)}, bf16[256,2048]{1,0:T(8,128)(2,1)S(1)}, u32[]{:S(2)}, u32[]{:S(2)}) collective-permute-start(bf16[256,2048]{1,0:T(8,128)(2,1)} %collective-permute-done), channel_id=1, source_target_pairs={{0,1},{1,2},{2,3},{3,0},{4,5},{5,6},{6,7},{7,4},{8,9},{9,10},{10,1... | collective-permute-start | bytes 3145736 | tf_op jit(solution)/shard_map/ppermute | solution.py:695
  118.9 29.8 %collective-permute-start.7 = (bf16[256,2048]{1,0:T(8,128)(2,1)S(1)}, bf16[256,2048]{1,0:T(8,128)(2,1)S(1)}, u32[]{:S(2)}, u32[]{:S(2)}) collective-permute-start(bf16[256,2048]{1,0:T(8,128)(2,1)S(1)} %collective-permute-done.1), channel_id=1, source_target_pairs={{0,1},{1,2},{2,3},{3,0},{4,5},{5,6},{6,7},{7,4},{8,9},{9,10},{10,1... | collective-permute-start | bytes 3145736 | tf_op jit(solution)/shard_map/ppermute | solution.py:695
  119.3 48.1 %collective-permute-start.8 = (bf16[256,2048]{1,0:T(8,128)(2,1)S(1)}, bf16[256,2048]{1,0:T(8,128)(2,1)S(1)}, u32[]{:S(2)}, u32[]{:S(2)}) collective-permute-start(bf16[256,2048]{1,0:T(8,128)(2,1)S(1)} %collective-permute-done.3), channel_id=1, source_target_pairs={{0,1},{1,2},{2,3},{3,0},{4,5},{5,6},{6,7},{7,4},{8,9},{9,10},{10,1... | collective-permute-start | bytes 3145736 | tf_op jit(solution)/shard_map/ppermute | solution.py:695
  147.1 41.0 %collective-permute-start.6 = (bf16[64,7168]{1,0:T(8,128)(2,1)S(1)}, bf16[64,7168]{1,0:T(8,128)(2,1)S(1)}, u32[]{:S(2)}, u32[]{:S(2)}) collective-permute-start(bf16[64,7168]{1,0:T(8,128)(2,1)S(1)} %pad_maximum_fusion.10), channel_id=1, source_target_pairs={{0,16},{4,20},{8,24},{12,28},{16,0},{20,4},{24,8},{28,12},{1,17},{... | collective-permute-start | bytes 2752520 | tf_op jit(solution)/shard_map/ppermute | solution.py:852
  167.5 43.6 %collective-permute-start.9 = (bf16[256,2048]{1,0:T(8,128)(2,1)}, bf16[256,2048]{1,0:T(8,128)(2,1)}, u32[]{:S(2)}, u32[]{:S(2)}) collective-permute-start(bf16[256,2048]{1,0:T(8,128)(2,1)} %refs_3_.1), channel_id=1, source_target_pairs={{0,1},{1,2},{2,3},{3,0},{4,5},{5,6},{6,7},{7,4},{8,9},{9,10},{10,1... | collective-permute-start | bytes 3145736 | tf_op jit(solution)/shard_map/ppermute | solution.py:695
  211.1 25.8 %collective-permute-start.10 = (bf16[256,2048]{1,0:T(8,128)(2,1)}, bf16[256,2048]{1,0:T(8,128)(2,1)}, u32[]{:S(2)}, u32[]{:S(2)}) collective-permute-start(bf16[256,2048]{1,0:T(8,128)(2,1)} %collective-permute-done.9), channel_id=1, source_target_pairs={{0,1},{1,2},{2,3},{3,0},{4,5},{5,6},{6,7},{7,4},{8,9},{9,10},{10,1... | collective-permute-start | bytes 3145736 | tf_op jit(solution)/shard_map/ppermute | solution.py:695
  236.9 25.5 %collective-permute-start.11 = (bf16[256,2048]{1,0:T(8,128)(2,1)}, bf16[256,2048]{1,0:T(8,128)(2,1)}, u32[]{:S(2)}, u32[]{:S(2)}) collective-permute-start(bf16[256,2048]{1,0:T(8,128)(2,1)} %collective-permute-done.10), channel_id=1, source_target_pairs={{0,1},{1,2},{2,3},{3,0},{4,5},{5,6},{6,7},{7,4},{8,9},{9,10},{10,1... | collective-permute-start | bytes 3145736 | tf_op jit(solution)/shard_map/ppermute | solution.py:695
  266.2 26.1 %collective-permute-start.12 = (bf16[256,2048]{1,0:T(8,128)(2,1)S(1)}, bf16[256,2048]{1,0:T(8,128)(2,1)}, u32[]{:S(2)}, u32[]{:S(2)}) collective-permute-start(bf16[256,2048]{1,0:T(8,128)(2,1)S(1)} %convolution_convert_fusion.7), channel_id=1, source_target_pairs={{0,1},{1,2},{2,3},{3,0},{4,5},{5,6},{6,7},{7,4},{8,9},{9,10},{10,1... | collective-permute-start | bytes 3145736 | tf_op jit(solution)/shard_map/ppermute | solution.py:695
  294.5 516.5 %reduce-scatter.7.cloned.1.call-start = ((), (), s32[]{:S(2)}) async-start(), calls=%async_computation.12 | async-start | bytes 4718592 | tf_op jit(solution)/shard_map/reduce_scatter | solution.py:870
  372.5 27.9 %collective-permute-start.17 = (bf16[256,2048]{1,0:T(8,128)(2,1)}, bf16[256,2048]{1,0:T(8,128)(2,1)S(1)}, u32[]{:S(2)}, u32[]{:S(2)}) collective-permute-start(bf16[256,2048]{1,0:T(8,128)(2,1)} %collective-permute-done.15), channel_id=1, source_target_pairs={{0,1},{1,2},{2,3},{3,0},{4,5},{5,6},{6,7},{7,4},{8,9},{9,10},{10,1... | collective-permute-start | bytes 3145736 | tf_op jit(solution)/shard_map/ppermute | solution.py:695
  389.1 33.8 %collective-permute-start.16 = (bf16[256,2048]{1,0:T(8,128)(2,1)S(1)}, bf16[256,2048]{1,0:T(8,128)(2,1)S(1)}, u32[]{:S(2)}, u32[]{:S(2)}) collective-permute-start(bf16[256,2048]{1,0:T(8,128)(2,1)S(1)} %convolution_convert_fusion.8), channel_id=1, source_target_pairs={{0,1},{1,2},{2,3},{3,0},{4,5},{5,6},{6,7},{7,4},{8,9},{9,10},{10,1... | collective-permute-start | bytes 3145736 | tf_op jit(solution)/shard_map/ppermute | solution.py:695
  400.4 44.9 %collective-permute-start.19 = (bf16[256,2048]{1,0:T(8,128)(2,1)S(1)}, bf16[256,2048]{1,0:T(8,128)(2,1)S(1)}, u32[]{:S(2)}, u32[]{:S(2)}) collective-permute-start(bf16[256,2048]{1,0:T(8,128)(2,1)S(1)} %collective-permute-done.17), channel_id=1, source_target_pairs={{0,1},{1,2},{2,3},{3,0},{4,5},{5,6},{6,7},{7,4},{8,9},{9,10},{10,1... | collective-permute-start | bytes 3145736 | tf_op jit(solution)/shard_map/ppermute | solution.py:695
  423.2 39.6 %collective-permute-start.18 = (bf16[256,2048]{1,0:T(8,128)(2,1)S(1)}, bf16[256,2048]{1,0:T(8,128)(2,1)S(1)}, u32[]{:S(2)}, u32[]{:S(2)}) collective-permute-start(bf16[256,2048]{1,0:T(8,128)(2,1)S(1)} %add_convert_fusion.9), channel_id=1, source_target_pairs={{0,1},{1,2},{2,3},{3,0},{4,5},{5,6},{6,7},{7,4},{8,9},{9,10},{10,1... | collective-permute-start | bytes 3145736 | tf_op jit(solution)/shard_map/ppermute | solution.py:695
  599.5 39.9 %collective-permute-start.24 = (bf16[256,2048]{1,0:T(8,128)(2,1)S(1)}, bf16[256,2048]{1,0:T(8,128)(2,1)S(1)}, u32[]{:S(2)}, u32[]{:S(2)}) collective-permute-start(bf16[256,2048]{1,0:T(8,128)(2,1)S(1)} %slice.518), channel_id=1, source_target_pairs={{0,1},{1,2},{2,3},{3,0},{4,5},{5,6},{6,7},{7,4},{8,9},{9,10},{10,1... | collective-permute-start | bytes 3145736 | tf_op jit(solution)/shard_map/ppermute | solution.py:695
  667.2 247.3 %reduce-scatter.9.cloned.1.call-start = ((), (), s32[]{:S(2)}) async-start(), calls=%async_computation.13 | async-start | bytes 11206656 | tf_op jit(solution)/shard_map/reduce_scatter | solution.py:870
  698.0 270.9 %reduce-scatter.11.cloned.1.call-start = ((), (), s32[]{:S(2)}) async-start(), calls=%async_computation.14 | async-start | bytes 9437184 | tf_op jit(solution)/shard_map/reduce_scatter | solution.py:870
  720.1 35.4 %collective-permute-start.30 = (f32[4,864]{1,0:T(4,128)S(1)}, f32[4,864]{1,0:T(4,128)S(1)}, u32[]{:S(2)}, u32[]{:S(2)}) collective-permute-start(f32[4,864]{1,0:T(4,128)S(1)} %slice_select_fusion.1), channel_id=1, source_target_pairs={{0,16},{4,20},{8,24},{12,28},{16,0},{20,4},{24,8},{28,12},{1,17},{... | collective-permute-start | bytes 41480 | tf_op jit(solution)/shard_map/ppermute | solution.py:712
  730.0 25.5 %collective-permute-start.29 = (bf16[256,2048]{1,0:T(8,128)(2,1)}, bf16[256,2048]{1,0:T(8,128)(2,1)}, u32[]{:S(2)}, u32[]{:S(2)}) collective-permute-start(bf16[256,2048]{1,0:T(8,128)(2,1)} %get-tuple-element.253), channel_id=1, source_target_pairs={{0,1},{1,2},{2,3},{3,0},{4,5},{5,6},{6,7},{7,4},{8,9},{9,10},{10,1... | collective-permute-start | bytes 3145736 | tf_op jit(solution)/shard_map/ppermute | solution.py:695
  755.6 27.0 %collective-permute-start.32 = (f32[2,864]{1,0:T(2,128)S(1)}, f32[2,864]{1,0:T(2,128)S(1)}, u32[]{:S(2)}, u32[]{:S(2)}) collective-permute-start(f32[2,864]{1,0:T(2,128)S(1)} %broadcast_select_fusion.8), channel_id=1, source_target_pairs={{0,8},{4,12},{8,0},{12,4},{16,24},{20,28},{24,16},{28,20},{1,9},{5... | collective-permute-start | bytes 20744 | tf_op jit(solution)/shard_map/ppermute | solution.py:712
  782.6 25.1 %collective-permute-start.34 = (f32[1,864]{1,0:T(1,128)S(1)}, f32[1,864]{1,0:T(1,128)S(1)}, u32[]{:S(2)}, u32[]{:S(2)}) collective-permute-start(f32[1,864]{1,0:T(1,128)S(1)} %broadcast_select_fusion.7), channel_id=1, source_target_pairs={{0,4},{4,0},{8,12},{12,8},{16,20},{20,16},{24,28},{28,24},{1,5},{5... | collective-permute-start | bytes 10376 | tf_op jit(solution)/shard_map/ppermute | solution.py:712
  782.6 28.1 %collective-permute-start.33 = (bf16[256,2048]{1,0:T(8,128)(2,1)}, bf16[256,2048]{1,0:T(8,128)(2,1)}, u32[]{:S(2)}, u32[]{:S(2)}) collective-permute-start(bf16[256,2048]{1,0:T(8,128)(2,1)} %collective-permute-done.31), channel_id=1, source_target_pairs={{0,1},{1,2},{2,3},{3,0},{4,5},{5,6},{6,7},{7,4},{8,9},{9,10},{10,1... | collective-permute-start | bytes 3145736 | tf_op jit(solution)/shard_map/ppermute | solution.py:695
  810.8 26.9 %collective-permute-start.35 = (bf16[256,2048]{1,0:T(8,128)(2,1)}, bf16[256,2048]{1,0:T(8,128)(2,1)S(1)}, u32[]{:S(2)}, u32[]{:S(2)}) collective-permute-start(bf16[256,2048]{1,0:T(8,128)(2,1)} %fusion.85), channel_id=1, source_target_pairs={{0,1},{1,2},{2,3},{3,0},{4,5},{5,6},{6,7},{7,4},{8,9},{9,10},{10,1... | collective-permute-start | bytes 3145736 | tf_op jit(solution)/shard_map/ppermute | solution.py:695
  838.7 206.8 %reduce-scatter.13.cloned.1.call-start = ((), (), s32[]{:S(2)}) async-start(), calls=%async_computation.15 | async-start | bytes 19464192 | tf_op jit(solution)/shard_map/reduce_scatter | solution.py:870
  842.0 25.9 %collective-permute-start.36 = (bf16[256,2048]{1,0:T(8,128)(2,1)}, bf16[256,2048]{1,0:T(8,128)(2,1)}, u32[]{:S(2)}, u32[]{:S(2)}) collective-permute-start(bf16[256,2048]{1,0:T(8,128)(2,1)} %add_convert_fusion.4), channel_id=1, source_target_pairs={{0,1},{1,2},{2,3},{3,0},{4,5},{5,6},{6,7},{7,4},{8,9},{9,10},{10,1... | collective-permute-start | bytes 3145736 | tf_op jit(solution)/shard_map/ppermute | solution.py:695
  870.4 29.9 %collective-permute-start.37 = (bf16[256,2048]{1,0:T(8,128)(2,1)}, bf16[256,2048]{1,0:T(8,128)(2,1)S(1)}, u32[]{:S(2)}, u32[]{:S(2)}) collective-permute-start(bf16[256,2048]{1,0:T(8,128)(2,1)} %add_convert_fusion.3), channel_id=1, source_target_pairs={{0,1},{1,2},{2,3},{3,0},{4,5},{5,6},{6,7},{7,4},{8,9},{9,10},{10,1... | collective-permute-start | bytes 3145736 | tf_op jit(solution)/shard_map/ppermute | solution.py:695
  900.3 268.9 %reduce-scatter.15.cloned.1.call-start = ((), (), s32[]{:S(2)}) async-start(), calls=%async_computation.16 | async-start | bytes 4718592 | tf_op jit(solution)/shard_map/reduce_scatter | solution.py:870
  914.5 25.0 %collective-permute-start.38 = (bf16[256,2048]{1,0:T(8,128)(2,1)}, bf16[256,2048]{1,0:T(8,128)(2,1)S(1)}, u32[]{:S(2)}, u32[]{:S(2)}) collective-permute-start(bf16[256,2048]{1,0:T(8,128)(2,1)} %get-tuple-element.287), channel_id=1, source_target_pairs={{0,1},{1,2},{2,3},{3,0},{4,5},{5,6},{6,7},{7,4},{8,9},{9,10},{10,1... | collective-permute-start | bytes 3145736 | tf_op jit(solution)/shard_map/ppermute | solution.py:695
  963.4 28.2 %collective-permute-start.42 = (bf16[256,2048]{1,0:T(8,128)(2,1)}, bf16[256,2048]{1,0:T(8,128)(2,1)}, u32[]{:S(2)}, u32[]{:S(2)}) collective-permute-start(bf16[256,2048]{1,0:T(8,128)(2,1)} %collective-permute-done.40), channel_id=1, source_target_pairs={{0,1},{1,2},{2,3},{3,0},{4,5},{5,6},{6,7},{7,4},{8,9},{9,10},{10,1... | collective-permute-start | bytes 3145736 | tf_op jit(solution)/shard_map/ppermute | solution.py:695
  965.1 80.3 %collective-permute-start.25 = (bf16[256,2048]{1,0:T(8,128)(2,1)S(1)}, bf16[256,2048]{1,0:T(8,128)(2,1)S(1)}, u32[]{:S(2)}, u32[]{:S(2)}) collective-permute-start(bf16[256,2048]{1,0:T(8,128)(2,1)S(1)} %add_convert_fusion.7), channel_id=1, source_target_pairs={{0,1},{1,2},{2,3},{3,0},{4,5},{5,6},{6,7},{7,4},{8,9},{9,10},{10,1... | collective-permute-start | bytes 3145736 | tf_op jit(solution)/shard_map/ppermute | solution.py:695
  1006.1 274.9 %reduce-scatter.17.cloned.1.call-start = ((), (), s32[]{:S(2)}) async-start(), calls=%async_computation.17 | async-start | bytes 31850496 | tf_op jit(solution)/shard_map/reduce_scatter | solution.py:870
  1047.2 38.3 %collective-permute-start.44 = (bf16[256,2048]{1,0:T(8,128)(2,1)S(1)}, bf16[256,2048]{1,0:T(8,128)(2,1)S(1)}, u32[]{:S(2)}, u32[]{:S(2)}) collective-permute-start(bf16[256,2048]{1,0:T(8,128)(2,1)S(1)} %add_convert_fusion.2), channel_id=1, source_target_pairs={{0,1},{1,2},{2,3},{3,0},{4,5},{5,6},{6,7},{7,4},{8,9},{9,10},{10,1... | collective-permute-start | bytes 3145736 | tf_op jit(solution)/shard_map/ppermute | solution.py:695
  1089.5 104.8 %collective-permute-start.48 = (f32[576]{0:T(1024)S(1)}, f32[576]{0:T(1024)S(1)}, u32[]{:S(2)}, u32[]{:S(2)}) collective-permute-start(f32[576]{0:T(1024)S(1)} %pad_maximum_fusion.19), channel_id=1, source_target_pairs={{0,1},{1,0},{2,3},{3,2},{4,5},{5,4},{6,7},{7,6},{8,9},{9,8},{10,11... | collective-permute-start | bytes 6920 | tf_op jit(solution)/shard_map/ppermute | solution.py:735
  1116.4 42.5 %collective-permute-start.45 = (bf16[256,4096]{1,0:T(8,128)(2,1)}, bf16[256,4096]{1,0:T(8,128)(2,1)}, u32[]{:S(2)}, u32[]{:S(2)}) collective-permute-start(bf16[256,4096]{1,0:T(8,128)(2,1)} %slice.820), channel_id=1, source_target_pairs={{0,1},{1,2},{2,3},{3,0},{4,5},{5,6},{6,7},{7,4},{8,9},{9,10},{10,1... | collective-permute-start | bytes 6291464 | tf_op jit(solution)/shard_map/ppermute | solution.py:695
  1162.7 48.7 %collective-permute-start.46 = (bf16[256,4096]{1,0:T(8,128)(2,1)}, bf16[256,4096]{1,0:T(8,128)(2,1)}, u32[]{:S(2)}, u32[]{:S(2)}) collective-permute-start(bf16[256,4096]{1,0:T(8,128)(2,1)} %add_convert_fusion.1), channel_id=1, source_target_pairs={{0,1},{1,2},{2,3},{3,0},{4,5},{5,6},{6,7},{7,4},{8,9},{9,10},{10,1... | collective-permute-start | bytes 6291464 | tf_op jit(solution)/shard_map/ppermute | solution.py:695
  1168.0 36.2 %collective-permute-start.47 = (bf16[4,16,7168]{2,1,0:T(8,128)(2,1)}, bf16[4,16,7168]{2,1,0:T(8,128)(2,1)S(1)}, u32[]{:S(2)}, u32[]{:S(2)}) collective-permute-start(bf16[4,16,7168]{2,1,0:T(8,128)(2,1)} %bitcast.37), channel_id=1, source_target_pairs={{0,16},{4,20},{8,24},{12,28},{16,0},{20,4},{24,8},{28,12},{1,17},{... | collective-permute-start | bytes 2752520 | tf_op jit(solution)/shard_map/ppermute | solution.py:712
  1174.8 59.0 %collective-permute-start.52 = (bf16[256,384]{1,0:T(8,128)(2,1)S(1)}, bf16[256,384]{1,0:T(8,128)(2,1)S(1)}, u32[]{:S(2)}, u32[]{:S(2)}) collective-permute-start(bf16[256,384]{1,0:T(8,128)(2,1)S(1)} %fusion.219), channel_id=1, source_target_pairs={{0,1},{1,0},{2,3},{3,2},{4,5},{5,4},{6,7},{7,6},{8,9},{9,8},{10,11... | collective-permute-start | bytes 589832 | tf_op jit(solution)/shard_map/ppermute | solution.py:735
  1213.7 37.7 %collective-permute-start.49 = (bf16[256,4096]{1,0:T(8,128)(2,1)S(1)}, bf16[256,4096]{1,0:T(8,128)(2,1)}, u32[]{:S(2)}, u32[]{:S(2)}) collective-permute-start(bf16[256,4096]{1,0:T(8,128)(2,1)S(1)} %add_convert_fusion), channel_id=1, source_target_pairs={{0,1},{1,2},{2,3},{3,0},{4,5},{5,6},{6,7},{7,4},{8,9},{9,10},{10,1... | collective-permute-start | bytes 6291464 | tf_op jit(solution)/shard_map/ppermute | solution.py:695
  1215.3 33.4 %collective-permute-start.51 = (f32[576]{0:T(1024)S(1)}, f32[576]{0:T(1024)S(1)}, u32[]{:S(2)}, u32[]{:S(2)}) collective-permute-start(f32[576]{0:T(1024)S(1)} %fusion.245), channel_id=1, source_target_pairs={{0,2},{1,3},{2,0},{3,1},{4,6},{5,7},{6,4},{7,5},{8,10},{9,11},{10,... | collective-permute-start | bytes 6920 | tf_op jit(solution)/shard_map/ppermute | solution.py:735
  1217.9 30.8 %collective-permute-start.50 = (bf16[2,16,7168]{2,1,0:T(8,128)(2,1)S(1)}, bf16[2,16,7168]{2,1,0:T(8,128)(2,1)S(1)}, u32[]{:S(2)}, u32[]{:S(2)}) collective-permute-start(bf16[2,16,7168]{2,1,0:T(8,128)(2,1)S(1)} %select_convert_fusion.1), channel_id=1, source_target_pairs={{0,8},{4,12},{8,0},{12,4},{16,24},{20,28},{24,16},{28,20},{1,9},{5... | collective-permute-start | bytes 1376264 | tf_op jit(solution)/shard_map/ppermute | solution.py:712
  (170 other events, 1992.1 us)
Sparse Core Ops, SparseCore 0:
  13.3 150.1 all-gather.8
  165.4 37.4 all-gather.10
  204.7 92.1 all-gather.12
  298.7 55.8 all-gather.14
  356.3 61.0 all-gather.16
  419.1 37.4 all-gather.18
  667.3 49.6 reduce-scatter.6
  721.0 78.9 reduce-scatter.8
  838.8 67.9 reduce-scatter.10
  910.3 118.5 reduce-scatter.12
  1033.2 51.3 reduce-scatter.14
  1088.1 192.7 reduce-scatter.16

commit v7 on v6

--- a/solution.py
+++ b/solution.py
@@ -617,6 +617,38 @@
     )(place, lengths, zx, zx, sd, sd, grad_scaled, stats, states, wide, narrow, rates)
 
 
+def norm_pairs_kernel(pairs, gain, *refs):
+    out = refs[2 * pairs]
+    width = refs[0].shape[1]
+    for j in range(pairs):
+        both = [refs[2 * j + i][...].astype(f32) for i in range(2)]
+        squares = sum(jnp.sum(v * v, axis=1, keepdims=True) for v in both)
+        inv_root = lax.rsqrt(squares / (2 * width) + norm_eps)
+        for i, v in enumerate(both):
+            cols = slice(i * width, (i + 1) * width)
+            out[j, :, cols] = (v * inv_root * gain[:, cols]).astype(bf16)
+
+
+def norm_pairs(pairs, gain):
+    rows, width = pairs[0][0].shape
+    block = math.gcd(rows, 64)
+    count = len(pairs)
+    result = pl.pallas_call(
+        functools.partial(norm_pairs_kernel, count),
+        out_shape=jax.ShapeDtypeStruct((count, rows, 2 * width), bf16),
+        grid=(rows // block,),
+        in_specs=[pl.BlockSpec((1, 2 * width), lambda i: (0, 0))]
+        + [pl.BlockSpec((block, width), lambda i: (i, 0))] * (2 * count),
+        out_specs=pl.BlockSpec((count, block, 2 * width), lambda i: (0, i, 0)),
+        compiler_params=pltpu.CompilerParams(vmem_limit_bytes=VMEM_LIMIT),
+        cost_estimate=pl.CostEstimate(
+            flops=10 * count * rows * width, bytes_accessed=8 * count * rows * width, transcendentals=rows
+        ),
+        name="norm_pairs",
+    )(gain, *[v for pair in pairs for v in pair])
+    return result.reshape(count * rows, 2 * width)
+
+
 def norm_back_kernel(parts, with_base, with_low, with_gain, *refs):
     values, refs = refs[:parts], refs[parts:]
     grad, gain, refs = refs[0], refs[1], refs[2:]
@@ -747,19 +779,19 @@
         return self.values
 
 
-def direct(values, name, sent_as=f32):
+def direct_send(values, name, sent_as=f32):
     count = lax.axis_size(name)
     here = lax.axis_index(name)
 
     def block(at):
         return lax.dynamic_index_in_dim(values, lax.rem(at, count), 0, keepdims=False)
 
-    total = block(here)
-    for step in range(1, count):
-        sent = block(here + step).astype(sent_as)
-        moved = lax.ppermute(sent, name, [(i, (i + step) % count) for i in range(count)])
-        total = total + moved.astype(f32)
-    return total
+    blocks = [block(here)] + [block(here + step).astype(sent_as) for step in range(1, count)]
+    blocks = lax.optimization_barrier(blocks)
+    return [
+        lax.ppermute(sent, name, [(i, (i + step) % count) for i in range(count)]) if step else sent
+        for step, sent in enumerate(blocks)
+    ]
 
 
 def begin(tasks):
@@ -977,21 +1009,18 @@
     weight_zx = gather(own_zx)
     weight_out = gather(mixer_output_weight, 1)
 
-    def norm_rows(pair):
-        pair = [v.astype(f32) for v in pair]
-        squares = sum(jnp.sum(v * v, axis=1, keepdims=True) for v in pair)
-        inv_root = lax.rsqrt(squares / (2 * width) + norm_eps)
-        return [
-            (v * inv_root * gain_attn[:, i * width : (i + 1) * width]).astype(bf16)
-            for i, v in enumerate(pair)
-        ]
-
-    raw, normed = [(hidden, embed), first_hop], []
+    raw, normed_parts = [(hidden, embed), first_hop], []
+    spans = [((tp * i) // (tp - 2), (tp * (i + 1)) // (tp - 2)) for i in range(tp - 2)]
+
+    def norm_ready(count):
+        fresh = [norm_pairs(raw[low:high], gain_attn) for low, high in spans[len(normed_parts) :] if high <= count]
+        normed_parts.extend(fresh)
+        return fresh
+
     for p in range(2, tp):
         moved = tuple(hop(v) for v in raw[-1])
-        normed.append(norm_rows(raw[p - 2]))
-        raw.append(tie(moved, normed[-1]))
-    normed += [norm_rows(v) for v in raw[len(normed) :]]
+        raw.append(tie(moved, norm_ready(p)))
+    norm_ready(tp)
 
     own_ups = jnp.concatenate(
         [attention_adapter_up[:, j, :] for j in range(3)]
@@ -1001,13 +1030,11 @@
     ups = doubling_gather(tie(own_ups, raw[-2]), "fsdp")
     fc_up = ups[:, 3 * head_cols :]
     out_grad = [tie(output_cotangent, raw[-1])]
-    normed_parts, projected = [], []
+    projected = []
     for i in range(tp - 1):
         moved = hop(out_grad[-1])
         if i < tp - 2:
-            low, high = (tp * i) // (tp - 2), (tp * (i + 1)) // (tp - 2)
-            normed_parts.append(jnp.concatenate([jnp.concatenate(v, axis=1) for v in normed[low:high]], axis=0))
-            projected.append(mm(normed_parts[-1], weight_qkv))
+            projected.append(mm(normed_parts[i], weight_qkv))
             moved = tie(moved, projected)
         else:
             attended, queries, keys, values = attention_forward(
@@ -1055,7 +1082,6 @@
     mixer_in, zxs = ring_gather((residual * mixer_root * gain_mixer).astype(bf16), mix)
     zxs = [v[0] for v in zxs]
     grad_scaled, units_rows, mlp_rows = kept
-    mixer_rows = jnp.concatenate(mixer_in, axis=0)
     zx = jnp.concatenate([v[:, : 2 * inner_cols].astype(bf16) for v in zxs], axis=0)
     sd = jnp.concatenate([v[:, 2 * inner_cols :] for v in zxs], axis=0)
     gated, chunk_states = mixer_forward(place, lengths, tp, zx, sd, wide, narrow, rates)
@@ -1098,11 +1124,17 @@
             by_fsdp(bars[:count].reshape(count, 2, LANES)[:, :, :states]),
         ]
 
-    grad_mixer_in, (sum_w_out, sum_w_zx, small) = ring_scatter(
+    mixer_rows = []
+
+    def out_fill(token, _):
+        mixer_rows.append(jnp.concatenate(tie(mixer_in, token), axis=0))
+        return mm_tn(tie(scaled, token), out_grad_rows).astype(bf16), mixer_rows[0]
+
+    grad_mixer_in, ((sum_w_out, _), sum_w_zx, small) = ring_scatter(
         lambda p, t: mm_nt(piece(after(grad_all, t), p), weight_zx),
         [
-            lambda t, _: mm_tn(tie(scaled, t), out_grad_rows).astype(bf16),
-            lambda t, _: mm_tn(tie(mixer_rows, t), grad_all).astype(bf16),
+            out_fill,
+            lambda t, _: mm_tn(tie(mixer_rows[0], t), grad_all).astype(bf16),
             lambda t, _: small_gradients(t),
         ],
     )
@@ -1150,22 +1182,23 @@
     sum_w_fc1 = scatter(sum_w_fc1)
     grad_gate_up_rows = jnp.concatenate(grad_gate_up, axis=0)
     _, grad_mixed_low, grad_gain_mlp = norm_back([mixed], grad_mlp_in, gain_mlp, grad_residual, True)
-    gain_task = Halving(
-        jnp.concatenate([grad_gain_mixer.reshape(fsdp, -1), grad_gain_mlp.reshape(fsdp, -1)], axis=1), "fsdp"
-    )
+    gain_tasks = []
 
     fc_ups = []
 
     def attended_back(p, rows_in):
         result = mm_nt(rows_in, weight_o).astype(bf16)
         if p == 0:
+            middle, first, second = tie((fc_mid, grad_gain_mixer, grad_gain_mlp), rows_in)
             fc_ups.append(
-                mm_tn(tie(jnp.concatenate(fc_mid, axis=0), rows_in), grad_gate_up_rows[:, : 2 * units_here])
+                mm_tn(jnp.concatenate(middle, axis=0), grad_gate_up_rows[:, : 2 * units_here])
             )
-            result = tie(result, fc_ups[0])
+            gains = jnp.concatenate([first.reshape(fsdp, -1), second.reshape(fsdp, -1)], axis=1)
+            result, gains = tie((result, gains), fc_ups[0])
+            gain_tasks.append(Halving(gains, "fsdp"))
         return result
 
-    grad_mixed, grad_attended = ring_gather(tie(grad_mixed_low, sum_w_zx), attended_back, [gain_task])
+    grad_mixed, grad_attended = ring_gather(tie(grad_mixed_low, sum_w_zx), attended_back, gain_tasks)
     sum_w_o = mm_tn(tie(attended, sum_w_fc2), jnp.concatenate(grad_mixed, axis=0)).astype(bf16)
     grad_attended[-1] = tie(grad_attended[-1], sum_w_o)
     sum_w_o = scatter(sum_w_o, 1)
@@ -1199,7 +1232,7 @@
         ]
         ups_grad = jnp.concatenate(grad_up + fc_ups, axis=1)
         tasks.append(Halving(ups_grad.reshape(fsdp, -1, ups_grad.shape[1]), "fsdp", bf16))
-        shared = jnp.concatenate([small_task.result()[small_cuts[4] :], gain_task.result()])
+        shared = jnp.concatenate([small_task.result()[small_cuts[4] :], gain_tasks[0].result()])
         tasks.append(Doubling(shared, "tp"))
         return ups_grad, shared
 
@@ -1252,11 +1285,17 @@
     )
     gain_rows = jnp.sum(sum_w_qkv.astype(f32) * own_qkv.astype(f32), axis=1)
     gain_rows = gain_rows / attention_norm_gain.astype(f32)
-    grad_down = direct(sum_w_qkv[:, 3 * head_cols :].astype(f32).reshape(tp, -1, 3 * rank), "tp", bf16)
-    grad_gain_attn = direct(gain_rows.reshape(tp, -1), "tp")
+    down_blocks = direct_send(
+        sum_w_qkv[:, 3 * head_cols :].astype(f32).reshape(tp, -1, 3 * rank), "tp", bf16
+    )
+    gain_blocks = direct_send(gain_rows.reshape(tp, -1), "tp")
+    sum_w_qkv = tie(sum_w_qkv, (down_blocks[0], gain_blocks[0]))
     grad_w_qkv = jnp.stack(
         [sum_w_qkv[:, j * head_cols : (j + 1) * head_cols].astype(f32) for j in range(3)], axis=1
     )
+    down_blocks, gain_blocks, grad_w_qkv = lax.optimization_barrier((down_blocks, gain_blocks, grad_w_qkv))
+    grad_down = sum(v.astype(f32) for v in down_blocks)
+    grad_gain_attn = sum(gain_blocks)
     small_sum = small_task.result()
     small_parts = [small_sum[small_cuts[i] : small_cuts[i + 1]] for i in range(len(small_sizes))]
     grad_ups, tail = tasks[0].result(), tasks[1].result()

time: 1320 us -> 1350 us (1.023)
  waiting for transfers between devices: 364 us -> 428 us
  other arithmetic: 153 us -> 106 us
    concatenate x5 -> x2, other arithmetic: 40.4 us -> 0.08 us  [the longest x1 0.08 us: finish_adapters(): jnp.concatenate([small_task.result()[small_cuts[4]:], gain_tasks[0].resul...]
    ppermute x39, waiting for transfers between devices: 327 us -> 357 us  [hop(): return lax.ppermute(values, 'tp', ring_pairs())]
    ppermute x3, waiting for transfers between devices: 2.62 us -> 20.3 us  [doubling_gather(): moved = lax.ppermute(values, name, [(i, i ^ step) for i in range(count)])]
    unnamed x325 -> x335, local copies, waits for them, and re-layouts: 59.8 us -> 67.4 us
  transfers between devices with their start and end apart: 73 -> 73, of which waited for: 35 -> 36; matrix products, arithmetic and copies ran while one was open for 50% -> 46% of each run, Pallas kernels for 9% -> 9%
where the time goes in v7:
time: 1350 us; the launch traced here: 1340 us
  matrix products  460 us (34%)
  waiting for transfers between devices  428 us (32%)
  Pallas kernels  144 us (11%)
  local copies, waits for them, and re-layouts  124 us (9%)
  other arithmetic  106 us (8%)
  starting transfers between devices  45.4 us (3%)
  blocking collectives  17.8 us (1%)
  between operations  17.2 us (1%)
    ppermute x39, waiting for transfers between devices, hop(): return lax.ppermute(values, 'tp', ring_pairs())  357 us
    dot_general x24, matrix products, mm_nt(): lax.dot_general(left, right, (((1,), (1,)), ((), ())), preferred_element_...  194 us
    dot_general x23, matrix products, mm(): return jnp.dot(left, right, preferred_element_type=f32)  135 us
    dot_general x10, matrix products, mm_tn(): lax.dot_general(left, right, (((0,), (0,)), ((), ())), preferred_element_...  130 us
    unnamed x335, local copies, waits for them, and re-layouts  67.4 us
    pallas_call x1, Pallas kernels, attention_backward(): pl.pallas_call(functools.partial(attention_backward_kernel, tp, heads), o...  39.2 us
    pallas_call x1, Pallas kernels, mixer_backward(): pl.pallas_call(functools.partial(mixer_backward_kernel, chunks), out_shap...  36.4 us
  transfers between devices with their start and end apart: 73, of which 36 were waited for; matrix products, arithmetic and copies ran while one was open for 46% of the time, Pallas kernels for 9%

profile of v7, /device:TPU:0, one launch (start us, length us, event | category | flops | bytes accessed | tf_op | source)
XLA Modules:
  0.0 1342.8 jit_solution(4649877932894491846)
XLA Ops:
  28.7 9.3 all-gather.1
  52.6 22.4 %collective-permute-done.refs_2_ = bf16[256,2048]{1,0:T(8,128)(2,1)} collective-permute-done((bf16[256,2048]{1,0:T(8,128)(2,1)S(1)}, bf16[256,2048]{1,0:T(8,128)(2,1)}, u32[]{:S(2)}, u32[]{:S(2)}) %collective-permute-start) | collective-permute-done | bytes 1048608 | tf_op jit(solution)/shard_map/ppermute | solution.py:727
  81.9 15.7 %collective-permute-done.3.refs_1_ = bf16[256,2048]{1,0:T(8,128)(2,1)} collective-permute-done((bf16[256,2048]{1,0:T(8,128)(2,1)}, bf16[256,2048]{1,0:T(8,128)(2,1)}, u32[]{:S(2)}, u32[]{:S(2)}) %collective-permute-start.3) | collective-permute-done | bytes 1048608 | tf_op jit(solution)/shard_map/ppermute | solution.py:727
  97.5 21.6 %collective-permute-done.1.refs_0_ = bf16[256,2048]{1,0:T(8,128)(2,1)} collective-permute-done((bf16[256,2048]{1,0:T(8,128)(2,1)}, bf16[256,2048]{1,0:T(8,128)(2,1)}, u32[]{:S(2)}, u32[]{:S(2)}) %collective-permute-start.1) | collective-permute-done | bytes 1048608 | tf_op jit(solution)/shard_map/ppermute | solution.py:727
  124.4 20.2 %collective-permute-done.5 = bf16[32,7168]{1,0:T(8,128)(2,1)S(1)} collective-permute-done((bf16[32,7168]{1,0:T(8,128)(2,1)S(1)}, bf16[32,7168]{1,0:T(8,128)(2,1)S(1)}, u32[]{:S(2)}, u32[]{:S(2)}) %collective-permute-start.5) | collective-permute-done | bytes 458784 | tf_op jit(solution)/shard_map/ppermute | solution.py:884
  152.0 21.0 %collective-permute-done.8.refs_3_ = bf16[256,2048]{1,0:T(8,128)(2,1)} collective-permute-done((bf16[256,2048]{1,0:T(8,128)(2,1)}, bf16[256,2048]{1,0:T(8,128)(2,1)}, u32[]{:S(2)}, u32[]{:S(2)}) %collective-permute-start.8) | collective-permute-done | bytes 1048608 | tf_op jit(solution)/shard_map/ppermute | solution.py:727
  180.3 21.5 %fusion.247.refs_0_.refs_1_.refs_2_.refs_3_ = f32[512,3456]{1,0:T(8,128)S(1)} fusion(bf16[512,4096]{1,0:T(8,128)(2,1)} %bitcast.231, bf16[4096,3456]{1,0:T(8,128)(2,1)} %all-gather.9.cloned.1.call-done), kind=kOutput, calls=%fused_computation.458 | convolution fusion | flops 14495514624 | bytes 39583744 | tf_op jit(solution)/shard_map/dot_general | solution.py:25
  201.9 21.8 %fusion.248.refs_4_.refs_5_.refs_6_.refs_7_ = f32[512,3456]{1,0:T(8,128)S(1)} fusion(bf16[512,4096]{1,0:T(8,128)(2,1)S(1)} %bitcast.234, bf16[4096,3456]{1,0:T(8,128)(2,1)} %all-gather.9.cloned.1.call-done), kind=kOutput, calls=%fused_computation.459 | convolution fusion | flops 14495514624 | bytes 39583744 | tf_op jit(solution)/shard_map/dot_general | solution.py:25
  230.9 21.7 %attention_forward.1 = (bf16[1024,1024]{1,0:T(8,128)(2,1)}, bf16[1024,1024]{1,0:T(8,128)(2,1)}, bf16[1024,1024]{1,0:T(8,128)(2,1)}, bf16[1024,1024]{1,0:T(8,128)(2,1)}) custom-call(s32[1]{0:T(128)} %bitcast.place_ref, s32[3]{0:T(128)} %bitcast.278, f32[1024,128]{1,0:T(8,128)} %get-tuple-element.530.cosine_ref, f32[1024,128]{1,0:T(8,128)} %get-tuple-element.531.sine_ref, ...), custom_call_target="tpu_custom_call" | custom-call | flops 4294967296 | bytes 20971520 | tf_op jit(solution)/shard_map/attention_forward/pallas_call | solution.py:119
  270.1 13.1 collective-permute-done.12
  290.9 18.2 %collective-permute-done.13 = bf16[256,2048]{1,0:T(8,128)(2,1)} collective-permute-done((bf16[256,2048]{1,0:T(8,128)(2,1)S(1)}, bf16[256,2048]{1,0:T(8,128)(2,1)}, u32[]{:S(2)}, u32[]{:S(2)}) %collective-permute-start.13) | collective-permute-done | bytes 1048608 | tf_op jit(solution)/shard_map/ppermute | solution.py:727
  317.7 16.8 %collective-permute-done.14 = bf16[256,2048]{1,0:T(8,128)(2,1)} collective-permute-done((bf16[256,2048]{1,0:T(8,128)(2,1)}, bf16[256,2048]{1,0:T(8,128)(2,1)}, u32[]{:S(2)}, u32[]{:S(2)}) %collective-permute-start.14) | collective-permute-done | bytes 1048608 | tf_op jit(solution)/shard_map/ppermute | solution.py:727
  337.8 9.3 fusion.250
  381.0 8.9 collective-permute-done.17
  413.0 21.9 %collective-permute-done.19 = bf16[256,2048]{1,0:T(8,128)(2,1)S(1)} collective-permute-done((bf16[256,2048]{1,0:T(8,128)(2,1)S(1)}, bf16[256,2048]{1,0:T(8,128)(2,1)S(1)}, u32[]{:S(2)}, u32[]{:S(2)}) %collective-permute-start.19) | collective-permute-done | bytes 1048608 | tf_op jit(solution)/shard_map/ppermute | solution.py:727
  434.9 9.3 fusion.254
  465.2 19.4 %collective-permute-done.20 = bf16[256,2048]{1,0:T(8,128)(2,1)} collective-permute-done((bf16[256,2048]{1,0:T(8,128)(2,1)}, bf16[256,2048]{1,0:T(8,128)(2,1)}, u32[]{:S(2)}, u32[]{:S(2)}) %collective-permute-start.20) | collective-permute-done | bytes 1048608 | tf_op jit(solution)/shard_map/ppermute | solution.py:727
  488.1 8.5 fusion.256
  504.7 9.0 collective-permute-done.21
  520.8 17.6 %collective-permute-done.22 = bf16[256,2048]{1,0:T(8,128)(2,1)S(1)} collective-permute-done((bf16[256,2048]{1,0:T(8,128)(2,1)}, bf16[256,2048]{1,0:T(8,128)(2,1)S(1)}, u32[]{:S(2)}, u32[]{:S(2)}) %collective-permute-start.22) | collective-permute-done | bytes 1048608 | tf_op jit(solution)/shard_map/ppermute | solution.py:727
  542.7 19.6 %collective-permute-done.23 = bf16[256,2048]{1,0:T(8,128)(2,1)S(1)} collective-permute-done((bf16[256,2048]{1,0:T(8,128)(2,1)S(1)}, bf16[256,2048]{1,0:T(8,128)(2,1)S(1)}, u32[]{:S(2)}, u32[]{:S(2)}) %collective-permute-start.23) | collective-permute-done | bytes 1048608 | tf_op jit(solution)/shard_map/ppermute | solution.py:727
  569.2 17.6 %mixer_forward.1 = (bf16[1024,1024]{1,0:T(8,128)(2,1)}, bf16[8,64,1024]{2,1,0:T(8,128)(2,1)}) custom-call(s32[1]{0:T(128)} %bitcast.place_ref, s32[3]{0:T(128)} %bitcast.279, bf16[1024,2048]{1,0:T(8,128)(2,1)} %pad_maximum_fusion.1.zx.before, bf16[1024,2048]{1,0:T(8,128)(2,1)} %pad_maximum_fusion.1.zx.before, f32[1024,384]{1,0:T(8,128)} %pad_maximum_fusion.8.sd.sd_before, ...), custom_call_target="tpu_custom_call" | custom-call | flops 1073741824 | bytes 8388608 | tf_op jit(solution)/shard_map/mixer_forward/pallas_call | solution.py:535
  589.7 8.5 psum.7
  610.7 36.4 %mixer_backward.1 = (bf16[1024,2432]{1,0:T(8,128)(2,1)}, f32[8,1024]{1,0:T(8,128)}, f32[8,256]{1,0:T(8,128)}, f32[8,128]{1,0:T(8,128)}) custom-call(s32[1]{0:T(128)} %bitcast.place_ref, s32[3]{0:T(128)} %bitcast.280, bf16[1024,2048]{1,0:T(8,128)(2,1)} %pad_maximum_fusion.1.zx.before, bf16[1024,2048]{1,0:T(8,128)(2,1)} %pad_maximum_fusion.1.zx.before, ...), custom_call_target="tpu_custom_call" | custom-call | flops 3221225472 | bytes 12582912 | tf_op jit(solution)/shard_map/mixer_backward/pallas_call | solution.py:573
  679.2 15.8 %convolution_convert_fusion.2 = bf16[2048,2432]{1,0:T(8,128)(2,1)} fusion(bf16[1024,2048]{1,0:T(8,128)(2,1)S(1)} %copy-done.84, bf16[1024,2432]{1,0:T(8,128)(2,1)} %get-tuple-element.275), kind=kOutput, calls=%fused_computation.2 | convolution fusion | flops 10205528064 | bytes 19136512 | tf_op jit(solution)/shard_map/dot_general | solution.py:33
  695.0 9.1 fusion.167
  719.8 8.7 collective-permute-done.28
  738.6 9.6 fusion.115
  750.3 13.6 %fusion.79 = f32[256,2048]{1,0:T(8,128)} fusion(bf16[2048,4224]{1,0:T(8,128)(2,1)} %all-gather.13.cloned.1.call-done, bf16[256,128]{1,0:T(8,128)(2,1)S(1)} %fusion.181, bf16[256,2048]{1,0:T(8,128)(2,1)} %copy-done.129, bf16[256,2048]{1,0:T(8,128)(2,1)} %copy-done.128), kind=kOutput, calls=%fused_computation.133 | convolution fusion | flops 4435673088 | bytes 21561344 | tf_op jit(solution)/shard_map/dot_general | solution.py:29
  776.0 12.6 fusion.85
  801.0 13.0 fusion.91
  817.6 13.9 %convolution_convert_fusion.3 = bf16[2048,2048]{1,0:T(8,128)(2,1)} fusion(bf16[1024,2048]{1,0:T(8,128)(2,1)} %pad_maximum_fusion.2, bf16[256,2048]{1,0:T(8,128)(2,1)} %collective-permute-done.33, bf16[256,2048]{1,0:T(8,128)(2,1)} %collective-permute-done.31, bf16[256,2048]{1,0:T(8,128)(2,1)} %collective-permute-done.29, bf16[256,2048]{1,0:T(8,128)(2,1)S(1)} %copy-done.126), kind=kOutput, calls=%fused_computation.51 | convolution fusion | flops 8610906112 | bytes 16777216 | tf_op jit(solution)/shard_map/dot_general | solution.py:33
  831.6 12.3 collective-permute-done.35
  848.2 9.1 fusion.109
  859.3 9.1 fusion.97
  877.2 29.6 %convolution_convert_fusion.1 = bf16[2048,4224]{1,0:T(8,128)(2,1)} fusion(bf16[1024,2048]{1,0:T(8,128)(2,1)} %copy-done.82, bf16[256,128]{1,0:T(8,128)(2,1)S(1)} %fusion.172, bf16[256,2048]{1,0:T(8,128)(2,1)} %copy-done.135, bf16[256,2048]{1,0:T(8,128)(2,1)} %copy-done.134, bf16[256,128]{1,0:T(8,128)(2,1)S(1)} %fusion.175, ...), kind=kOutput, calls=%fused_computation.1 | convolution fusion | flops 17829199872 | bytes 30146560 | tf_op jit(solution)/shard_map/dot_general | solution.py:33
  920.7 16.4 %fusion.23 = f32[128,4096]{1,0:T(8,128)} fusion(bf16[256,128]{1,0:T(8,128)(2,1)S(1)} %copy-done.139, bf16[256,2048]{1,0:T(8,128)(2,1)} %copy-done.135, bf16[256,2048]{1,0:T(8,128)(2,1)} %copy-done.134, bf16[256,128]{1,0:T(8,128)(2,1)S(1)} %copy-done.137, bf16[256,2048]{1,0:T(8,128)(2,1)} %copy-done.133, bf16[256,2048]{1,0:T(8,128)(2,1)} %copy-done.132, ...), kind=kOutput, calls=%fused_computation.26 | convolution fusion | flops 1175453696 | bytes 11010048 | tf_op jit(solution)/shard_map/dot_general | solution.py:33
  949.5 20.4 %collective-permute-done.39 = bf16[256,2048]{1,0:T(8,128)(2,1)} collective-permute-done((bf16[256,2048]{1,0:T(8,128)(2,1)S(1)}, bf16[256,2048]{1,0:T(8,128)(2,1)}, u32[]{:S(2)}, u32[]{:S(2)}) %collective-permute-start.39) | collective-permute-done | bytes 1048608 | tf_op jit(solution)/shard_map/ppermute | solution.py:727
  976.3 21.8 %collective-permute-done.41 = bf16[256,2048]{1,0:T(8,128)(2,1)} collective-permute-done((bf16[256,2048]{1,0:T(8,128)(2,1)}, bf16[256,2048]{1,0:T(8,128)(2,1)}, u32[]{:S(2)}, u32[]{:S(2)}) %collective-permute-start.41) | collective-permute-done | bytes 1048608 | tf_op jit(solution)/shard_map/ppermute | solution.py:727
  998.1 9.1 fusion.70
  1012.6 39.2 %attention_backward.1 = bf16[1024,3456]{1,0:T(8,128)(2,1)} custom-call(s32[1]{0:T(128)} %bitcast.place_ref, s32[3]{0:T(128)} %bitcast.281, f32[1024,128]{1,0:T(8,128)} %get-tuple-element.530.cosine_ref, f32[1024,128]{1,0:T(8,128)} %get-tuple-element.531.sine_ref, bf16[1024,1024]{1,0:T(8,128)(2,1)} %get-tuple-element.259.q_ref, ...), custom_call_target="tpu_custom_call" | custom-call | flops 10737418240 | bytes 14680064 | tf_op jit(solution)/shard_map/attention_backward/pallas_call | solution.py:233
  1053.9 38.0 %convolution_convert_fusion = bf16[4096,3456]{1,0:T(8,128)(2,1)} fusion(bf16[1024,4096]{1,0:T(8,128)(2,1)} %pad_maximum_fusion, bf16[1024,3456]{1,0:T(8,128)(2,1)} %attention_backward.1), kind=kOutput, calls=%fused_computation | convolution fusion | flops 29005185024 | bytes 43778048 | tf_op jit(solution)/shard_map/dot_general | solution.py:33
  1096.1 20.9 %fusion.73 = f32[512,4096]{1,0:T(8,128)S(1)} fusion(bf16[4096,3456]{1,0:T(8,128)(2,1)} %all-gather.9.cloned.1.call-done, bf16[1024,3456]{1,0:T(8,128)(2,1)} %attention_backward.1), kind=kOutput, calls=%fused_computation.114 | convolution fusion | flops 14495514624 | bytes 40239104 | tf_op jit(solution)/shard_map/dot_general | solution.py:29
  1138.8 17.7 %fusion.163 = f32[256,4096]{1,0:T(8,128)} fusion(bf16[4096,3456]{1,0:T(8,128)(2,1)} %all-gather.9.cloned.1.call-done, bf16[1024,3456]{1,0:T(8,128)(2,1)} %attention_backward.1), kind=kOutput, calls=%fused_computation.252 | convolution fusion | flops 7247757312 | bytes 34275328 | tf_op jit(solution)/shard_map/dot_general | solution.py:29
  1156.5 17.6 %collective-permute-done.44 = bf16[256,4096]{1,0:T(8,128)(2,1)} collective-permute-done((bf16[256,4096]{1,0:T(8,128)(2,1)}, bf16[256,4096]{1,0:T(8,128)(2,1)}, u32[]{:S(2)}, u32[]{:S(2)}) %collective-permute-start.44) | collective-permute-done | bytes 2097184 | tf_op jit(solution)/shard_map/ppermute | solution.py:727
  1206.8 16.2 %collective-permute-done.47 = bf16[4,16,7168]{2,1,0:T(8,128)(2,1)S(1)} collective-permute-done((bf16[4,16,7168]{2,1,0:T(8,128)(2,1)}, bf16[4,16,7168]{2,1,0:T(8,128)(2,1)S(1)}, u32[]{:S(2)}, u32[]{:S(2)}) %collective-permute-start.47) | collective-permute-done | bytes 917536 | tf_op jit(solution)/shard_map/ppermute | solution.py:744
  1232.8 15.6 %fusion.161 = f32[256,4096]{1,0:T(8,128)} fusion(bf16[4096,3456]{1,0:T(8,128)(2,1)} %all-gather.9.cloned.1.call-done, bf16[1024,3456]{1,0:T(8,128)(2,1)} %attention_backward.1), kind=kOutput, calls=%fused_computation.250 | convolution fusion | flops 7247757312 | bytes 34275328 | tf_op jit(solution)/shard_map/dot_general | solution.py:29
  1248.4 26.4 %collective-permute-done.51 = f32[576]{0:T(1024)S(1)} collective-permute-done((f32[576]{0:T(1024)S(1)}, f32[576]{0:T(1024)S(1)}, u32[]{:S(2)}, u32[]{:S(2)}) %collective-permute-start.51) | collective-permute-done | bytes 2336 | tf_op jit(solution)/shard_map/ppermute | solution.py:767
  (733 shorter events, 500.4 us)
Async XLA Ops:
  7.2 173.1 %all-gather.9.cloned.1.call-start = ((), (), s32[]{:S(2)}) async-start(), calls=%async_computation.6 | async-start | bytes 31850496 | tf_op jit(solution)/shard_map/all_gather | solution.py:898
  13.1 241.7 %all-gather.11.cloned.1.call-start = ((), (), s32[]{:S(2)}) async-start(), calls=%async_computation.7 | async-start | bytes 4718592 | tf_op jit(solution)/shard_map/all_gather | solution.py:898
  13.9 323.9 %all-gather.13.cloned.1.call-start = ((), (), s32[]{:S(2)}) async-start(), calls=%async_computation.8 | async-start | bytes 19464192 | tf_op jit(solution)/shard_map/all_gather | solution.py:898
  22.6 331.9 %all-gather.15.cloned.1.call-start = ((), (), s32[]{:S(2)}) async-start(), calls=%async_computation.9 | async-start | bytes 9437184 | tf_op jit(solution)/shard_map/all_gather | solution.py:898
  23.2 464.9 %all-gather.17.cloned.1.call-start = ((), (), s32[]{:S(2)}) async-start(), calls=%async_computation.10 | async-start | bytes 11206656 | tf_op jit(solution)/shard_map/all_gather | solution.py:898
  23.2 29.4 %collective-permute-start.2 = (bf16[256,2048]{1,0:T(8,128)(2,1)}, bf16[256,2048]{1,0:T(8,128)(2,1)}, u32[]{:S(2)}, u32[]{:S(2)}) collective-permute-start(bf16[256,2048]{1,0:T(8,128)(2,1)} %refs_1_.3), channel_id=1, source_target_pairs={{0,1},{1,2},{2,3},{3,0},{4,5},{5,6},{6,7},{7,4},{8,9},{9,10},{10,1... | collective-permute-start | bytes 3145736 | tf_op jit(solution)/shard_map/ppermute | solution.py:727
  26.3 48.8 %collective-permute-start = (bf16[256,2048]{1,0:T(8,128)(2,1)S(1)}, bf16[256,2048]{1,0:T(8,128)(2,1)}, u32[]{:S(2)}, u32[]{:S(2)}) collective-permute-start(bf16[256,2048]{1,0:T(8,128)(2,1)S(1)} %copy-done.11), channel_id=1, source_target_pairs={{0,1},{1,2},{2,3},{3,0},{4,5},{5,6},{6,7},{7,4},{8,9},{9,10},{10,1... | collective-permute-start | bytes 3145736 | tf_op jit(solution)/shard_map/ppermute | solution.py:727
  52.6 44.9 %collective-permute-start.3 = (bf16[256,2048]{1,0:T(8,128)(2,1)}, bf16[256,2048]{1,0:T(8,128)(2,1)}, u32[]{:S(2)}, u32[]{:S(2)}) collective-permute-start(bf16[256,2048]{1,0:T(8,128)(2,1)} %collective-permute-done.2.refs_3_), channel_id=1, source_target_pairs={{0,1},{1,2},{2,3},{3,0},{4,5},{5,6},{6,7},{7,4},{8,9},{9,10},{10,1... | collective-permute-start | bytes 3145736 | tf_op jit(solution)/shard_map/ppermute | solution.py:727
  75.1 44.1 %collective-permute-start.1 = (bf16[256,2048]{1,0:T(8,128)(2,1)}, bf16[256,2048]{1,0:T(8,128)(2,1)}, u32[]{:S(2)}, u32[]{:S(2)}) collective-permute-start(bf16[256,2048]{1,0:T(8,128)(2,1)} %collective-permute-done.refs_2_), channel_id=1, source_target_pairs={{0,1},{1,2},{2,3},{3,0},{4,5},{5,6},{6,7},{7,4},{8,9},{9,10},{10,1... | collective-permute-start | bytes 3145736 | tf_op jit(solution)/shard_map/ppermute | solution.py:727
  121.4 375.1 %all-gather.19.cloned.1.call-start = ((), (), s32[]{:S(2)}) async-start(), calls=%async_computation.11 | async-start | bytes 4718592 | tf_op jit(solution)/shard_map/all_gather | solution.py:898
  123.1 28.8 %collective-permute-start.7 = (bf16[256,2048]{1,0:T(8,128)(2,1)}, bf16[256,2048]{1,0:T(8,128)(2,1)}, u32[]{:S(2)}, u32[]{:S(2)}) collective-permute-start(bf16[256,2048]{1,0:T(8,128)(2,1)} %collective-permute-done.1.refs_0_), channel_id=1, source_target_pairs={{0,1},{1,2},{2,3},{3,0},{4,5},{5,6},{6,7},{7,4},{8,9},{9,10},{10,1... | collective-permute-start | bytes 3145736 | tf_op jit(solution)/shard_map/ppermute | solution.py:727
  123.2 49.9 %collective-permute-start.8 = (bf16[256,2048]{1,0:T(8,128)(2,1)}, bf16[256,2048]{1,0:T(8,128)(2,1)}, u32[]{:S(2)}, u32[]{:S(2)}) collective-permute-start(bf16[256,2048]{1,0:T(8,128)(2,1)} %collective-permute-done.3.refs_1_), channel_id=1, source_target_pairs={{0,1},{1,2},{2,3},{3,0},{4,5},{5,6},{6,7},{7,4},{8,9},{9,10},{10,1... | collective-permute-start | bytes 3145736 | tf_op jit(solution)/shard_map/ppermute | solution.py:727
  145.9 32.8 %collective-permute-start.6 = (bf16[64,7168]{1,0:T(8,128)(2,1)}, bf16[64,7168]{1,0:T(8,128)(2,1)}, u32[]{:S(2)}, u32[]{:S(2)}) collective-permute-start(bf16[64,7168]{1,0:T(8,128)(2,1)} %pad_maximum_fusion.9), channel_id=1, source_target_pairs={{0,16},{4,20},{8,24},{12,28},{16,0},{20,4},{24,8},{28,12},{1,17},{... | collective-permute-start | bytes 2752520 | tf_op jit(solution)/shard_map/ppermute | solution.py:884
  173.0 28.8 %collective-permute-start.9 = (bf16[256,2048]{1,0:T(8,128)(2,1)S(1)}, bf16[256,2048]{1,0:T(8,128)(2,1)}, u32[]{:S(2)}, u32[]{:S(2)}) collective-permute-start(bf16[256,2048]{1,0:T(8,128)(2,1)S(1)} %copy-done.27), channel_id=1, source_target_pairs={{0,1},{1,2},{2,3},{3,0},{4,5},{5,6},{6,7},{7,4},{8,9},{9,10},{10,1... | collective-permute-start | bytes 3145736 | tf_op jit(solution)/shard_map/ppermute | solution.py:727
  201.9 26.5 %collective-permute-start.10 = (bf16[256,2048]{1,0:T(8,128)(2,1)}, bf16[256,2048]{1,0:T(8,128)(2,1)S(1)}, u32[]{:S(2)}, u32[]{:S(2)}) collective-permute-start(bf16[256,2048]{1,0:T(8,128)(2,1)} %collective-permute-done.9), channel_id=1, source_target_pairs={{0,1},{1,2},{2,3},{3,0},{4,5},{5,6},{6,7},{7,4},{8,9},{9,10},{10,1... | collective-permute-start | bytes 3145736 | tf_op jit(solution)/shard_map/ppermute | solution.py:727
  228.4 25.4 %collective-permute-start.11 = (bf16[256,2048]{1,0:T(8,128)(2,1)S(1)}, bf16[256,2048]{1,0:T(8,128)(2,1)S(1)}, u32[]{:S(2)}, u32[]{:S(2)}) collective-permute-start(bf16[256,2048]{1,0:T(8,128)(2,1)S(1)} %collective-permute-done.10), channel_id=1, source_target_pairs={{0,1},{1,2},{2,3},{3,0},{4,5},{5,6},{6,7},{7,4},{8,9},{9,10},{10,1... | collective-permute-start | bytes 3145736 | tf_op jit(solution)/shard_map/ppermute | solution.py:727
  285.7 531.9 %reduce-scatter.7.cloned.1.call-start = ((), (), s32[]{:S(2)}) async-start(), calls=%async_computation.12 | async-start | bytes 4718592 | tf_op jit(solution)/shard_map/reduce_scatter | solution.py:902
  361.7 28.2 %collective-permute-start.17 = (bf16[256,2048]{1,0:T(8,128)(2,1)}, bf16[256,2048]{1,0:T(8,128)(2,1)S(1)}, u32[]{:S(2)}, u32[]{:S(2)}) collective-permute-start(bf16[256,2048]{1,0:T(8,128)(2,1)} %collective-permute-done.15), channel_id=1, source_target_pairs={{0,1},{1,2},{2,3},{3,0},{4,5},{5,6},{6,7},{7,4},{8,9},{9,10},{10,1... | collective-permute-start | bytes 3145736 | tf_op jit(solution)/shard_map/ppermute | solution.py:727
  379.6 32.8 %collective-permute-start.16 = (bf16[256,2048]{1,0:T(8,128)(2,1)S(1)}, bf16[256,2048]{1,0:T(8,128)(2,1)S(1)}, u32[]{:S(2)}, u32[]{:S(2)}) collective-permute-start(bf16[256,2048]{1,0:T(8,128)(2,1)S(1)} %convolution_convert_fusion.8), channel_id=1, source_target_pairs={{0,1},{1,2},{2,3},{3,0},{4,5},{5,6},{6,7},{7,4},{8,9},{9,10},{10,1... | collective-permute-start | bytes 3145736 | tf_op jit(solution)/shard_map/ppermute | solution.py:727
  389.9 44.9 %collective-permute-start.19 = (bf16[256,2048]{1,0:T(8,128)(2,1)S(1)}, bf16[256,2048]{1,0:T(8,128)(2,1)S(1)}, u32[]{:S(2)}, u32[]{:S(2)}) collective-permute-start(bf16[256,2048]{1,0:T(8,128)(2,1)S(1)} %collective-permute-done.17), channel_id=1, source_target_pairs={{0,1},{1,2},{2,3},{3,0},{4,5},{5,6},{6,7},{7,4},{8,9},{9,10},{10,1... | collective-permute-start | bytes 3145736 | tf_op jit(solution)/shard_map/ppermute | solution.py:727
  412.7 43.9 %collective-permute-start.18 = (bf16[256,2048]{1,0:T(8,128)(2,1)S(1)}, bf16[256,2048]{1,0:T(8,128)(2,1)S(1)}, u32[]{:S(2)}, u32[]{:S(2)}) collective-permute-start(bf16[256,2048]{1,0:T(8,128)(2,1)S(1)} %add_convert_fusion.9), channel_id=1, source_target_pairs={{0,1},{1,2},{2,3},{3,0},{4,5},{5,6},{6,7},{7,4},{8,9},{9,10},{10,1... | collective-permute-start | bytes 3145736 | tf_op jit(solution)/shard_map/ppermute | solution.py:727
  458.0 26.6 %collective-permute-start.20 = (bf16[256,2048]{1,0:T(8,128)(2,1)}, bf16[256,2048]{1,0:T(8,128)(2,1)}, u32[]{:S(2)}, u32[]{:S(2)}) collective-permute-start(bf16[256,2048]{1,0:T(8,128)(2,1)} %add_convert_fusion.8), channel_id=1, source_target_pairs={{0,1},{1,2},{2,3},{3,0},{4,5},{5,6},{6,7},{7,4},{8,9},{9,10},{10,1... | collective-permute-start | bytes 3145736 | tf_op jit(solution)/shard_map/ppermute | solution.py:727
  487.8 25.9 %collective-permute-start.21 = (bf16[256,2048]{1,0:T(8,128)(2,1)}, bf16[256,2048]{1,0:T(8,128)(2,1)}, u32[]{:S(2)}, u32[]{:S(2)}) collective-permute-start(bf16[256,2048]{1,0:T(8,128)(2,1)} %multiply_convert_fusion.4), channel_id=1, source_target_pairs={{0,1},{1,2},{2,3},{3,0},{4,5},{5,6},{6,7},{7,4},{8,9},{9,10},{10,1... | collective-permute-start | bytes 3145736 | tf_op jit(solution)/shard_map/ppermute | solution.py:727
  607.5 39.7 %collective-permute-start.24 = (bf16[256,2048]{1,0:T(8,128)(2,1)S(1)}, bf16[256,2048]{1,0:T(8,128)(2,1)S(1)}, u32[]{:S(2)}, u32[]{:S(2)}) collective-permute-start(bf16[256,2048]{1,0:T(8,128)(2,1)S(1)} %slice.504), channel_id=1, source_target_pairs={{0,1},{1,2},{2,3},{3,0},{4,5},{5,6},{6,7},{7,4},{8,9},{9,10},{10,1... | collective-permute-start | bytes 3145736 | tf_op jit(solution)/shard_map/ppermute | solution.py:727
  676.3 244.4 %reduce-scatter.9.cloned.1.call-start = ((), (), s32[]{:S(2)}) async-start(), calls=%async_computation.13 | async-start | bytes 11206656 | tf_op jit(solution)/shard_map/reduce_scatter | solution.py:902
  679.0 25.1 %collective-permute-start.27 = (bf16[256,2048]{1,0:T(8,128)(2,1)}, bf16[256,2048]{1,0:T(8,128)(2,1)S(1)}, u32[]{:S(2)}, u32[]{:S(2)}) collective-permute-start(bf16[256,2048]{1,0:T(8,128)(2,1)} %add_convert_fusion.6), channel_id=1, source_target_pairs={{0,1},{1,2},{2,3},{3,0},{4,5},{5,6},{6,7},{7,4},{8,9},{9,10},{10,1... | collective-permute-start | bytes 3145736 | tf_op jit(solution)/shard_map/ppermute | solution.py:727
  705.1 271.2 %reduce-scatter.11.cloned.1.call-start = ((), (), s32[]{:S(2)}) async-start(), calls=%async_computation.14 | async-start | bytes 9437184 | tf_op jit(solution)/shard_map/reduce_scatter | solution.py:902
  728.6 35.4 %collective-permute-start.30 = (f32[4,864]{1,0:T(4,128)S(1)}, f32[4,864]{1,0:T(4,128)S(1)}, u32[]{:S(2)}, u32[]{:S(2)}) collective-permute-start(f32[4,864]{1,0:T(4,128)S(1)} %slice_select_fusion.1), channel_id=1, source_target_pairs={{0,16},{4,20},{8,24},{12,28},{16,0},{20,4},{24,8},{28,12},{1,17},{... | collective-permute-start | bytes 41480 | tf_op jit(solution)/shard_map/ppermute | solution.py:744
  738.4 25.6 %collective-permute-start.29 = (bf16[256,2048]{1,0:T(8,128)(2,1)}, bf16[256,2048]{1,0:T(8,128)(2,1)}, u32[]{:S(2)}, u32[]{:S(2)}) collective-permute-start(bf16[256,2048]{1,0:T(8,128)(2,1)} %get-tuple-element.284), channel_id=1, source_target_pairs={{0,1},{1,2},{2,3},{3,0},{4,5},{5,6},{6,7},{7,4},{8,9},{9,10},{10,1... | collective-permute-start | bytes 3145736 | tf_op jit(solution)/shard_map/ppermute | solution.py:727
  788.6 25.4 %collective-permute-start.34 = (f32[1,864]{1,0:T(1,128)S(1)}, f32[1,864]{1,0:T(1,128)S(1)}, u32[]{:S(2)}, u32[]{:S(2)}) collective-permute-start(f32[1,864]{1,0:T(1,128)S(1)} %broadcast_select_fusion.7), channel_id=1, source_target_pairs={{0,4},{4,0},{8,12},{12,8},{16,20},{20,16},{24,28},{28,24},{1,5},{5... | collective-permute-start | bytes 10376 | tf_op jit(solution)/shard_map/ppermute | solution.py:744
  788.7 28.1 %collective-permute-start.33 = (bf16[256,2048]{1,0:T(8,128)(2,1)}, bf16[256,2048]{1,0:T(8,128)(2,1)}, u32[]{:S(2)}, u32[]{:S(2)}) collective-permute-start(bf16[256,2048]{1,0:T(8,128)(2,1)} %collective-permute-done.31), channel_id=1, source_target_pairs={{0,1},{1,2},{2,3},{3,0},{4,5},{5,6},{6,7},{7,4},{8,9},{9,10},{10,1... | collective-permute-start | bytes 3145736 | tf_op jit(solution)/shard_map/ppermute | solution.py:727
  816.8 27.1 %collective-permute-start.35 = (bf16[256,2048]{1,0:T(8,128)(2,1)}, bf16[256,2048]{1,0:T(8,128)(2,1)S(1)}, u32[]{:S(2)}, u32[]{:S(2)}) collective-permute-start(bf16[256,2048]{1,0:T(8,128)(2,1)} %fusion.85), channel_id=1, source_target_pairs={{0,1},{1,2},{2,3},{3,0},{4,5},{5,6},{6,7},{7,4},{8,9},{9,10},{10,1... | collective-permute-start | bytes 3145736 | tf_op jit(solution)/shard_map/ppermute | solution.py:727
  844.9 207.0 %reduce-scatter.13.cloned.1.call-start = ((), (), s32[]{:S(2)}) async-start(), calls=%async_computation.15 | async-start | bytes 19464192 | tf_op jit(solution)/shard_map/reduce_scatter | solution.py:902
  848.2 26.1 %collective-permute-start.36 = (bf16[256,2048]{1,0:T(8,128)(2,1)}, bf16[256,2048]{1,0:T(8,128)(2,1)}, u32[]{:S(2)}, u32[]{:S(2)}) collective-permute-start(bf16[256,2048]{1,0:T(8,128)(2,1)} %add_convert_fusion.4), channel_id=1, source_target_pairs={{0,1},{1,2},{2,3},{3,0},{4,5},{5,6},{6,7},{7,4},{8,9},{9,10},{10,1... | collective-permute-start | bytes 3145736 | tf_op jit(solution)/shard_map/ppermute | solution.py:727
  876.7 30.1 %collective-permute-start.37 = (bf16[256,2048]{1,0:T(8,128)(2,1)}, bf16[256,2048]{1,0:T(8,128)(2,1)S(1)}, u32[]{:S(2)}, u32[]{:S(2)}) collective-permute-start(bf16[256,2048]{1,0:T(8,128)(2,1)} %add_convert_fusion.3), channel_id=1, source_target_pairs={{0,1},{1,2},{2,3},{3,0},{4,5},{5,6},{6,7},{7,4},{8,9},{9,10},{10,1... | collective-permute-start | bytes 3145736 | tf_op jit(solution)/shard_map/ppermute | solution.py:727
  906.8 274.9 %reduce-scatter.15.cloned.1.call-start = ((), (), s32[]{:S(2)}) async-start(), calls=%async_computation.16 | async-start | bytes 4718592 | tf_op jit(solution)/shard_map/reduce_scatter | solution.py:902
  969.9 28.2 %collective-permute-start.41 = (bf16[256,2048]{1,0:T(8,128)(2,1)}, bf16[256,2048]{1,0:T(8,128)(2,1)}, u32[]{:S(2)}, u32[]{:S(2)}) collective-permute-start(bf16[256,2048]{1,0:T(8,128)(2,1)} %collective-permute-done.39), channel_id=1, source_target_pairs={{0,1},{1,2},{2,3},{3,0},{4,5},{5,6},{6,7},{7,4},{8,9},{9,10},{10,1... | collective-permute-start | bytes 3145736 | tf_op jit(solution)/shard_map/ppermute | solution.py:727
  971.5 80.3 %collective-permute-start.25 = (bf16[256,2048]{1,0:T(8,128)(2,1)S(1)}, bf16[256,2048]{1,0:T(8,128)(2,1)S(1)}, u32[]{:S(2)}, u32[]{:S(2)}) collective-permute-start(bf16[256,2048]{1,0:T(8,128)(2,1)S(1)} %add_convert_fusion.7), channel_id=1, source_target_pairs={{0,1},{1,2},{2,3},{3,0},{4,5},{5,6},{6,7},{7,4},{8,9},{9,10},{10,1... | collective-permute-start | bytes 3145736 | tf_op jit(solution)/shard_map/ppermute | solution.py:727
  1012.6 293.5 %reduce-scatter.17.cloned.1.call-start = ((), (), s32[]{:S(2)}) async-start(), calls=%async_computation.17 | async-start | bytes 31850496 | tf_op jit(solution)/shard_map/reduce_scatter | solution.py:902
  1053.6 38.3 %collective-permute-start.43 = (bf16[256,2048]{1,0:T(8,128)(2,1)S(1)}, bf16[256,2048]{1,0:T(8,128)(2,1)S(1)}, u32[]{:S(2)}, u32[]{:S(2)}) collective-permute-start(bf16[256,2048]{1,0:T(8,128)(2,1)S(1)} %add_convert_fusion.2), channel_id=1, source_target_pairs={{0,1},{1,2},{2,3},{3,0},{4,5},{5,6},{6,7},{7,4},{8,9},{9,10},{10,1... | collective-permute-start | bytes 3145736 | tf_op jit(solution)/shard_map/ppermute | solution.py:727
  1096.0 110.8 %collective-permute-start.48 = (f32[576]{0:T(1024)S(1)}, f32[576]{0:T(1024)S(1)}, u32[]{:S(2)}, u32[]{:S(2)}) collective-permute-start(f32[576]{0:T(1024)S(1)} %pad_maximum_fusion.18), channel_id=1, source_target_pairs={{0,1},{1,0},{2,3},{3,2},{4,5},{5,4},{6,7},{7,6},{8,9},{9,8},{10,11... | collective-permute-start | bytes 6920 | tf_op jit(solution)/shard_map/ppermute | solution.py:767
  1122.9 51.2 %collective-permute-start.44 = (bf16[256,4096]{1,0:T(8,128)(2,1)}, bf16[256,4096]{1,0:T(8,128)(2,1)}, u32[]{:S(2)}, u32[]{:S(2)}) collective-permute-start(bf16[256,4096]{1,0:T(8,128)(2,1)} %slice.797), channel_id=1, source_target_pairs={{0,1},{1,2},{2,3},{3,0},{4,5},{5,6},{6,7},{7,4},{8,9},{9,10},{10,1... | collective-permute-start | bytes 6291464 | tf_op jit(solution)/shard_map/ppermute | solution.py:727
  1177.7 50.7 %collective-permute-start.46 = (bf16[256,4096]{1,0:T(8,128)(2,1)}, bf16[256,4096]{1,0:T(8,128)(2,1)}, u32[]{:S(2)}, u32[]{:S(2)}) collective-permute-start(bf16[256,4096]{1,0:T(8,128)(2,1)} %add_convert_fusion.1), channel_id=1, source_target_pairs={{0,1},{1,2},{2,3},{3,0},{4,5},{5,6},{6,7},{7,4},{8,9},{9,10},{10,1... | collective-permute-start | bytes 6291464 | tf_op jit(solution)/shard_map/ppermute | solution.py:727
  1180.6 42.5 %collective-permute-start.47 = (bf16[4,16,7168]{2,1,0:T(8,128)(2,1)}, bf16[4,16,7168]{2,1,0:T(8,128)(2,1)S(1)}, u32[]{:S(2)}, u32[]{:S(2)}) collective-permute-start(bf16[4,16,7168]{2,1,0:T(8,128)(2,1)} %bitcast.39), channel_id=1, source_target_pairs={{0,16},{4,20},{8,24},{12,28},{16,0},{20,4},{24,8},{28,12},{1,17},{... | collective-permute-start | bytes 2752520 | tf_op jit(solution)/shard_map/ppermute | solution.py:744
  1187.3 61.1 %collective-permute-start.52 = (bf16[256,384]{1,0:T(8,128)(2,1)S(1)}, bf16[256,384]{1,0:T(8,128)(2,1)S(1)}, u32[]{:S(2)}, u32[]{:S(2)}) collective-permute-start(bf16[256,384]{1,0:T(8,128)(2,1)S(1)} %fusion.194), channel_id=1, source_target_pairs={{0,1},{1,0},{2,3},{3,2},{4,5},{5,4},{6,7},{7,6},{8,9},{9,8},{10,11... | collective-permute-start | bytes 589832 | tf_op jit(solution)/shard_map/ppermute | solution.py:767
  1230.7 48.2 %collective-permute-start.49 = (bf16[256,4096]{1,0:T(8,128)(2,1)S(1)}, bf16[256,4096]{1,0:T(8,128)(2,1)}, u32[]{:S(2)}, u32[]{:S(2)}) collective-permute-start(bf16[256,4096]{1,0:T(8,128)(2,1)S(1)} %add_convert_fusion), channel_id=1, source_target_pairs={{0,1},{1,2},{2,3},{3,0},{4,5},{5,6},{6,7},{7,4},{8,9},{9,10},{10,1... | collective-permute-start | bytes 6291464 | tf_op jit(solution)/shard_map/ppermute | solution.py:727
  1231.1 43.7 %collective-permute-start.51 = (f32[576]{0:T(1024)S(1)}, f32[576]{0:T(1024)S(1)}, u32[]{:S(2)}, u32[]{:S(2)}) collective-permute-start(f32[576]{0:T(1024)S(1)} %fusion.222), channel_id=1, source_target_pairs={{0,2},{1,3},{2,0},{3,1},{4,6},{5,7},{6,4},{7,5},{8,10},{9,11},{10,... | collective-permute-start | bytes 6920 | tf_op jit(solution)/shard_map/ppermute | solution.py:767
  1232.7 42.0 %collective-permute-start.50 = (bf16[2,16,7168]{2,1,0:T(8,128)(2,1)S(1)}, bf16[2,16,7168]{2,1,0:T(8,128)(2,1)S(1)}, u32[]{:S(2)}, u32[]{:S(2)}) collective-permute-start(bf16[2,16,7168]{2,1,0:T(8,128)(2,1)S(1)} %select_convert_fusion.1), channel_id=1, source_target_pairs={{0,8},{4,12},{8,0},{12,4},{16,24},{20,28},{24,16},{28,20},{1,9},{5... | collective-permute-start | bytes 1376264 | tf_op jit(solution)/shard_map/ppermute | solution.py:744
  (174 other events, 2033.6 us)
Sparse Core Ops, SparseCore 0:
  13.2 150.1 all-gather.8
  165.3 37.4 all-gather.10
  204.7 92.0 all-gather.12
  298.5 55.9 all-gather.14
  356.2 61.0 all-gather.16
  419.1 37.4 all-gather.18
  676.4 49.4 reduce-scatter.6
  729.9 78.9 reduce-scatter.8
  845.0 68.0 reduce-scatter.10
  916.6 118.5 reduce-scatter.12
  1039.5 51.3 reduce-scatter.14
  1094.5 192.7 reduce-scatter.16

commit v8 on v7

--- a/solution.py
+++ b/solution.py
@@ -779,19 +779,19 @@
         return self.values
 
 
-def direct_send(values, name, sent_as=f32):
+def direct(values, name, sent_as=f32):
     count = lax.axis_size(name)
     here = lax.axis_index(name)
 
     def block(at):
         return lax.dynamic_index_in_dim(values, lax.rem(at, count), 0, keepdims=False)
 
-    blocks = [block(here)] + [block(here + step).astype(sent_as) for step in range(1, count)]
-    blocks = lax.optimization_barrier(blocks)
-    return [
-        lax.ppermute(sent, name, [(i, (i + step) % count) for i in range(count)]) if step else sent
-        for step, sent in enumerate(blocks)
-    ]
+    total = block(here)
+    for step in range(1, count):
+        sent = block(here + step).astype(sent_as)
+        moved = lax.ppermute(sent, name, [(i, (i + step) % count) for i in range(count)])
+        total = total + moved.astype(f32)
+    return total
 
 
 def begin(tasks):
@@ -1231,7 +1231,8 @@
             for j in range(3)
         ]
         ups_grad = jnp.concatenate(grad_up + fc_ups, axis=1)
-        tasks.append(Halving(ups_grad.reshape(fsdp, -1, ups_grad.shape[1]), "fsdp", bf16))
+        ups_tasks.append(Halving(ups_grad.reshape(fsdp, -1, ups_grad.shape[1]), "fsdp", bf16))
+        ups_tasks[0].start()
         shared = jnp.concatenate([small_task.result()[small_cuts[4] :], gain_tasks[0].result()])
         tasks.append(Doubling(shared, "tp"))
         return ups_grad, shared
@@ -1263,7 +1264,7 @@
         values = jnp.stack([values[:, j * each : (j + 1) * each] for j in range(parts)], axis=1)
         return with_layout_constraint(values, Layout(major_to_minor=(0, 1, 2)))
 
-    tasks, bc_sums = [], []
+    tasks, ups_tasks, bc_sums = [], [], []
     normed_terms = {}
     pair = mm_nt(grad_projected[share : 3 * share], weight_qkv)
     normed_terms[1], normed_terms[2] = piece(pair, 0), piece(pair, 1)
@@ -1283,23 +1284,20 @@
     grad_hidden, grad_embed = norm_back(
         [hidden, embed], grad_normed, gain_attn, grad_residual, with_gain=False
     )
+    ups_tasks[0].finish()
+    grad_ups = ups_tasks[0].result()
+    sum_w_qkv = tie(sum_w_qkv, grad_ups)
     gain_rows = jnp.sum(sum_w_qkv.astype(f32) * own_qkv.astype(f32), axis=1)
     gain_rows = gain_rows / attention_norm_gain.astype(f32)
-    down_blocks = direct_send(
-        sum_w_qkv[:, 3 * head_cols :].astype(f32).reshape(tp, -1, 3 * rank), "tp", bf16
-    )
-    gain_blocks = direct_send(gain_rows.reshape(tp, -1), "tp")
-    sum_w_qkv = tie(sum_w_qkv, (down_blocks[0], gain_blocks[0]))
+    grad_down = direct(sum_w_qkv[:, 3 * head_cols :].astype(f32).reshape(tp, -1, 3 * rank), "tp", bf16)
+    grad_gain_attn = direct(gain_rows.reshape(tp, -1), "tp")
     grad_w_qkv = jnp.stack(
         [sum_w_qkv[:, j * head_cols : (j + 1) * head_cols].astype(f32) for j in range(3)], axis=1
     )
-    down_blocks, gain_blocks, grad_w_qkv = lax.optimization_barrier((down_blocks, gain_blocks, grad_w_qkv))
-    grad_down = sum(v.astype(f32) for v in down_blocks)
-    grad_gain_attn = sum(gain_blocks)
     small_sum = small_task.result()
     small_parts = [small_sum[small_cuts[i] : small_cuts[i + 1]] for i in range(len(small_sizes))]
-    grad_ups, tail = tasks[0].result(), tasks[1].result()
-    shared = tasks[2].result()
+    tail = tasks[0].result()
+    shared = tasks[1].result()
     tail_sizes = [small_sizes[4], width // fsdp, width // fsdp]
     tail_cuts = [sum(tail_sizes[:i]) for i in range(4)]
     grad_conv_bc, sum_gain_mixer, sum_gain_mlp = (

time: 1350 us -> 1350 us (level)
    ppermute x9, waiting for transfers between devices: 16.5 us -> 32.5 us  [start(): lax.ppermute(sent, self.name, [(i, i ^ half) for i in range(count)])]
    unnamed x335 -> x323, local copies, waits for them, and re-layouts: 67.4 us -> 64.6 us
  transfers between devices with their start and end apart: 73 -> 73, of which waited for: 36 -> 35; matrix products, arithmetic and copies ran while one was open for 46% -> 45% of each run, Pallas kernels for 9% -> 9%
where the time goes in v8:
time: 1350 us; the launch traced here: 1340 us
  matrix products  459 us (34%)
  waiting for transfers between devices  438 us (32%)
  Pallas kernels  144 us (11%)
  local copies, waits for them, and re-layouts  112 us (8%)
  other arithmetic  104 us (8%)
  starting transfers between devices  52.1 us (4%)
  blocking collectives  17.8 us (1%)
  between operations  17.2 us (1%)
    ppermute x39, waiting for transfers between devices, hop(): return lax.ppermute(values, 'tp', ring_pairs())  352 us
    dot_general x24, matrix products, mm_nt(): lax.dot_general(left, right, (((1,), (1,)), ((), ())), preferred_element_...  194 us
    dot_general x23, matrix products, mm(): return jnp.dot(left, right, preferred_element_type=f32)  134 us
    dot_general x10, matrix products, mm_tn(): lax.dot_general(left, right, (((0,), (0,)), ((), ())), preferred_element_...  130 us
    unnamed x323, local copies, waits for them, and re-layouts  64.6 us
    pallas_call x1, Pallas kernels, attention_backward(): pl.pallas_call(functools.partial(attention_backward_kernel, tp, heads), o...  39.2 us
    pallas_call x1, Pallas kernels, mixer_backward(): pl.pallas_call(functools.partial(mixer_backward_kernel, chunks), out_shap...  36.4 us
    ppermute x9, waiting for transfers between devices, start(): lax.ppermute(sent, self.name, [(i, i ^ half) for i in range(count)])  32.5 us
  transfers between devices with their start and end apart: 73, of which 35 were waited for; matrix products, arithmetic and copies ran while one was open for 45% of the time, Pallas kernels for 9%

profile of v8, /device:TPU:0, one launch (start us, length us, event | category | flops | bytes accessed | tf_op | source)
XLA Modules:
  0.0 1344.8 jit_solution(7662828506598899894)
XLA Ops:
  28.7 9.3 all-gather.1
  52.7 22.4 %collective-permute-done.refs_2_ = bf16[256,2048]{1,0:T(8,128)(2,1)} collective-permute-done((bf16[256,2048]{1,0:T(8,128)(2,1)S(1)}, bf16[256,2048]{1,0:T(8,128)(2,1)}, u32[]{:S(2)}, u32[]{:S(2)}) %collective-permute-start) | collective-permute-done | bytes 1048608 | tf_op jit(solution)/shard_map/ppermute | solution.py:727
  83.3 14.2 %collective-permute-done.3.refs_1_ = bf16[256,2048]{1,0:T(8,128)(2,1)S(1)} collective-permute-done((bf16[256,2048]{1,0:T(8,128)(2,1)}, bf16[256,2048]{1,0:T(8,128)(2,1)S(1)}, u32[]{:S(2)}, u32[]{:S(2)}) %collective-permute-start.3) | collective-permute-done | bytes 1048608 | tf_op jit(solution)/shard_map/ppermute | solution.py:727
  97.5 21.6 %collective-permute-done.1.refs_0_ = bf16[256,2048]{1,0:T(8,128)(2,1)S(1)} collective-permute-done((bf16[256,2048]{1,0:T(8,128)(2,1)}, bf16[256,2048]{1,0:T(8,128)(2,1)S(1)}, u32[]{:S(2)}, u32[]{:S(2)}) %collective-permute-start.1) | collective-permute-done | bytes 1048608 | tf_op jit(solution)/shard_map/ppermute | solution.py:727
  125.3 20.3 %collective-permute-done.5 = bf16[32,7168]{1,0:T(8,128)(2,1)} collective-permute-done((bf16[32,7168]{1,0:T(8,128)(2,1)S(1)}, bf16[32,7168]{1,0:T(8,128)(2,1)}, u32[]{:S(2)}, u32[]{:S(2)}) %collective-permute-start.5) | collective-permute-done | bytes 458784 | tf_op jit(solution)/shard_map/ppermute | solution.py:884
  153.9 19.7 %collective-permute-done.8.refs_3_ = bf16[256,2048]{1,0:T(8,128)(2,1)} collective-permute-done((bf16[256,2048]{1,0:T(8,128)(2,1)S(1)}, bf16[256,2048]{1,0:T(8,128)(2,1)}, u32[]{:S(2)}, u32[]{:S(2)}) %collective-permute-start.8) | collective-permute-done | bytes 1048608 | tf_op jit(solution)/shard_map/ppermute | solution.py:727
  181.7 21.7 %fusion.252.refs_0_.refs_1_.refs_2_.refs_3_ = f32[512,3456]{1,0:T(8,128)S(1)} fusion(bf16[512,4096]{1,0:T(8,128)(2,1)} %bitcast.242, bf16[4096,3456]{1,0:T(8,128)(2,1)} %all-gather.9.cloned.1.call-done), kind=kOutput, calls=%fused_computation.462 | convolution fusion | flops 14495514624 | bytes 39583744 | tf_op jit(solution)/shard_map/dot_general | solution.py:25
  203.5 21.9 %fusion.253.refs_4_.refs_5_.refs_6_.refs_7_ = f32[512,3456]{1,0:T(8,128)S(1)} fusion(bf16[512,4096]{1,0:T(8,128)(2,1)S(1)} %bitcast.245, bf16[4096,3456]{1,0:T(8,128)(2,1)} %all-gather.9.cloned.1.call-done), kind=kOutput, calls=%fused_computation.463 | convolution fusion | flops 14495514624 | bytes 39583744 | tf_op jit(solution)/shard_map/dot_general | solution.py:25
  232.6 21.6 %attention_forward.1 = (bf16[1024,1024]{1,0:T(8,128)(2,1)}, bf16[1024,1024]{1,0:T(8,128)(2,1)}, bf16[1024,1024]{1,0:T(8,128)(2,1)}, bf16[1024,1024]{1,0:T(8,128)(2,1)}) custom-call(s32[1]{0:T(128)} %bitcast.place_ref, s32[3]{0:T(128)} %bitcast.289, f32[1024,128]{1,0:T(8,128)} %get-tuple-element.491.cosine_ref, f32[1024,128]{1,0:T(8,128)} %get-tuple-element.492.sine_ref, ...), custom_call_target="tpu_custom_call" | custom-call | flops 4294967296 | bytes 20971520 | tf_op jit(solution)/shard_map/attention_forward/pallas_call | solution.py:119
  269.7 14.4 %collective-permute-done.12 = bf16[256,2048]{1,0:T(8,128)(2,1)} collective-permute-done((bf16[256,2048]{1,0:T(8,128)(2,1)S(1)}, bf16[256,2048]{1,0:T(8,128)(2,1)}, u32[]{:S(2)}, u32[]{:S(2)}) %collective-permute-start.12) | collective-permute-done | bytes 1048608 | tf_op jit(solution)/shard_map/ppermute | solution.py:727
  290.2 19.1 %collective-permute-done.13 = bf16[256,2048]{1,0:T(8,128)(2,1)} collective-permute-done((bf16[256,2048]{1,0:T(8,128)(2,1)S(1)}, bf16[256,2048]{1,0:T(8,128)(2,1)}, u32[]{:S(2)}, u32[]{:S(2)}) %collective-permute-start.13) | collective-permute-done | bytes 1048608 | tf_op jit(solution)/shard_map/ppermute | solution.py:727
  316.4 18.5 %collective-permute-done.14 = bf16[256,2048]{1,0:T(8,128)(2,1)} collective-permute-done((bf16[256,2048]{1,0:T(8,128)(2,1)}, bf16[256,2048]{1,0:T(8,128)(2,1)}, u32[]{:S(2)}, u32[]{:S(2)}) %collective-permute-start.14) | collective-permute-done | bytes 1048608 | tf_op jit(solution)/shard_map/ppermute | solution.py:727
  338.2 9.3 fusion.255
  381.0 9.0 collective-permute-done.17
  413.0 21.9 %collective-permute-done.19 = bf16[256,2048]{1,0:T(8,128)(2,1)S(1)} collective-permute-done((bf16[256,2048]{1,0:T(8,128)(2,1)S(1)}, bf16[256,2048]{1,0:T(8,128)(2,1)S(1)}, u32[]{:S(2)}, u32[]{:S(2)}) %collective-permute-start.19) | collective-permute-done | bytes 1048608 | tf_op jit(solution)/shard_map/ppermute | solution.py:727
  434.9 9.3 fusion.259
  466.6 16.9 %collective-permute-done.20 = bf16[256,2048]{1,0:T(8,128)(2,1)} collective-permute-done((bf16[256,2048]{1,0:T(8,128)(2,1)S(1)}, bf16[256,2048]{1,0:T(8,128)(2,1)}, u32[]{:S(2)}, u32[]{:S(2)}) %collective-permute-start.20) | collective-permute-done | bytes 1048608 | tf_op jit(solution)/shard_map/ppermute | solution.py:727
  487.0 8.5 fusion.261
  503.7 9.0 collective-permute-done.21
  519.7 17.6 %collective-permute-done.22 = bf16[256,2048]{1,0:T(8,128)(2,1)S(1)} collective-permute-done((bf16[256,2048]{1,0:T(8,128)(2,1)}, bf16[256,2048]{1,0:T(8,128)(2,1)S(1)}, u32[]{:S(2)}, u32[]{:S(2)}) %collective-permute-start.22) | collective-permute-done | bytes 1048608 | tf_op jit(solution)/shard_map/ppermute | solution.py:727
  541.7 19.6 %collective-permute-done.23 = bf16[256,2048]{1,0:T(8,128)(2,1)S(1)} collective-permute-done((bf16[256,2048]{1,0:T(8,128)(2,1)S(1)}, bf16[256,2048]{1,0:T(8,128)(2,1)S(1)}, u32[]{:S(2)}, u32[]{:S(2)}) %collective-permute-start.23) | collective-permute-done | bytes 1048608 | tf_op jit(solution)/shard_map/ppermute | solution.py:727
  568.2 17.6 %mixer_forward.1 = (bf16[1024,1024]{1,0:T(8,128)(2,1)}, bf16[8,64,1024]{2,1,0:T(8,128)(2,1)}) custom-call(s32[1]{0:T(128)} %bitcast.place_ref, s32[3]{0:T(128)} %bitcast.290, bf16[1024,2048]{1,0:T(8,128)(2,1)} %pad_maximum_fusion.1.zx.before, bf16[1024,2048]{1,0:T(8,128)(2,1)} %pad_maximum_fusion.1.zx.before, f32[1024,384]{1,0:T(8,128)} %pad_maximum_fusion.8.sd.sd_before, ...), custom_call_target="tpu_custom_call" | custom-call | flops 1073741824 | bytes 8388608 | tf_op jit(solution)/shard_map/mixer_forward/pallas_call | solution.py:535
  588.8 8.5 psum.7
  609.9 36.4 %mixer_backward.1 = (bf16[1024,2432]{1,0:T(8,128)(2,1)}, f32[8,1024]{1,0:T(8,128)}, f32[8,256]{1,0:T(8,128)}, f32[8,128]{1,0:T(8,128)}) custom-call(s32[1]{0:T(128)} %bitcast.place_ref, s32[3]{0:T(128)} %bitcast.291, bf16[1024,2048]{1,0:T(8,128)(2,1)} %pad_maximum_fusion.1.zx.before, bf16[1024,2048]{1,0:T(8,128)(2,1)} %pad_maximum_fusion.1.zx.before, ...), custom_call_target="tpu_custom_call" | custom-call | flops 3221225472 | bytes 12582912 | tf_op jit(solution)/shard_map/mixer_backward/pallas_call | solution.py:573
  678.4 15.8 %convolution_convert_fusion.2 = bf16[2048,2432]{1,0:T(8,128)(2,1)} fusion(bf16[1024,2048]{1,0:T(8,128)(2,1)S(1)} %copy-done.81, bf16[1024,2432]{1,0:T(8,128)(2,1)} %get-tuple-element.256), kind=kOutput, calls=%fused_computation.2 | convolution fusion | flops 10205528064 | bytes 19136512 | tf_op jit(solution)/shard_map/dot_general | solution.py:33
  694.1 9.1 fusion.167
  718.9 8.7 collective-permute-done.28
  737.7 9.6 fusion.115
  749.4 13.6 %fusion.79 = f32[256,2048]{1,0:T(8,128)} fusion(bf16[2048,4224]{1,0:T(8,128)(2,1)} %all-gather.13.cloned.1.call-done, bf16[256,128]{1,0:T(8,128)(2,1)S(1)} %fusion.181, bf16[256,2048]{1,0:T(8,128)(2,1)} %copy-done.123, bf16[256,2048]{1,0:T(8,128)(2,1)} %copy-done.122), kind=kOutput, calls=%fused_computation.133 | convolution fusion | flops 4435673088 | bytes 21561344 | tf_op jit(solution)/shard_map/dot_general | solution.py:29
  774.9 12.7 fusion.85
  800.0 13.0 fusion.91
  816.7 13.9 %convolution_convert_fusion.3 = bf16[2048,2048]{1,0:T(8,128)(2,1)} fusion(bf16[1024,2048]{1,0:T(8,128)(2,1)} %pad_maximum_fusion.2, bf16[256,2048]{1,0:T(8,128)(2,1)} %collective-permute-done.33, bf16[256,2048]{1,0:T(8,128)(2,1)} %collective-permute-done.31, bf16[256,2048]{1,0:T(8,128)(2,1)} %collective-permute-done.29, bf16[256,2048]{1,0:T(8,128)(2,1)S(1)} %copy-done.120), kind=kOutput, calls=%fused_computation.51 | convolution fusion | flops 8610906112 | bytes 16777216 | tf_op jit(solution)/shard_map/dot_general | solution.py:33
  830.6 12.3 collective-permute-done.35
  847.3 9.2 fusion.109
  858.5 9.1 fusion.97
  876.3 29.5 %convolution_convert_fusion.1 = bf16[2048,4224]{1,0:T(8,128)(2,1)} fusion(bf16[1024,2048]{1,0:T(8,128)(2,1)} %copy-done.79, bf16[256,128]{1,0:T(8,128)(2,1)S(1)} %fusion.172, bf16[256,2048]{1,0:T(8,128)(2,1)} %copy-done.129, bf16[256,2048]{1,0:T(8,128)(2,1)} %copy-done.128, bf16[256,128]{1,0:T(8,128)(2,1)S(1)} %fusion.175, ...), kind=kOutput, calls=%fused_computation.1 | convolution fusion | flops 17829199872 | bytes 30146560 | tf_op jit(solution)/shard_map/dot_general | solution.py:33
  919.7 16.4 %fusion.23 = f32[128,4096]{1,0:T(8,128)} fusion(bf16[256,128]{1,0:T(8,128)(2,1)S(1)} %copy-done.133, bf16[256,2048]{1,0:T(8,128)(2,1)} %copy-done.129, bf16[256,2048]{1,0:T(8,128)(2,1)} %copy-done.128, bf16[256,128]{1,0:T(8,128)(2,1)S(1)} %copy-done.131, bf16[256,2048]{1,0:T(8,128)(2,1)} %copy-done.127, bf16[256,2048]{1,0:T(8,128)(2,1)} %copy-done.126, ...), kind=kOutput, calls=%fused_computation.26 | convolution fusion | flops 1175453696 | bytes 11010048 | tf_op jit(solution)/shard_map/dot_general | solution.py:33
  948.6 20.4 %collective-permute-done.39 = bf16[256,2048]{1,0:T(8,128)(2,1)} collective-permute-done((bf16[256,2048]{1,0:T(8,128)(2,1)S(1)}, bf16[256,2048]{1,0:T(8,128)(2,1)}, u32[]{:S(2)}, u32[]{:S(2)}) %collective-permute-start.39) | collective-permute-done | bytes 1048608 | tf_op jit(solution)/shard_map/ppermute | solution.py:727
  975.3 21.8 %collective-permute-done.41 = bf16[256,2048]{1,0:T(8,128)(2,1)} collective-permute-done((bf16[256,2048]{1,0:T(8,128)(2,1)}, bf16[256,2048]{1,0:T(8,128)(2,1)}, u32[]{:S(2)}, u32[]{:S(2)}) %collective-permute-start.41) | collective-permute-done | bytes 1048608 | tf_op jit(solution)/shard_map/ppermute | solution.py:727
  997.1 9.1 fusion.70
  1011.6 39.2 %attention_backward.1 = bf16[1024,3456]{1,0:T(8,128)(2,1)} custom-call(s32[1]{0:T(128)} %bitcast.place_ref, s32[3]{0:T(128)} %bitcast.292, f32[1024,128]{1,0:T(8,128)} %get-tuple-element.491.cosine_ref, f32[1024,128]{1,0:T(8,128)} %get-tuple-element.492.sine_ref, bf16[1024,1024]{1,0:T(8,128)(2,1)} %get-tuple-element.240.q_ref, ...), custom_call_target="tpu_custom_call" | custom-call | flops 10737418240 | bytes 14680064 | tf_op jit(solution)/shard_map/attention_backward/pallas_call | solution.py:233
  1052.9 38.0 %convolution_convert_fusion = bf16[4096,3456]{1,0:T(8,128)(2,1)} fusion(bf16[1024,4096]{1,0:T(8,128)(2,1)} %pad_maximum_fusion, bf16[1024,3456]{1,0:T(8,128)(2,1)} %attention_backward.1), kind=kOutput, calls=%fused_computation | convolution fusion | flops 29005185024 | bytes 43778048 | tf_op jit(solution)/shard_map/dot_general | solution.py:33
  1095.1 20.9 %fusion.73 = f32[512,4096]{1,0:T(8,128)S(1)} fusion(bf16[4096,3456]{1,0:T(8,128)(2,1)} %all-gather.9.cloned.1.call-done, bf16[1024,3456]{1,0:T(8,128)(2,1)} %attention_backward.1), kind=kOutput, calls=%fused_computation.114 | convolution fusion | flops 14495514624 | bytes 40239104 | tf_op jit(solution)/shard_map/dot_general | solution.py:29
  1130.3 32.1 %collective-permute-done.51 = bf16[4,16,7168]{2,1,0:T(8,128)(2,1)S(1)} collective-permute-done((bf16[4,16,7168]{2,1,0:T(8,128)(2,1)S(1)}, bf16[4,16,7168]{2,1,0:T(8,128)(2,1)S(1)}, u32[]{:S(2)}, u32[]{:S(2)}) %collective-permute-start.51) | collective-permute-done | bytes 917536 | tf_op jit(solution)/shard_map/ppermute | solution.py:744
  1162.8 16.5 %fusion.163 = f32[256,4096]{1,0:T(8,128)} fusion(bf16[4096,3456]{1,0:T(8,128)(2,1)} %all-gather.9.cloned.1.call-done, bf16[1024,3456]{1,0:T(8,128)(2,1)} %attention_backward.1), kind=kOutput, calls=%fused_computation.252 | convolution fusion | flops 7247757312 | bytes 34275328 | tf_op jit(solution)/shard_map/dot_general | solution.py:29
  1220.9 21.3 %collective-permute-done.46 = bf16[256,4096]{1,0:T(8,128)(2,1)} collective-permute-done((bf16[256,4096]{1,0:T(8,128)(2,1)}, bf16[256,4096]{1,0:T(8,128)(2,1)}, u32[]{:S(2)}, u32[]{:S(2)}) %collective-permute-start.46) | collective-permute-done | bytes 2097184 | tf_op jit(solution)/shard_map/ppermute | solution.py:727
  1248.4 16.7 %fusion.161 = f32[256,4096]{1,0:T(8,128)} fusion(bf16[4096,3456]{1,0:T(8,128)(2,1)} %all-gather.9.cloned.1.call-done, bf16[1024,3456]{1,0:T(8,128)(2,1)} %attention_backward.1), kind=kOutput, calls=%fused_computation.250 | convolution fusion | flops 7247757312 | bytes 34275328 | tf_op jit(solution)/shard_map/dot_general | solution.py:29
  1265.1 26.3 %collective-permute-done.49 = f32[576]{0:T(1024)S(1)} collective-permute-done((f32[576]{0:T(1024)S(1)}, f32[576]{0:T(1024)S(1)}, u32[]{:S(2)}, u32[]{:S(2)}) %collective-permute-start.49) | collective-permute-done | bytes 2336 | tf_op jit(solution)/shard_map/ppermute | solution.py:767
  (721 shorter events, 483.9 us)
Async XLA Ops:
  7.2 174.5 %all-gather.9.cloned.1.call-start = ((), (), s32[]{:S(2)}) async-start(), calls=%async_computation.6 | async-start | bytes 31850496 | tf_op jit(solution)/shard_map/all_gather | solution.py:898
  13.2 242.5 %all-gather.11.cloned.1.call-start = ((), (), s32[]{:S(2)}) async-start(), calls=%async_computation.7 | async-start | bytes 4718592 | tf_op jit(solution)/shard_map/all_gather | solution.py:898
  13.9 324.2 %all-gather.13.cloned.1.call-start = ((), (), s32[]{:S(2)}) async-start(), calls=%async_computation.8 | async-start | bytes 19464192 | tf_op jit(solution)/shard_map/all_gather | solution.py:898
  22.6 331.9 %all-gather.15.cloned.1.call-start = ((), (), s32[]{:S(2)}) async-start(), calls=%async_computation.9 | async-start | bytes 9437184 | tf_op jit(solution)/shard_map/all_gather | solution.py:898
  23.2 463.8 %all-gather.17.cloned.1.call-start = ((), (), s32[]{:S(2)}) async-start(), calls=%async_computation.10 | async-start | bytes 11206656 | tf_op jit(solution)/shard_map/all_gather | solution.py:898
  23.2 29.4 %collective-permute-start.2 = (bf16[256,2048]{1,0:T(8,128)(2,1)}, bf16[256,2048]{1,0:T(8,128)(2,1)}, u32[]{:S(2)}, u32[]{:S(2)}) collective-permute-start(bf16[256,2048]{1,0:T(8,128)(2,1)} %refs_1_.3), channel_id=1, source_target_pairs={{0,1},{1,2},{2,3},{3,0},{4,5},{5,6},{6,7},{7,4},{8,9},{9,10},{10,1... | collective-permute-start | bytes 3145736 | tf_op jit(solution)/shard_map/ppermute | solution.py:727
  26.3 48.8 %collective-permute-start = (bf16[256,2048]{1,0:T(8,128)(2,1)S(1)}, bf16[256,2048]{1,0:T(8,128)(2,1)}, u32[]{:S(2)}, u32[]{:S(2)}) collective-permute-start(bf16[256,2048]{1,0:T(8,128)(2,1)S(1)} %copy-done.11), channel_id=1, source_target_pairs={{0,1},{1,2},{2,3},{3,0},{4,5},{5,6},{6,7},{7,4},{8,9},{9,10},{10,1... | collective-permute-start | bytes 3145736 | tf_op jit(solution)/shard_map/ppermute | solution.py:727
  52.6 44.8 %collective-permute-start.3 = (bf16[256,2048]{1,0:T(8,128)(2,1)}, bf16[256,2048]{1,0:T(8,128)(2,1)S(1)}, u32[]{:S(2)}, u32[]{:S(2)}) collective-permute-start(bf16[256,2048]{1,0:T(8,128)(2,1)} %collective-permute-done.2.refs_3_), channel_id=1, source_target_pairs={{0,1},{1,2},{2,3},{3,0},{4,5},{5,6},{6,7},{7,4},{8,9},{9,10},{10,1... | collective-permute-start | bytes 3145736 | tf_op jit(solution)/shard_map/ppermute | solution.py:727
  75.1 44.0 %collective-permute-start.1 = (bf16[256,2048]{1,0:T(8,128)(2,1)}, bf16[256,2048]{1,0:T(8,128)(2,1)S(1)}, u32[]{:S(2)}, u32[]{:S(2)}) collective-permute-start(bf16[256,2048]{1,0:T(8,128)(2,1)} %collective-permute-done.refs_2_), channel_id=1, source_target_pairs={{0,1},{1,2},{2,3},{3,0},{4,5},{5,6},{6,7},{7,4},{8,9},{9,10},{10,1... | collective-permute-start | bytes 3145736 | tf_op jit(solution)/shard_map/ppermute | solution.py:727
  121.4 374.1 %all-gather.19.cloned.1.call-start = ((), (), s32[]{:S(2)}) async-start(), calls=%async_computation.11 | async-start | bytes 4718592 | tf_op jit(solution)/shard_map/all_gather | solution.py:898
  124.0 29.9 %collective-permute-start.7 = (bf16[256,2048]{1,0:T(8,128)(2,1)S(1)}, bf16[256,2048]{1,0:T(8,128)(2,1)}, u32[]{:S(2)}, u32[]{:S(2)}) collective-permute-start(bf16[256,2048]{1,0:T(8,128)(2,1)S(1)} %collective-permute-done.1.refs_0_), channel_id=1, source_target_pairs={{0,1},{1,2},{2,3},{3,0},{4,5},{5,6},{6,7},{7,4},{8,9},{9,10},{10,1... | collective-permute-start | bytes 3145736 | tf_op jit(solution)/shard_map/ppermute | solution.py:727
  124.0 49.6 %collective-permute-start.8 = (bf16[256,2048]{1,0:T(8,128)(2,1)S(1)}, bf16[256,2048]{1,0:T(8,128)(2,1)}, u32[]{:S(2)}, u32[]{:S(2)}) collective-permute-start(bf16[256,2048]{1,0:T(8,128)(2,1)S(1)} %collective-permute-done.3.refs_1_), channel_id=1, source_target_pairs={{0,1},{1,2},{2,3},{3,0},{4,5},{5,6},{6,7},{7,4},{8,9},{9,10},{10,1... | collective-permute-start | bytes 3145736 | tf_op jit(solution)/shard_map/ppermute | solution.py:727
  147.8 31.4 %collective-permute-start.6 = (bf16[64,7168]{1,0:T(8,128)(2,1)}, bf16[64,7168]{1,0:T(8,128)(2,1)}, u32[]{:S(2)}, u32[]{:S(2)}) collective-permute-start(bf16[64,7168]{1,0:T(8,128)(2,1)} %pad_maximum_fusion.9), channel_id=1, source_target_pairs={{0,16},{4,20},{8,24},{12,28},{16,0},{20,4},{24,8},{28,12},{1,17},{... | collective-permute-start | bytes 2752520 | tf_op jit(solution)/shard_map/ppermute | solution.py:884
  173.7 29.8 %collective-permute-start.9 = (bf16[256,2048]{1,0:T(8,128)(2,1)}, bf16[256,2048]{1,0:T(8,128)(2,1)}, u32[]{:S(2)}, u32[]{:S(2)}) collective-permute-start(bf16[256,2048]{1,0:T(8,128)(2,1)} %refs_3_.1), channel_id=1, source_target_pairs={{0,1},{1,2},{2,3},{3,0},{4,5},{5,6},{6,7},{7,4},{8,9},{9,10},{10,1... | collective-permute-start | bytes 3145736 | tf_op jit(solution)/shard_map/ppermute | solution.py:727
  203.5 26.6 %collective-permute-start.10 = (bf16[256,2048]{1,0:T(8,128)(2,1)}, bf16[256,2048]{1,0:T(8,128)(2,1)}, u32[]{:S(2)}, u32[]{:S(2)}) collective-permute-start(bf16[256,2048]{1,0:T(8,128)(2,1)} %collective-permute-done.9), channel_id=1, source_target_pairs={{0,1},{1,2},{2,3},{3,0},{4,5},{5,6},{6,7},{7,4},{8,9},{9,10},{10,1... | collective-permute-start | bytes 3145736 | tf_op jit(solution)/shard_map/ppermute | solution.py:727
  230.1 25.6 %collective-permute-start.11 = (bf16[256,2048]{1,0:T(8,128)(2,1)}, bf16[256,2048]{1,0:T(8,128)(2,1)}, u32[]{:S(2)}, u32[]{:S(2)}) collective-permute-start(bf16[256,2048]{1,0:T(8,128)(2,1)} %collective-permute-done.10), channel_id=1, source_target_pairs={{0,1},{1,2},{2,3},{3,0},{4,5},{5,6},{6,7},{7,4},{8,9},{9,10},{10,1... | collective-permute-start | bytes 3145736 | tf_op jit(solution)/shard_map/ppermute | solution.py:727
  285.7 531.0 %reduce-scatter.7.cloned.1.call-start = ((), (), s32[]{:S(2)}) async-start(), calls=%async_computation.12 | async-start | bytes 4718592 | tf_op jit(solution)/shard_map/reduce_scatter | solution.py:902
  361.7 28.2 %collective-permute-start.17 = (bf16[256,2048]{1,0:T(8,128)(2,1)}, bf16[256,2048]{1,0:T(8,128)(2,1)S(1)}, u32[]{:S(2)}, u32[]{:S(2)}) collective-permute-start(bf16[256,2048]{1,0:T(8,128)(2,1)} %collective-permute-done.15), channel_id=1, source_target_pairs={{0,1},{1,2},{2,3},{3,0},{4,5},{5,6},{6,7},{7,4},{8,9},{9,10},{10,1... | collective-permute-start | bytes 3145736 | tf_op jit(solution)/shard_map/ppermute | solution.py:727
  379.6 32.9 %collective-permute-start.16 = (bf16[256,2048]{1,0:T(8,128)(2,1)S(1)}, bf16[256,2048]{1,0:T(8,128)(2,1)S(1)}, u32[]{:S(2)}, u32[]{:S(2)}) collective-permute-start(bf16[256,2048]{1,0:T(8,128)(2,1)S(1)} %convolution_convert_fusion.8), channel_id=1, source_target_pairs={{0,1},{1,2},{2,3},{3,0},{4,5},{5,6},{6,7},{7,4},{8,9},{9,10},{10,1... | collective-permute-start | bytes 3145736 | tf_op jit(solution)/shard_map/ppermute | solution.py:727
  390.0 44.9 %collective-permute-start.19 = (bf16[256,2048]{1,0:T(8,128)(2,1)S(1)}, bf16[256,2048]{1,0:T(8,128)(2,1)S(1)}, u32[]{:S(2)}, u32[]{:S(2)}) collective-permute-start(bf16[256,2048]{1,0:T(8,128)(2,1)S(1)} %collective-permute-done.17), channel_id=1, source_target_pairs={{0,1},{1,2},{2,3},{3,0},{4,5},{5,6},{6,7},{7,4},{8,9},{9,10},{10,1... | collective-permute-start | bytes 3145736 | tf_op jit(solution)/shard_map/ppermute | solution.py:727
  412.8 43.9 %collective-permute-start.18 = (bf16[256,2048]{1,0:T(8,128)(2,1)S(1)}, bf16[256,2048]{1,0:T(8,128)(2,1)S(1)}, u32[]{:S(2)}, u32[]{:S(2)}) collective-permute-start(bf16[256,2048]{1,0:T(8,128)(2,1)S(1)} %add_convert_fusion.9), channel_id=1, source_target_pairs={{0,1},{1,2},{2,3},{3,0},{4,5},{5,6},{6,7},{7,4},{8,9},{9,10},{10,1... | collective-permute-start | bytes 3145736 | tf_op jit(solution)/shard_map/ppermute | solution.py:727
  457.0 26.5 %collective-permute-start.20 = (bf16[256,2048]{1,0:T(8,128)(2,1)S(1)}, bf16[256,2048]{1,0:T(8,128)(2,1)}, u32[]{:S(2)}, u32[]{:S(2)}) collective-permute-start(bf16[256,2048]{1,0:T(8,128)(2,1)S(1)} %add_convert_fusion.8), channel_id=1, source_target_pairs={{0,1},{1,2},{2,3},{3,0},{4,5},{5,6},{6,7},{7,4},{8,9},{9,10},{10,1... | collective-permute-start | bytes 3145736 | tf_op jit(solution)/shard_map/ppermute | solution.py:727
  486.8 25.9 %collective-permute-start.21 = (bf16[256,2048]{1,0:T(8,128)(2,1)}, bf16[256,2048]{1,0:T(8,128)(2,1)}, u32[]{:S(2)}, u32[]{:S(2)}) collective-permute-start(bf16[256,2048]{1,0:T(8,128)(2,1)} %multiply_convert_fusion.4), channel_id=1, source_target_pairs={{0,1},{1,2},{2,3},{3,0},{4,5},{5,6},{6,7},{7,4},{8,9},{9,10},{10,1... | collective-permute-start | bytes 3145736 | tf_op jit(solution)/shard_map/ppermute | solution.py:727
  606.7 39.6 %collective-permute-start.24 = (bf16[256,2048]{1,0:T(8,128)(2,1)S(1)}, bf16[256,2048]{1,0:T(8,128)(2,1)S(1)}, u32[]{:S(2)}, u32[]{:S(2)}) collective-permute-start(bf16[256,2048]{1,0:T(8,128)(2,1)S(1)} %slice.504), channel_id=1, source_target_pairs={{0,1},{1,2},{2,3},{3,0},{4,5},{5,6},{6,7},{7,4},{8,9},{9,10},{10,1... | collective-permute-start | bytes 3145736 | tf_op jit(solution)/shard_map/ppermute | solution.py:727
  675.5 244.2 %reduce-scatter.9.cloned.1.call-start = ((), (), s32[]{:S(2)}) async-start(), calls=%async_computation.13 | async-start | bytes 11206656 | tf_op jit(solution)/shard_map/reduce_scatter | solution.py:902
  678.2 25.1 %collective-permute-start.27 = (bf16[256,2048]{1,0:T(8,128)(2,1)}, bf16[256,2048]{1,0:T(8,128)(2,1)S(1)}, u32[]{:S(2)}, u32[]{:S(2)}) collective-permute-start(bf16[256,2048]{1,0:T(8,128)(2,1)} %add_convert_fusion.6), channel_id=1, source_target_pairs={{0,1},{1,2},{2,3},{3,0},{4,5},{5,6},{6,7},{7,4},{8,9},{9,10},{10,1... | collective-permute-start | bytes 3145736 | tf_op jit(solution)/shard_map/ppermute | solution.py:727
  704.3 271.0 %reduce-scatter.11.cloned.1.call-start = ((), (), s32[]{:S(2)}) async-start(), calls=%async_computation.14 | async-start | bytes 9437184 | tf_op jit(solution)/shard_map/reduce_scatter | solution.py:902
  727.7 35.3 %collective-permute-start.30 = (f32[4,864]{1,0:T(4,128)S(1)}, f32[4,864]{1,0:T(4,128)S(1)}, u32[]{:S(2)}, u32[]{:S(2)}) collective-permute-start(f32[4,864]{1,0:T(4,128)S(1)} %slice_select_fusion.1), channel_id=1, source_target_pairs={{0,16},{4,20},{8,24},{12,28},{16,0},{20,4},{24,8},{28,12},{1,17},{... | collective-permute-start | bytes 41480 | tf_op jit(solution)/shard_map/ppermute | solution.py:744
  737.5 25.5 %collective-permute-start.29 = (bf16[256,2048]{1,0:T(8,128)(2,1)}, bf16[256,2048]{1,0:T(8,128)(2,1)}, u32[]{:S(2)}, u32[]{:S(2)}) collective-permute-start(bf16[256,2048]{1,0:T(8,128)(2,1)} %get-tuple-element.265), channel_id=1, source_target_pairs={{0,1},{1,2},{2,3},{3,0},{4,5},{5,6},{6,7},{7,4},{8,9},{9,10},{10,1... | collective-permute-start | bytes 3145736 | tf_op jit(solution)/shard_map/ppermute | solution.py:727
  787.7 25.4 %collective-permute-start.34 = (f32[1,864]{1,0:T(1,128)S(1)}, f32[1,864]{1,0:T(1,128)S(1)}, u32[]{:S(2)}, u32[]{:S(2)}) collective-permute-start(f32[1,864]{1,0:T(1,128)S(1)} %broadcast_select_fusion.7), channel_id=1, source_target_pairs={{0,4},{4,0},{8,12},{12,8},{16,20},{20,16},{24,28},{28,24},{1,5},{5... | collective-permute-start | bytes 10376 | tf_op jit(solution)/shard_map/ppermute | solution.py:744
  787.8 28.1 %collective-permute-start.33 = (bf16[256,2048]{1,0:T(8,128)(2,1)}, bf16[256,2048]{1,0:T(8,128)(2,1)}, u32[]{:S(2)}, u32[]{:S(2)}) collective-permute-start(bf16[256,2048]{1,0:T(8,128)(2,1)} %collective-permute-done.31), channel_id=1, source_target_pairs={{0,1},{1,2},{2,3},{3,0},{4,5},{5,6},{6,7},{7,4},{8,9},{9,10},{10,1... | collective-permute-start | bytes 3145736 | tf_op jit(solution)/shard_map/ppermute | solution.py:727
  815.9 27.1 %collective-permute-start.35 = (bf16[256,2048]{1,0:T(8,128)(2,1)}, bf16[256,2048]{1,0:T(8,128)(2,1)S(1)}, u32[]{:S(2)}, u32[]{:S(2)}) collective-permute-start(bf16[256,2048]{1,0:T(8,128)(2,1)} %fusion.85), channel_id=1, source_target_pairs={{0,1},{1,2},{2,3},{3,0},{4,5},{5,6},{6,7},{7,4},{8,9},{9,10},{10,1... | collective-permute-start | bytes 3145736 | tf_op jit(solution)/shard_map/ppermute | solution.py:727
  843.9 207.0 %reduce-scatter.13.cloned.1.call-start = ((), (), s32[]{:S(2)}) async-start(), calls=%async_computation.15 | async-start | bytes 19464192 | tf_op jit(solution)/shard_map/reduce_scatter | solution.py:902
  847.3 26.1 %collective-permute-start.36 = (bf16[256,2048]{1,0:T(8,128)(2,1)}, bf16[256,2048]{1,0:T(8,128)(2,1)}, u32[]{:S(2)}, u32[]{:S(2)}) collective-permute-start(bf16[256,2048]{1,0:T(8,128)(2,1)} %add_convert_fusion.4), channel_id=1, source_target_pairs={{0,1},{1,2},{2,3},{3,0},{4,5},{5,6},{6,7},{7,4},{8,9},{9,10},{10,1... | collective-permute-start | bytes 3145736 | tf_op jit(solution)/shard_map/ppermute | solution.py:727
  875.9 30.0 %collective-permute-start.37 = (bf16[256,2048]{1,0:T(8,128)(2,1)}, bf16[256,2048]{1,0:T(8,128)(2,1)S(1)}, u32[]{:S(2)}, u32[]{:S(2)}) collective-permute-start(bf16[256,2048]{1,0:T(8,128)(2,1)} %add_convert_fusion.3), channel_id=1, source_target_pairs={{0,1},{1,2},{2,3},{3,0},{4,5},{5,6},{6,7},{7,4},{8,9},{9,10},{10,1... | collective-permute-start | bytes 3145736 | tf_op jit(solution)/shard_map/ppermute | solution.py:727
  905.9 291.8 %reduce-scatter.15.cloned.1.call-start = ((), (), s32[]{:S(2)}) async-start(), calls=%async_computation.16 | async-start | bytes 4718592 | tf_op jit(solution)/shard_map/reduce_scatter | solution.py:902
  919.7 25.1 %collective-permute-start.38 = (bf16[256,2048]{1,0:T(8,128)(2,1)}, bf16[256,2048]{1,0:T(8,128)(2,1)S(1)}, u32[]{:S(2)}, u32[]{:S(2)}) collective-permute-start(bf16[256,2048]{1,0:T(8,128)(2,1)} %get-tuple-element.299), channel_id=1, source_target_pairs={{0,1},{1,2},{2,3},{3,0},{4,5},{5,6},{6,7},{7,4},{8,9},{9,10},{10,1... | collective-permute-start | bytes 3145736 | tf_op jit(solution)/shard_map/ppermute | solution.py:727
  968.9 28.2 %collective-permute-start.41 = (bf16[256,2048]{1,0:T(8,128)(2,1)}, bf16[256,2048]{1,0:T(8,128)(2,1)}, u32[]{:S(2)}, u32[]{:S(2)}) collective-permute-start(bf16[256,2048]{1,0:T(8,128)(2,1)} %collective-permute-done.39), channel_id=1, source_target_pairs={{0,1},{1,2},{2,3},{3,0},{4,5},{5,6},{6,7},{7,4},{8,9},{9,10},{10,1... | collective-permute-start | bytes 3145736 | tf_op jit(solution)/shard_map/ppermute | solution.py:727
  970.6 80.3 %collective-permute-start.25 = (bf16[256,2048]{1,0:T(8,128)(2,1)S(1)}, bf16[256,2048]{1,0:T(8,128)(2,1)S(1)}, u32[]{:S(2)}, u32[]{:S(2)}) collective-permute-start(bf16[256,2048]{1,0:T(8,128)(2,1)S(1)} %add_convert_fusion.7), channel_id=1, source_target_pairs={{0,1},{1,2},{2,3},{3,0},{4,5},{5,6},{6,7},{7,4},{8,9},{9,10},{10,1... | collective-permute-start | bytes 3145736 | tf_op jit(solution)/shard_map/ppermute | solution.py:727
  1011.6 301.5 %reduce-scatter.17.cloned.1.call-start = ((), (), s32[]{:S(2)}) async-start(), calls=%async_computation.17 | async-start | bytes 31850496 | tf_op jit(solution)/shard_map/reduce_scatter | solution.py:902
  1052.6 38.3 %collective-permute-start.43 = (bf16[256,2048]{1,0:T(8,128)(2,1)S(1)}, bf16[256,2048]{1,0:T(8,128)(2,1)S(1)}, u32[]{:S(2)}, u32[]{:S(2)}) collective-permute-start(bf16[256,2048]{1,0:T(8,128)(2,1)S(1)} %add_convert_fusion.2), channel_id=1, source_target_pairs={{0,1},{1,2},{2,3},{3,0},{4,5},{5,6},{6,7},{7,4},{8,9},{9,10},{10,1... | collective-permute-start | bytes 3145736 | tf_op jit(solution)/shard_map/ppermute | solution.py:727
  1095.0 125.9 %collective-permute-start.47 = (f32[576]{0:T(1024)S(1)}, f32[576]{0:T(1024)S(1)}, u32[]{:S(2)}, u32[]{:S(2)}) collective-permute-start(f32[576]{0:T(1024)S(1)} %pad_maximum_fusion.18), channel_id=1, source_target_pairs={{0,1},{1,0},{2,3},{3,2},{4,5},{5,4},{6,7},{7,6},{8,9},{9,8},{10,11... | collective-permute-start | bytes 6920 | tf_op jit(solution)/shard_map/ppermute | solution.py:767
  1123.5 63.8 %collective-permute-start.44 = (bf16[256,4096]{1,0:T(8,128)(2,1)}, bf16[256,4096]{1,0:T(8,128)(2,1)}, u32[]{:S(2)}, u32[]{:S(2)}) collective-permute-start(bf16[256,4096]{1,0:T(8,128)(2,1)} %slice.796), channel_id=1, source_target_pairs={{0,1},{1,2},{2,3},{3,0},{4,5},{5,6},{6,7},{7,4},{8,9},{9,10},{10,1... | collective-permute-start | bytes 6291464 | tf_op jit(solution)/shard_map/ppermute | solution.py:727
  1129.3 33.2 %collective-permute-start.51 = (bf16[4,16,7168]{2,1,0:T(8,128)(2,1)S(1)}, bf16[4,16,7168]{2,1,0:T(8,128)(2,1)S(1)}, u32[]{:S(2)}, u32[]{:S(2)}) collective-permute-start(bf16[4,16,7168]{2,1,0:T(8,128)(2,1)S(1)} %bitcast.252), channel_id=1, source_target_pairs={{0,16},{4,20},{8,24},{12,28},{16,0},{20,4},{24,8},{28,12},{1,17},{... | collective-permute-start | bytes 2752520 | tf_op jit(solution)/shard_map/ppermute | solution.py:744
  1191.0 51.2 %collective-permute-start.46 = (bf16[256,4096]{1,0:T(8,128)(2,1)}, bf16[256,4096]{1,0:T(8,128)(2,1)}, u32[]{:S(2)}, u32[]{:S(2)}) collective-permute-start(bf16[256,4096]{1,0:T(8,128)(2,1)} %add_convert_fusion.1), channel_id=1, source_target_pairs={{0,1},{1,2},{2,3},{3,0},{4,5},{5,6},{6,7},{7,4},{8,9},{9,10},{10,1... | collective-permute-start | bytes 6291464 | tf_op jit(solution)/shard_map/ppermute | solution.py:727
  1202.3 62.8 %collective-permute-start.50 = (bf16[256,384]{1,0:T(8,128)(2,1)S(1)}, bf16[256,384]{1,0:T(8,128)(2,1)S(1)}, u32[]{:S(2)}, u32[]{:S(2)}) collective-permute-start(bf16[256,384]{1,0:T(8,128)(2,1)S(1)} %fusion.194), channel_id=1, source_target_pairs={{0,1},{1,0},{2,3},{3,2},{4,5},{5,4},{6,7},{7,6},{8,9},{9,8},{10,11... | collective-permute-start | bytes 589832 | tf_op jit(solution)/shard_map/ppermute | solution.py:767
  1244.4 48.7 %collective-permute-start.48 = (bf16[256,4096]{1,0:T(8,128)(2,1)S(1)}, bf16[256,4096]{1,0:T(8,128)(2,1)S(1)}, u32[]{:S(2)}, u32[]{:S(2)}) collective-permute-start(bf16[256,4096]{1,0:T(8,128)(2,1)S(1)} %add_convert_fusion), channel_id=1, source_target_pairs={{0,1},{1,2},{2,3},{3,0},{4,5},{5,6},{6,7},{7,4},{8,9},{9,10},{10,1... | collective-permute-start | bytes 6291464 | tf_op jit(solution)/shard_map/ppermute | solution.py:727
  1247.6 43.7 %collective-permute-start.49 = (f32[576]{0:T(1024)S(1)}, f32[576]{0:T(1024)S(1)}, u32[]{:S(2)}, u32[]{:S(2)}) collective-permute-start(f32[576]{0:T(1024)S(1)} %fusion.227), channel_id=1, source_target_pairs={{0,2},{1,3},{2,0},{3,1},{4,6},{5,7},{6,4},{7,5},{8,10},{9,11},{10,... | collective-permute-start | bytes 6920 | tf_op jit(solution)/shard_map/ppermute | solution.py:767
  (168 other events, 2201.9 us)
Sparse Core Ops, SparseCore 0:
  13.3 150.1 all-gather.8
  165.3 37.4 all-gather.10
  204.7 92.0 all-gather.12
  298.5 55.9 all-gather.14
  356.3 61.0 all-gather.16
  419.1 37.4 all-gather.18
  675.6 49.3 reduce-scatter.6
  729.0 78.9 reduce-scatter.8
  844.1 67.9 reduce-scatter.10
  915.6 118.5 reduce-scatter.12
  1038.5 51.3 reduce-scatter.14
  1093.4 183.7 reduce-scatter.16

commit v9 on v8

--- a/solution.py
+++ b/solution.py
@@ -1082,6 +1082,7 @@
     mixer_in, zxs = ring_gather((residual * mixer_root * gain_mixer).astype(bf16), mix)
     zxs = [v[0] for v in zxs]
     grad_scaled, units_rows, mlp_rows = kept
+    mixer_rows = jnp.concatenate(mixer_in, axis=0)
     zx = jnp.concatenate([v[:, : 2 * inner_cols].astype(bf16) for v in zxs], axis=0)
     sd = jnp.concatenate([v[:, 2 * inner_cols :] for v in zxs], axis=0)
     gated, chunk_states = mixer_forward(place, lengths, tp, zx, sd, wide, narrow, rates)
@@ -1124,17 +1125,11 @@
             by_fsdp(bars[:count].reshape(count, 2, LANES)[:, :, :states]),
         ]
 
-    mixer_rows = []
-
-    def out_fill(token, _):
-        mixer_rows.append(jnp.concatenate(tie(mixer_in, token), axis=0))
-        return mm_tn(tie(scaled, token), out_grad_rows).astype(bf16), mixer_rows[0]
-
-    grad_mixer_in, ((sum_w_out, _), sum_w_zx, small) = ring_scatter(
+    grad_mixer_in, (sum_w_out, sum_w_zx, small) = ring_scatter(
         lambda p, t: mm_nt(piece(after(grad_all, t), p), weight_zx),
         [
-            out_fill,
-            lambda t, _: mm_tn(tie(mixer_rows[0], t), grad_all).astype(bf16),
+            lambda t, _: mm_tn(tie(scaled, t), out_grad_rows).astype(bf16),
+            lambda t, _: mm_tn(tie(mixer_rows, t), grad_all).astype(bf16),
             lambda t, _: small_gradients(t),
         ],
     )
@@ -1182,23 +1177,22 @@
     sum_w_fc1 = scatter(sum_w_fc1)
     grad_gate_up_rows = jnp.concatenate(grad_gate_up, axis=0)
     _, grad_mixed_low, grad_gain_mlp = norm_back([mixed], grad_mlp_in, gain_mlp, grad_residual, True)
-    gain_tasks = []
+    gain_task = Halving(
+        jnp.concatenate([grad_gain_mixer.reshape(fsdp, -1), grad_gain_mlp.reshape(fsdp, -1)], axis=1), "fsdp"
+    )
 
     fc_ups = []
 
     def attended_back(p, rows_in):
         result = mm_nt(rows_in, weight_o).astype(bf16)
         if p == 0:
-            middle, first, second = tie((fc_mid, grad_gain_mixer, grad_gain_mlp), rows_in)
             fc_ups.append(
-                mm_tn(jnp.concatenate(middle, axis=0), grad_gate_up_rows[:, : 2 * units_here])
+                mm_tn(tie(jnp.concatenate(fc_mid, axis=0), rows_in), grad_gate_up_rows[:, : 2 * units_here])
             )
-            gains = jnp.concatenate([first.reshape(fsdp, -1), second.reshape(fsdp, -1)], axis=1)
-            result, gains = tie((result, gains), fc_ups[0])
-            gain_tasks.append(Halving(gains, "fsdp"))
+            result = tie(result, fc_ups[0])
         return result
 
-    grad_mixed, grad_attended = ring_gather(tie(grad_mixed_low, sum_w_zx), attended_back, gain_tasks)
+    grad_mixed, grad_attended = ring_gather(tie(grad_mixed_low, sum_w_zx), attended_back, [gain_task])
     sum_w_o = mm_tn(tie(attended, sum_w_fc2), jnp.concatenate(grad_mixed, axis=0)).astype(bf16)
     grad_attended[-1] = tie(grad_attended[-1], sum_w_o)
     sum_w_o = scatter(sum_w_o, 1)
@@ -1231,9 +1225,8 @@
             for j in range(3)
         ]
         ups_grad = jnp.concatenate(grad_up + fc_ups, axis=1)
-        ups_tasks.append(Halving(ups_grad.reshape(fsdp, -1, ups_grad.shape[1]), "fsdp", bf16))
-        ups_tasks[0].start()
-        shared = jnp.concatenate([small_task.result()[small_cuts[4] :], gain_tasks[0].result()])
+        tasks.append(Halving(ups_grad.reshape(fsdp, -1, ups_grad.shape[1]), "fsdp", bf16))
+        shared = jnp.concatenate([small_task.result()[small_cuts[4] :], gain_task.result()])
         tasks.append(Doubling(shared, "tp"))
         return ups_grad, shared
 
@@ -1264,7 +1257,7 @@
         values = jnp.stack([values[:, j * each : (j + 1) * each] for j in range(parts)], axis=1)
         return with_layout_constraint(values, Layout(major_to_minor=(0, 1, 2)))
 
-    tasks, ups_tasks, bc_sums = [], [], []
+    tasks, bc_sums = [], []
     normed_terms = {}
     pair = mm_nt(grad_projected[share : 3 * share], weight_qkv)
     normed_terms[1], normed_terms[2] = piece(pair, 0), piece(pair, 1)
@@ -1284,9 +1277,6 @@
     grad_hidden, grad_embed = norm_back(
         [hidden, embed], grad_normed, gain_attn, grad_residual, with_gain=False
     )
-    ups_tasks[0].finish()
-    grad_ups = ups_tasks[0].result()
-    sum_w_qkv = tie(sum_w_qkv, grad_ups)
     gain_rows = jnp.sum(sum_w_qkv.astype(f32) * own_qkv.astype(f32), axis=1)
     gain_rows = gain_rows / attention_norm_gain.astype(f32)
     grad_down = direct(sum_w_qkv[:, 3 * head_cols :].astype(f32).reshape(tp, -1, 3 * rank), "tp", bf16)
@@ -1296,8 +1286,8 @@
     )
     small_sum = small_task.result()
     small_parts = [small_sum[small_cuts[i] : small_cuts[i + 1]] for i in range(len(small_sizes))]
-    tail = tasks[0].result()
-    shared = tasks[1].result()
+    grad_ups, tail = tasks[0].result(), tasks[1].result()
+    shared = tasks[2].result()
     tail_sizes = [small_sizes[4], width // fsdp, width // fsdp]
     tail_cuts = [sum(tail_sizes[:i]) for i in range(4)]
     grad_conv_bc, sum_gain_mixer, sum_gain_mlp = (

time: 1350 us -> 1330 us (0.985)
  waiting for transfers between devices: 438 us -> 415 us
    ppermute x9, waiting for transfers between devices: 32.5 us -> 11.4 us  [start(): lax.ppermute(sent, self.name, [(i, i ^ half) for i in range(count)])]
    unnamed x323 -> x321, local copies, waits for them, and re-layouts: 64.6 us -> 56.7 us
  transfers between devices with their start and end apart: 73 -> 73, of which waited for: 35 -> 36; matrix products, arithmetic and copies ran while one was open for 45% -> 46% of each run, Pallas kernels for 9% -> 10%
where the time goes in v9:
time: 1330 us; the launch traced here: 1320 us
  matrix products  457 us (34%)
  waiting for transfers between devices  415 us (31%)
  Pallas kernels  145 us (11%)
  local copies, waits for them, and re-layouts  111 us (8%)
  other arithmetic  109 us (8%)
  starting transfers between devices  49.3 us (4%)
  blocking collectives  17.8 us (1%)
  between operations  17.2 us (1%)
    ppermute x39, waiting for transfers between devices, hop(): return lax.ppermute(values, 'tp', ring_pairs())  358 us
    dot_general x24, matrix products, mm_nt(): lax.dot_general(left, right, (((1,), (1,)), ((), ())), preferred_element_...  190 us
    dot_general x23, matrix products, mm(): return jnp.dot(left, right, preferred_element_type=f32)  135 us
    dot_general x10, matrix products, mm_tn(): lax.dot_general(left, right, (((0,), (0,)), ((), ())), preferred_element_...  132 us
    unnamed x321, local copies, waits for them, and re-layouts  56.7 us
    pallas_call x1, Pallas kernels, attention_backward(): pl.pallas_call(functools.partial(attention_backward_kernel, tp, heads), o...  39.4 us
    pallas_call x1, Pallas kernels, mixer_backward(): pl.pallas_call(functools.partial(mixer_backward_kernel, chunks), out_shap...  36.4 us
  transfers between devices with their start and end apart: 73, of which 36 were waited for; matrix products, arithmetic and copies ran while one was open for 46% of the time, Pallas kernels for 10%

profile of v9, /device:TPU:0, one launch (start us, length us, event | category | flops | bytes accessed | tf_op | source)
XLA Modules:
  0.0 1321.4 jit_solution(7234071500247959670)
XLA Ops:
  28.6 9.3 all-gather.1
  52.6 22.4 %collective-permute-done.refs_2_ = bf16[256,2048]{1,0:T(8,128)(2,1)} collective-permute-done((bf16[256,2048]{1,0:T(8,128)(2,1)S(1)}, bf16[256,2048]{1,0:T(8,128)(2,1)}, u32[]{:S(2)}, u32[]{:S(2)}) %collective-permute-start) | collective-permute-done | bytes 1048608 | tf_op jit(solution)/shard_map/ppermute | solution.py:727
  81.8 15.7 %collective-permute-done.3.refs_1_ = bf16[256,2048]{1,0:T(8,128)(2,1)} collective-permute-done((bf16[256,2048]{1,0:T(8,128)(2,1)}, bf16[256,2048]{1,0:T(8,128)(2,1)}, u32[]{:S(2)}, u32[]{:S(2)}) %collective-permute-start.3) | collective-permute-done | bytes 1048608 | tf_op jit(solution)/shard_map/ppermute | solution.py:727
  97.5 21.6 %collective-permute-done.1.refs_0_ = bf16[256,2048]{1,0:T(8,128)(2,1)} collective-permute-done((bf16[256,2048]{1,0:T(8,128)(2,1)}, bf16[256,2048]{1,0:T(8,128)(2,1)}, u32[]{:S(2)}, u32[]{:S(2)}) %collective-permute-start.1) | collective-permute-done | bytes 1048608 | tf_op jit(solution)/shard_map/ppermute | solution.py:727
  124.4 20.2 %collective-permute-done.5 = bf16[32,7168]{1,0:T(8,128)(2,1)S(1)} collective-permute-done((bf16[32,7168]{1,0:T(8,128)(2,1)S(1)}, bf16[32,7168]{1,0:T(8,128)(2,1)S(1)}, u32[]{:S(2)}, u32[]{:S(2)}) %collective-permute-start.5) | collective-permute-done | bytes 458784 | tf_op jit(solution)/shard_map/ppermute | solution.py:884
  151.9 21.0 %collective-permute-done.8.refs_3_ = bf16[256,2048]{1,0:T(8,128)(2,1)} collective-permute-done((bf16[256,2048]{1,0:T(8,128)(2,1)}, bf16[256,2048]{1,0:T(8,128)(2,1)}, u32[]{:S(2)}, u32[]{:S(2)}) %collective-permute-start.8) | collective-permute-done | bytes 1048608 | tf_op jit(solution)/shard_map/ppermute | solution.py:727
  180.3 21.5 %fusion.245.refs_0_.refs_1_.refs_2_.refs_3_ = f32[512,3456]{1,0:T(8,128)S(1)} fusion(bf16[512,4096]{1,0:T(8,128)(2,1)} %bitcast.241, bf16[4096,3456]{1,0:T(8,128)(2,1)} %all-gather.9.cloned.1.call-done), kind=kOutput, calls=%fused_computation.456 | convolution fusion | flops 14495514624 | bytes 39583744 | tf_op jit(solution)/shard_map/dot_general | solution.py:25
  201.9 21.8 %fusion.246.refs_4_.refs_5_.refs_6_.refs_7_ = f32[512,3456]{1,0:T(8,128)S(1)} fusion(bf16[512,4096]{1,0:T(8,128)(2,1)S(1)} %bitcast.244, bf16[4096,3456]{1,0:T(8,128)(2,1)} %all-gather.9.cloned.1.call-done), kind=kOutput, calls=%fused_computation.457 | convolution fusion | flops 14495514624 | bytes 39583744 | tf_op jit(solution)/shard_map/dot_general | solution.py:25
  231.0 21.6 %attention_forward.1 = (bf16[1024,1024]{1,0:T(8,128)(2,1)}, bf16[1024,1024]{1,0:T(8,128)(2,1)}, bf16[1024,1024]{1,0:T(8,128)(2,1)}, bf16[1024,1024]{1,0:T(8,128)(2,1)}) custom-call(s32[1]{0:T(128)} %bitcast.place_ref, s32[3]{0:T(128)} %bitcast.285, f32[1024,128]{1,0:T(8,128)} %get-tuple-element.475.cosine_ref, f32[1024,128]{1,0:T(8,128)} %get-tuple-element.476.sine_ref, ...), custom_call_target="tpu_custom_call" | custom-call | flops 4294967296 | bytes 20971520 | tf_op jit(solution)/shard_map/attention_forward/pallas_call | solution.py:119
  270.1 13.0 collective-permute-done.12
  290.9 18.2 %collective-permute-done.13 = bf16[256,2048]{1,0:T(8,128)(2,1)} collective-permute-done((bf16[256,2048]{1,0:T(8,128)(2,1)S(1)}, bf16[256,2048]{1,0:T(8,128)(2,1)}, u32[]{:S(2)}, u32[]{:S(2)}) %collective-permute-start.13) | collective-permute-done | bytes 1048608 | tf_op jit(solution)/shard_map/ppermute | solution.py:727
  317.7 16.8 %collective-permute-done.14 = bf16[256,2048]{1,0:T(8,128)(2,1)} collective-permute-done((bf16[256,2048]{1,0:T(8,128)(2,1)}, bf16[256,2048]{1,0:T(8,128)(2,1)}, u32[]{:S(2)}, u32[]{:S(2)}) %collective-permute-start.14) | collective-permute-done | bytes 1048608 | tf_op jit(solution)/shard_map/ppermute | solution.py:727
  337.8 9.3 fusion.248
  381.0 8.9 collective-permute-done.17
  413.0 21.9 %collective-permute-done.19 = bf16[256,2048]{1,0:T(8,128)(2,1)S(1)} collective-permute-done((bf16[256,2048]{1,0:T(8,128)(2,1)S(1)}, bf16[256,2048]{1,0:T(8,128)(2,1)S(1)}, u32[]{:S(2)}, u32[]{:S(2)}) %collective-permute-start.19) | collective-permute-done | bytes 1048608 | tf_op jit(solution)/shard_map/ppermute | solution.py:727
  434.9 9.3 fusion.252
  465.2 19.4 %collective-permute-done.20 = bf16[256,2048]{1,0:T(8,128)(2,1)} collective-permute-done((bf16[256,2048]{1,0:T(8,128)(2,1)}, bf16[256,2048]{1,0:T(8,128)(2,1)}, u32[]{:S(2)}, u32[]{:S(2)}) %collective-permute-start.20) | collective-permute-done | bytes 1048608 | tf_op jit(solution)/shard_map/ppermute | solution.py:727
  488.1 8.5 fusion.254
  504.7 9.0 collective-permute-done.21
  520.8 17.6 %collective-permute-done.22 = bf16[256,2048]{1,0:T(8,128)(2,1)S(1)} collective-permute-done((bf16[256,2048]{1,0:T(8,128)(2,1)}, bf16[256,2048]{1,0:T(8,128)(2,1)S(1)}, u32[]{:S(2)}, u32[]{:S(2)}) %collective-permute-start.22) | collective-permute-done | bytes 1048608 | tf_op jit(solution)/shard_map/ppermute | solution.py:727
  542.7 19.6 %collective-permute-done.23 = bf16[256,2048]{1,0:T(8,128)(2,1)S(1)} collective-permute-done((bf16[256,2048]{1,0:T(8,128)(2,1)S(1)}, bf16[256,2048]{1,0:T(8,128)(2,1)S(1)}, u32[]{:S(2)}, u32[]{:S(2)}) %collective-permute-start.23) | collective-permute-done | bytes 1048608 | tf_op jit(solution)/shard_map/ppermute | solution.py:727
  569.2 17.6 %mixer_forward.1 = (bf16[1024,1024]{1,0:T(8,128)(2,1)}, bf16[8,64,1024]{2,1,0:T(8,128)(2,1)}) custom-call(s32[1]{0:T(128)} %bitcast.place_ref, s32[3]{0:T(128)} %bitcast.286, bf16[1024,2048]{1,0:T(8,128)(2,1)} %pad_maximum_fusion.1.zx.before, bf16[1024,2048]{1,0:T(8,128)(2,1)} %pad_maximum_fusion.1.zx.before, f32[1024,384]{1,0:T(8,128)} %pad_maximum_fusion.9.sd.sd_before, ...), custom_call_target="tpu_custom_call" | custom-call | flops 1073741824 | bytes 8388608 | tf_op jit(solution)/shard_map/mixer_forward/pallas_call | solution.py:535
  589.7 8.5 psum.7
  610.7 36.4 %mixer_backward.1 = (bf16[1024,2432]{1,0:T(8,128)(2,1)}, f32[8,1024]{1,0:T(8,128)}, f32[8,256]{1,0:T(8,128)}, f32[8,128]{1,0:T(8,128)}) custom-call(s32[1]{0:T(128)} %bitcast.place_ref, s32[3]{0:T(128)} %bitcast.287, bf16[1024,2048]{1,0:T(8,128)(2,1)} %pad_maximum_fusion.1.zx.before, bf16[1024,2048]{1,0:T(8,128)(2,1)} %pad_maximum_fusion.1.zx.before, ...), custom_call_target="tpu_custom_call" | custom-call | flops 3221225472 | bytes 12582912 | tf_op jit(solution)/shard_map/mixer_backward/pallas_call | solution.py:573
  647.2 8.5 convolution_convert_fusion.6
  681.6 16.2 %convolution_convert_fusion.2 = bf16[2048,2432]{1,0:T(8,128)(2,1)} fusion(bf16[1024,2048]{1,0:T(8,128)(2,1)S(1)} %pad_maximum_fusion.2, bf16[1024,2432]{1,0:T(8,128)(2,1)} %get-tuple-element.244), kind=kOutput, calls=%fused_computation.2 | convolution fusion | flops 10205528064 | bytes 19136512 | tf_op jit(solution)/shard_map/dot_general | solution.py:33
  721.7 8.8 collective-permute-done.28
  740.8 9.3 fusion.115
  752.2 13.6 %fusion.79 = f32[256,2048]{1,0:T(8,128)} fusion(bf16[2048,4224]{1,0:T(8,128)(2,1)} %all-gather.13.cloned.1.call-done, bf16[256,128]{1,0:T(8,128)(2,1)S(1)} %fusion.181, bf16[256,2048]{1,0:T(8,128)(2,1)} %copy-done.121, bf16[256,2048]{1,0:T(8,128)(2,1)} %copy-done.119), kind=kOutput, calls=%fused_computation.134 | convolution fusion | flops 4435673088 | bytes 21561344 | tf_op jit(solution)/shard_map/dot_general | solution.py:29
  778.0 12.7 fusion.85
  802.5 13.0 fusion.91
  819.4 13.9 %convolution_convert_fusion.3 = bf16[2048,2048]{1,0:T(8,128)(2,1)} fusion(bf16[1024,2048]{1,0:T(8,128)(2,1)} %pad_maximum_fusion.3, bf16[256,2048]{1,0:T(8,128)(2,1)} %collective-permute-done.33, bf16[256,2048]{1,0:T(8,128)(2,1)} %collective-permute-done.31, bf16[256,2048]{1,0:T(8,128)(2,1)} %collective-permute-done.29, bf16[256,2048]{1,0:T(8,128)(2,1)S(1)} %copy-done.117), kind=kOutput, calls=%fused_computation.51 | convolution fusion | flops 8610906112 | bytes 16777216 | tf_op jit(solution)/shard_map/dot_general | solution.py:33
  833.4 12.5 collective-permute-done.35
  850.2 8.9 fusion.109
  861.1 9.1 fusion.97
  879.3 29.5 %convolution_convert_fusion.1 = bf16[2048,4224]{1,0:T(8,128)(2,1)} fusion(bf16[1024,2048]{1,0:T(8,128)(2,1)} %copy-done.78, bf16[256,128]{1,0:T(8,128)(2,1)S(1)} %fusion.172, bf16[256,2048]{1,0:T(8,128)(2,1)} %copy-done.127, bf16[256,2048]{1,0:T(8,128)(2,1)} %copy-done.126, bf16[256,128]{1,0:T(8,128)(2,1)S(1)} %fusion.175, ...), kind=kOutput, calls=%fused_computation.1 | convolution fusion | flops 17829199872 | bytes 30146560 | tf_op jit(solution)/shard_map/dot_general | solution.py:33
  924.3 17.5 %fusion.23 = f32[128,4096]{1,0:T(8,128)} fusion(bf16[1024,128]{1,0:T(8,128)(2,1)S(1)} %pad_maximum_fusion.16, bf16[256,128]{1,0:T(8,128)(2,1)S(1)} %copy-done.133, bf16[256,2048]{1,0:T(8,128)(2,1)} %copy-done.127, bf16[256,2048]{1,0:T(8,128)(2,1)} %copy-done.126, bf16[256,128]{1,0:T(8,128)(2,1)S(1)} %copy-done.131, bf16[256,2048]{1,0:T(8,128)(2,1)} %copy-done.125, ...), kind=kOutput, calls=%fused_computation.26 | convolution fusion | flops 1174405120 | bytes 11010048 | tf_op jit(solution)/shard_map/dot_general | solution.py:33
  952.8 20.1 %collective-permute-done.40 = bf16[256,2048]{1,0:T(8,128)(2,1)} collective-permute-done((bf16[256,2048]{1,0:T(8,128)(2,1)S(1)}, bf16[256,2048]{1,0:T(8,128)(2,1)}, u32[]{:S(2)}, u32[]{:S(2)}) %collective-permute-start.40) | collective-permute-done | bytes 1048608 | tf_op jit(solution)/shard_map/ppermute | solution.py:727
  978.6 22.6 %collective-permute-done.42 = bf16[256,2048]{1,0:T(8,128)(2,1)} collective-permute-done((bf16[256,2048]{1,0:T(8,128)(2,1)}, bf16[256,2048]{1,0:T(8,128)(2,1)}, u32[]{:S(2)}, u32[]{:S(2)}) %collective-permute-start.42) | collective-permute-done | bytes 1048608 | tf_op jit(solution)/shard_map/ppermute | solution.py:727
  1001.1 9.2 fusion.70
  1015.5 39.4 %attention_backward.1 = bf16[1024,3456]{1,0:T(8,128)(2,1)} custom-call(s32[1]{0:T(128)} %bitcast.place_ref, s32[3]{0:T(128)} %bitcast.288, f32[1024,128]{1,0:T(8,128)} %get-tuple-element.475.cosine_ref, f32[1024,128]{1,0:T(8,128)} %get-tuple-element.476.sine_ref, bf16[1024,1024]{1,0:T(8,128)(2,1)} %get-tuple-element.232.q_ref, ...), custom_call_target="tpu_custom_call" | custom-call | flops 10737418240 | bytes 14680064 | tf_op jit(solution)/shard_map/attention_backward/pallas_call | solution.py:233
  1056.8 38.0 %convolution_convert_fusion = bf16[4096,3456]{1,0:T(8,128)(2,1)} fusion(bf16[1024,4096]{1,0:T(8,128)(2,1)} %pad_maximum_fusion, bf16[1024,3456]{1,0:T(8,128)(2,1)} %attention_backward.1), kind=kOutput, calls=%fused_computation | convolution fusion | flops 29005185024 | bytes 43778048 | tf_op jit(solution)/shard_map/dot_general | solution.py:33
  1098.9 21.4 %fusion.73 = f32[512,4096]{1,0:T(8,128)S(1)} fusion(bf16[4096,3456]{1,0:T(8,128)(2,1)} %all-gather.9.cloned.1.call-done, bf16[1024,3456]{1,0:T(8,128)(2,1)} %attention_backward.1), kind=kOutput, calls=%fused_computation.115 | convolution fusion | flops 14495514624 | bytes 40239104 | tf_op jit(solution)/shard_map/dot_general | solution.py:29
  1141.6 17.8 %fusion.163 = f32[256,4096]{1,0:T(8,128)} fusion(bf16[4096,3456]{1,0:T(8,128)(2,1)} %all-gather.9.cloned.1.call-done, bf16[1024,3456]{1,0:T(8,128)(2,1)} %attention_backward.1), kind=kOutput, calls=%fused_computation.253 | convolution fusion | flops 7247757312 | bytes 34275328 | tf_op jit(solution)/shard_map/dot_general | solution.py:29
  1159.4 9.4 collective-permute-done.45
  1203.1 10.6 collective-permute-done.47
  1228.5 15.9 %fusion.161 = f32[256,4096]{1,0:T(8,128)} fusion(bf16[4096,3456]{1,0:T(8,128)(2,1)} %all-gather.9.cloned.1.call-done, bf16[1024,3456]{1,0:T(8,128)(2,1)} %attention_backward.1), kind=kOutput, calls=%fused_computation.251 | convolution fusion | flops 7247757312 | bytes 34275328 | tf_op jit(solution)/shard_map/dot_general | solution.py:29
  1244.4 13.8 %collective-permute-done.51 = f32[576]{0:T(1024)S(1)} collective-permute-done((f32[576]{0:T(1024)S(1)}, f32[576]{0:T(1024)S(1)}, u32[]{:S(2)}, u32[]{:S(2)}) %collective-permute-start.51) | collective-permute-done | bytes 2336 | tf_op jit(solution)/shard_map/ppermute | solution.py:767
  (720 shorter events, 503.3 us)
Async XLA Ops:
  7.2 173.1 %all-gather.9.cloned.1.call-start = ((), (), s32[]{:S(2)}) async-start(), calls=%async_computation.6 | async-start | bytes 31850496 | tf_op jit(solution)/shard_map/all_gather | solution.py:898
  13.1 241.6 %all-gather.11.cloned.1.call-start = ((), (), s32[]{:S(2)}) async-start(), calls=%async_computation.7 | async-start | bytes 4718592 | tf_op jit(solution)/shard_map/all_gather | solution.py:898
  13.9 323.9 %all-gather.13.cloned.1.call-start = ((), (), s32[]{:S(2)}) async-start(), calls=%async_computation.8 | async-start | bytes 19464192 | tf_op jit(solution)/shard_map/all_gather | solution.py:898
  22.5 332.0 %all-gather.15.cloned.1.call-start = ((), (), s32[]{:S(2)}) async-start(), calls=%async_computation.9 | async-start | bytes 9437184 | tf_op jit(solution)/shard_map/all_gather | solution.py:898
  23.1 465.0 %all-gather.17.cloned.1.call-start = ((), (), s32[]{:S(2)}) async-start(), calls=%async_computation.10 | async-start | bytes 11206656 | tf_op jit(solution)/shard_map/all_gather | solution.py:898
  23.2 29.4 %collective-permute-start.2 = (bf16[256,2048]{1,0:T(8,128)(2,1)}, bf16[256,2048]{1,0:T(8,128)(2,1)}, u32[]{:S(2)}, u32[]{:S(2)}) collective-permute-start(bf16[256,2048]{1,0:T(8,128)(2,1)} %refs_1_.3), channel_id=1, source_target_pairs={{0,1},{1,2},{2,3},{3,0},{4,5},{5,6},{6,7},{7,4},{8,9},{9,10},{10,1... | collective-permute-start | bytes 3145736 | tf_op jit(solution)/shard_map/ppermute | solution.py:727
  26.2 48.8 %collective-permute-start = (bf16[256,2048]{1,0:T(8,128)(2,1)S(1)}, bf16[256,2048]{1,0:T(8,128)(2,1)}, u32[]{:S(2)}, u32[]{:S(2)}) collective-permute-start(bf16[256,2048]{1,0:T(8,128)(2,1)S(1)} %copy-done.10), channel_id=1, source_target_pairs={{0,1},{1,2},{2,3},{3,0},{4,5},{5,6},{6,7},{7,4},{8,9},{9,10},{10,1... | collective-permute-start | bytes 3145736 | tf_op jit(solution)/shard_map/ppermute | solution.py:727
  52.6 44.9 %collective-permute-start.3 = (bf16[256,2048]{1,0:T(8,128)(2,1)}, bf16[256,2048]{1,0:T(8,128)(2,1)}, u32[]{:S(2)}, u32[]{:S(2)}) collective-permute-start(bf16[256,2048]{1,0:T(8,128)(2,1)} %collective-permute-done.2.refs_3_), channel_id=1, source_target_pairs={{0,1},{1,2},{2,3},{3,0},{4,5},{5,6},{6,7},{7,4},{8,9},{9,10},{10,1... | collective-permute-start | bytes 3145736 | tf_op jit(solution)/shard_map/ppermute | solution.py:727
  75.0 44.1 %collective-permute-start.1 = (bf16[256,2048]{1,0:T(8,128)(2,1)}, bf16[256,2048]{1,0:T(8,128)(2,1)}, u32[]{:S(2)}, u32[]{:S(2)}) collective-permute-start(bf16[256,2048]{1,0:T(8,128)(2,1)} %collective-permute-done.refs_2_), channel_id=1, source_target_pairs={{0,1},{1,2},{2,3},{3,0},{4,5},{5,6},{6,7},{7,4},{8,9},{9,10},{10,1... | collective-permute-start | bytes 3145736 | tf_op jit(solution)/shard_map/ppermute | solution.py:727
  121.4 375.2 %all-gather.19.cloned.1.call-start = ((), (), s32[]{:S(2)}) async-start(), calls=%async_computation.11 | async-start | bytes 4718592 | tf_op jit(solution)/shard_map/all_gather | solution.py:898
  123.1 28.8 %collective-permute-start.7 = (bf16[256,2048]{1,0:T(8,128)(2,1)}, bf16[256,2048]{1,0:T(8,128)(2,1)}, u32[]{:S(2)}, u32[]{:S(2)}) collective-permute-start(bf16[256,2048]{1,0:T(8,128)(2,1)} %collective-permute-done.1.refs_0_), channel_id=1, source_target_pairs={{0,1},{1,2},{2,3},{3,0},{4,5},{5,6},{6,7},{7,4},{8,9},{9,10},{10,1... | collective-permute-start | bytes 3145736 | tf_op jit(solution)/shard_map/ppermute | solution.py:727
  123.1 49.9 %collective-permute-start.8 = (bf16[256,2048]{1,0:T(8,128)(2,1)}, bf16[256,2048]{1,0:T(8,128)(2,1)}, u32[]{:S(2)}, u32[]{:S(2)}) collective-permute-start(bf16[256,2048]{1,0:T(8,128)(2,1)} %collective-permute-done.3.refs_1_), channel_id=1, source_target_pairs={{0,1},{1,2},{2,3},{3,0},{4,5},{5,6},{6,7},{7,4},{8,9},{9,10},{10,1... | collective-permute-start | bytes 3145736 | tf_op jit(solution)/shard_map/ppermute | solution.py:727
  145.9 32.8 %collective-permute-start.6 = (bf16[64,7168]{1,0:T(8,128)(2,1)}, bf16[64,7168]{1,0:T(8,128)(2,1)}, u32[]{:S(2)}, u32[]{:S(2)}) collective-permute-start(bf16[64,7168]{1,0:T(8,128)(2,1)} %pad_maximum_fusion.10), channel_id=1, source_target_pairs={{0,16},{4,20},{8,24},{12,28},{16,0},{20,4},{24,8},{28,12},{1,17},{... | collective-permute-start | bytes 2752520 | tf_op jit(solution)/shard_map/ppermute | solution.py:884
  173.0 28.8 %collective-permute-start.9 = (bf16[256,2048]{1,0:T(8,128)(2,1)S(1)}, bf16[256,2048]{1,0:T(8,128)(2,1)}, u32[]{:S(2)}, u32[]{:S(2)}) collective-permute-start(bf16[256,2048]{1,0:T(8,128)(2,1)S(1)} %copy-done.26), channel_id=1, source_target_pairs={{0,1},{1,2},{2,3},{3,0},{4,5},{5,6},{6,7},{7,4},{8,9},{9,10},{10,1... | collective-permute-start | bytes 3145736 | tf_op jit(solution)/shard_map/ppermute | solution.py:727
  201.8 26.6 %collective-permute-start.10 = (bf16[256,2048]{1,0:T(8,128)(2,1)}, bf16[256,2048]{1,0:T(8,128)(2,1)S(1)}, u32[]{:S(2)}, u32[]{:S(2)}) collective-permute-start(bf16[256,2048]{1,0:T(8,128)(2,1)} %collective-permute-done.9), channel_id=1, source_target_pairs={{0,1},{1,2},{2,3},{3,0},{4,5},{5,6},{6,7},{7,4},{8,9},{9,10},{10,1... | collective-permute-start | bytes 3145736 | tf_op jit(solution)/shard_map/ppermute | solution.py:727
  228.4 25.4 %collective-permute-start.11 = (bf16[256,2048]{1,0:T(8,128)(2,1)S(1)}, bf16[256,2048]{1,0:T(8,128)(2,1)S(1)}, u32[]{:S(2)}, u32[]{:S(2)}) collective-permute-start(bf16[256,2048]{1,0:T(8,128)(2,1)S(1)} %collective-permute-done.10), channel_id=1, source_target_pairs={{0,1},{1,2},{2,3},{3,0},{4,5},{5,6},{6,7},{7,4},{8,9},{9,10},{10,1... | collective-permute-start | bytes 3145736 | tf_op jit(solution)/shard_map/ppermute | solution.py:727
  285.7 533.8 %reduce-scatter.7.cloned.1.call-start = ((), (), s32[]{:S(2)}) async-start(), calls=%async_computation.12 | async-start | bytes 4718592 | tf_op jit(solution)/shard_map/reduce_scatter | solution.py:902
  361.7 28.2 %collective-permute-start.17 = (bf16[256,2048]{1,0:T(8,128)(2,1)}, bf16[256,2048]{1,0:T(8,128)(2,1)S(1)}, u32[]{:S(2)}, u32[]{:S(2)}) collective-permute-start(bf16[256,2048]{1,0:T(8,128)(2,1)} %collective-permute-done.15), channel_id=1, source_target_pairs={{0,1},{1,2},{2,3},{3,0},{4,5},{5,6},{6,7},{7,4},{8,9},{9,10},{10,1... | collective-permute-start | bytes 3145736 | tf_op jit(solution)/shard_map/ppermute | solution.py:727
  379.6 32.8 %collective-permute-start.16 = (bf16[256,2048]{1,0:T(8,128)(2,1)S(1)}, bf16[256,2048]{1,0:T(8,128)(2,1)S(1)}, u32[]{:S(2)}, u32[]{:S(2)}) collective-permute-start(bf16[256,2048]{1,0:T(8,128)(2,1)S(1)} %convolution_convert_fusion.8), channel_id=1, source_target_pairs={{0,1},{1,2},{2,3},{3,0},{4,5},{5,6},{6,7},{7,4},{8,9},{9,10},{10,1... | collective-permute-start | bytes 3145736 | tf_op jit(solution)/shard_map/ppermute | solution.py:727
  389.9 44.9 %collective-permute-start.19 = (bf16[256,2048]{1,0:T(8,128)(2,1)S(1)}, bf16[256,2048]{1,0:T(8,128)(2,1)S(1)}, u32[]{:S(2)}, u32[]{:S(2)}) collective-permute-start(bf16[256,2048]{1,0:T(8,128)(2,1)S(1)} %collective-permute-done.17), channel_id=1, source_target_pairs={{0,1},{1,2},{2,3},{3,0},{4,5},{5,6},{6,7},{7,4},{8,9},{9,10},{10,1... | collective-permute-start | bytes 3145736 | tf_op jit(solution)/shard_map/ppermute | solution.py:727
  412.7 43.9 %collective-permute-start.18 = (bf16[256,2048]{1,0:T(8,128)(2,1)S(1)}, bf16[256,2048]{1,0:T(8,128)(2,1)S(1)}, u32[]{:S(2)}, u32[]{:S(2)}) collective-permute-start(bf16[256,2048]{1,0:T(8,128)(2,1)S(1)} %add_convert_fusion.9), channel_id=1, source_target_pairs={{0,1},{1,2},{2,3},{3,0},{4,5},{5,6},{6,7},{7,4},{8,9},{9,10},{10,1... | collective-permute-start | bytes 3145736 | tf_op jit(solution)/shard_map/ppermute | solution.py:727
  458.0 26.6 %collective-permute-start.20 = (bf16[256,2048]{1,0:T(8,128)(2,1)}, bf16[256,2048]{1,0:T(8,128)(2,1)}, u32[]{:S(2)}, u32[]{:S(2)}) collective-permute-start(bf16[256,2048]{1,0:T(8,128)(2,1)} %add_convert_fusion.8), channel_id=1, source_target_pairs={{0,1},{1,2},{2,3},{3,0},{4,5},{5,6},{6,7},{7,4},{8,9},{9,10},{10,1... | collective-permute-start | bytes 3145736 | tf_op jit(solution)/shard_map/ppermute | solution.py:727
  487.9 25.9 %collective-permute-start.21 = (bf16[256,2048]{1,0:T(8,128)(2,1)}, bf16[256,2048]{1,0:T(8,128)(2,1)}, u32[]{:S(2)}, u32[]{:S(2)}) collective-permute-start(bf16[256,2048]{1,0:T(8,128)(2,1)} %multiply_convert_fusion.4), channel_id=1, source_target_pairs={{0,1},{1,2},{2,3},{3,0},{4,5},{5,6},{6,7},{7,4},{8,9},{9,10},{10,1... | collective-permute-start | bytes 3145736 | tf_op jit(solution)/shard_map/ppermute | solution.py:727
  607.5 39.6 %collective-permute-start.24 = (bf16[256,2048]{1,0:T(8,128)(2,1)S(1)}, bf16[256,2048]{1,0:T(8,128)(2,1)S(1)}, u32[]{:S(2)}, u32[]{:S(2)}) collective-permute-start(bf16[256,2048]{1,0:T(8,128)(2,1)S(1)} %slice.504), channel_id=1, source_target_pairs={{0,1},{1,2},{2,3},{3,0},{4,5},{5,6},{6,7},{7,4},{8,9},{9,10},{10,1... | collective-permute-start | bytes 3145736 | tf_op jit(solution)/shard_map/ppermute | solution.py:727
  676.3 248.0 %reduce-scatter.9.cloned.1.call-start = ((), (), s32[]{:S(2)}) async-start(), calls=%async_computation.13 | async-start | bytes 11206656 | tf_op jit(solution)/shard_map/reduce_scatter | solution.py:902
  681.4 24.8 %collective-permute-start.27 = (bf16[256,2048]{1,0:T(8,128)(2,1)}, bf16[256,2048]{1,0:T(8,128)(2,1)S(1)}, u32[]{:S(2)}, u32[]{:S(2)}) collective-permute-start(bf16[256,2048]{1,0:T(8,128)(2,1)} %add_convert_fusion.6), channel_id=1, source_target_pairs={{0,1},{1,2},{2,3},{3,0},{4,5},{5,6},{6,7},{7,4},{8,9},{9,10},{10,1... | collective-permute-start | bytes 3145736 | tf_op jit(solution)/shard_map/ppermute | solution.py:727
  707.2 271.3 %reduce-scatter.11.cloned.1.call-start = ((), (), s32[]{:S(2)}) async-start(), calls=%async_computation.14 | async-start | bytes 9437184 | tf_op jit(solution)/shard_map/reduce_scatter | solution.py:902
  730.6 35.1 %collective-permute-start.30 = (f32[4,864]{1,0:T(4,128)S(1)}, f32[4,864]{1,0:T(4,128)S(1)}, u32[]{:S(2)}, u32[]{:S(2)}) collective-permute-start(f32[4,864]{1,0:T(4,128)S(1)} %slice_select_fusion.1), channel_id=1, source_target_pairs={{0,16},{4,20},{8,24},{12,28},{16,0},{20,4},{24,8},{28,12},{1,17},{... | collective-permute-start | bytes 41480 | tf_op jit(solution)/shard_map/ppermute | solution.py:744
  740.5 25.2 %collective-permute-start.29 = (bf16[256,2048]{1,0:T(8,128)(2,1)}, bf16[256,2048]{1,0:T(8,128)(2,1)}, u32[]{:S(2)}, u32[]{:S(2)}) collective-permute-start(bf16[256,2048]{1,0:T(8,128)(2,1)} %get-tuple-element.253), channel_id=1, source_target_pairs={{0,1},{1,2},{2,3},{3,0},{4,5},{5,6},{6,7},{7,4},{8,9},{9,10},{10,1... | collective-permute-start | bytes 3145736 | tf_op jit(solution)/shard_map/ppermute | solution.py:727
  765.8 24.9 %collective-permute-start.32 = (f32[2,864]{1,0:T(2,128)S(1)}, f32[2,864]{1,0:T(2,128)S(1)}, u32[]{:S(2)}, u32[]{:S(2)}) collective-permute-start(f32[2,864]{1,0:T(2,128)S(1)} %broadcast_select_fusion.8), channel_id=1, source_target_pairs={{0,8},{4,12},{8,0},{12,4},{16,24},{20,28},{24,16},{28,20},{1,9},{5... | collective-permute-start | bytes 20744 | tf_op jit(solution)/shard_map/ppermute | solution.py:744
  790.9 28.0 %collective-permute-start.33 = (bf16[256,2048]{1,0:T(8,128)(2,1)}, bf16[256,2048]{1,0:T(8,128)(2,1)}, u32[]{:S(2)}, u32[]{:S(2)}) collective-permute-start(bf16[256,2048]{1,0:T(8,128)(2,1)} %collective-permute-done.31), channel_id=1, source_target_pairs={{0,1},{1,2},{2,3},{3,0},{4,5},{5,6},{6,7},{7,4},{8,9},{9,10},{10,1... | collective-permute-start | bytes 3145736 | tf_op jit(solution)/shard_map/ppermute | solution.py:727
  818.8 27.1 %collective-permute-start.35 = (bf16[256,2048]{1,0:T(8,128)(2,1)}, bf16[256,2048]{1,0:T(8,128)(2,1)S(1)}, u32[]{:S(2)}, u32[]{:S(2)}) collective-permute-start(bf16[256,2048]{1,0:T(8,128)(2,1)} %fusion.85), channel_id=1, source_target_pairs={{0,1},{1,2},{2,3},{3,0},{4,5},{5,6},{6,7},{7,4},{8,9},{9,10},{10,1... | collective-permute-start | bytes 3145736 | tf_op jit(solution)/shard_map/ppermute | solution.py:727
  846.9 208.0 %reduce-scatter.13.cloned.1.call-start = ((), (), s32[]{:S(2)}) async-start(), calls=%async_computation.15 | async-start | bytes 19464192 | tf_op jit(solution)/shard_map/reduce_scatter | solution.py:902
  850.2 26.1 %collective-permute-start.36 = (bf16[256,2048]{1,0:T(8,128)(2,1)}, bf16[256,2048]{1,0:T(8,128)(2,1)}, u32[]{:S(2)}, u32[]{:S(2)}) collective-permute-start(bf16[256,2048]{1,0:T(8,128)(2,1)} %add_convert_fusion.4), channel_id=1, source_target_pairs={{0,1},{1,2},{2,3},{3,0},{4,5},{5,6},{6,7},{7,4},{8,9},{9,10},{10,1... | collective-permute-start | bytes 3145736 | tf_op jit(solution)/shard_map/ppermute | solution.py:727
  878.8 30.0 %collective-permute-start.37 = (bf16[256,2048]{1,0:T(8,128)(2,1)}, bf16[256,2048]{1,0:T(8,128)(2,1)S(1)}, u32[]{:S(2)}, u32[]{:S(2)}) collective-permute-start(bf16[256,2048]{1,0:T(8,128)(2,1)} %add_convert_fusion.3), channel_id=1, source_target_pairs={{0,1},{1,2},{2,3},{3,0},{4,5},{5,6},{6,7},{7,4},{8,9},{9,10},{10,1... | collective-permute-start | bytes 3145736 | tf_op jit(solution)/shard_map/ppermute | solution.py:727
  908.8 269.2 %reduce-scatter.15.cloned.1.call-start = ((), (), s32[]{:S(2)}) async-start(), calls=%async_computation.16 | async-start | bytes 4718592 | tf_op jit(solution)/shard_map/reduce_scatter | solution.py:902
  972.9 28.2 %collective-permute-start.42 = (bf16[256,2048]{1,0:T(8,128)(2,1)}, bf16[256,2048]{1,0:T(8,128)(2,1)}, u32[]{:S(2)}, u32[]{:S(2)}) collective-permute-start(bf16[256,2048]{1,0:T(8,128)(2,1)} %collective-permute-done.40), channel_id=1, source_target_pairs={{0,1},{1,2},{2,3},{3,0},{4,5},{5,6},{6,7},{7,4},{8,9},{9,10},{10,1... | collective-permute-start | bytes 3145736 | tf_op jit(solution)/shard_map/ppermute | solution.py:727
  974.7 80.2 %collective-permute-start.25 = (bf16[256,2048]{1,0:T(8,128)(2,1)S(1)}, bf16[256,2048]{1,0:T(8,128)(2,1)S(1)}, u32[]{:S(2)}, u32[]{:S(2)}) collective-permute-start(bf16[256,2048]{1,0:T(8,128)(2,1)S(1)} %add_convert_fusion.7), channel_id=1, source_target_pairs={{0,1},{1,2},{2,3},{3,0},{4,5},{5,6},{6,7},{7,4},{8,9},{9,10},{10,1... | collective-permute-start | bytes 3145736 | tf_op jit(solution)/shard_map/ppermute | solution.py:727
  1015.4 274.3 %reduce-scatter.17.cloned.1.call-start = ((), (), s32[]{:S(2)}) async-start(), calls=%async_computation.17 | async-start | bytes 31850496 | tf_op jit(solution)/shard_map/reduce_scatter | solution.py:902
  1056.5 38.3 %collective-permute-start.44 = (bf16[256,2048]{1,0:T(8,128)(2,1)S(1)}, bf16[256,2048]{1,0:T(8,128)(2,1)S(1)}, u32[]{:S(2)}, u32[]{:S(2)}) collective-permute-start(bf16[256,2048]{1,0:T(8,128)(2,1)S(1)} %add_convert_fusion.2), channel_id=1, source_target_pairs={{0,1},{1,2},{2,3},{3,0},{4,5},{5,6},{6,7},{7,4},{8,9},{9,10},{10,1... | collective-permute-start | bytes 3145736 | tf_op jit(solution)/shard_map/ppermute | solution.py:727
  1098.9 104.2 %collective-permute-start.48 = (f32[576]{0:T(1024)S(1)}, f32[576]{0:T(1024)S(1)}, u32[]{:S(2)}, u32[]{:S(2)}) collective-permute-start(f32[576]{0:T(1024)S(1)} %pad_maximum_fusion.19), channel_id=1, source_target_pairs={{0,1},{1,0},{2,3},{3,2},{4,5},{5,4},{6,7},{7,6},{8,9},{9,8},{10,11... | collective-permute-start | bytes 6920 | tf_op jit(solution)/shard_map/ppermute | solution.py:767
  1126.3 42.6 %collective-permute-start.45 = (bf16[256,4096]{1,0:T(8,128)(2,1)}, bf16[256,4096]{1,0:T(8,128)(2,1)}, u32[]{:S(2)}, u32[]{:S(2)}) collective-permute-start(bf16[256,4096]{1,0:T(8,128)(2,1)} %slice.804), channel_id=1, source_target_pairs={{0,1},{1,2},{2,3},{3,0},{4,5},{5,6},{6,7},{7,4},{8,9},{9,10},{10,1... | collective-permute-start | bytes 6291464 | tf_op jit(solution)/shard_map/ppermute | solution.py:727
  1172.4 49.0 %collective-permute-start.46 = (bf16[256,4096]{1,0:T(8,128)(2,1)}, bf16[256,4096]{1,0:T(8,128)(2,1)}, u32[]{:S(2)}, u32[]{:S(2)}) collective-permute-start(bf16[256,4096]{1,0:T(8,128)(2,1)} %add_convert_fusion.1), channel_id=1, source_target_pairs={{0,1},{1,2},{2,3},{3,0},{4,5},{5,6},{6,7},{7,4},{8,9},{9,10},{10,1... | collective-permute-start | bytes 6291464 | tf_op jit(solution)/shard_map/ppermute | solution.py:727
  1177.7 36.0 %collective-permute-start.47 = (bf16[4,16,7168]{2,1,0:T(8,128)(2,1)}, bf16[4,16,7168]{2,1,0:T(8,128)(2,1)S(1)}, u32[]{:S(2)}, u32[]{:S(2)}) collective-permute-start(bf16[4,16,7168]{2,1,0:T(8,128)(2,1)} %bitcast.37), channel_id=1, source_target_pairs={{0,16},{4,20},{8,24},{12,28},{16,0},{20,4},{24,8},{28,12},{1,17},{... | collective-permute-start | bytes 2752520 | tf_op jit(solution)/shard_map/ppermute | solution.py:744
  1183.6 60.8 %collective-permute-start.52 = (bf16[256,384]{1,0:T(8,128)(2,1)S(1)}, bf16[256,384]{1,0:T(8,128)(2,1)S(1)}, u32[]{:S(2)}, u32[]{:S(2)}) collective-permute-start(bf16[256,384]{1,0:T(8,128)(2,1)S(1)} %fusion.194), channel_id=1, source_target_pairs={{0,1},{1,0},{2,3},{3,2},{4,5},{5,4},{6,7},{7,6},{8,9},{9,8},{10,11... | collective-permute-start | bytes 589832 | tf_op jit(solution)/shard_map/ppermute | solution.py:767
  1223.6 37.3 %collective-permute-start.49 = (bf16[256,4096]{1,0:T(8,128)(2,1)S(1)}, bf16[256,4096]{1,0:T(8,128)(2,1)}, u32[]{:S(2)}, u32[]{:S(2)}) collective-permute-start(bf16[256,4096]{1,0:T(8,128)(2,1)S(1)} %add_convert_fusion), channel_id=1, source_target_pairs={{0,1},{1,2},{2,3},{3,0},{4,5},{5,6},{6,7},{7,4},{8,9},{9,10},{10,1... | collective-permute-start | bytes 6291464 | tf_op jit(solution)/shard_map/ppermute | solution.py:727
  1225.2 33.0 %collective-permute-start.51 = (f32[576]{0:T(1024)S(1)}, f32[576]{0:T(1024)S(1)}, u32[]{:S(2)}, u32[]{:S(2)}) collective-permute-start(f32[576]{0:T(1024)S(1)} %fusion.220), channel_id=1, source_target_pairs={{0,2},{1,3},{2,0},{3,1},{4,6},{5,7},{6,4},{7,5},{8,10},{9,11},{10,... | collective-permute-start | bytes 6920 | tf_op jit(solution)/shard_map/ppermute | solution.py:767
  1228.2 30.0 %collective-permute-start.50 = (bf16[2,16,7168]{2,1,0:T(8,128)(2,1)S(1)}, bf16[2,16,7168]{2,1,0:T(8,128)(2,1)S(1)}, u32[]{:S(2)}, u32[]{:S(2)}) collective-permute-start(bf16[2,16,7168]{2,1,0:T(8,128)(2,1)S(1)} %select_convert_fusion.1), channel_id=1, source_target_pairs={{0,8},{4,12},{8,0},{12,4},{16,24},{20,28},{24,16},{28,20},{1,9},{5... | collective-permute-start | bytes 1376264 | tf_op jit(solution)/shard_map/ppermute | solution.py:744
  (168 other events, 2085.6 us)
Sparse Core Ops, SparseCore 0:
  13.2 150.1 all-gather.8
  165.3 37.4 all-gather.10
  204.7 92.0 all-gather.12
  298.5 55.9 all-gather.14
  356.2 61.0 all-gather.16
  419.0 37.4 all-gather.18
  676.4 48.5 reduce-scatter.6
  729.1 79.0 reduce-scatter.8
  847.0 68.5 reduce-scatter.10
  919.1 118.5 reduce-scatter.12
  1042.0 51.3 reduce-scatter.14
  1096.9 192.8 reduce-scatter.16
